TPU v7x, 32 devices: a whole 2x2x4 slice. The times are simulated.
32 devices in a mesh: dp: 8 (over z, x), tensor: 4 (over y, core).
Axes of the slice: x: 2, y: 2, z: 4, core: 2. Of those that a mesh axis runs over, the one named last changes fastest.
Arguments:
- layer_input: bfloat16 [32768, 1024], P(('dp', 'tensor')), may hold values from -6 to 6
- row_ids: int32 [32768], P('dp'), may hold values from 0 to 1, as said below
- input_gain: bfloat16 [1024], replicated, may hold values from 0.5 to 1.5
- input_shift: bfloat16 [1024], replicated, may hold values from -1.796875 to 1.796875
- query_weight: bfloat16 [1024, 1024], P(None, 'tensor'), may hold values from -0.1875 to 0.1875
- query_bias: bfloat16 [1024], P('tensor'), may hold values from -1.796875 to 1.796875
- key_weight: bfloat16 [1024, 1024], P(None, 'tensor'), may hold values from -0.1875 to 0.1875
- value_weight: bfloat16 [1024, 1024], P(None, 'tensor'), may hold values from -0.1875 to 0.1875
- value_bias: bfloat16 [1024], P('tensor'), may hold values from -1.796875 to 1.796875
- dense_weight: bfloat16 [1024, 1024], P('tensor'), may hold values from -0.75 to 0.75
- dense_bias: bfloat16 [1024], replicated, may hold values from -1.796875 to 1.796875
- post_gain: bfloat16 [1024], replicated, may hold values from 0.5 to 1.5
- post_shift: bfloat16 [1024], replicated, may hold values from -1.796875 to 1.796875
- up_weight: bfloat16 [1024, 4096], P(None, 'tensor'), may hold values from -0.1875 to 0.1875
- up_bias: bfloat16 [4096], P('tensor'), may hold values from -1.796875 to 1.796875
- down_weight: bfloat16 [4096, 1024], P('tensor'), may hold values from -0.1875 to 0.1875
- down_bias: bfloat16 [1024], replicated, may hold values from -1.796875 to 1.796875
- cotangent: bfloat16 [32768, 1024], P(('dp', 'tensor')), may hold values from -6 to 6
Outputs:
- layer_output: bfloat16 [32768, 1024], P(('dp', 'tensor'))
- input_grad: float32 [32768, 1024], P(('dp', 'tensor'))
- input_gain_grad: float32 [1024], replicated
- input_shift_grad: float32 [1024], replicated
- query_weight_grad: float32 [1024, 1024], P(None, 'tensor')
- query_bias_grad: float32 [1024], P('tensor')
- key_weight_grad: float32 [1024, 1024], P(None, 'tensor')
- value_weight_grad: float32 [1024, 1024], P(None, 'tensor')
- value_bias_grad: float32 [1024], P('tensor')
- dense_weight_grad: float32 [1024, 1024], P('tensor')
- dense_bias_grad: float32 [1024], replicated
- post_gain_grad: float32 [1024], replicated
- post_shift_grad: float32 [1024], replicated
- up_weight_grad: float32 [1024, 4096], P(None, 'tensor')
- up_bias_grad: float32 [4096], P('tensor')
- down_weight_grad: float32 [4096, 1024], P('tensor')
- down_bias_grad: float32 [1024], replicated
Inputs may be any that keep to these rules, and one draw needn't show every extreme that they name: `row_ids`: within each data group of 4096 consecutive tokens, the tokens form rows of 2048 or 4096 consecutive tokens, each row starting at a multiple of its own length within the group; every token of a row carries the index, within its group, of the row's last block of 2048 tokens, so ids never fall within a group and two rows of a group never share an id.
All inputs are finite; a program needn't handle non-finite values.
Results may differ from a plain program's by a relative error of at most 0.013.
Values may be sent and summed in bfloat16 or wider, within the bound.
A program may use at most 576 MiB of HBM per device.

v0:
```python
import jax
import jax.numpy as jnp
from jax import lax
from jax.sharding import PartitionSpec as P

HEADS = 16
HD = 64
SHORT = 2048
BLOCK = 512


EPSILON = 1e-05


def layer_norm(inputs, gain_vec, shift_vec):
    center = jnp.mean(inputs, axis=-1, keepdims=True)
    centered = inputs - center
    spread = jnp.mean(centered * centered, axis=-1, keepdims=True)
    return centered * lax.rsqrt(spread + EPSILON) * gain_vec + shift_vec


def gelu_tanh(inputs):
    return jax.nn.gelu(inputs, approximate=True)


def split_heads(matrix, head_count):
    return matrix.reshape(matrix.shape[0], head_count, HD).transpose(1, 0, 2)


def join_heads(stacked):
    return stacked.transpose(1, 0, 2).reshape(stacked.shape[1], stacked.shape[0] * stacked.shape[2])


def block_scores(query_block, key_block, slopes, query_first, key_first, query_ids, key_ids):
    products = jnp.einsum(
        "hqd,hkd->hqk", query_block, key_block, preferred_element_type=jnp.float32
    )
    query_pos = query_first + jnp.arange(query_block.shape[1])
    key_pos = key_first + jnp.arange(key_block.shape[1])
    offsets = (key_pos[None, :] - query_pos[:, None]).astype(jnp.float32)
    scores = products * HD ** (-0.5) + slopes[:, None, None] * offsets[None]
    allowed = (query_ids[:, None] == key_ids[None, :]) & (offsets <= 0)
    return jnp.where(allowed[None], scores, -1e30)


def shards(
    layer_input,
    row_ids,
    input_gain,
    input_shift,
    query_weight,
    query_bias,
    key_weight,
    value_weight,
    value_bias,
    dense_weight,
    dense_bias,
    post_gain,
    post_shift,
    up_weight,
    up_bias,
    down_weight,
    down_bias,
    cotangent,
):
    group_len = row_ids.shape[0]
    head_cols = query_weight.shape[1]
    head_count = head_cols // HD
    window_len = 2 * SHORT
    block_count = group_len // BLOCK

    def block_bounds(block_index):
        row_first = block_index * BLOCK
        key_first = row_first // window_len * window_len
        return (row_first, key_first, row_first + BLOCK)

    inputs = layer_input.astype(jnp.float32)
    normed, norm_pull = jax.vjp(
        layer_norm, inputs, input_gain.astype(jnp.float32), input_shift.astype(jnp.float32)
    )
    normed_low = normed.astype(jnp.bfloat16)
    normed_all = lax.all_gather(normed_low, "tensor", axis=0, tiled=True)
    joined = jnp.concatenate([query_weight, key_weight, value_weight], axis=1)
    projected = jnp.dot(normed_all, joined, preferred_element_type=jnp.float32)
    queries = (projected[:, :head_cols] + query_bias.astype(jnp.float32)).astype(jnp.bfloat16)
    key_rows = projected[:, head_cols : 2 * head_cols].astype(jnp.bfloat16)
    values = (projected[:, 2 * head_cols :] + value_bias.astype(jnp.float32)).astype(jnp.bfloat16)
    query_heads = split_heads(queries, head_count)
    key_heads = split_heads(key_rows, head_count)
    value_heads = split_heads(values, head_count)
    head_index = lax.axis_index("tensor") * head_count + jnp.arange(head_count)
    slopes = jnp.exp2(-8.0 * (head_index + 1).astype(jnp.float32) / HEADS)
    out_blocks = []
    total_blocks = []
    for block_index in range(block_count):
        row_first, key_first, row_last = block_bounds(block_index)
        masked = block_scores(
            query_heads[:, row_first:row_last],
            key_heads[:, key_first:row_last],
            slopes,
            row_first,
            key_first,
            row_ids[row_first:row_last],
            row_ids[key_first:row_last],
        )
        log_total = jax.nn.logsumexp(masked, axis=-1, keepdims=True)
        prob_low = jnp.exp(masked - log_total).astype(jnp.bfloat16)
        out_blocks.append(
            jnp.einsum(
                "hqk,hkd->hqd",
                prob_low,
                value_heads[:, key_first:row_last],
                preferred_element_type=jnp.float32,
            )
        )
        total_blocks.append(log_total)
    mixed_heads = join_heads(jnp.concatenate(out_blocks, axis=1)).astype(jnp.bfloat16)
    attended = lax.psum_scatter(
        jnp.dot(mixed_heads, dense_weight, preferred_element_type=jnp.float32),
        "tensor",
        scatter_dimension=0,
        tiled=True,
    )
    residual = inputs + attended + dense_bias.astype(jnp.float32)
    post_rows, post_pull = jax.vjp(
        layer_norm, residual, post_gain.astype(jnp.float32), post_shift.astype(jnp.float32)
    )
    post_low = post_rows.astype(jnp.bfloat16)
    post_all = lax.all_gather(post_low, "tensor", axis=0, tiled=True)
    hidden = jnp.dot(post_all, up_weight, preferred_element_type=jnp.float32) + up_bias.astype(
        jnp.float32
    )
    active, gelu_pull = jax.vjp(gelu_tanh, hidden)
    active_low = active.astype(jnp.bfloat16)
    ffn_out = lax.psum_scatter(
        jnp.dot(active_low, down_weight, preferred_element_type=jnp.float32),
        "tensor",
        scatter_dimension=0,
        tiled=True,
    )
    layer_output = (residual + ffn_out + down_bias.astype(jnp.float32)).astype(jnp.bfloat16)
    grad_rows = cotangent.astype(jnp.float32)
    down_bias_part = jnp.sum(grad_rows, axis=0)
    grad_all = lax.all_gather(cotangent, "tensor", axis=0, tiled=True)
    act_grad = jnp.einsum("td,fd->tf", grad_all, down_weight, preferred_element_type=jnp.float32)
    hidden_grad = gelu_pull(act_grad)[0].astype(jnp.bfloat16)
    up_part = jnp.einsum("td,tf->df", post_all, hidden_grad, preferred_element_type=jnp.float32)
    down_part = jnp.einsum("tf,td->fd", active_low, grad_all, preferred_element_type=jnp.float32)
    up_bias_part = jnp.sum(hidden_grad.astype(jnp.float32), axis=0)
    post_grad = lax.psum_scatter(
        jnp.einsum("tf,df->td", hidden_grad, up_weight, preferred_element_type=jnp.float32),
        "tensor",
        scatter_dimension=0,
        tiled=True,
    )
    norm_grad_resid, post_gain_part, post_shift_part = post_pull(post_grad)
    resid_grad = grad_rows + norm_grad_resid
    dense_bias_part = jnp.sum(resid_grad, axis=0)
    attended_all = lax.all_gather(resid_grad.astype(jnp.bfloat16), "tensor", axis=0, tiled=True)
    dense_part = jnp.einsum(
        "tc,td->cd", mixed_heads, attended_all, preferred_element_type=jnp.float32
    )
    mixed_grad = jnp.einsum(
        "td,cd->tc", attended_all, dense_weight, preferred_element_type=jnp.float32
    ).astype(jnp.bfloat16)
    grad_heads = split_heads(mixed_grad, head_count)
    query_grads = []
    key_acc = jnp.zeros((head_count, group_len, HD), jnp.float32)
    value_acc = jnp.zeros((head_count, group_len, HD), jnp.float32)
    for block_index in range(block_count):
        row_first, key_first, row_last = block_bounds(block_index)
        query_block = query_heads[:, row_first:row_last]
        key_block = key_heads[:, key_first:row_last]
        value_block = value_heads[:, key_first:row_last]
        out_grad = grad_heads[:, row_first:row_last]
        masked = block_scores(
            query_block,
            key_block,
            slopes,
            row_first,
            key_first,
            row_ids[row_first:row_last],
            row_ids[key_first:row_last],
        )
        prob_full = jnp.exp(masked - total_blocks[block_index])
        prob_low = prob_full.astype(jnp.bfloat16)
        value_acc = value_acc.at[:, key_first:row_last].add(
            jnp.einsum("hqk,hqd->hkd", prob_low, out_grad, preferred_element_type=jnp.float32)
        )
        prob_grad = jnp.einsum(
            "hqd,hkd->hqk", out_grad, value_block, preferred_element_type=jnp.float32
        )
        row_dot = jnp.sum(prob_full * prob_grad, axis=-1, keepdims=True)
        score_grad = (prob_full * (prob_grad - row_dot)).astype(jnp.bfloat16)
        query_grads.append(
            jnp.einsum("hqk,hkd->hqd", score_grad, key_block, preferred_element_type=jnp.float32)
            * HD ** (-0.5)
        )
        key_acc = key_acc.at[:, key_first:row_last].add(
            jnp.einsum("hqk,hqd->hkd", score_grad, query_block, preferred_element_type=jnp.float32)
            * HD ** (-0.5)
        )
    query_grad = join_heads(jnp.concatenate(query_grads, axis=1)).astype(jnp.bfloat16)
    key_grad = join_heads(key_acc).astype(jnp.bfloat16)
    value_grad = join_heads(value_acc).astype(jnp.bfloat16)
    proj_grad = jnp.concatenate([query_grad, key_grad, value_grad], axis=1)
    joined_part = jnp.einsum("td,tc->dc", normed_all, proj_grad, preferred_element_type=jnp.float32)
    query_bias_part = jnp.sum(query_grad.astype(jnp.float32), axis=0)
    value_bias_part = jnp.sum(value_grad.astype(jnp.float32), axis=0)
    normed_grad = lax.psum_scatter(
        jnp.einsum("tc,dc->td", proj_grad, joined, preferred_element_type=jnp.float32),
        "tensor",
        scatter_dimension=0,
        tiled=True,
    )
    input_norm_grad, input_gain_part, input_shift_part = norm_pull(normed_grad)
    input_grad = resid_grad + input_norm_grad
    summed = lax.psum(
        (
            joined_part[:, :head_cols],
            query_bias_part,
            joined_part[:, head_cols : 2 * head_cols],
            joined_part[:, 2 * head_cols :],
            value_bias_part,
            dense_part,
            up_part,
            up_bias_part,
            down_part,
        ),
        "dp",
    )
    shared = lax.psum(
        (
            input_gain_part,
            input_shift_part,
            dense_bias_part,
            post_gain_part,
            post_shift_part,
            down_bias_part,
        ),
        ("dp", "tensor"),
    )
    return (
        layer_output,
        input_grad,
        shared[0],
        shared[1],
        summed[0],
        summed[1],
        summed[2],
        summed[3],
        summed[4],
        summed[5],
        shared[2],
        shared[3],
        shared[4],
        summed[6],
        summed[7],
        summed[8],
        shared[5],
    )


def solution(mesh):
    in_specs = (
        P(("dp", "tensor"), None),
        P("dp"),
        P(),
        P(),
        P(None, "tensor"),
        P("tensor"),
        P(None, "tensor"),
        P(None, "tensor"),
        P("tensor"),
        P("tensor", None),
        P(),
        P(),
        P(),
        P(None, "tensor"),
        P("tensor"),
        P("tensor", None),
        P(),
        P(("dp", "tensor"), None),
    )
    out_specs = (
        P(("dp", "tensor"), None),
        P(("dp", "tensor"), None),
        P(),
        P(),
        P(None, "tensor"),
        P("tensor"),
        P(None, "tensor"),
        P(None, "tensor"),
        P("tensor"),
        P("tensor", None),
        P(),
        P(),
        P(),
        P(None, "tensor"),
        P("tensor"),
        P("tensor", None),
        P(),
    )
    return jax.shard_map(shards, mesh=mesh, in_specs=in_specs, out_specs=out_specs, check_vma=False)
```

profile of v0, /device:TPU:0, one launch (start us, length us, event | category | flops | bytes accessed | tf_op | source)
XLA Modules:
  0.0 1910.5 jit_solution(7665269605376054188)
XLA Ops:
  60.0 17.7 all-gather.5.cloned.1.call-done
  77.7 10.3 fusion.231
  110.2 10.2 fusion.226
  120.5 8.1 exponential_reduce_fusion.4
  128.6 12.6 fusion.227
  141.2 10.0 exponential_reduce_fusion.3
  151.3 13.4 fusion.228
  164.7 11.1 exponential_reduce_fusion.2
  175.8 15.9 fusion.229
  191.8 13.0 exponential_reduce_fusion.1
  204.8 18.3 fusion.230
  223.2 16.4 exponential_reduce_fusion
  243.5 7.4 fusion.133
  250.8 9.4 fusion.130
  260.3 10.2 fusion.127
  270.5 11.0 fusion.141
  281.5 12.5 fusion.136
  294.0 14.6 fusion.124
  308.6 9.9 fusion.232
  319.2 125.6 %reduce-scatter.5.cloned.1.call-done = f32[1024,1024]{1,0:T(8,128)} async-done(((f32[4096,1024]{1,0:T(8,128)}), f32[1024,1024]{1,0:T(8,128)}) %reduce-scatter.5.cloned.1.call-update) | async-done | bytes 4194320 | tf_op jit(solution)/shard_map/reduce_scatter | solution.py:118
  453.0 57.8 %all-gather.7.cloned.1.call-done = bf16[4096,1024]{1,0:T(8,128)(2,1)} async-done(((bf16[1024,1024]{1,0:T(8,128)(2,1)}), bf16[4096,1024]{1,0:T(8,128)(2,1)}) %all-gather.7.cloned.1.call-update) | async-done | bytes 8388624 | tf_op jit(solution)/shard_map/all_gather | solution.py:129
  510.8 16.1 fusion.233
  526.9 43.8 %all-gather.9.cloned.1.call-done = bf16[4096,1024]{1,0:T(8,128)(2,1)} async-done(((bf16[1024,1024]{1,0:T(8,128)(2,1)}), bf16[4096,1024]{1,0:T(8,128)(2,1)}) %all-gather.9.cloned.1.call-update) | async-done | bytes 8388624 | tf_op jit(solution)/shard_map/all_gather | solution.py:144
  570.6 27.1 %convert_reduce_fusion = (f32[1024]{0:T(1024)}, bf16[4096,1024]{1,0:T(8,128)(2,1)S(1)}, bf16[4096,1024]{1,0:T(8,128)(2,1)}) fusion(f32[4096,1024]{1,0:T(8,128)} %fusion.233, f32[1024]{0:T(1024)S(1)} %convert_element_type.310, bf16[4096,1024]{1,0:T(8,128)(2,1)} %all-gather.9.cloned.1.call-done, bf16[1024,1024]{1,0:T(8,128)(2,1)S(1)} %copy-done), kind=kOutput, calls=%fused_computation.32 | convolution fusion | flops 8694791168 | bytes 44048384 | tf_op jit(solution)/shard_map/td,fd->tf/dot_general | solution.py:145
  601.0 12.2 fusion.235
  613.3 16.6 fusion.234
  630.6 109.0 %reduce-scatter.9.cloned.1.call-done = f32[1024,1024]{1,0:T(8,128)} async-done(((f32[4096,1024]{1,0:T(8,128)}), f32[1024,1024]{1,0:T(8,128)}) %reduce-scatter.9.cloned.1.call-update) | async-done | bytes 4194320 | tf_op jit(solution)/shard_map/reduce_scatter | solution.py:150
  744.4 123.7 %reduce-scatter.7.cloned.1.call-done = f32[1024,1024]{1,0:T(8,128)} async-done(((f32[4096,1024]{1,0:T(8,128)}), f32[1024,1024]{1,0:T(8,128)}) %reduce-scatter.7.cloned.1.call-update) | async-done | bytes 4194320 | tf_op jit(solution)/shard_map/reduce_scatter | solution.py:135
  868.1 6.6 fusion.218
  878.7 58.4 %all-gather.11.cloned.1.call-done = bf16[4096,1024]{1,0:T(8,128)(2,1)} async-done(((bf16[1024,1024]{1,0:T(8,128)(2,1)}), bf16[4096,1024]{1,0:T(8,128)(2,1)}) %all-gather.11.cloned.1.call-update) | async-done | bytes 8388624 | tf_op jit(solution)/shard_map/all_gather | solution.py:159
  937.1 5.9 convolution_convert_fusion
  958.7 11.0 multiply_reduce_fusion.5
  969.8 9.5 multiply_reduce_fusion.4
  979.3 14.2 multiply_reduce_fusion.3
  993.5 16.4 multiply_reduce_fusion.2
  1009.9 21.0 %multiply_reduce_fusion.1 = (f32[4,512]{1,0:T(4,128)}, f32[4,512,3584]{2,1,0:T(8,128)}) fusion(f32[4,512,3584]{2,1,0:T(8,128)} %get-tuple-element.284, f32[4,512]{1,0:T(4,128)S(1)} %copy-done.39, bf16[4,4096,64]{1,2,0:T(8,128)(2,1)S(1)} %bitcast.87, bf16[4,4096,64]{1,2,0:T(8,128)(2,1)} %bitcast.116), kind=kOutput, calls=%fused_computation.6 | convolution fusion | flops 961542144 | bytes 60833792 | tf_op jit(solution)/shard_map/hqd,hkd->hqk/dot_general | solution.py:190
  1030.9 22.6 %multiply_reduce_fusion = (f32[4,512]{1,0:T(4,128)}, f32[4,512,4096]{2,1,0:T(8,128)}) fusion(f32[4,512,4096]{2,1,0:T(8,128)} %get-tuple-element.286, f32[4,512]{1,0:T(4,128)S(1)} %copy-done.43, bf16[4,4096,64]{1,2,0:T(8,128)(2,1)S(1)} %bitcast.88, bf16[4,4096,64]{1,2,0:T(8,128)(2,1)S(1)} %bitcast.117), kind=kOutput, calls=%fused_computation.1 | convolution fusion | flops 1098905600 | bytes 69484544 | tf_op jit(solution)/shard_map/hqd,hkd->hqk/dot_general | solution.py:190
  1061.8 8.3 fusion.50
  1070.1 9.4 fusion.56
  1079.5 11.3 fusion.37
  1090.7 13.1 fusion.40
  1103.9 15.2 fusion.18
  1119.1 16.5 convert_reduce_fusion.3
  1138.1 6.9 multiply_convert_fusion.7
  1150.6 7.2 multiply_convert_fusion.6
  1170.1 8.2 multiply_convert_fusion.4
  1186.4 14.3 multiply_convert_fusion.3
  1210.0 8.0 fusion.93
  1218.0 16.8 multiply_convert_fusion.2
  1239.3 6.1 fusion.42
  1245.4 9.3 fusion.89
  1254.7 24.6 %multiply_convert_fusion.1 = bf16[4,512,3584]{2,1,0:T(8,128)(2,1)} fusion(f32[4,512,3584]{2,1,0:T(8,128)} %get-tuple-element.300, f32[4,512,3584]{2,1,0:T(8,128)} %get-tuple-element.284, f32[4,512]{1,0:T(4,128)S(1)} %copy-done.84, f32[4,512]{1,0:T(4,128)S(1)} %copy-done.39), kind=kLoop, calls=%fused_computation.5 | loop fusion | flops 29360128 | bytes 73416704 | tf_op jit(solution)/shard_map/convert_element_type | solution.py:194
  1279.2 10.9 fusion.20
  1295.8 27.6 %multiply_convert_fusion = bf16[4,512,4096]{2,1,0:T(8,128)(2,1)} fusion(f32[4,512,4096]{2,1,0:T(8,128)} %get-tuple-element.302, f32[4,512,4096]{2,1,0:T(8,128)} %get-tuple-element.286, f32[4,512]{1,0:T(4,128)S(1)} %copy-done.83, f32[4,512]{1,0:T(4,128)S(1)} %copy-done.43), kind=kLoop, calls=%fused_computation | loop fusion | flops 33554432 | bytes 83902464 | tf_op jit(solution)/shard_map/convert_element_type | solution.py:194
  1323.4 11.7 fusion.23
  1341.9 12.7 fusion.60
  1354.7 15.8 fusion.238
  1370.4 18.2 fusion.237
  1388.7 6.8 fusion.59
  1397.3 7.3 fusion.236
  1407.5 22.4 %all-reduce.3 = (f32[256]{0:T(256)}, f32[256]{0:T(256)}, f32[1024]{0:T(1024)}) all-reduce(f32[256]{0:T(256)S(1)} %reduce_sum.360, f32[256]{0:T(256)S(1)} %reduce_sum.362, f32[1024]{0:T(1024)S(1)} %copy-done.92), channel_id=1, replica_groups=mesh['dp'=8,'tensor'=4] {'dp'}, use_global_device_ids=true, to_apply=%region_42.43 | all-reduce | flops 1536 | bytes 12288 | tf_op jit(solution)/shard_map/psum | solution.py:218
  1429.9 51.0 %reduce-scatter.11.cloned.1.call-done = f32[1024,1024]{1,0:T(8,128)} async-done(((f32[4096,1024]{1,0:T(8,128)}), f32[1024,1024]{1,0:T(8,128)}) %reduce-scatter.11.cloned.1.call-update) | async-done | bytes 4194320 | tf_op jit(solution)/shard_map/reduce_scatter | solution.py:210
  1490.8 44.6 %all-reduce.2 = (f32[1024]{0:T(1024)}, f32[1024]{0:T(1024)}, f32[1024]{0:T(1024)}, f32[1024]{0:T(1024)}, f32[1024]{0:T(1024)}, /*index=5*/f32[1024]{0:T(1024)}) all-reduce(f32[1024]{0:T(1024)S(1)} %get-tuple-element.227, f32[1024]{0:T(1024)S(1)} %get-tuple-element.230, ...), channel_id=1, replica_groups=mesh['dp'=8,'tensor'=4] {'dp','tensor'}, use_global_device_ids=true, to_apply=%region_37.38 | all-reduce | flops 6144 | bytes 49152 | tf_op jit(solution)/shard_map/psum | solution.py:232
  1535.4 355.9 %all-reduce.7.cloned.1.call-done = (f32[1024,256]{1,0:T(8,128)}, f32[1024,256]{1,0:T(8,128)}, f32[1024,256]{1,0:T(8,128)}, f32[256,1024]{1,0:T(8,128)}, f32[1024,1024]{1,0:T(8,128)}, /*index=5*/f32[1024,1024]{1,0:T(8,128)}) async-done(((f32[1024,256]{1,0:T(8,128)}, f32[1024,256]{1,0:T(8,128)}, f32[1024,256]{1,0:T(8,128)}, f32[256,1024]{1,0:T(8,128)}, f32[1024,1024]{1,0:T(8,128)}, ...) | async-done | bytes 12582928 | tf_op jit(solution)/shard_map/psum | solution.py:218
  (382 shorter events, 205.9 us)
Async XLA Ops:
  7.2 563.4 %copy-start = (bf16[1024,1024]{1,0:T(8,128)(2,1)S(1)}, bf16[1024,1024]{1,0:T(8,128)(2,1)}, u32[]{:S(2)}) copy-start(bf16[1024,1024]{1,0:T(8,128)(2,1)} %param.69) | copy-start | bytes 6291460
  7.2 70.5 %all-gather.5.cloned.1.call-start = ((), (), s32[]{:S(2)}) async-start(), calls=%async_computation.4 | async-start | bytes 10485760 | tf_op jit(solution)/shard_map/all_gather | solution.py:82
  16.6 428.2 %reduce-scatter.5.cloned.1.call-start = ((), (), s32[]{:S(2)}) async-start(), calls=%async_computation.5 | async-start | bytes 20971520 | tf_op jit(solution)/shard_map/reduce_scatter | solution.py:118
  88.3 12.9 copy-start.21
  90.9 10.3 copy-start.28
  94.4 145.1 %copy-start.66 = (f32[4,512]{1,0:T(4,128)}, f32[4,512]{1,0:T(4,128)S(1)}, u32[]{:S(2)}) copy-start(f32[4,512]{1,0:T(4,128)S(1)} %log_add_fusion.7) | copy-start | bytes 24580
  102.0 139.1 %copy-start.63 = (f32[4,512]{1,0:T(4,128)}, f32[4,512]{1,0:T(4,128)S(1)}, u32[]{:S(2)}) copy-start(f32[4,512]{1,0:T(4,128)S(1)} %log_add_fusion.6) | copy-start | bytes 24580
  110.2 133.3 %copy-start.59 = (f32[4,512]{1,0:T(4,128)}, f32[4,512]{1,0:T(4,128)S(1)}, u32[]{:S(2)}) copy-start(f32[4,512]{1,0:T(4,128)S(1)} %log_add_fusion.5) | copy-start | bytes 24580
  128.6 122.2 %copy-start.68 = (f32[4,512]{1,0:T(4,128)}, f32[4,512]{1,0:T(4,128)S(1)}, u32[]{:S(2)}) copy-start(f32[4,512]{1,0:T(4,128)S(1)} %log_add_fusion.4) | copy-start | bytes 24580
  141.2 10.0 copy-start.22
  141.2 10.0 copy-start.44
  151.3 109.0 %copy-start.51 = (f32[4,512]{1,0:T(4,128)}, f32[4,512]{1,0:T(4,128)S(1)}, u32[]{:S(2)}) copy-start(f32[4,512]{1,0:T(4,128)S(1)} %log_add_fusion.3) | copy-start | bytes 24580
  164.7 11.1 copy-start.37
  175.8 94.6 %copy-start.40 = (f32[4,512]{1,0:T(4,128)}, f32[4,512]{1,0:T(4,128)S(1)}, u32[]{:S(2)}) copy-start(f32[4,512]{1,0:T(4,128)S(1)} %log_add_fusion.2) | copy-start | bytes 24580
  204.8 76.6 %copy-start.38 = (f32[4,512]{1,0:T(4,128)}, f32[4,512]{1,0:T(4,128)S(1)}, u32[]{:S(2)}) copy-start(f32[4,512]{1,0:T(4,128)S(1)} %log_add_fusion.1) | copy-start | bytes 24580
  223.1 18.0 slice-start.11
  223.1 16.5 copy-start.3
  223.1 16.5 copy-start.10
  223.1 17.9 slice-start.12
  239.6 54.4 %copy-start.42 = (f32[4,512]{1,0:T(4,128)}, f32[4,512]{1,0:T(4,128)S(1)}, u32[]{:S(2)}) copy-start(f32[4,512]{1,0:T(4,128)S(1)} %log_add_fusion) | copy-start | bytes 24580
  260.3 10.2 copy-start.4
  294.0 14.7 copy-start.54
  318.5 192.3 %all-gather.7.cloned.1.call-start = ((), (), s32[]{:S(2)}) async-start(), calls=%async_computation.6 | async-start | bytes 10485760 | tf_op jit(solution)/shard_map/all_gather | solution.py:129
  452.3 118.3 %all-gather.9.cloned.1.call-start = ((), (), s32[]{:S(2)}) async-start(), calls=%async_computation.8 | async-start | bytes 10485760 | tf_op jit(solution)/shard_map/all_gather | solution.py:144
  452.9 286.6 %reduce-scatter.9.cloned.1.call-start = ((), (), s32[]{:S(2)}) async-start(), calls=%async_computation.9 | async-start | bytes 20971520 | tf_op jit(solution)/shard_map/reduce_scatter | solution.py:150
  570.6 30.3 %copy-start.98 = (bf16[1024,1024]{1,0:T(8,128)(2,1)S(1)}, bf16[1024,1024]{1,0:T(8,128)(2,1)}, u32[]{:S(2)}) copy-start(bf16[1024,1024]{1,0:T(8,128)(2,1)} %param.67) | copy-start | bytes 6291460
  613.2 254.9 %reduce-scatter.7.cloned.1.call-start = ((), (), s32[]{:S(2)}) async-start(), calls=%async_computation.7 | async-start | bytes 20971520 | tf_op jit(solution)/shard_map/reduce_scatter | solution.py:135
  629.9 307.2 %all-gather.11.cloned.1.call-start = ((), (), s32[]{:S(2)}) async-start(), calls=%async_computation.10 | async-start | bytes 10485760 | tf_op jit(solution)/shard_map/all_gather | solution.py:159
  744.4 132.3 %copy-start.24 = (bf16[1024,1024]{1,0:T(8,128)(2,1)S(1)}, bf16[1024,1024]{1,0:T(8,128)(2,1)}, u32[]{:S(2)}) copy-start(bf16[1024,1024]{1,0:T(8,128)(2,1)} %param.71) | copy-start | bytes 6291460
  878.7 64.4 %copy-start.67 = (f32[4,512]{1,0:T(4,128)S(1)}, f32[4,512]{1,0:T(4,128)}, u32[]{:S(2)}) copy-start(f32[4,512]{1,0:T(4,128)} %copy-done.66) | copy-start | bytes 24580
  878.7 602.2 %reduce-scatter.11.cloned.1.call-start = ((), (), s32[]{:S(2)}) async-start(), calls=%async_computation.11 | async-start | bytes 20971520 | tf_op jit(solution)/shard_map/reduce_scatter | solution.py:210
  943.0 9.8 copy-start.26
  952.8 16.9 slice-start
  952.8 16.9 slice-start.1
  958.7 11.0 slice-start.2
  958.7 11.0 slice-start.3
  958.7 11.0 copy-start.69
  969.8 9.5 copy-start.52
  979.3 14.2 copy-start.41
  993.5 16.4 copy-start.39
  1009.9 21.0 %copy-start.27 = (bf16[4096,256]{0,1:T(8,128)(2,1)S(1)}, bf16[4096,256]{0,1:T(8,128)(2,1)}, u32[]{:S(2)}) copy-start(bf16[4096,256]{0,1:T(8,128)(2,1)} %copy-done.26) | copy-start | bytes 6291460
  1009.9 21.0 %copy-start.43 = (f32[4,512]{1,0:T(4,128)S(1)}, f32[4,512]{1,0:T(4,128)}, u32[]{:S(2)}) copy-start(f32[4,512]{1,0:T(4,128)} %copy-done.42) | copy-start | bytes 24580
  1070.1 9.4 copy-start.53
  1119.1 16.5 copy-start.29
  1138.1 12.5 slice-start.8
  1138.1 12.5 slice-start.9
  1150.6 19.5 %slice-start.4 = ((s8[16777216]{0:T(1024)(128)(4,1)}), s8[4194304]{0:T(1024)(128)(4,1)S(1)}, s32[]{:S(2)}) async-start(s8[16777216]{0:T(1024)(128)(4,1)} %bitcast.69), calls=%async_computation.17 | async-start | bytes 8388608
  1150.6 19.5 %slice-start.5 = ((s8[16777216]{0:T(1024)(128)(4,1)}), s8[4194304]{0:T(1024)(128)(4,1)S(1)}, s32[]{:S(2)}) async-start(s8[16777216]{0:T(1024)(128)(4,1)} %bitcast.69), calls=%async_computation.18 | async-start | bytes 8388608
  1150.6 19.5 %slice-start.6 = ((s8[16777216]{0:T(1024)(128)(4,1)}), s8[4194304]{0:T(1024)(128)(4,1)S(1)}, s32[]{:S(2)}) async-start(s8[16777216]{0:T(1024)(128)(4,1)} %bitcast.69), calls=%async_computation.19 | async-start | bytes 8388608
  1160.5 9.6 slice-start.7
  1245.4 9.3 copy-start.84
  1279.2 11.4 copy-start.8
  1323.4 12.6 copy-start.7
  1354.6 536.7 %all-reduce.7.cloned.1.call-start = ((), (), s32[]{:S(2)}) async-start(), calls=%async_computation.12 | async-start | bytes 25165824 | tf_op jit(solution)/shard_map/psum | solution.py:218
  1354.6 34.0 %slice-start.20 = ((s8[8388608]{0:T(1024)(128)(4,1)}), s8[4194304]{0:T(1024)(128)(4,1)S(1)}, s32[]{:S(2)}) async-start(s8[8388608]{0:T(1024)(128)(4,1)} %bitcast.148), calls=%async_computation.33 | async-start | bytes 8388608
  1370.4 18.3 copy-start.32
  1370.4 18.3 copy-start.34
  1370.4 18.3 copy-start.35
  1370.4 18.3 slice-start.21
  1404.7 76.2 %copy-start.14 = (bf16[1024,1024]{1,0:T(8,128)(2,1)S(1)}, bf16[1024,1024]{1,0:T(8,128)(2,1)}, u32[]{:S(2)}) copy-start(bf16[1024,1024]{1,0:T(8,128)(2,1)} %param.54) | copy-start | bytes 6291460
  1404.7 76.2 %copy-start.73 = (f32[1024]{0:T(1024)S(1)}, f32[1024]{0:T(1024)}, u32[]{:S(2)}) copy-start(f32[1024]{0:T(1024)} %copy-done.72) | copy-start | bytes 12292
  1404.7 76.2 %copy-start.75 = (f32[1024]{0:T(1024)S(1)}, f32[1024]{0:T(1024)}, u32[]{:S(2)}) copy-start(f32[1024]{0:T(1024)} %copy-done.74) | copy-start | bytes 12292
  1405.4 78.8 %copy-start.79 = (f32[1024]{0:T(1024)S(1)}, f32[1024]{0:T(1024)}, u32[]{:S(2)}) copy-start(f32[1024]{0:T(1024)} %copy-done.78) | copy-start | bytes 12292
  1405.4 78.9 %copy-start.77 = (f32[1024]{0:T(1024)S(1)}, f32[1024]{0:T(1024)}, u32[]{:S(2)}) copy-start(f32[1024]{0:T(1024)} %copy-done.76) | copy-start | bytes 12292
  (69 other events, 273.0 us)
Sparse Core Ops, SparseCore 0:
  16.7 60.9 all-gather.4
  318.6 126.0 reduce-scatter.4
  452.5 58.2 all-gather.6
  512.3 58.2 all-gather.8
  613.3 126.1 reduce-scatter.8
  741.9 126.1 reduce-scatter.6
  878.8 58.2 all-gather.10
  1354.7 126.0 reduce-scatter.10
  1487.4 403.8 all-reduce.6
where the time goes:
time: 1920 us; the launch traced here: 1910 us
  waiting for transfers between devices  943 us (49%)
  matrix products  579 us (30%)
  other arithmetic  253 us (13%)
  blocking collectives  67 us (3%)
  local copies, waits for them, and re-layouts  52.7 us (3%)
    psum x1, waiting for transfers between devices, shards(): lax.psum((joined_part[:, :head_cols], query_bias_part, joined_part[:, hea...  356 us
    reduce_scatter x1, waiting for transfers between devices, shards(): lax.psum_scatter(jnp.dot(mixed_heads, dense_weight, preferred_element_typ...  126 us
    reduce_scatter x1, waiting for transfers between devices, shards(): lax.psum_scatter(jnp.dot(active_low, down_weight, preferred_element_type=...  124 us
    reduce_scatter x1, waiting for transfers between devices, shards(): lax.psum_scatter(jnp.einsum('tf,df->td', hidden_grad, up_weight, preferre...  109 us
    convert_element_type x8, other arithmetic, shards(): score_grad = (prob_full * (prob_grad - row_dot)).astype(jnp.bfloat16)  107 us
    dot_general x8, matrix products, shards(): jnp.einsum('hqd,hkd->hqk', out_grad, value_block, preferred_element_type=...  102 us
    dot_general x8, matrix products, shards(): jnp.einsum('hqk,hqd->hkd', prob_low, out_grad, preferred_element_type=jnp...  80.3 us
    dot_general x8, matrix products, block_scores(): jnp.einsum('hqd,hkd->hqk', query_block, key_block, preferred_element_type...  78.1 us
  transfers between devices with their start and end apart: 9, of which 9 were waited for; matrix products, arithmetic and copies ran while one was open for 7% of the time, Pallas kernels for 0%

commit v1 on v0

v1 whole, which is shorter than its diff:
```python
import functools
import math

import jax
import jax.numpy as jnp
from jax import lax
from jax.experimental import pallas as pl
from jax.experimental.pallas import tpu as pltpu
from jax.sharding import PartitionSpec as P

HD=64; HEADS=16; SHORT=2048
LOG2E=math.log2(math.e)
f32=jnp.float32; bf=jnp.bfloat16
NT=(((1,),(1,)),((),()))
NN=(((1,),(0,)),((),()))
def dot(a,b,d): return lax.dot_general(a,b,d,preferred_element_type=f32)
def split3(x):
    h=x.astype(bf); r=x-h.astype(f32); m=r.astype(bf); l=(r-m.astype(f32)).astype(bf)
    return h,m,l
def lane(n): return lax.broadcasted_iota(jnp.int32,(n,128),1)
def row(n): return lax.broadcasted_iota(jnp.int32,(n,128),0)
def key_cols(x, base, n):
    ln=lane(n); pos=row(n)+base
    coarse=((pos>>6)<<6).astype(f32); fine=(pos&63).astype(f32)
    c=jnp.where(ln<67,coarse,jnp.where(ln<70,fine,jnp.where(ln<73,-1.0,jnp.where(ln==73,jnp.where(pos<SHORT,-1e30,0.0),0.0))))
    pad=jnp.concatenate([x.astype(f32),jnp.zeros((n,64),f32)],axis=1)
    return jnp.where(ln<64,pad,c).astype(bf)
def query_cols(x, base, n, slope2, apart, lse=None):
    ln=lane(n); pos=row(n)+base
    sh=slope2.astype(bf).astype(f32); r=slope2-sh; sm=r.astype(bf).astype(f32); sl=r-sm
    k3=jnp.where(ln<67,ln-64,ln-67)
    c=jnp.where(k3==0,sh,jnp.where(k3==1,sm,sl))
    c=jnp.where(ln<70,c,0.0)
    if lse is not None:
        h,m,l=split3(lse)
        c=jnp.where(ln==70,h.astype(f32),jnp.where(ln==71,m.astype(f32),jnp.where(ln==72,l.astype(f32),c)))
    c=jnp.where(ln==73,jnp.where(pos>=SHORT,apart,0.0),c)
    pad=jnp.concatenate([x.astype(f32),jnp.zeros((n,64),f32)],axis=1)
    return jnp.where(ln<64,pad,c).astype(bf)
def ones_cols(x,n,at,cnt):
    ln=lane(n)
    pad=jnp.concatenate([x.astype(f32),jnp.zeros((n,64),f32)],axis=1)
    return jnp.where(ln<64,pad,jnp.where((ln>=at)&(ln<at+cnt),1.0,0.0)).astype(bf)

def fwd_kernel(apart_ref, slope_ref, q_ref,k_ref,v_ref,o_ref,lse_ref,qa,ka,va,*,T,pair,bq,bk,form):
    g=pl.program_id(0)
    apart=apart_ref[0].astype(f32)
    nq=T//bq
    for s in range(pair):
        slope2=slope_ref[g*pair+s]
        C=512
        @pl.loop(0,T//C)
        def _(c):
            o=pl.multiple_of(c*C,C); sl=pl.ds(o,C)
            cs=slice(s*64,s*64+64)
            qa[s,sl,:]=query_cols(q_ref[sl,cs],o,C,slope2,apart)
            ka[s,sl,:]=key_cols(k_ref[sl,cs],o,C)
            if form=="A":
                va[s,sl,:]=ones_cols(v_ref[sl,cs],C,64,1)
            else:
                va[s,:,sl]=ones_cols(v_ref[sl,cs],C,64,1).astype(f32).T.astype(bf)
    tri=lax.broadcasted_iota(jnp.int32,(bq,bq),1)<=lax.broadcasted_iota(jnp.int32,(bq,bq),0)
    triT=lax.broadcasted_iota(jnp.int32,(bq,bq),0)<=lax.broadcasted_iota(jnp.int32,(bq,bq),1)
    def q_body(qi,_):
        qo=pl.multiple_of(qi*bq,bq)
        if form=="A":
            qs=[qa[s,pl.ds(qo,bq),:] for s in range(pair)]
            def step(ko,carry,diag,w):
                out=[]
                for s in range(pair):
                    m,acc=carry[s]
                    kk=ka[s,pl.ds(ko,w),:]
                    sc=dot(qs[s],kk,NT)
                    if diag: sc=jnp.where(tri,sc,-1e30)
                    mn=jnp.maximum(m,jnp.max(sc,axis=1,keepdims=True))
                    p=jnp.exp2(sc-mn).astype(bf)
                    acc=acc*jnp.exp2(m-mn)+dot(p,va[s,pl.ds(ko,w),:],NN)
                    out.append((mn,acc))
                return tuple(out)
            init=tuple((jnp.full((bq,1),-1e38,f32),jnp.zeros((bq,128),f32)) for _ in range(pair))
            carry=step(qo,init,True,bq)
            carry=lax.fori_loop(0,qo//bk,lambda t,c:step(pl.multiple_of(t*bk,bk),c,False,bk),carry)
            rem=(qo%bk)//bq
            if bk>bq:
                carry=lax.fori_loop(0,rem,lambda t,c:step(pl.multiple_of(qo-(t+1)*bq,bq),c,False,bq),carry)
            outs=[]
            for s in range(pair):
                m,acc=carry[s]
                l=acc[:,64:65]
                outs.append(acc[:,:64]*(1.0/l))
                lse_ref[s,0,pl.ds(qo,bq)]=(m+jnp.log2(l))[:,0]
            o_ref[pl.ds(qo,bq),:]=jnp.concatenate(outs,axis=1).astype(o_ref.dtype)
        else:
            qs=[qa[s,pl.ds(qo,bq),:] for s in range(pair)]
            def step(ko,carry,diag,w):
                out=[]
                for s in range(pair):
                    m,acc=carry[s]
                    kk=ka[s,pl.ds(ko,w),:]
                    sc=dot(kk,qs[s],NT)
                    if diag: sc=jnp.where(triT,sc,-1e30)
                    mn=jnp.maximum(m,jnp.max(sc,axis=0,keepdims=True))
                    p=jnp.exp2(sc-mn).astype(bf)
                    acc=acc*jnp.exp2(m-mn)+dot(va[s,:,pl.ds(ko,w)],p,NN)
                    out.append((mn,acc))
                return tuple(out)
            init=tuple((jnp.full((1,bq),-1e38,f32),jnp.zeros((va.shape[1],bq),f32)) for _ in range(pair))
            carry=step(qo,init,True,bq)
            carry=lax.fori_loop(0,qo//bk,lambda t,c:step(pl.multiple_of(t*bk,bk),c,False,bk),carry)
            rem=(qo%bk)//bq
            if bk>bq:
                carry=lax.fori_loop(0,rem,lambda t,c:step(pl.multiple_of(qo-(t+1)*bq,bq),c,False,bq),carry)
            outs=[]
            for s in range(pair):
                m,acc=carry[s]
                l=acc[64:65,:]
                outs.append(acc[:64,:]*(1.0/l))
                lse_ref[s,:,pl.ds(qo,bq)]=m+jnp.log2(l)
            o_ref[pl.ds(qo,bq),:]=jnp.concatenate(outs,axis=0).T.astype(o_ref.dtype)
        return 0
    lax.fori_loop(0,nq,q_body,0)

def attn_fwd(q,k,v,slopes2,apart,*,bq=512,bk=512,form="A"):
    T,W=q.shape; H=W//HD; pair=min(2,H)
    spec=pl.BlockSpec((T,pair*HD),lambda g:(0,g))
    return pl.pallas_call(
        functools.partial(fwd_kernel,T=T,pair=pair,bq=bq,bk=bk,form=form),
        grid=(H//pair,),
        in_specs=[pl.BlockSpec(memory_space=pltpu.SMEM),pl.BlockSpec(memory_space=pltpu.SMEM),spec,spec,spec],
        out_specs=[spec,pl.BlockSpec((pair,1,T),lambda g:(g,0,0))],
        out_shape=[jax.ShapeDtypeStruct((T,W),bf),jax.ShapeDtypeStruct((H,1,T),f32)],
        scratch_shapes=[pltpu.VMEM((pair,T,128),bf),pltpu.VMEM((pair,T,128),bf),pltpu.VMEM((pair,T,128) if form=="A" else (pair,128,T),bf)],
        compiler_params=pltpu.CompilerParams(vmem_limit_bytes=56<<20),
        name="attn_fwd_"+form+f"{bq}_{bk}",
    )(apart,slopes2,q,k,v)

def bwd_kernel(apart_ref, slope_ref, q_ref,k_ref,v_ref,do_ref,o_ref,lse_ref,dq_ref,dk_ref,dv_ref,qa,ka,va,da,kt_s,dq_s,*,T,pair,bq,bk):
    g=pl.program_id(0)
    apart=apart_ref[0].astype(f32)
    C=512
    for s in range(pair):
        slope2=slope_ref[g*pair+s]
        cs=slice(s*64,s*64+64)
        @pl.loop(0,T//C)
        def _(c):
            o=pl.multiple_of(c*C,C); sl=pl.ds(o,C)
            lse=lse_ref[s,:,sl].T
            qa[s,sl,:]=query_cols(q_ref[sl,cs],o,C,slope2,apart,lse)
            kc=key_cols(k_ref[sl,cs],o,C)
            ka[s,sl,:]=kc
            kt_s[s,:,sl]=kc.astype(f32).T.astype(bf)
            va[s,sl,:]=ones_cols(v_ref[sl,cs],C,64,3)
            do=do_ref[sl,cs].astype(f32)
            dl=jnp.sum(do*o_ref[sl,cs].astype(f32),axis=1,keepdims=True)
            h,m,l=split3(-dl)
            ln=lane(C)
            pad=jnp.concatenate([do,jnp.zeros((C,64),f32)],axis=1)
            da[s,sl,:]=jnp.where(ln<64,pad,jnp.where(ln==64,h.astype(f32),jnp.where(ln==65,m.astype(f32),jnp.where(ln==66,l.astype(f32),0.0)))).astype(bf)
            dq_s[s,:,sl]=jnp.zeros((128,C),f32)
    triT=lax.broadcasted_iota(jnp.int32,(bk,bk),0)<=lax.broadcasted_iota(jnp.int32,(bk,bk),1)
    nk=T//bk
    def k_body(ki,_):
        ko=pl.multiple_of(ki*bk,bk)
        kk=[ka[s,pl.ds(ko,bk),:] for s in range(pair)]
        vv=[va[s,pl.ds(ko,bk),:] for s in range(pair)]
        def step(qo,carry,diag,w):
            out=[]
            for s in range(pair):
                dk,dv=carry[s]
                qq=qa[s,pl.ds(qo,w),:]; dd=da[s,pl.ds(qo,w),:]
                p=jnp.exp2(dot(kk[s],qq,NT))
                if diag: p=jnp.where(triT,p,0.0)
                dv=dv+dot(p.astype(bf),dd,NN)
                ds=(p*dot(vv[s],dd,NT)).astype(bf)
                dk=dk+dot(ds,qq,NN)
                dq_s[s,:,pl.ds(qo,w)]+=dot(kt_s[s,:,pl.ds(ko,bk)],ds,NN)
                out.append((dk,dv))
            return tuple(out)
        z=jnp.zeros((bk,128),f32)
        carry=step(ko,tuple((z,z) for _ in range(pair)),True,bk)
        start=ko+bk
        r=jnp.minimum((-start)%bq, T-start)//bk
        if bq>bk:
            carry=lax.fori_loop(0,r,lambda t,c:step(pl.multiple_of(start+t*bk,bk),c,False,bk),carry)
            start=start+r*bk
        carry=lax.fori_loop(0,(T-start)//bq,lambda t,c:step(pl.multiple_of(start+t*bq,min(bq,bk)),c,False,bq),carry)
        dk_ref[pl.ds(ko,bk),:]=jnp.concatenate([carry[s][0][:,:64]*(1.0/LOG2E) for s in range(pair)],axis=1).astype(bf)
        dv_ref[pl.ds(ko,bk),:]=jnp.concatenate([carry[s][1][:,:64] for s in range(pair)],axis=1).astype(bf)
        return 0
    lax.fori_loop(0,nk,k_body,0)
    @pl.loop(0,T//C)
    def _(c):
        o=pl.multiple_of(c*C,C); sl=pl.ds(o,C)
        dq_ref[sl,:]=(jnp.concatenate([dq_s[s,:64,sl] for s in range(pair)],axis=0).T*(HD**-0.5)).astype(bf)

def attn_bwd(q,k,v,do,o,lse,slopes2,apart,*,bq=512,bk=512):
    T,W=q.shape; H=W//HD; pair=min(2,H)
    spec=pl.BlockSpec((T,pair*HD),lambda g:(0,g))
    return pl.pallas_call(
        functools.partial(bwd_kernel,T=T,pair=pair,bq=bq,bk=bk),
        grid=(H//pair,),
        in_specs=[pl.BlockSpec(memory_space=pltpu.SMEM),pl.BlockSpec(memory_space=pltpu.SMEM)]+[spec]*5+[pl.BlockSpec((pair,1,T),lambda g:(g,0,0))],
        out_specs=[spec]*3,
        out_shape=[jax.ShapeDtypeStruct((T,W),bf)]*3,
        scratch_shapes=[pltpu.VMEM((pair,T,128),bf)]*4+[pltpu.VMEM((pair,128,T),bf),pltpu.VMEM((pair,128,T),f32)],
        compiler_params=pltpu.CompilerParams(vmem_limit_bytes=60<<20),
        name=f"attn_bwd{bq}_{bk}",
    )(apart,slopes2,q,k,v,do,o,lse)


EPSILON = 1e-05


def layer_norm(inputs, gain_vec, shift_vec):
    center = jnp.mean(inputs, axis=-1, keepdims=True)
    centered = inputs - center
    spread = jnp.mean(centered * centered, axis=-1, keepdims=True)
    return centered * lax.rsqrt(spread + EPSILON) * gain_vec + shift_vec


def gelu_tanh(inputs):
    return jax.nn.gelu(inputs, approximate=True)


def shards(
    layer_input,
    row_ids,
    input_gain,
    input_shift,
    query_weight,
    query_bias,
    key_weight,
    value_weight,
    value_bias,
    dense_weight,
    dense_bias,
    post_gain,
    post_shift,
    up_weight,
    up_bias,
    down_weight,
    down_bias,
    cotangent,
):
    group_len = row_ids.shape[0]
    head_cols = query_weight.shape[1]
    head_count = head_cols // HD
    inputs = layer_input.astype(jnp.float32)
    normed, norm_pull = jax.vjp(
        layer_norm, inputs, input_gain.astype(jnp.float32), input_shift.astype(jnp.float32)
    )
    normed_low = normed.astype(jnp.bfloat16)
    normed_all = lax.all_gather(normed_low, "tensor", axis=0, tiled=True)
    joined = jnp.concatenate([query_weight, key_weight, value_weight], axis=1)
    projected = jnp.dot(normed_all, joined, preferred_element_type=jnp.float32)
    queries = (
        (projected[:, :head_cols] + query_bias.astype(jnp.float32)) * (LOG2E * HD**-0.5)
    ).astype(jnp.bfloat16)
    key_rows = projected[:, head_cols : 2 * head_cols].astype(jnp.bfloat16)
    values = (projected[:, 2 * head_cols :] + value_bias.astype(jnp.float32)).astype(jnp.bfloat16)
    head_index = lax.axis_index("tensor") * head_count + jnp.arange(head_count)
    slopes = jnp.exp2(-8.0 * (head_index + 1).astype(jnp.float32) / HEADS) * LOG2E
    apart = (row_ids[:1] != row_ids[SHORT : SHORT + 1]).astype(jnp.int32)
    mixed_heads, log_total = attn_fwd(queries, key_rows, values, slopes, apart, bq=1024, bk=1024)
    attended = lax.psum_scatter(
        jnp.dot(mixed_heads, dense_weight, preferred_element_type=jnp.float32).astype(jnp.bfloat16),
        "tensor",
        scatter_dimension=0,
        tiled=True,
    ).astype(jnp.float32)
    residual = inputs + attended + dense_bias.astype(jnp.float32)
    post_rows, post_pull = jax.vjp(
        layer_norm, residual, post_gain.astype(jnp.float32), post_shift.astype(jnp.float32)
    )
    post_low = post_rows.astype(jnp.bfloat16)
    post_all = lax.all_gather(post_low, "tensor", axis=0, tiled=True)
    hidden = jnp.dot(post_all, up_weight, preferred_element_type=jnp.float32) + up_bias.astype(
        jnp.float32
    )
    active, gelu_pull = jax.vjp(gelu_tanh, hidden)
    active_low = active.astype(jnp.bfloat16)
    ffn_out = lax.psum_scatter(
        jnp.dot(active_low, down_weight, preferred_element_type=jnp.float32).astype(jnp.bfloat16),
        "tensor",
        scatter_dimension=0,
        tiled=True,
    ).astype(jnp.float32)
    layer_output = (residual + ffn_out + down_bias.astype(jnp.float32)).astype(jnp.bfloat16)
    grad_rows = cotangent.astype(jnp.float32)
    down_bias_part = jnp.sum(grad_rows, axis=0)
    grad_all = lax.all_gather(cotangent, "tensor", axis=0, tiled=True)
    act_grad = jnp.einsum("td,fd->tf", grad_all, down_weight, preferred_element_type=jnp.float32)
    hidden_grad = gelu_pull(act_grad)[0].astype(jnp.bfloat16)
    up_part = jnp.einsum("td,tf->df", post_all, hidden_grad, preferred_element_type=jnp.float32)
    down_part = jnp.einsum("tf,td->fd", active_low, grad_all, preferred_element_type=jnp.float32)
    up_bias_part = jnp.sum(hidden_grad.astype(jnp.float32), axis=0)
    post_grad = lax.psum_scatter(
        jnp.einsum("tf,df->td", hidden_grad, up_weight, preferred_element_type=jnp.float32).astype(jnp.bfloat16),
        "tensor",
        scatter_dimension=0,
        tiled=True,
    ).astype(jnp.float32)
    norm_grad_resid, post_gain_part, post_shift_part = post_pull(post_grad)
    resid_grad = grad_rows + norm_grad_resid
    dense_bias_part = jnp.sum(resid_grad, axis=0)
    attended_all = lax.all_gather(resid_grad.astype(jnp.bfloat16), "tensor", axis=0, tiled=True)
    dense_part = jnp.einsum(
        "tc,td->cd", mixed_heads, attended_all, preferred_element_type=jnp.float32
    )
    mixed_grad = jnp.einsum(
        "td,cd->tc", attended_all, dense_weight, preferred_element_type=jnp.float32
    ).astype(jnp.bfloat16)
    query_grad, key_grad, value_grad = attn_bwd(
        queries, key_rows, values, mixed_grad, mixed_heads, log_total, slopes, apart, bq=1024, bk=512
    )
    proj_grad = jnp.concatenate([query_grad, key_grad, value_grad], axis=1)
    joined_part = jnp.einsum("td,tc->dc", normed_all, proj_grad, preferred_element_type=jnp.float32)
    query_bias_part = jnp.sum(query_grad.astype(jnp.float32), axis=0)
    value_bias_part = jnp.sum(value_grad.astype(jnp.float32), axis=0)
    normed_grad = lax.psum_scatter(
        jnp.einsum("tc,dc->td", proj_grad, joined, preferred_element_type=jnp.float32).astype(jnp.bfloat16),
        "tensor",
        scatter_dimension=0,
        tiled=True,
    ).astype(jnp.float32)
    input_norm_grad, input_gain_part, input_shift_part = norm_pull(normed_grad)
    input_grad = resid_grad + input_norm_grad
    weight_parts = (
        joined_part[:, :head_cols],
        joined_part[:, head_cols : 2 * head_cols],
        joined_part[:, 2 * head_cols :],
        dense_part,
        up_part,
        down_part,
    )
    query_w, key_w, value_w, dense_w, up_w, down_w = (
        total.astype(jnp.float32)
        for total in lax.psum(tuple(part.astype(jnp.bfloat16) for part in weight_parts), "dp")
    )
    query_b, value_b, up_b = lax.psum((query_bias_part, value_bias_part, up_bias_part), "dp")
    summed = (query_w, query_b, key_w, value_w, value_b, dense_w, up_w, up_b, down_w)
    shared = lax.psum(
        (
            input_gain_part,
            input_shift_part,
            dense_bias_part,
            post_gain_part,
            post_shift_part,
            down_bias_part,
        ),
        ("dp", "tensor"),
    )
    return (
        layer_output,
        input_grad,
        shared[0],
        shared[1],
        summed[0],
        summed[1],
        summed[2],
        summed[3],
        summed[4],
        summed[5],
        shared[2],
        shared[3],
        shared[4],
        summed[6],
        summed[7],
        summed[8],
        shared[5],
    )


def solution(mesh):
    in_specs = (
        P(("dp", "tensor"), None),
        P("dp"),
        P(),
        P(),
        P(None, "tensor"),
        P("tensor"),
        P(None, "tensor"),
        P(None, "tensor"),
        P("tensor"),
        P("tensor", None),
        P(),
        P(),
        P(),
        P(None, "tensor"),
        P("tensor"),
        P("tensor", None),
        P(),
        P(("dp", "tensor"), None),
    )
    out_specs = (
        P(("dp", "tensor"), None),
        P(("dp", "tensor"), None),
        P(),
        P(),
        P(None, "tensor"),
        P("tensor"),
        P(None, "tensor"),
        P(None, "tensor"),
        P("tensor"),
        P("tensor", None),
        P(),
        P(),
        P(),
        P(None, "tensor"),
        P("tensor"),
        P("tensor", None),
        P(),
    )
    return jax.shard_map(shards, mesh=mesh, in_specs=in_specs, out_specs=out_specs, check_vma=False)
```

time: 1920 us -> 1150 us (0.60)
  matrix products: 579 us -> 149 us
  waiting for transfers between devices: 943 us -> 614 us
  Pallas kernels: 0 us -> 211 us
  other arithmetic: 253 us -> 60.7 us
  local copies, waits for them, and re-layouts: 52.7 us -> 19.7 us
    dot_general x48 -> x0, matrix products: 420 us -> none  [the longest x8 102 us: shards(): jnp.einsum('hqd,hkd->hqk', out_grad, value_block, preferred_element_type=...]
    pallas_call x0 -> x2, Pallas kernels: none -> 211 us  [the longest x1 139 us: attn_bwd(): pl.pallas_call(functools.partial(bwd_kernel, T=T, pair=pair, bq=bq, bk=bk...]
    psum x1, waiting for transfers between devices: 356 us -> 179 us  [shards(): lax.psum(tuple((part.astype(jnp.bfloat16) for part in weight_parts)), 'dp')]
    convert_element_type x16 -> x6, other arithmetic: 129 us -> 13.3 us  [shards(): total.astype(jnp.float32)]
    reduce_sum x11 -> x2, other arithmetic: 75.3 us -> 9.11 us  [the longest x1 6.3 us: shards(): dense_bias_part = jnp.sum(resid_grad, axis=0)]
    reduce_scatter x1, waiting for transfers between devices: 124 us -> 66.9 us  [shards(): lax.psum_scatter(jnp.dot(active_low, down_weight, preferred_element_type=...]
    reduce_scatter x1, waiting for transfers between devices: 109 us -> 54.2 us  [shards(): lax.psum_scatter(jnp.einsum('tf,df->td', hidden_grad, up_weight, preferre...]
    reduce_scatter x1, waiting for transfers between devices: 126 us -> 71.2 us  [shards(): lax.psum_scatter(jnp.dot(mixed_heads, dense_weight, preferred_element_typ...]
  transfers between devices with their start and end apart: 9 -> 9, of which waited for: 9 -> 9; matrix products, arithmetic and copies ran while one was open for 7% -> 9% of each run, Pallas kernels for 0% -> 0%
where the time goes in v1:
time: 1150 us; the launch traced here: 1130 us
  waiting for transfers between devices  614 us (53%)
  Pallas kernels  211 us (18%)
  matrix products  149 us (13%)
  blocking collectives  64 us (6%)
  other arithmetic  60.7 us (5%)
  local copies, waits for them, and re-layouts  19.7 us (2%)
  between operations  15.7 us (1%)
    psum x1, waiting for transfers between devices, shards(): lax.psum(tuple((part.astype(jnp.bfloat16) for part in weight_parts)), 'dp')  179 us
    pallas_call x1, Pallas kernels, attn_bwd(): pl.pallas_call(functools.partial(bwd_kernel, T=T, pair=pair, bq=bq, bk=bk...  139 us
    pallas_call x1, Pallas kernels, attn_fwd(): pl.pallas_call(functools.partial(fwd_kernel, T=T, pair=pair, bq=bq, bk=bk...  72.3 us
    reduce_scatter x1, waiting for transfers between devices, shards(): lax.psum_scatter(jnp.dot(mixed_heads, dense_weight, preferred_element_typ...  71.2 us
    reduce_scatter x1, waiting for transfers between devices, shards(): lax.psum_scatter(jnp.dot(active_low, down_weight, preferred_element_type=...  66.9 us
    reduce_scatter x1, waiting for transfers between devices, shards(): lax.psum_scatter(jnp.einsum('tc,dc->td', proj_grad, joined, preferred_ele...  59.8 us
    all_gather x1, waiting for transfers between devices, shards(): post_all = lax.all_gather(post_low, 'tensor', axis=0, tiled=True)  57.8 us
    all_gather x1, waiting for transfers between devices, shards(): normed_all = lax.all_gather(normed_low, 'tensor', axis=0, tiled=True)  54.3 us
  transfers between devices with their start and end apart: 9, of which 9 were waited for; matrix products, arithmetic and copies ran while one was open for 9% of the time, Pallas kernels for 0%

profile of v1, /device:TPU:0, one launch (start us, length us, event | category | flops | bytes accessed | tf_op | source)
XLA Modules:
  0.0 1134.7 jit_solution(8528184202913396695)
XLA Ops:
  7.3 0.8 convert_element_type.133
  8.1 0.8 convert_element_type.134
  8.9 1.9 convert_reduce_fusion.3
  10.9 2.3 fusion.18
  13.2 0.6 copy-done.27
  13.8 0.6 copy-done.25
  14.4 2.1 fusion.16
  16.7 1.2 fusion.35
  19.2 0.5 exponential_multiply_fusion.slope_ref
  19.7 0.9 constant_dynamic-update-slice_fusion.2
  20.6 0.9 constant_dynamic-update-slice_fusion.1
  21.5 1.9 constant_dynamic-update-slice_fusion
  23.4 54.3 %all-gather.5.cloned.1.call-done = bf16[4096,1024]{1,0:T(8,128)(2,1)} async-done(((bf16[1024,1024]{1,0:T(8,128)(2,1)}), bf16[4096,1024]{1,0:T(8,128)(2,1)}) %all-gather.5.cloned.1.call-update) | async-done | bytes 8388624 | tf_op jit(solution)/shard_map/all_gather | solution.py:253
  77.7 9.6 fusion.36
  87.3 1.6 slice.51.k_ref
  88.9 2.7 fusion.23
  91.6 72.3 %attn_fwd_A1024_1024.1 = (bf16[4096,256]{1,0:T(8,128)(2,1)}, f32[4,1,4096]{2,1,0:T(1,128)}) custom-call(s32[1]{0:T(128)S(6)} %convert_element_type.131.apart_ref, f32[4]{0:T(128)} %exponential_multiply_fusion.slope_ref, bf16[4096,256]{1,0:T(8,128)(2,1)} %get-tuple-element.55.q_ref, bf16[4096,256]{1,0:T(8,128)(2,1)} %slice.51.k_ref, ...), custom_call_target="tpu_custom_call" | custom-call | tf_op jit(solution)/shard_map/attn_fwd_A1024_1024/pallas_call | solution.py:126
  164.0 7.2 convolution_convert_fusion.3
  171.2 0.6 copy-done.29
  171.9 71.2 %reduce-scatter.5.cloned.1.call-done = bf16[1024,1024]{1,0:T(8,128)(2,1)} async-done(((bf16[4096,1024]{1,0:T(8,128)(2,1)}), bf16[1024,1024]{1,0:T(8,128)(2,1)}) %reduce-scatter.5.cloned.1.call-update) | async-done | bytes 2097168 | tf_op jit(solution)/shard_map/reduce_scatter | solution.py:265
  243.1 3.1 fusion.27
  246.5 1.0 multiply_reduce_fusion
  247.6 2.4 add_convert_fusion.1
  250.1 0.5 all-gather.9.cloned.1.call-update
  250.7 57.8 %all-gather.7.cloned.1.call-done = bf16[4096,1024]{1,0:T(8,128)(2,1)} async-done(((bf16[1024,1024]{1,0:T(8,128)(2,1)}), bf16[4096,1024]{1,0:T(8,128)(2,1)}) %all-gather.7.cloned.1.call-update) | async-done | bytes 8388624 | tf_op jit(solution)/shard_map/all_gather | solution.py:276
  308.5 16.1 %fusion.37 = f32[4096,1024]{1,0:T(8,128)} fusion(bf16[4096,1024]{1,0:T(8,128)(2,1)} %all-gather.7.cloned.1.call-done, bf16[1024,1024]{1,0:T(8,128)(2,1)} %param.31), kind=kOutput, calls=%fused_computation.86 | convolution fusion | flops 8589934592 | bytes 27262976 | tf_op jit(solution)/shard_map/dot_general | solution.py:277
  324.6 43.7 %all-gather.9.cloned.1.call-done = bf16[4096,1024]{1,0:T(8,128)(2,1)} async-done(((bf16[1024,1024]{1,0:T(8,128)(2,1)}), bf16[4096,1024]{1,0:T(8,128)(2,1)}) %all-gather.9.cloned.1.call-update) | async-done | bytes 8388624 | tf_op jit(solution)/shard_map/all_gather | solution.py:291
  368.3 23.3 %convert_reduce_fusion = (f32[1024]{0:T(1024)S(1)}, bf16[4096,1024]{1,0:T(8,128)(2,1)S(1)}) fusion(f32[4096,1024]{1,0:T(8,128)} %fusion.37, f32[1024]{0:T(1024)S(1)} %convert_element_type.146, bf16[4096,1024]{1,0:T(8,128)(2,1)} %all-gather.9.cloned.1.call-done, bf16[1024,1024]{1,0:T(8,128)(2,1)S(1)} %copy-done), kind=kOutput, calls=%fused_computation.9 | convolution fusion | flops 8686402560 | bytes 35659776 | tf_op jit(solution)/shard_map/td,fd->tf/dot_general | solution.py:292
  391.6 3.2 copy-done.37
  394.8 11.2 convolution_convert_fusion.1
  406.0 16.9 %convolution_convert_fusion.2 = bf16[4096,1024]{1,0:T(8,128)(2,1)} fusion(bf16[1024,1024]{1,0:T(8,128)(2,1)S(1)} %copy-done, f32[4096,1024]{1,0:T(8,128)} %fusion.37, f32[1024]{0:T(1024)S(1)} %convert_element_type.146), kind=kOutput, calls=%fused_computation.13 | convolution fusion | flops 8636071936 | bytes 27267072 | tf_op jit(solution)/shard_map/dot_general | solution.py:283
  423.0 0.6 copy-done.33
  423.7 54.2 %reduce-scatter.9.cloned.1.call-done = bf16[1024,1024]{1,0:T(8,128)(2,1)} async-done(((bf16[4096,1024]{1,0:T(8,128)(2,1)}), bf16[1024,1024]{1,0:T(8,128)(2,1)}) %reduce-scatter.9.cloned.1.call-update) | async-done | bytes 2097168 | tf_op jit(solution)/shard_map/reduce_scatter | solution.py:297
  477.9 4.0 convert_reduce_fusion.2
  482.0 3.2 fusion.21
  485.2 66.9 %reduce-scatter.7.cloned.1.call-done = bf16[1024,1024]{1,0:T(8,128)(2,1)} async-done(((bf16[4096,1024]{1,0:T(8,128)(2,1)}), bf16[1024,1024]{1,0:T(8,128)(2,1)}) %reduce-scatter.7.cloned.1.call-update) | async-done | bytes 2097168 | tf_op jit(solution)/shard_map/reduce_scatter | solution.py:282
  552.0 6.3 fusion.33
  558.4 2.0 copy-done.7
  560.4 1.7 convert_element_type.156
  562.1 15.0 %convolution_convert_fusion.6 = bf16[1024,1024]{1,0:T(8,128)(2,1)} fusion(bf16[4096,1024]{1,0:T(8,128)(2,1)} %all-gather.7.cloned.1.call-done, bf16[4096,1024]{1,0:T(8,128)(2,1)} %copy-done.37), kind=kOutput, calls=%fused_computation.61 | convolution fusion | flops 8590983168 | bytes 18874368 | tf_op jit(solution)/shard_map/td,tf->df/dot_general | solution.py:294
  577.1 16.2 %convolution_convert_fusion.5 = bf16[1024,1024]{1,0:T(8,128)(2,1)} fusion(bf16[4096,1024]{1,0:T(8,128)(2,1)} %all-gather.9.cloned.1.call-done, f32[4096,1024]{1,0:T(8,128)} %fusion.37, f32[1024]{0:T(1024)S(1)} %convert_element_type.146), kind=kOutput, calls=%fused_computation.60 | convolution fusion | flops 8632926208 | bytes 27267072 | tf_op jit(solution)/shard_map/tf,td->fd/dot_general | solution.py:295
  593.4 27.2 %all-gather.11.cloned.1.call-done = bf16[4096,1024]{1,0:T(8,128)(2,1)} async-done(((bf16[1024,1024]{1,0:T(8,128)(2,1)}), bf16[4096,1024]{1,0:T(8,128)(2,1)}) %all-gather.11.cloned.1.call-update) | async-done | bytes 8388624 | tf_op jit(solution)/shard_map/all_gather | solution.py:306
  620.5 7.1 convolution_convert_fusion.4.do_ref
  627.6 138.7 %attn_bwd1024_512.1 = (bf16[4096,256]{1,0:T(8,128)(2,1)}, bf16[4096,256]{1,0:T(8,128)(2,1)}, bf16[4096,256]{1,0:T(8,128)(2,1)}) custom-call(s32[1]{0:T(128)S(6)} %convert_element_type.131.apart_ref, f32[4]{0:T(128)} %exponential_multiply_fusion.slope_ref, bf16[4096,256]{1,0:T(8,128)(2,1)} %get-tuple-element.55.q_ref, bf16[4096,256]{1,0:T(8,128)(2,1)} %slice.51.k_ref, ...), custom_call_target="tpu_custom_call" | custom-call | tf_op jit(solution)/shard_map/attn_bwd1024_512/pallas_call | solution.py:199
  766.3 1.9 constant_dynamic-update-slice_fusion.5
  769.3 11.8 %convolution_convert_fusion.7 = bf16[1024,768]{1,0:T(8,128)(2,1)S(1)} fusion(bf16[4096,1024]{1,0:T(8,128)(2,1)} %all-gather.5.cloned.1.call-done, bf16[4096,768]{1,0:T(8,128)(2,1)S(1)} %constant_dynamic-update-slice_fusion.3), kind=kOutput, calls=%fused_computation.62 | convolution fusion | flops 6443237376 | bytes 16252928 | tf_op jit(solution)/shard_map/td,tc->dc/dot_general | solution.py:317
  781.1 1.2 fusion.34
  782.3 1.0 copy-done.8
  783.3 3.2 convolution_convert_fusion.8
  786.5 11.3 convolution_convert_fusion
  797.8 2.8 convert_reduce_fusion.5
  800.6 24.0 %all-reduce.1 = (f32[256]{0:T(256)}, f32[256]{0:T(256)}, f32[1024]{0:T(1024)}) all-reduce(f32[256]{0:T(256)S(1)} %get-tuple-element.64, f32[256]{0:T(256)S(1)} %get-tuple-element.63, f32[1024]{0:T(1024)S(1)} %get-tuple-element.50), channel_id=1, replica_groups=mesh['dp'=8,'tensor'=4] {'dp'}, use_global_device_ids=true, to_apply=%region_18.0 | all-reduce | flops 1536 | bytes 12288 | tf_op jit(solution)/shard_map/psum | solution.py:340
  824.7 178.6 %all-reduce.5.cloned.1.call-done = (bf16[1024,256]{1,0:T(8,128)(2,1)}, bf16[1024,256]{1,0:T(8,128)(2,1)}, bf16[1024,256]{1,0:T(8,128)(2,1)}, bf16[256,1024]{1,0:...) async-done(((bf16[1024,256]{1,0:T(8,128)(2,1)}, bf16[1024,256]{1,0:T(8,128)(2,1)}, bf16[1024,256]{1,0:T(8,128)(2,1)}, bf16[256,1024]{1,0:T(8,128)(2,1)}, ...) | async-done | bytes 6291472 | tf_op jit(solution)/shard_map/psum | solution.py:338
  1003.3 2.2 convert_element_type.160
  1005.5 2.1 convert_element_type.162
  1007.6 2.1 convert_element_type.163
  1009.7 1.1 convert_element_type.166
  1010.8 2.9 convert_element_type.168
  1013.8 2.9 convert_element_type.171
  1016.6 59.8 %reduce-scatter.11.cloned.1.call-done = bf16[1024,1024]{1,0:T(8,128)(2,1)} async-done(((bf16[4096,1024]{1,0:T(8,128)(2,1)}), bf16[1024,1024]{1,0:T(8,128)(2,1)}) %reduce-scatter.11.cloned.1.call-update) | async-done | bytes 2097168 | tf_op jit(solution)/shard_map/reduce_scatter | solution.py:320
  1076.5 3.1 convert_reduce_fusion.1
  1079.6 2.7 fusion.22
  1082.3 40.0 %all-reduce = (f32[1024]{0:T(1024)}, f32[1024]{0:T(1024)}, f32[1024]{0:T(1024)}, f32[1024]{0:T(1024)}, f32[1024]{0:T(1024)}, /*index=5*/f32[1024]{0:T(1024)}) all-reduce(f32[1024]{0:T(1024)S(1)} %get-tuple-element.29, f32[1024]{0:T(1024)S(1)} %get-tuple-element.33, ...), channel_id=1, replica_groups=mesh['dp'=8,'tensor'=4] {'dp','tensor'}, use_global_device_ids=true, to_apply=%region_13.0 | all-reduce | flops 6144 | bytes 49152 | tf_op jit(solution)/shard_map/psum | solution.py:342
  1122.4 5.6 add_add_fusion.2
  (108 shorter events, 2.2 us)
Async XLA Ops:
  7.2 361.1 %copy-start = (bf16[1024,1024]{1,0:T(8,128)(2,1)S(1)}, bf16[1024,1024]{1,0:T(8,128)(2,1)}, u32[]{:S(2)}) copy-start(bf16[1024,1024]{1,0:T(8,128)(2,1)} %param.33) | copy-start | bytes 6291460
  7.2 70.5 %all-gather.5.cloned.1.call-start = ((), (), s32[]{:S(2)}) async-start(), calls=%async_computation.4 | async-start | bytes 10485760 | tf_op jit(solution)/shard_map/all_gather | solution.py:253
  7.3 7.2 copy-start.2
  8.1 5.7 copy-start.23
  10.8 3.0 copy-start.21
  10.8 5.8 copy-start.35
  10.9 5.8 copy-start.36
  10.9 8.9 copy-start.19
  13.2 0.6 copy-start.27
  13.8 6.8 copy-start.20
  13.8 0.6 copy-start.25
  16.6 226.4 %reduce-scatter.5.cloned.1.call-start = ((), (), s32[]{:S(2)}) async-start(), calls=%async_computation.5 | async-start | bytes 10485760 | tf_op jit(solution)/shard_map/reduce_scatter | solution.py:265
  91.6 72.3 %copy-start.16 = (bf16[256,1024]{1,0:T(8,128)(2,1)S(1)}, bf16[256,1024]{1,0:T(8,128)(2,1)}, u32[]{:S(2)}) copy-start(bf16[256,1024]{1,0:T(8,128)(2,1)} %param.27) | copy-start | bytes 1572868
  171.1 0.7 copy-start.29
  171.1 0.7 copy-start.30
  171.1 0.7 copy-start.31
  171.2 137.3 %all-gather.7.cloned.1.call-start = ((), (), s32[]{:S(2)}) async-start(), calls=%async_computation.6 | async-start | bytes 10485760 | tf_op jit(solution)/shard_map/all_gather | solution.py:276
  243.0 3.1 copy-start.3
  243.0 3.5 copy-start.5
  247.6 3.1 copy-start.32
  250.1 118.3 %all-gather.9.cloned.1.call-start = ((), (), s32[]{:S(2)}) async-start(), calls=%async_computation.8 | async-start | bytes 10485760 | tf_op jit(solution)/shard_map/all_gather | solution.py:291
  250.6 227.2 %reduce-scatter.9.cloned.1.call-start = ((), (), s32[]{:S(2)}) async-start(), calls=%async_computation.9 | async-start | bytes 10485760 | tf_op jit(solution)/shard_map/reduce_scatter | solution.py:297
  368.3 26.5 %copy-start.34 = (bf16[1024,1024]{1,0:T(8,128)(2,1)S(1)}, bf16[1024,1024]{1,0:T(8,128)(2,1)}, u32[]{:S(2)}) copy-start(bf16[1024,1024]{1,0:T(8,128)(2,1)} %param.31) | copy-start | bytes 6291460
  391.6 3.2 copy-start.37
  406.0 146.1 %reduce-scatter.7.cloned.1.call-start = ((), (), s32[]{:S(2)}) async-start(), calls=%async_computation.7 | async-start | bytes 10485760 | tf_op jit(solution)/shard_map/reduce_scatter | solution.py:282
  423.0 0.7 copy-start.33
  423.0 54.9 %copy-start.4 = (bf16[1024,1024]{1,0:T(8,128)(2,1)S(1)}, bf16[1024,1024]{1,0:T(8,128)(2,1)}, u32[]{:S(2)}) copy-start(bf16[1024,1024]{1,0:T(8,128)(2,1)} %param.18) | copy-start | bytes 6291460
  423.0 197.5 %all-gather.11.cloned.1.call-start = ((), (), s32[]{:S(2)}) async-start(), calls=%async_computation.10 | async-start | bytes 10485760 | tf_op jit(solution)/shard_map/all_gather | solution.py:306
  477.9 4.1 copy-start.6
  477.9 4.1 copy-start.9
  558.4 2.0 copy-start.7
  562.1 441.2 %all-reduce.5.cloned.1.call-start = ((), (), s32[]{:S(2)}) async-start(), calls=%async_computation.12 | async-start | bytes 12582912 | tf_op jit(solution)/shard_map/psum | solution.py:338
  577.1 43.4 %copy-start.17 = (bf16[256,1024]{1,0:T(8,128)(2,1)S(1)}, bf16[256,1024]{1,0:T(8,128)(2,1)}, u32[]{:S(2)}) copy-start(bf16[256,1024]{1,0:T(8,128)(2,1)} %param.27) | copy-start | bytes 1572868
  766.3 2.2 copy-start.14
  766.3 2.8 copy-start.11
  769.2 13.1 %slice-start = ((s8[8388608]{0:T(1024)(128)(4,1)}), s8[4194304]{0:T(1024)(128)(4,1)S(1)}, s32[]{:S(2)}) async-start(s8[8388608]{0:T(1024)(128)(4,1)} %bitcast.22), calls=%async_computation.13 | async-start | bytes 8388608
  769.3 11.8 %copy-start.15 = (bf16[4096,768]{1,0:T(8,128)(2,1)}, bf16[4096,768]{1,0:T(8,128)(2,1)S(1)}, u32[]{:S(2)}) copy-start(bf16[4096,768]{1,0:T(8,128)(2,1)S(1)} %constant_dynamic-update-slice_fusion.3) | copy-start | bytes 18874372
  769.3 13.0 %slice-start.1 = ((s8[8388608]{0:T(1024)(128)(4,1)}), s8[4194304]{0:T(1024)(128)(4,1)S(1)}, s32[]{:S(2)}) async-start(s8[8388608]{0:T(1024)(128)(4,1)} %bitcast.22), calls=%async_computation.14 | async-start | bytes 8388608
  781.1 2.2 copy-start.8
  786.5 290.0 %reduce-scatter.11.cloned.1.call-start = ((), (), s32[]{:S(2)}) async-start(), calls=%async_computation.11 | async-start | bytes 10485760 | tf_op jit(solution)/shard_map/reduce_scatter | solution.py:320
  1003.3 6.4 copy-start.18
  1003.3 7.5 copy-start.13
  1009.7 4.0 copy-start.12
  1013.7 62.7 %copy-start.22 = (f32[1024]{0:T(1024)S(1)}, f32[1024]{0:T(1024)}, u32[]{:S(2)}) copy-start(f32[1024]{0:T(1024)} %copy-done.21) | copy-start | bytes 12292
  1013.7 62.7 %copy-start.24 = (f32[1024]{0:T(1024)S(1)}, f32[1024]{0:T(1024)}, u32[]{:S(2)}) copy-start(f32[1024]{0:T(1024)} %copy-done.23) | copy-start | bytes 12292
  1013.7 65.8 %copy-start.28 = (f32[1024]{0:T(1024)S(1)}, f32[1024]{0:T(1024)}, u32[]{:S(2)}) copy-start(f32[1024]{0:T(1024)} %copy-done.27) | copy-start | bytes 12292
  1013.7 65.8 %copy-start.26 = (f32[1024]{0:T(1024)S(1)}, f32[1024]{0:T(1024)}, u32[]{:S(2)}) copy-start(f32[1024]{0:T(1024)} %copy-done.25) | copy-start | bytes 12292
  1076.5 3.1 copy-start.10
  1082.3 45.7 %copy-start.1 = (bf16[1024,1024]{1,0:T(8,128)(2,1)S(1)}, bf16[1024,1024]{1,0:T(8,128)(2,1)}, u32[]{:S(2)}) copy-start(bf16[1024,1024]{1,0:T(8,128)(2,1)} %param.33) | copy-start | bytes 6291460
Sparse Core Ops, SparseCore 0:
  16.7 60.9 all-gather.4
  171.3 71.7 reduce-scatter.4
  250.2 58.2 all-gather.6
  310.0 58.2 all-gather.8
  406.1 71.7 reduce-scatter.8
  480.3 71.6 reduce-scatter.6
  562.2 58.2 all-gather.10
  786.6 216.6 all-reduce.4
  1005.9 70.5 reduce-scatter.10

commit v2 on v0

v2 whole, which is shorter than its diff:
```python
import functools
import math

import jax
import jax.numpy as jnp
from jax import lax
from jax.experimental import pallas as pl
from jax.experimental.pallas import tpu as pltpu
from jax.sharding import PartitionSpec as P

HEADS = 16
HD = 64
SHORT = 2048
EPSILON = 1e-05
LOG2E = math.log2(math.e)
F32 = jnp.float32
BF16 = jnp.bfloat16
NT = (((1,), (1,)), ((), ()))
NN = (((1,), (0,)), ((), ()))
TN = (((0,), (0,)), ((), ()))


def dot(lhs, rhs, dims=NN):
    return lax.dot_general(lhs, rhs, dims, preferred_element_type=F32)


def low(array):
    return array.astype(BF16)


def norm_stats(rows):
    center = jnp.mean(rows, axis=-1, keepdims=True)
    centered = rows - center
    inverse = lax.rsqrt(jnp.mean(centered * centered, axis=-1, keepdims=True) + EPSILON)
    return centered * inverse, inverse


def norm_pull(grad, normal, inverse):
    grad_mean = jnp.mean(grad, axis=-1, keepdims=True)
    dot_mean = jnp.mean(grad * normal, axis=-1, keepdims=True)
    return inverse * (grad - grad_mean - normal * dot_mean)


def lanes(count):
    return lax.broadcasted_iota(jnp.int32, (count, 128), 1)


def places(count, first):
    return lax.broadcasted_iota(jnp.int32, (count, 128), 0) + first


def widen(head):
    return jnp.concatenate([head.astype(F32), jnp.zeros((head.shape[0], HD), F32)], axis=1)


def split3(value):
    high = low(value).astype(F32)
    middle = low(value - high).astype(F32)
    return high, middle, value - high - middle


def pick3(index, parts):
    return jnp.where(index == 0, parts[0], jnp.where(index == 1, parts[1], parts[2]))


def key_columns(head, first):
    count = head.shape[0]
    lane, place = lanes(count), places(count, first)
    coarse = ((place >> 6) << 6).astype(F32)
    fine = (place & 63).astype(F32)
    wall = jnp.where(place < SHORT, -1e30, 0.0)
    extra = jnp.where(lane < 73, -1.0, jnp.where(lane == 73, wall, 0.0))
    extra = jnp.where(lane < 67, coarse, jnp.where(lane < 70, fine, extra))
    return low(jnp.where(lane < HD, widen(head), extra))


def query_columns(head, first, slope, apart, log_total=None):
    count = head.shape[0]
    lane, place = lanes(count), places(count, first)
    extra = pick3(jnp.where(lane < 67, lane - 64, lane - 67), split3(slope))
    extra = jnp.where(lane < 70, extra, 0.0)
    if log_total is not None:
        extra = jnp.where((lane >= 70) & (lane < 73), pick3(lane - 70, split3(log_total)), extra)
    extra = jnp.where(lane == 73, jnp.where(place >= SHORT, apart, 0.0), extra)
    return low(jnp.where(lane < HD, widen(head), extra))


def ones_columns(head, count):
    lane = lanes(head.shape[0])
    return low(jnp.where(lane < HD, widen(head), jnp.where(lane < HD + count, 1.0, 0.0)))


def grad_columns(head, shift):
    lane = lanes(head.shape[0])
    extra = jnp.where(lane < 67, pick3(lane - 64, split3(shift)), 0.0)
    return low(jnp.where(lane < HD, widen(head), extra))


def each_chunk(me, slots, rows, body):
    chunk = min(rows, 512)
    for slot in range(slots):
        home = (me ^ slot) * rows

        @pl.loop(0, rows // chunk)
        def _(step):
            offset = pl.multiple_of(step * chunk, chunk)
            body(slot, pl.ds(offset, chunk), pl.ds(slot * rows + offset, chunk), home + offset)


def attend_kernel(
    me_ref, apart_ref, slope_ref, q_ref, k_ref, v_ref, o_ref, lse_ref, qa, ka, va, *, slots, pair, tile
):
    me = me_ref[0]
    total = q_ref.shape[0]
    rows = total // slots
    chunk = min(rows, 512)
    apart = apart_ref[0].astype(F32)

    def prepare(slot, inner, spot, place):
        place = pl.multiple_of(place, chunk)
        home = pl.ds(place, chunk)
        for s in range(pair):
            cols = slice(s * HD, (s + 1) * HD)
            qa[s, home, :] = query_columns(q_ref[spot, cols], place, slope_ref[s], apart)
            ka[s, home, :] = key_columns(k_ref[spot, cols], place)
            va[s, home, :] = ones_columns(v_ref[spot, cols], 1)

    each_chunk(me, slots, rows, prepare)
    causal = lax.broadcasted_iota(jnp.int32, (tile, tile), 1) <= lax.broadcasted_iota(
        jnp.int32, (tile, tile), 0
    )
    piece = min(rows, tile)

    def query_tile(index, _):
        first = pl.multiple_of(index * tile, tile)
        queries = [qa[s, pl.ds(first, tile), :] for s in range(pair)]

        def step(at, carry, diagonal):
            after = []
            for s in range(pair):
                top, mix = carry[s]
                scores = dot(queries[s], ka[s, pl.ds(at, tile), :], NT)
                if diagonal:
                    scores = jnp.where(causal, scores, -1e30)
                higher = jnp.maximum(top, jnp.max(scores, axis=1, keepdims=True))
                weights = low(jnp.exp2(scores - higher))
                mix = mix * jnp.exp2(top - higher) + dot(weights, va[s, pl.ds(at, tile), :])
                after.append((higher, mix))
            return tuple(after)

        carry = tuple(
            (jnp.full((tile, 1), -1e38, F32), jnp.zeros((tile, 128), F32)) for _ in range(pair)
        )
        carry = step(first, carry, True)
        carry = lax.fori_loop(
            0, index, lambda at, held: step(pl.multiple_of(at * tile, tile), held, False), carry
        )
        outs = []
        for s in range(pair):
            top, mix = carry[s]
            weight = mix[:, HD : HD + 1]
            outs.append(mix[:, :HD] * (1.0 / weight))
            lse_ref[s, 0, pl.ds(first, tile)] = (top + jnp.log2(weight))[:, 0]
        out = low(jnp.concatenate(outs, axis=1))
        for part in range(tile // piece):
            block = (index * (tile // piece) + part) // (rows // piece)
            offset = first + part * piece - block * rows
            spot = pl.multiple_of((block ^ me) * rows + offset, piece)
            o_ref[pl.ds(spot, piece), :] = out[part * piece : (part + 1) * piece]
        return 0

    lax.fori_loop(0, total // tile, query_tile, 0)


def attend(me, apart, slopes, queries, key_rows, values, slots, group, tile=1024):
    total, width = queries.shape
    pair = min(2, width // HD)
    cols = pair * HD
    spec = pl.BlockSpec((total, cols), lambda g: (0, group))
    scalars = pl.BlockSpec(memory_space=pltpu.SMEM)
    return pl.pallas_call(
        functools.partial(attend_kernel, slots=slots, pair=pair, tile=tile),
        grid=(1,),
        in_specs=[scalars] * 3 + [spec] * 3,
        out_specs=[
            pl.BlockSpec((total, cols), lambda g: (0, 0)),
            pl.BlockSpec((pair, 1, total), lambda g: (0, 0, 0)),
        ],
        out_shape=[
            jax.ShapeDtypeStruct((total, cols), BF16),
            jax.ShapeDtypeStruct((pair, 1, total), F32),
        ],
        scratch_shapes=[pltpu.VMEM((pair, total, 128), BF16)] * 3,
        compiler_params=pltpu.CompilerParams(vmem_limit_bytes=56 << 20),
        cost_estimate=pl.CostEstimate(
            flops=pair * 1100 * total * total, transcendentals=0, bytes_accessed=8 * total * cols
        ),
        name="attend",
    )(me, apart, slopes[group * pair : (group + 1) * pair], queries, key_rows, values)


def attend_back_kernel(*refs, slots, pair, tile, key_tile):
    me_ref, apart_ref, slope_ref, q_ref, k_ref, v_ref, o_ref, lse_ref = refs[:8]
    g_refs = refs[8 : 8 + slots]
    dq_ref, dk_ref, dv_ref, qa, ka, va, ga, kt, dq_sum = refs[8 + slots :]
    me = me_ref[0]
    total = q_ref.shape[0]
    rows = total // slots
    chunk = min(rows, 512)
    apart = apart_ref[0].astype(F32)

    def prepare(slot, inner, spot, place):
        place = pl.multiple_of(place, chunk)
        home = pl.ds(place, chunk)
        for s in range(pair):
            cols = slice(s * HD, (s + 1) * HD)
            log_total = lse_ref[s, :, home].T
            qa[s, home, :] = query_columns(q_ref[spot, cols], place, slope_ref[s], apart, log_total)
            keys = key_columns(k_ref[spot, cols], place)
            ka[s, home, :] = keys
            kt[s, :, home] = low(keys.astype(F32).T)
            va[s, home, :] = ones_columns(v_ref[spot, cols], 3)
            grad = g_refs[slot][inner, cols]
            row_dot = jnp.sum(
                grad.astype(F32) * o_ref[spot, cols].astype(F32), axis=1, keepdims=True
            )
            ga[s, home, :] = grad_columns(grad, -row_dot)
            dq_sum[s, :, home] = jnp.zeros((128, chunk), F32)

    each_chunk(me, slots, rows, prepare)
    causal = lax.broadcasted_iota(jnp.int32, (key_tile, key_tile), 0) <= lax.broadcasted_iota(
        jnp.int32, (key_tile, key_tile), 1
    )
    piece = min(rows, key_tile)

    def place_of(place, size):
        block = place // rows
        return pl.multiple_of((block ^ me) * rows + (place - block * rows), size)

    def keys_tile(index, _):
        first = pl.multiple_of(index * key_tile, key_tile)
        here = pl.ds(first, key_tile)

        def step(at, carry, diagonal, width):
            after = []
            for s in range(pair):
                dk, dv = carry[s]
                there = pl.ds(at, width)
                queries, grads = qa[s, there, :], ga[s, there, :]
                probs = jnp.exp2(dot(ka[s, here, :], queries, NT))
                if diagonal:
                    probs = jnp.where(causal, probs, 0.0)
                dv = dv + dot(low(probs), grads)
                score_grad = low(probs * dot(va[s, here, :], grads, NT))
                dk = dk + dot(score_grad, queries)
                dq_sum[s, :, there] += dot(kt[s, :, here], score_grad)
                after.append((dk, dv))
            return tuple(after)

        zeros = jnp.zeros((key_tile, 128), F32)
        carry = step(first, tuple((zeros, zeros) for _ in range(pair)), True, key_tile)
        start = first + key_tile
        short = jnp.minimum((-start) % tile, total - start) // key_tile
        if tile > key_tile:
            carry = lax.fori_loop(
                0,
                short,
                lambda at, held: step(
                    pl.multiple_of(start + at * key_tile, key_tile), held, False, key_tile
                ),
                carry,
            )
            start = start + short * key_tile
        carry = lax.fori_loop(
            0,
            (total - start) // tile,
            lambda at, held: step(
                pl.multiple_of(start + at * tile, min(tile, key_tile)), held, False, tile
            ),
            carry,
        )
        dk = low(jnp.concatenate([held[0][:, :HD] * (1.0 / LOG2E) for held in carry], axis=1))
        dv = low(jnp.concatenate([held[1][:, :HD] for held in carry], axis=1))
        for part in range(key_tile // piece):
            spot = pl.ds(place_of(first + part * piece, piece), piece)
            dk_ref[spot, :] = dk[part * piece : (part + 1) * piece]
            dv_ref[spot, :] = dv[part * piece : (part + 1) * piece]
        return 0

    lax.fori_loop(0, total // key_tile, keys_tile, 0)

    def finish(slot, inner, spot, place):
        home = pl.ds(pl.multiple_of(place, chunk), chunk)
        joined = jnp.concatenate([dq_sum[s, :HD, home] for s in range(pair)], axis=0)
        dq_ref[spot, :] = low(joined.T * HD**-0.5)

    each_chunk(me, slots, rows, finish)


def attend_back(
    me, apart, slopes, queries, key_rows, values, mixed, log_total, grads, group, tile=1024, key_tile=512
):
    slots = len(grads)
    total, width = queries.shape
    pair = min(2, width // HD)
    cols = pair * HD
    spec = pl.BlockSpec((total, cols), lambda g: (0, group))
    out_spec = pl.BlockSpec((total, cols), lambda g: (0, 0))
    scalars = pl.BlockSpec(memory_space=pltpu.SMEM)
    return pl.pallas_call(
        functools.partial(
            attend_back_kernel, slots=slots, pair=pair, tile=tile, key_tile=key_tile
        ),
        grid=(1,),
        in_specs=[scalars] * 3
        + [spec] * 3
        + [out_spec, pl.BlockSpec((pair, 1, total), lambda g: (0, 0, 0))]
        + [pl.BlockSpec((total // slots, cols), lambda g: (0, group))] * slots,
        out_specs=[out_spec] * 3,
        out_shape=[jax.ShapeDtypeStruct((total, cols), BF16)] * 3,
        scratch_shapes=[pltpu.VMEM((pair, total, 128), BF16)] * 4
        + [pltpu.VMEM((pair, 128, total), BF16), pltpu.VMEM((pair, 128, total), F32)],
        compiler_params=pltpu.CompilerParams(vmem_limit_bytes=60 << 20),
        cost_estimate=pl.CostEstimate(
            flops=pair * 2200 * total * total, transcendentals=0, bytes_accessed=16 * total * cols
        ),
        name="attend_back",
    )(
        me,
        apart,
        slopes[group * pair : (group + 1) * pair],
        queries,
        key_rows,
        values,
        mixed,
        log_total,
        *grads,
    )


def post_kernel(*refs, slots, groups):
    mixed_refs = refs[: slots * groups]
    x_ref, weight_ref, bias_ref, gain_ref, shift_ref, post_ref, residual_ref = refs[slots * groups :]
    mixed = jnp.concatenate([ref[...] for ref in mixed_refs], axis=1)
    residual = x_ref[...].astype(F32) + dot(mixed, weight_ref[...]) + bias_ref[...].astype(F32)
    normal, _ = norm_stats(residual)
    post_ref[...] = low(normal * gain_ref[...].astype(F32) + shift_ref[...].astype(F32))
    own = residual_ref.shape[0]
    step = pl.program_id(0)

    @pl.when(step < pl.num_programs(0) // slots)
    def _():
        residual_ref[...] = residual


def post_norm(mixed, x_all, weight, bias, gain, shift):
    slots, groups = len(mixed), len(mixed[0])
    total, width = x_all.shape
    rows = total // slots
    block = min(rows, 512)
    per = rows // block
    specs = []
    for slot in range(slots):
        for part in mixed[slot]:
            specs.append(
                pl.BlockSpec(
                    (block, part.shape[1]),
                    lambda i, slot=slot: (((i // per) ^ slot) * per + i % per, 0),
                )
            )
    whole = lambda shape: pl.BlockSpec(shape, lambda i: (0, 0))
    return pl.pallas_call(
        functools.partial(post_kernel, slots=slots, groups=groups),
        grid=(total // block,),
        in_specs=specs
        + [
            pl.BlockSpec((block, width), lambda i: (i, 0)),
            whole(weight.shape),
            whole((1, width)),
            whole((1, width)),
            whole((1, width)),
        ],
        out_specs=[
            pl.BlockSpec((block, width), lambda i: (i, 0)),
            pl.BlockSpec((block, width), lambda i: (jnp.minimum(i, per - 1), 0)),
        ],
        out_shape=[
            jax.ShapeDtypeStruct((total, width), BF16),
            jax.ShapeDtypeStruct((rows, width), F32),
        ],
        compiler_params=pltpu.CompilerParams(vmem_limit_bytes=48 << 20),
        cost_estimate=pl.CostEstimate(
            flops=2 * total * width * width, transcendentals=0, bytes_accessed=6 * total * width
        ),
        name="post_norm",
    )(
        *[part for parts in mixed for part in parts],
        x_all,
        weight,
        bias[None],
        gain[None],
        shift[None],
    )


def shards(
    slots,
    layer_input,
    row_ids,
    input_gain,
    input_shift,
    query_weight,
    query_bias,
    key_weight,
    value_weight,
    value_bias,
    dense_weight,
    dense_bias,
    post_gain,
    post_shift,
    up_weight,
    up_bias,
    down_weight,
    down_bias,
    cotangent,
):
    me = lax.axis_index("tensor")
    me_word = me.astype(jnp.int32)[None]
    rows = layer_input.shape[0]
    head_cols = query_weight.shape[1]
    head_count = head_cols // HD
    groups = max(1, head_count // 2)
    bits = [1 << level for level in range(slots.bit_length() - 1)]
    after = lambda array, *others: lax.optimization_barrier((array, *others))[0]

    def swap(array, mask):
        return lax.ppermute(array, "tensor", [(i, i ^ mask) for i in range(slots)])

    def gather(array):
        held = {0: array}
        for bit in reversed(bits):
            held.update({slot ^ bit: swap(part, bit) for slot, part in held.items()})
        return [held[slot] for slot in range(slots)]

    def scatter_sum(parts):
        held = dict(enumerate(parts))
        for bit in bits:
            held = {
                slot: part.astype(F32) + swap(low(held[slot | bit]), bit).astype(F32)
                for slot, part in held.items()
                if not slot & bit
            }
        return held[0]

    def blocks(array):
        return [array[slot * rows : (slot + 1) * rows] for slot in range(slots)]

    x_parts = gather(layer_input)
    cot_own = after(cotangent, x_parts[-1])
    dense_parts = gather(after(dense_weight, x_parts[-1]))
    cot_parts = gather(cot_own)

    x_all = jnp.concatenate(x_parts, axis=0)
    gain, shift = input_gain.astype(F32), input_shift.astype(F32)
    normed = low(norm_stats(x_all.astype(F32))[0] * gain + shift)
    joined = jnp.concatenate([query_weight, key_weight, value_weight], axis=1)
    projected = dot(normed, joined)
    queries = low((projected[:, :head_cols] + query_bias.astype(F32)) * (LOG2E * HD**-0.5))
    key_rows = low(projected[:, head_cols : 2 * head_cols])
    values = low(projected[:, 2 * head_cols :] + value_bias.astype(F32))
    heads = me * head_count + jnp.arange(head_count)
    slopes = jnp.exp2(-8.0 * (heads + 1).astype(F32) / HEADS) * LOG2E
    apart = (row_ids[:1] != row_ids[SHORT : SHORT + 1]).astype(jnp.int32)

    mixed_own, log_totals, mixed_parts = [], [], []
    for group in range(groups):
        mixed, log_total = attend(
            me_word, apart, slopes, queries, key_rows, values, slots, group
        )
        mixed_own.append(mixed)
        log_totals.append(log_total)
        mixed_parts.append(gather(mixed))
    mixed_all = [[mixed_parts[group][slot] for group in range(groups)] for slot in range(slots)]
    dense_all = jnp.concatenate(dense_parts, axis=0)
    post_all, residual = post_norm(mixed_all, x_all, dense_all, dense_bias, post_gain, post_shift)

    cot_all = jnp.concatenate(cot_parts, axis=0)
    hidden = dot(post_all, up_weight) + up_bias.astype(F32)
    active, gelu_pull = jax.vjp(lambda v: jax.nn.gelu(v, approximate=True), hidden)
    active = low(active)
    hidden_grad = low(gelu_pull(dot(cot_all, down_weight, NT))[0])
    half = slots // 2 * rows
    far = low(dot(hidden_grad[half:], up_weight, NT))
    near = low(dot(after(hidden_grad[:half], far), up_weight, NT))
    post_grad = scatter_sum(blocks(jnp.concatenate([near, far], axis=0)))
    hidden_late, active_late = lax.optimization_barrier((hidden_grad, active, near))[:2]
    up_part = dot(post_all, hidden_late, TN)
    down_part = dot(active_late, cot_all, TN)
    up_bias_part = jnp.sum(hidden_grad.astype(F32), axis=0)
    up_sum, down_sum = lax.psum((low(up_part), low(down_part)), "dp")

    cot_rows = cotangent.astype(F32)
    post_normal, post_inverse = norm_stats(residual)
    resid_grad = cot_rows + norm_pull(
        post_grad * post_gain.astype(F32), post_normal, post_inverse
    )
    attended_grad = low(resid_grad)
    mixed_grad = low(dot(attended_grad, dense_all, NT))
    mixed_grads = [
        swap(part, slot) if slot else part
        for slot, part in enumerate(jnp.split(mixed_grad, slots, axis=1))
    ]

    ffn_part = low(dot(after(active, *mixed_grads), down_weight))
    ffn_out = scatter_sum(blocks(ffn_part))
    layer_output = low(residual + ffn_out + down_bias.astype(F32))
    mixed_rows = jnp.concatenate(
        [
            part[slot * rows : (slot + 1) * rows]
            for slot, parts in enumerate(mixed_all)
            for part in parts
        ],
        axis=1,
    )
    dense_part = dot(mixed_rows, attended_grad, TN)
    dense_part = scatter_sum(
        [dense_part[slot * head_cols : (slot + 1) * head_cols] for slot in range(slots)]
    )

    def total_of(vectors, own):
        flat = jnp.concatenate(vectors + own)
        pad = -flat.shape[0] % 1024
        flat = jnp.pad(flat, (0, pad)).reshape(-1, 1024)
        every = lax.all_gather(flat, ("dp", "tensor"), axis=0)
        every = every.reshape(-1, slots, flat.size)
        shared = jnp.sum(every, axis=(0, 1))
        mine = jnp.sum(lax.dynamic_index_in_dim(every, me, 1, keepdims=False), axis=0)
        outs, at = [], 0
        for vector, source in [(v, shared) for v in vectors] + [(v, mine) for v in own]:
            outs.append(source[at : at + vector.shape[0]])
            at += vector.shape[0]
        return outs

    down_bias_grad, dense_bias_grad, post_gain_grad, post_shift_grad, up_bias_grad = total_of(
        [
            jnp.sum(cot_rows, axis=0),
            jnp.sum(resid_grad, axis=0),
            jnp.sum(post_grad * post_normal, axis=0),
            jnp.sum(post_grad, axis=0),
        ],
        [up_bias_part],
    )

    head_grads = [
        attend_back(
            me_word,
            apart,
            slopes,
            queries,
            key_rows,
            values,
            mixed_own[group],
            log_totals[group],
            mixed_grads,
            group,
        )
        for group in range(groups)
    ]
    proj_grad = jnp.concatenate(
        [head_grads[group][kind] for kind in range(3) for group in range(groups)], axis=1
    )
    far = low(dot(proj_grad[half:], joined, NT))
    near = low(dot(after(proj_grad[:half], far), joined, NT))
    normed_grad = scatter_sum(blocks(jnp.concatenate([near, far], axis=0)))
    proj_late = after(proj_grad, near)
    joined_part = dot(normed, proj_late, TN)
    proj_sum = jnp.sum(proj_grad.astype(F32), axis=0)
    joined_high = joined.astype(F32)
    shift_part = jnp.sum(joined_high * proj_sum, axis=1)
    gain_part = (jnp.sum(joined_high * joined_part, axis=1) - shift * shift_part) / gain
    late = lax.optimization_barrier((low(joined_part), low(dense_part), up_sum, down_sum))
    joined_sum, dense_sum = lax.psum(late[:2], "dp")
    input_gain_grad, input_shift_grad, query_bias_grad, value_bias_grad = total_of(
        [gain_part, shift_part], [proj_sum[:head_cols], proj_sum[2 * head_cols :]]
    )

    input_normal, input_inverse = norm_stats(layer_input.astype(F32))
    input_grad = resid_grad + norm_pull(normed_grad * gain, input_normal, input_inverse)
    joined_sum = joined_sum.astype(F32)
    return (
        layer_output,
        input_grad,
        input_gain_grad,
        input_shift_grad,
        joined_sum[:, :head_cols],
        query_bias_grad,
        joined_sum[:, head_cols : 2 * head_cols],
        joined_sum[:, 2 * head_cols :],
        value_bias_grad,
        dense_sum.astype(F32),
        dense_bias_grad,
        post_gain_grad,
        post_shift_grad,
        late[2].astype(F32),
        up_bias_grad,
        late[3].astype(F32),
        down_bias_grad,
    )


def solution(mesh):
    in_specs = (
        P(("dp", "tensor"), None),
        P("dp"),
        P(),
        P(),
        P(None, "tensor"),
        P("tensor"),
        P(None, "tensor"),
        P(None, "tensor"),
        P("tensor"),
        P("tensor", None),
        P(),
        P(),
        P(),
        P(None, "tensor"),
        P("tensor"),
        P("tensor", None),
        P(),
        P(("dp", "tensor"), None),
    )
    out_specs = (
        P(("dp", "tensor"), None),
        P(("dp", "tensor"), None),
        P(),
        P(),
        P(None, "tensor"),
        P("tensor"),
        P(None, "tensor"),
        P(None, "tensor"),
        P("tensor"),
        P("tensor", None),
        P(),
        P(),
        P(),
        P(None, "tensor"),
        P("tensor"),
        P("tensor", None),
        P(),
    )
    return jax.shard_map(
        functools.partial(shards, mesh.shape["tensor"]), mesh=mesh, in_specs=in_specs, out_specs=out_specs, check_vma=False)
```

time: 1920 us -> 819 us (0.43)
  waiting for transfers between devices: 943 us -> 115 us
  matrix products: 579 us -> 140 us
  Pallas kernels: 0 us -> 233 us
  other arithmetic: 253 us -> 75.3 us
  blocking collectives: 67 us -> 134 us
  local copies, waits for them, and re-layouts: 52.7 us -> 80.2 us
    dot_general x60 -> x13, matrix products: 579 us -> 140 us  [dot(): return lax.dot_general(lhs, rhs, dims, preferred_element_type=F32)]
    reduce_scatter x4 -> x0, waiting for transfers between devices: 409 us -> none  [the longest x1 126 us: shards(): lax.psum_scatter(jnp.dot(mixed_heads, dense_weight, preferred_element_typ...]
    psum x1 -> x2, waiting for transfers between devices: 356 us -> 0.01 us  [the longest x1 0.01 us: shards(): up_sum, down_sum = lax.psum((low(up_part), low(down_part)), 'dp')]
    pallas_call x0 -> x5, Pallas kernels: none -> 233 us  [the longest x2 140 us: attend_back(): pl.pallas_call(functools.partial(attend_back_kernel, slots=slots, pair=pa...]
    all_gather x4 -> x0, waiting for transfers between devices: 178 us -> none  [the longest x1 58.4 us: shards(): lax.all_gather(resid_grad.astype(jnp.bfloat16), 'tensor', axis=0, tiled=T...]
    all_gather x0 -> x2, blocking collectives: none -> 134 us  [total_of(): every = lax.all_gather(flat, ('dp', 'tensor'), axis=0)]
    ppermute x0 -> x30, waiting for transfers between devices: none -> 115 us  [swap(): return lax.ppermute(array, 'tensor', [(i, i ^ mask) for i in range(slots)])]
    convert_element_type x29 -> x17, other arithmetic: 139 us -> 43.6 us  [the longest x7 27.4 us: low(): return array.astype(BF16)]
  transfers between devices with their start and end apart: 9 -> 32, of which waited for: 9 -> 4; matrix products, arithmetic and copies ran while one was open for 7% -> 31% of each run, Pallas kernels for 0% -> 29%
where the time goes in v2:
time: 819 us; the launch traced here: 809 us
  Pallas kernels  233 us (28%)
  matrix products  140 us (17%)
  blocking collectives  134 us (16%)
  waiting for transfers between devices  115 us (14%)
  local copies, waits for them, and re-layouts  80.2 us (10%)
  other arithmetic  75.3 us (9%)
  between operations  16.7 us (2%)
  starting transfers between devices  15.4 us (2%)
    pallas_call x2, Pallas kernels, attend_back(): pl.pallas_call(functools.partial(attend_back_kernel, slots=slots, pair=pa...  140 us
    dot_general x13, matrix products, dot(): return lax.dot_general(lhs, rhs, dims, preferred_element_type=F32)  140 us
    all_gather x2, blocking collectives, total_of(): every = lax.all_gather(flat, ('dp', 'tensor'), axis=0)  134 us
    ppermute x30, waiting for transfers between devices, swap(): return lax.ppermute(array, 'tensor', [(i, i ^ mask) for i in range(slots)])  115 us
    pallas_call x2, Pallas kernels, attend(): pl.pallas_call(functools.partial(attend_kernel, slots=slots, pair=pair, t...  73.1 us
    unnamed x151, local copies, waits for them, and re-layouts  45.7 us
    convert_element_type x7, other arithmetic, low(): return array.astype(BF16)  27.4 us
    pallas_call x1, Pallas kernels, post_norm(): pl.pallas_call(functools.partial(post_kernel, slots=slots, groups=groups)...  19.9 us
  transfers between devices with their start and end apart: 32, of which 4 were waited for; matrix products, arithmetic and copies ran while one was open for 31% of the time, Pallas kernels for 29%

profile of v2, /device:TPU:0, one launch (start us, length us, event | category | flops | bytes accessed | tf_op | source)
XLA Modules:
  0.0 809.2 jit_solution(2753003993639182014)
XLA Ops:
  7.3 3.0 collective-permute-start.1
  10.3 45.9 %collective-permute-done.1 = bf16[1024,1024]{1,0:T(8,128)(2,1)} collective-permute-done((bf16[1024,1024]{1,0:T(8,128)(2,1)}, bf16[1024,1024]{1,0:T(8,128)(2,1)}, u32[]{:S(2)}, u32[]{:S(2)}) %collective-permute-start.1) | collective-permute-done | bytes 2097184 | tf_op jit(solution)/shard_map/ppermute | solution.py:437
  69.5 2.2 copy.51
  71.7 1.9 constant_dynamic-update-slice_fusion.3
  76.2 1.8 constant_dynamic-update-slice_fusion.2
  78.0 1.8 constant_dynamic-update-slice_fusion.1
  79.8 1.8 collective-permute-start.10
  82.2 1.8 constant_dynamic-update-slice_fusion.refs_8_
  85.1 2.8 fusion.2
  88.0 11.0 %fusion.40 = f32[4096,768]{1,0:T(8,128)} fusion(bf16[1024,256]{0,1:T(8,128)(2,1)S(1)} %copy-done.28, bf16[1024,256]{0,1:T(8,128)(2,1)S(1)} %copy.50, bf16[1024,256]{0,1:T(8,128)(2,1)S(1)} %copy.49, bf16[4096,1024]{1,0:T(8,128)(2,1)S(1)} %constant_dynamic-update-slice_fusion.refs_8_, f32[1024]{0:T(1024)S(1)} %convert_element_type.183, ...), kind=kOutput, calls=%fused_computation.124 | convolution fusion | flops 6472335360 | bytes 22585344 | tf_op jit(solution)/shard_map/dot_general | solution.py:24
  99.1 3.7 slice.319.k_ref.refs_4_
  102.8 6.3 fusion.24
  109.1 36.6 %attend.3 = (bf16[4096,128]{1,0:T(8,128)(2,1)}, f32[2,1,4096]{2,1,0:T(1,128)}) custom-call(s32[1]{0:T(128)} %bitcast.me_ref.refs_0_, s32[1]{0:T(128)S(6)} %convert_element_type.179.apart_ref.refs_1_, f32[2]{0:T(128)} %get-tuple-element.160.slope_ref.refs_2_, bf16[4096,256]{1,0:T(8,128)(2,1)} %get-tuple-element.134.q_ref.refs_3_, ...), custom_call_target="tpu_custom_call" | custom-call | flops 36909875200 | bytes 4194304 | tf_op jit(solution)/shard_map/attend/pallas_call | solution.py:181
  147.6 36.4 %attend.2 = (bf16[4096,128]{1,0:T(8,128)(2,1)}, f32[2,1,4096]{2,1,0:T(1,128)}) custom-call(s32[1]{0:T(128)} %bitcast.me_ref.refs_0_, s32[1]{0:T(128)S(6)} %convert_element_type.179.apart_ref.refs_1_, f32[2]{0:T(128)} %get-tuple-element.161.slope_ref.refs_2_, bf16[4096,256]{1,0:T(8,128)(2,1)} %get-tuple-element.134.q_ref.refs_3_, ...), custom_call_target="tpu_custom_call" | custom-call | flops 36909875200 | bytes 4194304 | tf_op jit(solution)/shard_map/attend/pallas_call | solution.py:181
  186.9 3.1 constant_dynamic-update-slice_fusion.11
  190.3 20.2 %collective-permute-done.5.refs_4_ = bf16[4096,128]{1,0:T(8,128)(2,1)S(1)} collective-permute-done((bf16[4096,128]{1,0:T(8,128)(2,1)}, bf16[4096,128]{1,0:T(8,128)(2,1)S(1)}, u32[]{:S(2)}, u32[]{:S(2)}) %collective-permute-start.5) | collective-permute-done | bytes 1048608 | tf_op jit(solution)/shard_map/ppermute | solution.py:437
  212.4 4.0 constant_dynamic-update-slice_fusion.10
  216.4 3.1 constant_dynamic-update-slice_fusion.9
  221.4 19.9 %post_norm.1 = (bf16[4096,1024]{1,0:T(8,128)(2,1)}, f32[1024,1024]{1,0:T(8,128)}) custom-call(bf16[4096,128]{1,0:T(8,128)(2,1)S(1)} %copy-done.3, bf16[4096,128]{1,0:T(8,128)(2,1)S(1)} %copy-done.2, bf16[4096,128]{1,0:T(8,128)(2,1)S(1)} %collective-permute-done.3.refs_2_, bf16[4096,128]{1,0:T(8,128)(2,1)S(1)} %collective-permute-done.4.refs_3_, ...), custom_call_target="tpu_custom_call" | custom-call | flops 8589934592 | bytes 25165824 | tf_op jit(solution)/shard_map/post_norm/pallas_call | solution.py:372
  241.3 2.4 reduce_sum.200
  243.7 16.3 %fusion.58 = f32[4096,1024]{1,0:T(8,128)} fusion(bf16[4096,1024]{1,0:T(8,128)(2,1)} %get-tuple-element.45, bf16[1024,1024]{1,0:T(8,128)(2,1)} %param.31), kind=kOutput, calls=%fused_computation.139 | convolution fusion | flops 8589934592 | bytes 27262976 | tf_op jit(solution)/shard_map/dot_general | solution.py:24
  260.0 3.1 constant_dynamic-update-slice_fusion.8
  263.1 26.6 %convert_reduce_fusion.1 = (f32[1024]{0:T(1024)S(1)}, bf16[4096,1024]{1,0:T(8,128)(2,1)S(1)}, bf16[4096,1024]{1,0:T(8,128)(2,1)}) fusion(f32[4096,1024]{1,0:T(8,128)} %fusion.58, f32[1024]{0:T(1024)S(1)} %convert_element_type.189, bf16[4096,1024]{1,0:T(8,128)(2,1)} %constant_dynamic-update-slice_fusion.8, bf16[1024,1024]{1,0:T(8,128)(2,1)S(1)} %copy-done), kind=kOutput, calls=%fused_computation.17 | convolution fusion | flops 8694791168 | bytes 44048384 | tf_op jit(solution)/shard_map/dot_general | solution.py:24
  289.7 5.3 fusion.27
  295.4 1.8 copy-done.4
  297.7 1.7 slice_dynamic-update-slice_fusion.1
  299.4 1.7 slice_dynamic-update-slice_fusion
  301.6 5.0 convolution_convert_fusion.3
  308.5 2.3 add_convert_fusion.3
  311.2 14.9 %convolution_convert_fusion.4 = bf16[1024,1024]{1,0:T(8,128)(2,1)} fusion(bf16[4096,1024]{1,0:T(8,128)(2,1)} %get-tuple-element.60, bf16[4096,1024]{1,0:T(8,128)(2,1)} %constant_dynamic-update-slice_fusion.8), kind=kOutput, calls=%fused_computation.62 | convolution fusion | flops 8590983168 | bytes 18874368 | tf_op jit(solution)/shard_map/dot_general | solution.py:24
  326.1 10.2 %convolution_convert_fusion.5 = bf16[1024,1024]{1,0:T(8,128)(2,1)} fusion(bf16[4096,1024]{1,0:T(8,128)(2,1)S(1)} %bitcast.33, bf16[4096,1024]{1,0:T(8,128)(2,1)S(1)} %get-tuple-element.59), kind=kOutput, calls=%fused_computation.63 | convolution fusion | flops 8590983168 | bytes 18874368 | tf_op jit(solution)/shard_map/dot_general | solution.py:24
  336.4 22.6 %collective-permute-done.17 = bf16[1024,1024]{1,0:T(8,128)(2,1)} collective-permute-done((bf16[1024,1024]{1,0:T(8,128)(2,1)}, bf16[1024,1024]{1,0:T(8,128)(2,1)}, u32[]{:S(2)}, u32[]{:S(2)}) %collective-permute-start.17) | collective-permute-done | bytes 2097184 | tf_op jit(solution)/shard_map/ppermute | solution.py:437
  359.1 5.4 multiply_reduce_fusion
  364.5 4.7 fusion.46
  369.2 2.4 convolution_convert_fusion.6
  375.0 7.9 fusion.57
  382.9 55.3 %all_gather.7 = f32[32,5,1024]{2,1,0:T(8,128)S(1)} all-gather(f32[1,5,1024]{2,1,0:T(8,128)S(1)} %all_gather_reshape.7), channel_id=1, replica_groups=mesh['dp'=8,'tensor'=4] {'dp','tensor'}, dimensions={0}, use_global_device_ids=true | all-gather | bytes 675840 | tf_op jit(solution)/shard_map/all_gather | solution.py:534
  442.0 2.3 fusion.48
  444.8 15.4 %convolution_convert_fusion = bf16[4096,1024]{1,0:T(8,128)(2,1)} fusion(bf16[4096,1024]{1,0:T(8,128)(2,1)} %get-tuple-element.60, bf16[1024,1024]{1,0:T(8,128)(2,1)S(1)} %copy-done), kind=kOutput, calls=%fused_computation.20 | convolution fusion | flops 8594128896 | bytes 18874368 | tf_op jit(solution)/shard_map/dot_general | solution.py:24
  460.2 70.1 %attend_back.2 = (bf16[4096,128]{1,0:T(8,128)(2,1)}, bf16[4096,128]{1,0:T(8,128)(2,1)}, bf16[4096,128]{1,0:T(8,128)(2,1)}) custom-call(s32[1]{0:T(128)} %bitcast.me_ref.refs_0_, s32[1]{0:T(128)S(6)} %convert_element_type.179.apart_ref.refs_1_, f32[2]{0:T(128)} %get-tuple-element.161.slope_ref.refs_2_, bf16[4096,256]{1,0:T(8,128)(2,1)} %get-tuple-element.134.q_ref.refs_3_, ...), custom_call_target="tpu_custom_call" | custom-call | flops 73819750400 | bytes 8388608 | tf_op jit(solution)/shard_map/attend_back/pallas_call | solution.py:310
  530.4 2.3 constant_dynamic-update-slice_fusion.17
  532.7 70.0 %attend_back.3 = (bf16[4096,128]{1,0:T(8,128)(2,1)}, bf16[4096,128]{1,0:T(8,128)(2,1)}, bf16[4096,128]{1,0:T(8,128)(2,1)}) custom-call(s32[1]{0:T(128)} %bitcast.me_ref.refs_0_, s32[1]{0:T(128)S(6)} %convert_element_type.179.apart_ref.refs_1_, f32[2]{0:T(128)} %get-tuple-element.160.slope_ref.refs_2_, bf16[4096,256]{1,0:T(8,128)(2,1)} %get-tuple-element.134.q_ref.refs_3_, ...), custom_call_target="tpu_custom_call" | custom-call | flops 73819750400 | bytes 8388608 | tf_op jit(solution)/shard_map/attend_back/pallas_call | solution.py:310
  602.7 2.5 constant_dynamic-update-slice_fusion.16
  609.8 5.7 convolution_convert_fusion.2
  615.8 3.9 convolution_convert_fusion.1
  621.3 1.7 slice.243
  623.1 2.6 fusion.47
  626.8 2.1 fusion.33
  630.3 15.0 %fusion.30 = (f32[1024]{0:T(1024)S(1)}, f32[1024]{0:T(1024)S(1)}, bf16[1024,768]{0,1:T(8,128)(2,1)}) fusion(bf16[1024,256]{0,1:T(8,128)(2,1)} %copy.51, bf16[1024,256]{0,1:T(8,128)(2,1)S(1)} %copy-done.27, bf16[1024,256]{0,1:T(8,128)(2,1)S(1)} %copy-done.25, f32[768]{0:T(1024)S(1)} %convert_reduce_fusion.2, ...), kind=kOutput, calls=%fused_computation.59 | convolution fusion | flops 6476265472 | bytes 17878016 | tf_op jit(solution)/shard_map/dot_general | solution.py:24
  645.3 2.1 fusion.35
  647.4 4.2 add_convert_fusion
  651.6 2.0 collective-permute-start.26
  654.4 78.8 %all_gather.6 = f32[32,3,1024]{2,1,0:T(4,128)S(1)} all-gather(f32[1,3,1024]{2,1,0:T(4,128)S(1)} %all_gather_reshape.6), channel_id=1, replica_groups=mesh['dp'=8,'tensor'=4] {'dp','tensor'}, dimensions={0}, use_global_device_ids=true | all-gather | bytes 405504 | tf_op jit(solution)/shard_map/all_gather | solution.py:534
  735.3 4.1 convert_element_type.235
  739.4 4.1 convert_element_type.236
  743.5 4.6 add_convert_fusion.2
  748.1 2.1 convert_element_type.233
  750.2 3.1 fusion.50
  753.2 2.7 copy.55
  755.9 2.5 copy.54
  759.8 4.3 fusion.39
  764.5 5.5 fusion.20
  770.0 26.1 %collective-permute-done.23 = bf16[1024,1024]{1,0:T(8,128)(2,1)} collective-permute-done((bf16[1024,1024]{1,0:T(8,128)(2,1)}, bf16[1024,1024]{1,0:T(8,128)(2,1)}, u32[]{:S(2)}, u32[]{:S(2)}) %collective-permute-start.23) | collective-permute-done | bytes 2097184 | tf_op jit(solution)/shard_map/ppermute | solution.py:437
  796.1 5.9 add_convert_fusion.1
  (250 shorter events, 49.9 us)
Async XLA Ops:
  7.2 255.9 %copy-start = (bf16[1024,1024]{1,0:T(8,128)(2,1)S(1)}, bf16[1024,1024]{1,0:T(8,128)(2,1)}, u32[]{:S(2)}) copy-start(bf16[1024,1024]{1,0:T(8,128)(2,1)} %param.33) | copy-start | bytes 6291460
  7.2 640.2 %all-reduce.8.cloned.1.call-start = ((), (), s32[]{:S(2)}) async-start(), calls=%async_computation.1 | async-start | bytes 8388608 | tf_op jit(solution)/shard_map/psum | solution.py:500
  7.3 49.0 %collective-permute-start.1 = (bf16[1024,1024]{1,0:T(8,128)(2,1)}, bf16[1024,1024]{1,0:T(8,128)(2,1)}, u32[]{:S(2)}, u32[]{:S(2)}) collective-permute-start(bf16[1024,1024]{1,0:T(8,128)(2,1)} %param.18), channel_id=1, source_target_pairs={{0,2},{1,3},{2,0},{3,1},{4,6},{5,7},{6,4},{7,5},{8,10},{9,11},{10,... | collective-permute-start | bytes 6291464 | tf_op jit(solution)/shard_map/ppermute | solution.py:437
  10.3 65.9 %collective-permute-start = (bf16[1024,1024]{1,0:T(8,128)(2,1)}, bf16[1024,1024]{1,0:T(8,128)(2,1)}, u32[]{:S(2)}, u32[]{:S(2)}) collective-permute-start(bf16[1024,1024]{1,0:T(8,128)(2,1)} %param.18), channel_id=1, source_target_pairs={{0,1},{1,0},{2,3},{3,2},{4,5},{5,4},{6,7},{7,6},{8,9},{9,8},{10,11... | collective-permute-start | bytes 6291464 | tf_op jit(solution)/shard_map/ppermute | solution.py:437
  56.2 23.5 %collective-permute-start.2 = (bf16[1024,1024]{1,0:T(8,128)(2,1)}, bf16[1024,1024]{1,0:T(8,128)(2,1)}, u32[]{:S(2)}, u32[]{:S(2)}) collective-permute-start(bf16[1024,1024]{1,0:T(8,128)(2,1)} %collective-permute-done.1), channel_id=1, source_target_pairs={{0,1},{1,0},{2,3},{3,2},{4,5},{5,4},{6,7},{7,6},{8,9},{9,8},{10,11... | collective-permute-start | bytes 6291464 | tf_op jit(solution)/shard_map/ppermute | solution.py:437
  62.7 25.2 %copy-start.44 = (f32[1024]{0:T(1024)}, f32[1024]{0:T(1024)S(1)}, u32[]{:S(2)}) copy-start(f32[1024]{0:T(1024)S(1)} %convert_element_type.182) | copy-start | bytes 12292
  63.4 24.6 %copy-start.53 = (f32[1024]{0:T(1024)}, f32[1024]{0:T(1024)S(1)}, u32[]{:S(2)}) copy-start(f32[1024]{0:T(1024)S(1)} %convert_element_type.183) | copy-start | bytes 12292
  68.0 20.0 %copy-start.24 = (bf16[1024,256]{0,1:T(8,128)(2,1)}, bf16[1024,256]{0,1:T(8,128)(2,1)S(1)}, u32[]{:S(2)}) copy-start(bf16[1024,256]{0,1:T(8,128)(2,1)S(1)} %copy.49) | copy-start | bytes 1572868
  69.4 18.5 %copy-start.26 = (bf16[1024,256]{0,1:T(8,128)(2,1)}, bf16[1024,256]{0,1:T(8,128)(2,1)S(1)}, u32[]{:S(2)}) copy-start(bf16[1024,256]{0,1:T(8,128)(2,1)S(1)} %copy.50) | copy-start | bytes 1572868
  79.8 67.6 %collective-permute-start.10 = (bf16[256,1024]{1,0:T(8,128)(2,1)S(1)}, bf16[256,1024]{1,0:T(8,128)(2,1)S(1)}, u32[]{:S(2)}, u32[]{:S(2)}) collective-permute-start(bf16[256,1024]{1,0:T(8,128)(2,1)S(1)} %copy-done.23), channel_id=1, source_target_pairs={{0,2},{1,3},{2,0},{3,1},{4,6},{5,7},{6,4},{7,5},{8,10},{9,11},{10,... | collective-permute-start | bytes 1572872 | tf_op jit(solution)/shard_map/ppermute | solution.py:437
  81.6 102.5 %collective-permute-start.9 = (bf16[256,1024]{1,0:T(8,128)(2,1)S(1)}, bf16[256,1024]{1,0:T(8,128)(2,1)S(1)}, u32[]{:S(2)}, u32[]{:S(2)}) collective-permute-start(bf16[256,1024]{1,0:T(8,128)(2,1)S(1)} %copy-done.23), channel_id=1, source_target_pairs={{0,1},{1,0},{2,3},{3,2},{4,5},{5,4},{6,7},{7,6},{8,9},{9,8},{10,11... | collective-permute-start | bytes 1572872 | tf_op jit(solution)/shard_map/ppermute | solution.py:437
  81.8 130.5 %collective-permute-start.13 = (bf16[1024,1024]{1,0:T(8,128)(2,1)}, bf16[1024,1024]{1,0:T(8,128)(2,1)}, u32[]{:S(2)}, u32[]{:S(2)}) collective-permute-start(bf16[1024,1024]{1,0:T(8,128)(2,1)} %param.35), channel_id=1, source_target_pairs={{0,2},{1,3},{2,0},{3,1},{4,6},{5,7},{6,4},{7,5},{8,10},{9,11},{10,... | collective-permute-start | bytes 6291464 | tf_op jit(solution)/shard_map/ppermute | solution.py:437
  82.2 130.2 %collective-permute-start.12 = (bf16[1024,1024]{1,0:T(8,128)(2,1)}, bf16[1024,1024]{1,0:T(8,128)(2,1)}, u32[]{:S(2)}, u32[]{:S(2)}) collective-permute-start(bf16[1024,1024]{1,0:T(8,128)(2,1)} %param.35), channel_id=1, source_target_pairs={{0,1},{1,0},{2,3},{3,2},{4,5},{5,4},{6,7},{7,6},{8,9},{9,8},{10,11... | collective-permute-start | bytes 6291464 | tf_op jit(solution)/shard_map/ppermute | solution.py:437
  88.0 11.0 %copy-start.49 = (f32[4096]{0:T(1024)}, f32[4096]{0:T(1024)S(1)}, u32[]{:S(2)}) copy-start(f32[4096]{0:T(1024)S(1)} %add_rsqrt_fusion) | copy-start | bytes 49156
  145.7 40.6 %collective-permute-start.6 = (bf16[4096,128]{1,0:T(8,128)(2,1)}, bf16[4096,128]{1,0:T(8,128)(2,1)}, u32[]{:S(2)}, u32[]{:S(2)}) collective-permute-start(bf16[4096,128]{1,0:T(8,128)(2,1)} %get-tuple-element.42.refs_1_.refs_6_), channel_id=1, source_target_pairs={{0,2},{1,3},{2,0},{3,1},{4,6},{5,7},{6,4},{7,5},{8,10},{9,11},{10,... | collective-permute-start | bytes 3145736 | tf_op jit(solution)/shard_map/ppermute | solution.py:437
  147.4 36.7 %copy-start.30 = (bf16[256,1024]{1,0:T(8,128)(2,1)}, bf16[256,1024]{1,0:T(8,128)(2,1)S(1)}, u32[]{:S(2)}) copy-start(bf16[256,1024]{1,0:T(8,128)(2,1)S(1)} %collective-permute-done.10) | copy-start | bytes 1572868
  147.4 37.8 %collective-permute-start.11 = (bf16[256,1024]{1,0:T(8,128)(2,1)S(1)}, bf16[256,1024]{1,0:T(8,128)(2,1)S(1)}, u32[]{:S(2)}, u32[]{:S(2)}) collective-permute-start(bf16[256,1024]{1,0:T(8,128)(2,1)S(1)} %collective-permute-done.10), channel_id=1, source_target_pairs={{0,1},{1,0},{2,3},{3,2},{4,5},{5,4},{6,7},{7,6},{8,9},{9,8},{10,11... | collective-permute-start | bytes 1572872 | tf_op jit(solution)/shard_map/ppermute | solution.py:437
  147.6 38.7 %copy-start.2 = (bf16[4096,128]{1,0:T(8,128)(2,1)S(1)}, bf16[4096,128]{1,0:T(8,128)(2,1)}, u32[]{:S(2)}) copy-start(bf16[4096,128]{1,0:T(8,128)(2,1)} %get-tuple-element.42.refs_1_.refs_6_) | copy-start | bytes 3145732
  184.9 25.6 %collective-permute-start.5 = (bf16[4096,128]{1,0:T(8,128)(2,1)}, bf16[4096,128]{1,0:T(8,128)(2,1)S(1)}, u32[]{:S(2)}, u32[]{:S(2)}) collective-permute-start(bf16[4096,128]{1,0:T(8,128)(2,1)} %get-tuple-element.41.refs_0_.refs_6_), channel_id=1, source_target_pairs={{0,2},{1,3},{2,0},{3,1},{4,6},{5,7},{6,4},{7,5},{8,10},{9,11},{10,... | collective-permute-start | bytes 3145736 | tf_op jit(solution)/shard_map/ppermute | solution.py:437
  185.2 25.2 %collective-permute-start.3 = (bf16[4096,128]{1,0:T(8,128)(2,1)}, bf16[4096,128]{1,0:T(8,128)(2,1)S(1)}, u32[]{:S(2)}, u32[]{:S(2)}) collective-permute-start(bf16[4096,128]{1,0:T(8,128)(2,1)} %get-tuple-element.41.refs_0_.refs_6_), channel_id=1, source_target_pairs={{0,1},{1,0},{2,3},{3,2},{4,5},{5,4},{6,7},{7,6},{8,9},{9,8},{10,11... | collective-permute-start | bytes 3145736 | tf_op jit(solution)/shard_map/ppermute | solution.py:437
  186.3 24.7 %collective-permute-start.4 = (bf16[4096,128]{1,0:T(8,128)(2,1)S(1)}, bf16[4096,128]{1,0:T(8,128)(2,1)S(1)}, u32[]{:S(2)}, u32[]{:S(2)}) collective-permute-start(bf16[4096,128]{1,0:T(8,128)(2,1)S(1)} %copy-done.2), channel_id=1, source_target_pairs={{0,1},{1,0},{2,3},{3,2},{4,5},{5,4},{6,7},{7,6},{8,9},{9,8},{10,11... | collective-permute-start | bytes 3145736 | tf_op jit(solution)/shard_map/ppermute | solution.py:437
  190.2 29.2 %copy-start.34 = (bf16[1024,1024]{1,0:T(8,128)(2,1)}, bf16[1024,1024]{1,0:T(8,128)(2,1)S(1)}, u32[]{:S(2)}) copy-start(bf16[1024,1024]{1,0:T(8,128)(2,1)S(1)} %constant_dynamic-update-slice_fusion.4.refs_9_) | copy-start | bytes 6291460
  210.4 9.0 %collective-permute-start.8 = (bf16[4096,128]{1,0:T(8,128)(2,1)}, bf16[4096,128]{1,0:T(8,128)(2,1)S(1)}, u32[]{:S(2)}, u32[]{:S(2)}) collective-permute-start(bf16[4096,128]{1,0:T(8,128)(2,1)} %collective-permute-done.6.refs_5_), channel_id=1, source_target_pairs={{0,1},{1,0},{2,3},{3,2},{4,5},{5,4},{6,7},{7,6},{8,9},{9,8},{10,11... | collective-permute-start | bytes 3145736 | tf_op jit(solution)/shard_map/ppermute | solution.py:437
  210.4 9.0 %collective-permute-start.7 = (bf16[4096,128]{1,0:T(8,128)(2,1)S(1)}, bf16[4096,128]{1,0:T(8,128)(2,1)S(1)}, u32[]{:S(2)}, u32[]{:S(2)}) collective-permute-start(bf16[4096,128]{1,0:T(8,128)(2,1)S(1)} %collective-permute-done.5.refs_4_), channel_id=1, source_target_pairs={{0,1},{1,0},{2,3},{3,2},{4,5},{5,4},{6,7},{7,6},{8,9},{9,8},{10,11... | collective-permute-start | bytes 3145736 | tf_op jit(solution)/shard_map/ppermute | solution.py:437
  212.3 7.2 copy-start.47
  212.3 9.1 %copy-start.3 = (bf16[4096,128]{1,0:T(8,128)(2,1)S(1)}, bf16[4096,128]{1,0:T(8,128)(2,1)}, u32[]{:S(2)}) copy-start(bf16[4096,128]{1,0:T(8,128)(2,1)} %get-tuple-element.41.refs_0_.refs_6_) | copy-start | bytes 3145732
  212.3 47.7 %collective-permute-start.14 = (bf16[1024,1024]{1,0:T(8,128)(2,1)}, bf16[1024,1024]{1,0:T(8,128)(2,1)}, u32[]{:S(2)}, u32[]{:S(2)}) collective-permute-start(bf16[1024,1024]{1,0:T(8,128)(2,1)} %collective-permute-done.13), channel_id=1, source_target_pairs={{0,1},{1,0},{2,3},{3,2},{4,5},{5,4},{6,7},{7,6},{8,9},{9,8},{10,11... | collective-permute-start | bytes 6291464 | tf_op jit(solution)/shard_map/ppermute | solution.py:437
  263.1 26.6 %copy-start.55 = (bf16[1024,1024]{1,0:T(8,128)(2,1)S(1)}, bf16[1024,1024]{1,0:T(8,128)(2,1)}, u32[]{:S(2)}) copy-start(bf16[1024,1024]{1,0:T(8,128)(2,1)} %param.31) | copy-start | bytes 6291460
  295.2 13.3 %collective-permute-start.16 = (bf16[1024,1024]{1,0:T(8,128)(2,1)S(1)}, bf16[1024,1024]{1,0:T(8,128)(2,1)S(1)}, u32[]{:S(2)}, u32[]{:S(2)}) collective-permute-start(bf16[1024,1024]{1,0:T(8,128)(2,1)S(1)} %slice.233), channel_id=1, source_target_pairs={{0,1},{1,0},{2,3},{3,2},{4,5},{5,4},{6,7},{7,6},{8,9},{9,8},{10,11... | collective-permute-start | bytes 6291464 | tf_op jit(solution)/shard_map/ppermute | solution.py:437
  308.3 28.1 %collective-permute-start.15 = (bf16[1024,1024]{1,0:T(8,128)(2,1)}, bf16[1024,1024]{1,0:T(8,128)(2,1)}, u32[]{:S(2)}, u32[]{:S(2)}) collective-permute-start(bf16[1024,1024]{1,0:T(8,128)(2,1)} %slice.231), channel_id=1, source_target_pairs={{0,1},{1,0},{2,3},{3,2},{4,5},{5,4},{6,7},{7,6},{8,9},{9,8},{10,11... | collective-permute-start | bytes 6291464 | tf_op jit(solution)/shard_map/ppermute | solution.py:437
  308.5 17.6 %slice-start.2 = ((s8[8388608]{0:T(1024)(128)(4,1)}), s8[4194304]{0:T(1024)(128)(4,1)S(1)}, s32[]{:S(2)}) async-start(s8[8388608]{0:T(1024)(128)(4,1)} %bitcast.32), calls=%async_computation.4 | async-start | bytes 8388608
  310.8 15.2 %slice-start.3 = ((s8[8388608]{0:T(1024)(128)(4,1)}), s8[4194304]{0:T(1024)(128)(4,1)S(1)}, s32[]{:S(2)}) async-start(s8[8388608]{0:T(1024)(128)(4,1)} %bitcast.32), calls=%async_computation.5 | async-start | bytes 8388608
  310.8 48.2 %collective-permute-start.17 = (bf16[1024,1024]{1,0:T(8,128)(2,1)}, bf16[1024,1024]{1,0:T(8,128)(2,1)}, u32[]{:S(2)}, u32[]{:S(2)}) collective-permute-start(bf16[1024,1024]{1,0:T(8,128)(2,1)} %add_convert_fusion.3), channel_id=1, source_target_pairs={{0,2},{1,3},{2,0},{3,1},{4,6},{5,7},{6,4},{7,5},{8,10},{9,11},{10,... | collective-permute-start | bytes 6291464 | tf_op jit(solution)/shard_map/ppermute | solution.py:437
  336.3 22.7 %copy-start.43 = (f32[1024]{0:T(1024)S(1)}, f32[1024]{0:T(1024)}, u32[]{:S(2)}) copy-start(f32[1024]{0:T(1024)} %convert_element_type.201) | copy-start | bytes 12292
  336.3 411.7 %all-reduce.6.cloned.1.call-start = ((), (), s32[]{:S(2)}) async-start(), calls=%async_computation | async-start | bytes 4194304 | tf_op jit(solution)/shard_map/psum | solution.py:582
  336.4 28.1 %copy-start.5 = (f32[1024,1024]{1,0:T(8,128)S(1)}, f32[1024,1024]{1,0:T(8,128)}, u32[]{:S(2)}) copy-start(f32[1024,1024]{1,0:T(8,128)} %get-tuple-element.44) | copy-start | bytes 12582916
  336.4 28.1 %copy-start.15 = (bf16[2048,1024]{1,0:T(8,128)(2,1)S(1)}, bf16[2048,1024]{1,0:T(8,128)(2,1)}, u32[]{:S(2)}) copy-start(bf16[2048,1024]{1,0:T(8,128)(2,1)} %copy-done.14) | copy-start | bytes 12582916
  373.1 71.7 %collective-permute-start.20 = (bf16[1024,256]{1,0:T(8,128)(2,1)}, bf16[1024,256]{1,0:T(8,128)(2,1)}, u32[]{:S(2)}, u32[]{:S(2)}) collective-permute-start(bf16[1024,256]{1,0:T(8,128)(2,1)} %get-tuple-element.141), channel_id=1, source_target_pairs={{0,3},{1,2},{2,1},{3,0},{4,7},{5,6},{6,5},{7,4},{8,11},{9,10},{10,... | collective-permute-start | bytes 1572872 | tf_op jit(solution)/shard_map/ppermute | solution.py:437
  373.1 71.7 %collective-permute-start.19 = (bf16[1024,256]{1,0:T(8,128)(2,1)}, bf16[1024,256]{1,0:T(8,128)(2,1)}, u32[]{:S(2)}, u32[]{:S(2)}) collective-permute-start(bf16[1024,256]{1,0:T(8,128)(2,1)} %get-tuple-element.142), channel_id=1, source_target_pairs={{0,2},{1,3},{2,0},{3,1},{4,6},{5,7},{6,4},{7,5},{8,10},{9,11},{10,... | collective-permute-start | bytes 1572872 | tf_op jit(solution)/shard_map/ppermute | solution.py:437
  374.3 70.5 %collective-permute-start.18 = (bf16[1024,256]{1,0:T(8,128)(2,1)}, bf16[1024,256]{1,0:T(8,128)(2,1)}, u32[]{:S(2)}, u32[]{:S(2)}) collective-permute-start(bf16[1024,256]{1,0:T(8,128)(2,1)} %get-tuple-element.143), channel_id=1, source_target_pairs={{0,1},{1,0},{2,3},{3,2},{4,5},{5,4},{6,7},{7,6},{8,9},{9,8},{10,11... | collective-permute-start | bytes 1572872 | tf_op jit(solution)/shard_map/ppermute | solution.py:437
  444.3 201.0 %collective-permute-start.27 = (bf16[256,1024]{1,0:T(8,128)(2,1)}, bf16[256,1024]{1,0:T(8,128)(2,1)}, u32[]{:S(2)}, u32[]{:S(2)}) collective-permute-start(bf16[256,1024]{1,0:T(8,128)(2,1)} %get-tuple-element.139), channel_id=1, source_target_pairs={{0,1},{1,0},{2,3},{3,2},{4,5},{5,4},{6,7},{7,6},{8,9},{9,8},{10,11... | collective-permute-start | bytes 1572872 | tf_op jit(solution)/shard_map/ppermute | solution.py:437
  444.6 181.4 %collective-permute-start.28 = (bf16[256,1024]{1,0:T(8,128)(2,1)}, bf16[256,1024]{1,0:T(8,128)(2,1)}, u32[]{:S(2)}, u32[]{:S(2)}) collective-permute-start(bf16[256,1024]{1,0:T(8,128)(2,1)} %get-tuple-element.140), channel_id=1, source_target_pairs={{0,1},{1,0},{2,3},{3,2},{4,5},{5,4},{6,7},{7,6},{8,9},{9,8},{10,11... | collective-permute-start | bytes 1572872 | tf_op jit(solution)/shard_map/ppermute | solution.py:437
  532.7 72.5 %copy-start.20 = (bf16[4096,128]{1,0:T(8,128)(2,1)S(1)}, bf16[4096,128]{1,0:T(8,128)(2,1)}, u32[]{:S(2)}) copy-start(bf16[4096,128]{1,0:T(8,128)(2,1)} %get-tuple-element.53) | copy-start | bytes 3145732
  602.6 6.0 copy-start.21
  609.8 5.7 copy-start.11
  615.5 5.8 copy-start.17
  615.5 7.5 slice-start
  615.8 7.3 slice-start.1
  625.6 117.8 %collective-permute-start.22 = (bf16[1024,1024]{1,0:T(8,128)(2,1)}, bf16[1024,1024]{1,0:T(8,128)(2,1)}, u32[]{:S(2)}, u32[]{:S(2)}) collective-permute-start(bf16[1024,1024]{1,0:T(8,128)(2,1)} %get-tuple-element.136), channel_id=1, source_target_pairs={{0,1},{1,0},{2,3},{3,2},{4,5},{5,4},{6,7},{7,6},{8,9},{9,8},{10,11... | collective-permute-start | bytes 6291464 | tf_op jit(solution)/shard_map/ppermute | solution.py:437
  628.8 16.4 %collective-permute-start.29 = (bf16[256,1024]{1,0:T(8,128)(2,1)}, bf16[256,1024]{1,0:T(8,128)(2,1)S(1)}, u32[]{:S(2)}, u32[]{:S(2)}) collective-permute-start(bf16[256,1024]{1,0:T(8,128)(2,1)} %fusion.33), channel_id=1, source_target_pairs={{0,2},{1,3},{2,0},{3,1},{4,6},{5,7},{6,4},{7,5},{8,10},{9,11},{10,... | collective-permute-start | bytes 1572872 | tf_op jit(solution)/shard_map/ppermute | solution.py:437
  628.8 18.6 %collective-permute-start.25 = (bf16[1024,1024]{1,0:T(8,128)(2,1)}, bf16[1024,1024]{1,0:T(8,128)(2,1)S(1)}, u32[]{:S(2)}, u32[]{:S(2)}) collective-permute-start(bf16[1024,1024]{1,0:T(8,128)(2,1)} %slice.243), channel_id=1, source_target_pairs={{0,1},{1,0},{2,3},{3,2},{4,5},{5,4},{6,7},{7,6},{8,9},{9,8},{10,11... | collective-permute-start | bytes 6291464 | tf_op jit(solution)/shard_map/ppermute | solution.py:437
  629.2 130.6 %collective-permute-start.24 = (bf16[1024,1024]{1,0:T(8,128)(2,1)}, bf16[1024,1024]{1,0:T(8,128)(2,1)}, u32[]{:S(2)}, u32[]{:S(2)}) collective-permute-start(bf16[1024,1024]{1,0:T(8,128)(2,1)} %slice.241), channel_id=1, source_target_pairs={{0,1},{1,0},{2,3},{3,2},{4,5},{5,4},{6,7},{7,6},{8,9},{9,8},{10,11... | collective-permute-start | bytes 6291464 | tf_op jit(solution)/shard_map/ppermute | solution.py:437
  647.4 6.3 copy-start.36
  647.4 6.9 copy-start.51
  647.4 6.9 copy-start.52
  651.6 108.1 %collective-permute-start.26 = (bf16[1024,1024]{1,0:T(8,128)(2,1)}, bf16[1024,1024]{1,0:T(8,128)(2,1)}, u32[]{:S(2)}, u32[]{:S(2)}) collective-permute-start(bf16[1024,1024]{1,0:T(8,128)(2,1)} %add_convert_fusion), channel_id=1, source_target_pairs={{0,2},{1,3},{2,0},{3,1},{4,6},{5,7},{6,4},{7,5},{8,10},{9,11},{10,... | collective-permute-start | bytes 6291464 | tf_op jit(solution)/shard_map/ppermute | solution.py:437
  733.6 36.4 %collective-permute-start.21 = (bf16[1024,1024]{1,0:T(8,128)(2,1)}, bf16[1024,1024]{1,0:T(8,128)(2,1)}, u32[]{:S(2)}, u32[]{:S(2)}) collective-permute-start(bf16[1024,1024]{1,0:T(8,128)(2,1)} %get-tuple-element.135), channel_id=1, source_target_pairs={{0,1},{1,0},{2,3},{3,2},{4,5},{5,4},{6,7},{7,6},{8,9},{9,8},{10,11... | collective-permute-start | bytes 6291464 | tf_op jit(solution)/shard_map/ppermute | solution.py:437
  748.0 48.0 %collective-permute-start.23 = (bf16[1024,1024]{1,0:T(8,128)(2,1)}, bf16[1024,1024]{1,0:T(8,128)(2,1)}, u32[]{:S(2)}, u32[]{:S(2)}) collective-permute-start(bf16[1024,1024]{1,0:T(8,128)(2,1)} %add_convert_fusion.2), channel_id=1, source_target_pairs={{0,2},{1,3},{2,0},{3,1},{4,6},{5,7},{6,4},{7,5},{8,10},{9,11},{10,... | collective-permute-start | bytes 6291464 | tf_op jit(solution)/shard_map/ppermute | solution.py:437
  753.2 6.5 copy-start.8
  753.2 6.5 copy-start.42
  753.2 6.6 copy-start.46
  764.5 31.6 %copy-start.6 = (f32[1024,1024]{1,0:T(8,128)S(1)}, f32[1024,1024]{1,0:T(8,128)}, u32[]{:S(2)}) copy-start(f32[1024,1024]{1,0:T(8,128)} %get-tuple-element.44) | copy-start | bytes 12582916
  764.5 31.6 %copy-start.48 = (f32[1024]{0:T(1024)S(1)}, f32[1024]{0:T(1024)}, u32[]{:S(2)}) copy-start(f32[1024]{0:T(1024)} %convert_element_type.211) | copy-start | bytes 12292
  764.5 37.4 %copy-start.1 = (bf16[1024,1024]{1,0:T(8,128)(2,1)S(1)}, bf16[1024,1024]{1,0:T(8,128)(2,1)}, u32[]{:S(2)}) copy-start(bf16[1024,1024]{1,0:T(8,128)(2,1)} %param.33) | copy-start | bytes 6291460
  (28 other events, 99.7 us)
Sparse Core Ops, SparseCore 0:
  336.5 161.2 all-reduce.7
  647.5 100.3 all-reduce.5

commit v3 on v2

--- a/solution.py
+++ b/solution.py
@@ -202,7 +202,8 @@
 def attend_back_kernel(*refs, slots, pair, tile, key_tile):
     me_ref, apart_ref, slope_ref, q_ref, k_ref, v_ref, o_ref, lse_ref = refs[:8]
     g_refs = refs[8 : 8 + slots]
-    dq_ref, dk_ref, dv_ref, qa, ka, va, ga, kt, dq_sum = refs[8 + slots :]
+    out_ref, qa, ka, va, ga, kt, dq_sum = refs[8 + slots :]
+    cols = pair * HD
     me = me_ref[0]
     total = q_ref.shape[0]
     rows = total // slots
@@ -213,16 +214,16 @@
         place = pl.multiple_of(place, chunk)
         home = pl.ds(place, chunk)
         for s in range(pair):
-            cols = slice(s * HD, (s + 1) * HD)
+            mine = slice(s * HD, (s + 1) * HD)
             log_total = lse_ref[s, :, home].T
-            qa[s, home, :] = query_columns(q_ref[spot, cols], place, slope_ref[s], apart, log_total)
-            keys = key_columns(k_ref[spot, cols], place)
+            qa[s, home, :] = query_columns(q_ref[spot, mine], place, slope_ref[s], apart, log_total)
+            keys = key_columns(k_ref[spot, mine], place)
             ka[s, home, :] = keys
             kt[s, :, home] = low(keys.astype(F32).T)
-            va[s, home, :] = ones_columns(v_ref[spot, cols], 3)
-            grad = g_refs[slot][inner, cols]
+            va[s, home, :] = ones_columns(v_ref[spot, mine], 3)
+            grad = g_refs[slot][inner, mine]
             row_dot = jnp.sum(
-                grad.astype(F32) * o_ref[spot, cols].astype(F32), axis=1, keepdims=True
+                grad.astype(F32) * o_ref[spot, mine].astype(F32), axis=1, keepdims=True
             )
             ga[s, home, :] = grad_columns(grad, -row_dot)
             dq_sum[s, :, home] = jnp.zeros((128, chunk), F32)
@@ -283,8 +284,8 @@
         dv = low(jnp.concatenate([held[1][:, :HD] for held in carry], axis=1))
         for part in range(key_tile // piece):
             spot = pl.ds(place_of(first + part * piece, piece), piece)
-            dk_ref[spot, :] = dk[part * piece : (part + 1) * piece]
-            dv_ref[spot, :] = dv[part * piece : (part + 1) * piece]
+            out_ref[spot, cols : 2 * cols] = dk[part * piece : (part + 1) * piece]
+            out_ref[spot, 2 * cols :] = dv[part * piece : (part + 1) * piece]
         return 0
 
     lax.fori_loop(0, total // key_tile, keys_tile, 0)
@@ -292,7 +293,7 @@
     def finish(slot, inner, spot, place):
         home = pl.ds(pl.multiple_of(place, chunk), chunk)
         joined = jnp.concatenate([dq_sum[s, :HD, home] for s in range(pair)], axis=0)
-        dq_ref[spot, :] = low(joined.T * HD**-0.5)
+        out_ref[spot, :cols] = low(joined.T * HD**-0.5)
 
     each_chunk(me, slots, rows, finish)
 
@@ -316,8 +317,8 @@
         + [spec] * 3
         + [out_spec, pl.BlockSpec((pair, 1, total), lambda g: (0, 0, 0))]
         + [pl.BlockSpec((total // slots, cols), lambda g: (0, group))] * slots,
-        out_specs=[out_spec] * 3,
-        out_shape=[jax.ShapeDtypeStruct((total, cols), BF16)] * 3,
+        out_specs=pl.BlockSpec((total, 3 * cols), lambda g: (0, 0)),
+        out_shape=jax.ShapeDtypeStruct((total, 3 * cols), BF16),
         scratch_shapes=[pltpu.VMEM((pair, total, 128), BF16)] * 4
         + [pltpu.VMEM((pair, 128, total), BF16), pltpu.VMEM((pair, 128, total), F32)],
         compiler_params=pltpu.CompilerParams(vmem_limit_bytes=60 << 20),
@@ -338,64 +339,139 @@
     )
 
 
-def post_kernel(*refs, slots, groups):
+def whole(shape):
+    return pl.BlockSpec(shape, lambda i: (0,) * len(shape))
+
+
+def choose(slot, refs, first=0):
+    rows = refs[0][...]
+    for at, ref in enumerate(refs[1:], 1):
+        rows = jnp.where(slot == first + at, ref[...], rows)
+    return rows
+
+
+def slot_specs(count, per, block, width, order=lambda i: i):
+    return [
+        pl.BlockSpec(
+            (block, width), lambda i, at=at: (jnp.clip(order(i) - at * per, 0, per - 1), 0)
+        )
+        for at in range(count)
+    ]
+
+
+def kernel_params(mib=56):
+    return pltpu.CompilerParams(vmem_limit_bytes=mib << 20)
+
+
+def project_kernel(*refs, count, per):
+    x_refs = refs[:count]
+    gain_ref, shift_ref = refs[count : count + 2]
+    wq_ref, wk_ref, wv_ref, qb_ref, vb_ref = refs[count + 2 : count + 7]
+    normed_ref, q_ref, k_ref, v_ref = refs[-4:]
+    x = choose(pl.program_id(0) // per, x_refs).astype(F32)
+    normed = low(norm_stats(x)[0] * gain_ref[...].astype(F32) + shift_ref[...].astype(F32))
+    normed_ref[...] = normed
+    q_ref[...] = low((dot(normed, wq_ref[...]) + qb_ref[...].astype(F32)) * (LOG2E * HD**-0.5))
+    k_ref[...] = low(dot(normed, wk_ref[...]))
+    v_ref[...] = low(dot(normed, wv_ref[...]) + vb_ref[...].astype(F32))
+
+
+def project(x_parts, vectors, weights, biases, held, total):
+    count = len(x_parts)
+    rows, width = x_parts[0].shape
+    block = min(rows, 512)
+    per = rows // block
+    first = 0 if held is None else count * per
+    out_shape = [jax.ShapeDtypeStruct((total, width), BF16)] + [
+        jax.ShapeDtypeStruct((total, weight.shape[1]), BF16) for weight in weights
+    ]
+    held = [] if held is None else list(held)
+    inputs = [*x_parts, *[v[None] for v in vectors], *weights, *[v[None] for v in biases]]
+    return pl.pallas_call(
+        functools.partial(project_kernel, count=count, per=per),
+        grid=(count * per,),
+        in_specs=slot_specs(count, per, block, width)
+        + [whole((1, width))] * 2
+        + [whole(weight.shape) for weight in weights]
+        + [whole((1, v.shape[0])) for v in biases]
+        + [pl.BlockSpec(memory_space=pl.ANY)] * len(held),
+        out_specs=[
+            pl.BlockSpec((block, shape.shape[1]), lambda i: (i + first, 0)) for shape in out_shape
+        ],
+        out_shape=out_shape,
+        input_output_aliases={len(inputs) + at: at for at in range(len(held))},
+        compiler_params=kernel_params(),
+        cost_estimate=pl.CostEstimate(
+            flops=6 * count * rows * width * weights[0].shape[1],
+            transcendentals=0,
+            bytes_accessed=count * rows * width * 6,
+        ),
+        name="project",
+    )(*inputs, *held)
+
+
+def post_kernel(*refs, slots, groups, per):
     mixed_refs = refs[: slots * groups]
-    x_ref, weight_ref, bias_ref, gain_ref, shift_ref, post_ref, residual_ref = refs[slots * groups :]
+    x_refs = refs[slots * groups : slots * groups + slots]
+    weight_ref, bias_ref, gain_ref, shift_ref, post_ref, residual_ref = refs[-6:]
+    blocks = pl.num_programs(0)
+    at = (pl.program_id(0) + blocks // 2) % blocks
     mixed = jnp.concatenate([ref[...] for ref in mixed_refs], axis=1)
-    residual = x_ref[...].astype(F32) + dot(mixed, weight_ref[...]) + bias_ref[...].astype(F32)
+    x = choose(at // per, x_refs).astype(F32)
+    residual = x + dot(mixed, weight_ref[...]) + bias_ref[...].astype(F32)
     normal, _ = norm_stats(residual)
     post_ref[...] = low(normal * gain_ref[...].astype(F32) + shift_ref[...].astype(F32))
-    own = residual_ref.shape[0]
-    step = pl.program_id(0)
-
-    @pl.when(step < pl.num_programs(0) // slots)
+
+    @pl.when(at < per)
     def _():
         residual_ref[...] = residual
 
 
-def post_norm(mixed, x_all, weight, bias, gain, shift):
+def post_norm(mixed, x_parts, weight, bias, gain, shift):
     slots, groups = len(mixed), len(mixed[0])
-    total, width = x_all.shape
-    rows = total // slots
+    rows, width = x_parts[0].shape
+    total = slots * rows
     block = min(rows, 512)
     per = rows // block
+    blocks = total // block
+    order = lambda i: (i + blocks // 2) % blocks
     specs = []
     for slot in range(slots):
         for part in mixed[slot]:
             specs.append(
                 pl.BlockSpec(
                     (block, part.shape[1]),
-                    lambda i, slot=slot: (((i // per) ^ slot) * per + i % per, 0),
+                    lambda i, slot=slot: (
+                        ((order(i) // per) ^ slot) * per + order(i) % per,
+                        0,
+                    ),
                 )
             )
-    whole = lambda shape: pl.BlockSpec(shape, lambda i: (0, 0))
     return pl.pallas_call(
-        functools.partial(post_kernel, slots=slots, groups=groups),
-        grid=(total // block,),
+        functools.partial(post_kernel, slots=slots, groups=groups, per=per),
+        grid=(blocks,),
         in_specs=specs
-        + [
-            pl.BlockSpec((block, width), lambda i: (i, 0)),
-            whole(weight.shape),
-            whole((1, width)),
-            whole((1, width)),
-            whole((1, width)),
-        ],
+        + slot_specs(slots, per, block, width, order)
+        + [whole(weight.shape)]
+        + [whole((1, width))] * 3,
         out_specs=[
-            pl.BlockSpec((block, width), lambda i: (i, 0)),
-            pl.BlockSpec((block, width), lambda i: (jnp.minimum(i, per - 1), 0)),
+            pl.BlockSpec((block, width), lambda i: (order(i), 0)),
+            pl.BlockSpec(
+                (block, width), lambda i: (jnp.clip(i - blocks // 2, 0, per - 1), 0)
+            ),
         ],
         out_shape=[
             jax.ShapeDtypeStruct((total, width), BF16),
             jax.ShapeDtypeStruct((rows, width), F32),
         ],
-        compiler_params=pltpu.CompilerParams(vmem_limit_bytes=48 << 20),
+        compiler_params=kernel_params(),
         cost_estimate=pl.CostEstimate(
             flops=2 * total * width * width, transcendentals=0, bytes_accessed=6 * total * width
         ),
         name="post_norm",
     )(
         *[part for parts in mixed for part in parts],
-        x_all,
+        *x_parts,
         weight,
         bias[None],
         gain[None],
@@ -403,8 +479,202 @@
     )
 
 
+def feed_kernel(*refs, count, per, held):
+    post_ref = refs[0]
+    cot_refs = refs[1 : 1 + count]
+    up_ref, down_ref, bias_ref = refs[1 + count : 4 + count]
+    active_ref, grad_ref, cot_ref, sum_ref = refs[4 + count + held : 8 + count + held]
+    back_refs = refs[8 + count + held :]
+    slot = pl.program_id(0) // per
+
+    @pl.when(pl.program_id(0) == 0)
+    def _():
+        sum_ref[...] = jnp.zeros_like(sum_ref)
+
+    post = post_ref[...]
+    cot = choose(slot, cot_refs)
+    cot_ref[...] = cot
+    units = active_ref.shape[1]
+    chunk = min(512, units)
+    scale, cubic = math.sqrt(2 / math.pi), 0.044715
+    for first in range(0, units, chunk):
+        cols = slice(first, first + chunk)
+        hidden = dot(post, up_ref[:, cols]) + bias_ref[:, cols].astype(F32)
+        act_grad = dot(cot, down_ref[cols, :], NT)
+        square = hidden * hidden
+        curve = jnp.tanh(hidden * (scale + scale * cubic * square))
+        half = 0.5 + 0.5 * curve
+        active_ref[:, cols] = low(hidden * half)
+        slope = half + (0.5 * hidden) * (1.0 - curve * curve) * (
+            scale + 3 * scale * cubic * square
+        )
+        grad = low(act_grad * slope)
+        grad_ref[:, cols] = grad
+        sum_ref[:, cols] += jnp.sum(grad.astype(F32), axis=0, keepdims=True)
+    back = low(dot(grad_ref[...], up_ref[...], NT))
+    for at, back_ref in enumerate(back_refs):
+
+        @pl.when(slot == at)
+        def _():
+            back_ref[...] = back
+
+
+def feed(post_all, cot_parts, up, up_bias, down, half, held):
+    count = len(cot_parts)
+    rows, width = cot_parts[0].shape
+    total, units = post_all.shape[0], up.shape[1]
+    block = min(rows, 512)
+    per = rows // block
+    first = half * count * per
+    tall = lambda cols: pl.BlockSpec((block, cols), lambda i: (i + first, 0))
+    held = [] if held is None else list(held)
+    inputs = [post_all, *cot_parts, up, down, up_bias[None]]
+    return pl.pallas_call(
+        functools.partial(feed_kernel, count=count, per=per, held=len(held)),
+        grid=(count * per,),
+        in_specs=[tall(width)]
+        + slot_specs(count, per, block, width)
+        + [whole(up.shape), whole(down.shape), whole((1, units))]
+        + [pl.BlockSpec(memory_space=pl.ANY)] * len(held),
+        out_specs=[tall(units), tall(units), tall(width), whole((1, units))]
+        + slot_specs(count, per, block, width),
+        out_shape=[
+            jax.ShapeDtypeStruct((total, units), BF16),
+            jax.ShapeDtypeStruct((total, units), BF16),
+            jax.ShapeDtypeStruct((total, width), BF16),
+            jax.ShapeDtypeStruct((1, units), F32),
+        ]
+        + [jax.ShapeDtypeStruct((rows, width), BF16)] * count,
+        input_output_aliases={len(inputs) + at: at for at in range(len(held))},
+        compiler_params=kernel_params(),
+        cost_estimate=pl.CostEstimate(
+            flops=6 * count * rows * width * units,
+            transcendentals=0,
+            bytes_accessed=count * rows * width * 12,
+        ),
+        name="feed",
+    )(*inputs, *held)
+
+
+def resid_kernel(*refs, terms, slots):
+    term_refs = refs[:terms]
+    residual_ref, cot_ref, gain_ref, weight_ref = refs[terms : terms + 4]
+    grad_ref, low_ref, sums_ref = refs[terms + 4 : terms + 7]
+    part_refs = refs[terms + 7 :]
+
+    @pl.when(pl.program_id(0) == 0)
+    def _():
+        sums_ref[...] = jnp.zeros_like(sums_ref)
+
+    post_grad = term_refs[0][...].astype(F32)
+    for ref in term_refs[1:]:
+        post_grad = post_grad + ref[...].astype(F32)
+    cot = cot_ref[...].astype(F32)
+    normal, inverse = norm_stats(residual_ref[...])
+    grad = cot + norm_pull(post_grad * gain_ref[...].astype(F32), normal, inverse)
+    grad_ref[...] = grad
+    grad_low = low(grad)
+    low_ref[...] = grad_low
+    for at, value in enumerate((cot, grad, post_grad * normal, post_grad)):
+        sums_ref[at : at + 1, :] += jnp.sum(value, axis=0, keepdims=True)
+    mixed_grad = low(dot(grad_low, weight_ref[...], NT))
+    cols = part_refs[0].shape[1]
+    for slot, ref in enumerate(part_refs):
+        ref[...] = mixed_grad[:, slot * cols : (slot + 1) * cols]
+
+
+def resid_step(terms, residual, cotangent, gain, weight, slots):
+    rows, width = residual.shape
+    block = min(rows, 256)
+    tall = lambda cols: pl.BlockSpec((block, cols), lambda i: (i, 0))
+    cols = weight.shape[0] // slots
+    return pl.pallas_call(
+        functools.partial(resid_kernel, terms=len(terms), slots=slots),
+        grid=(rows // block,),
+        in_specs=[tall(width)] * (len(terms) + 2) + [whole((1, width)), whole(weight.shape)],
+        out_specs=[tall(width), tall(width), whole((8, width))] + [tall(cols)] * slots,
+        out_shape=[
+            jax.ShapeDtypeStruct((rows, width), F32),
+            jax.ShapeDtypeStruct((rows, width), BF16),
+            jax.ShapeDtypeStruct((8, width), F32),
+        ]
+        + [jax.ShapeDtypeStruct((rows, cols), BF16)] * slots,
+        compiler_params=kernel_params(),
+        cost_estimate=pl.CostEstimate(
+            flops=2 * rows * width * width, transcendentals=0, bytes_accessed=20 * rows * width
+        ),
+        name="resid_step",
+    )(*terms, residual, cotangent, gain[None], weight)
+
+
+def unproject_kernel(*refs, groups, per):
+    grad_refs, weight_refs, out_refs = refs[:groups], refs[groups : 2 * groups], refs[2 * groups :]
+    slot = pl.program_id(0) // per
+    total = dot(grad_refs[0][...], weight_refs[0][...], NT)
+    for grad_ref, weight_ref in zip(grad_refs[1:], weight_refs[1:]):
+        total = total + dot(grad_ref[...], weight_ref[...], NT)
+    total = low(total)
+    for at, ref in enumerate(out_refs):
+
+        @pl.when(slot == at)
+        def _():
+            ref[...] = total
+
+
+def unproject(grads, weights, rows, count, half):
+    width = weights[0].shape[0]
+    block = min(rows, 512)
+    per = rows // block
+    first = half * count * per
+    return pl.pallas_call(
+        functools.partial(unproject_kernel, groups=len(grads), per=per),
+        grid=(count * per,),
+        in_specs=[
+            pl.BlockSpec((block, grad.shape[1]), lambda i: (i + first, 0)) for grad in grads
+        ]
+        + [whole(weight.shape) for weight in weights],
+        out_specs=slot_specs(count, per, block, width),
+        out_shape=[jax.ShapeDtypeStruct((rows, width), BF16)] * count,
+        compiler_params=kernel_params(),
+        cost_estimate=pl.CostEstimate(
+            flops=2 * count * rows * width * len(grads) * weights[0].shape[1],
+            transcendentals=0,
+            bytes_accessed=count * rows * width * 4,
+        ),
+        name="unproject",
+    )(*grads, *weights)
+
+
+def input_kernel(*refs, terms):
+    x_ref, resid_ref, gain_ref, out_ref = refs[terms:]
+    grad = refs[0][...].astype(F32)
+    for ref in refs[1:terms]:
+        grad = grad + ref[...].astype(F32)
+    normal, inverse = norm_stats(x_ref[...].astype(F32))
+    out_ref[...] = resid_ref[...] + norm_pull(grad * gain_ref[...].astype(F32), normal, inverse)
+
+
+def input_step(terms, layer_input, resid_grad, gain):
+    rows, width = resid_grad.shape
+    block = min(rows, 256)
+    tall = pl.BlockSpec((block, width), lambda i: (i, 0))
+    return pl.pallas_call(
+        functools.partial(input_kernel, terms=len(terms)),
+        grid=(rows // block,),
+        in_specs=[tall] * (len(terms) + 2) + [whole((1, width))],
+        out_specs=tall,
+        out_shape=jax.ShapeDtypeStruct((rows, width), F32),
+        compiler_params=kernel_params(),
+        cost_estimate=pl.CostEstimate(
+            flops=20 * rows * width, transcendentals=0, bytes_accessed=16 * rows * width
+        ),
+        name="input_step",
+    )(*terms, layer_input, resid_grad, gain[None])
+
+
 def shards(
     slots,
+    streams,
     layer_input,
     row_ids,
     input_gain,
@@ -442,32 +712,51 @@
             held.update({slot ^ bit: swap(part, bit) for slot, part in held.items()})
         return [held[slot] for slot in range(slots)]
 
-    def scatter_sum(parts):
-        held = dict(enumerate(parts))
-        for bit in bits:
-            held = {
-                slot: part.astype(F32) + swap(low(held[slot | bit]), bit).astype(F32)
-                for slot, part in held.items()
-                if not slot & bit
-            }
-        return held[0]
-
     def blocks(array):
         return [array[slot * rows : (slot + 1) * rows] for slot in range(slots)]
+
+    def swap_data(array, mask):
+        return lax.ppermute(array, "dp", [(i, i ^ mask) for i in range(streams)])
+
+    def scatter_terms(parts):
+        held, terms = dict(enumerate(parts)), [parts[0]]
+        for bit in bits:
+            come = {slot ^ bit: swap(part, bit) for slot, part in held.items() if slot & bit}
+            terms.append(come.pop(0))
+            held = {
+                slot: low(held[slot].astype(F32) + part.astype(F32)) for slot, part in come.items()
+            }
+        return terms
+
+    def add_up(terms):
+        return functools.reduce(lambda sum_now, term: sum_now + term.astype(F32), terms[1:], terms[0].astype(F32))
+
+    def total_of(shared, own):
+        for bit in bits:
+            shared = shared + swap(shared, bit)
+        flat = jnp.concatenate([shared.reshape(-1), own])
+        pad = -flat.shape[0] % 1024
+        flat = jnp.pad(flat, (0, pad)).reshape(-1, 1024)
+        for level in range(streams.bit_length() - 1):
+            flat = flat + swap_data(flat, 1 << level)
+        flat = flat.reshape(-1)
+        return flat[: shared.size].reshape(shared.shape), flat[shared.size :][: own.shape[0]]
 
     x_parts = gather(layer_input)
     cot_own = after(cotangent, x_parts[-1])
     dense_parts = gather(after(dense_weight, x_parts[-1]))
     cot_parts = gather(cot_own)
 
-    x_all = jnp.concatenate(x_parts, axis=0)
+    total = slots * rows
+    half = slots // 2
     gain, shift = input_gain.astype(F32), input_shift.astype(F32)
-    normed = low(norm_stats(x_all.astype(F32))[0] * gain + shift)
-    joined = jnp.concatenate([query_weight, key_weight, value_weight], axis=1)
-    projected = dot(normed, joined)
-    queries = low((projected[:, :head_cols] + query_bias.astype(F32)) * (LOG2E * HD**-0.5))
-    key_rows = low(projected[:, head_cols : 2 * head_cols])
-    values = low(projected[:, 2 * head_cols :] + value_bias.astype(F32))
+    norm_vectors = (input_gain, input_shift)
+    weights = (query_weight, key_weight, value_weight)
+    biases = (query_bias, value_bias)
+    held = project(x_parts[:half], norm_vectors, weights, biases, None, total)
+    normed, queries, key_rows, values = project(
+        x_parts[half:], norm_vectors, weights, biases, held, total
+    )
     heads = me * head_count + jnp.arange(head_count)
     slopes = jnp.exp2(-8.0 * (heads + 1).astype(F32) / HEADS) * LOG2E
     apart = (row_ids[:1] != row_ids[SHORT : SHORT + 1]).astype(jnp.int32)
@@ -482,38 +771,27 @@
         mixed_parts.append(gather(mixed))
     mixed_all = [[mixed_parts[group][slot] for group in range(groups)] for slot in range(slots)]
     dense_all = jnp.concatenate(dense_parts, axis=0)
-    post_all, residual = post_norm(mixed_all, x_all, dense_all, dense_bias, post_gain, post_shift)
-
-    cot_all = jnp.concatenate(cot_parts, axis=0)
-    hidden = dot(post_all, up_weight) + up_bias.astype(F32)
-    active, gelu_pull = jax.vjp(lambda v: jax.nn.gelu(v, approximate=True), hidden)
-    active = low(active)
-    hidden_grad = low(gelu_pull(dot(cot_all, down_weight, NT))[0])
-    half = slots // 2 * rows
-    far = low(dot(hidden_grad[half:], up_weight, NT))
-    near = low(dot(after(hidden_grad[:half], far), up_weight, NT))
-    post_grad = scatter_sum(blocks(jnp.concatenate([near, far], axis=0)))
-    hidden_late, active_late = lax.optimization_barrier((hidden_grad, active, near))[:2]
-    up_part = dot(post_all, hidden_late, TN)
-    down_part = dot(active_late, cot_all, TN)
-    up_bias_part = jnp.sum(hidden_grad.astype(F32), axis=0)
-    up_sum, down_sum = lax.psum((low(up_part), low(down_part)), "dp")
-
-    cot_rows = cotangent.astype(F32)
-    post_normal, post_inverse = norm_stats(residual)
-    resid_grad = cot_rows + norm_pull(
-        post_grad * post_gain.astype(F32), post_normal, post_inverse
-    )
-    attended_grad = low(resid_grad)
-    mixed_grad = low(dot(attended_grad, dense_all, NT))
-    mixed_grads = [
-        swap(part, slot) if slot else part
-        for slot, part in enumerate(jnp.split(mixed_grad, slots, axis=1))
-    ]
-
-    ffn_part = low(dot(after(active, *mixed_grads), down_weight))
-    ffn_out = scatter_sum(blocks(ffn_part))
-    layer_output = low(residual + ffn_out + down_bias.astype(F32))
+    post_all, residual = post_norm(
+        mixed_all, x_parts, dense_all, dense_bias, post_gain, post_shift
+    )
+
+    far = feed(post_all, cot_parts[half:], up_weight, up_bias, down_weight, 1, None)
+    near = feed(post_all, cot_parts[:half], up_weight, up_bias, down_weight, 0, far[:3])
+    active, hidden_grad, cot_all = near[:3]
+    up_bias_part = far[3][0] + near[3][0]
+    post_terms = scatter_terms([*near[4:], *far[4:]])
+    up_part = low(dot(post_all, hidden_grad, TN))
+    down_part = low(dot(active, cot_all, TN))
+    up_sum, down_sum = lax.psum((up_part, down_part), "dp")
+
+    resid_grad, attended_grad, row_sums, *mixed_grads = resid_step(
+        post_terms, residual, cotangent, post_gain, dense_all, slots
+    )
+    mixed_grads = [swap(part, slot) if slot else part for slot, part in enumerate(mixed_grads)]
+
+    ffn_part = low(dot(active, down_weight))
+    ffn_terms = scatter_terms(blocks(ffn_part))
+    layer_output = low(residual + add_up(ffn_terms) + down_bias.astype(F32))
     mixed_rows = jnp.concatenate(
         [
             part[slot * rows : (slot + 1) * rows]
@@ -522,89 +800,87 @@
         ],
         axis=1,
     )
-    dense_part = dot(mixed_rows, attended_grad, TN)
-    dense_part = scatter_sum(
-        [dense_part[slot * head_cols : (slot + 1) * head_cols] for slot in range(slots)]
-    )
-
-    def total_of(vectors, own):
-        flat = jnp.concatenate(vectors + own)
-        pad = -flat.shape[0] % 1024
-        flat = jnp.pad(flat, (0, pad)).reshape(-1, 1024)
-        every = lax.all_gather(flat, ("dp", "tensor"), axis=0)
-        every = every.reshape(-1, slots, flat.size)
-        shared = jnp.sum(every, axis=(0, 1))
-        mine = jnp.sum(lax.dynamic_index_in_dim(every, me, 1, keepdims=False), axis=0)
-        outs, at = [], 0
-        for vector, source in [(v, shared) for v in vectors] + [(v, mine) for v in own]:
-            outs.append(source[at : at + vector.shape[0]])
-            at += vector.shape[0]
-        return outs
-
-    down_bias_grad, dense_bias_grad, post_gain_grad, post_shift_grad, up_bias_grad = total_of(
-        [
-            jnp.sum(cot_rows, axis=0),
-            jnp.sum(resid_grad, axis=0),
-            jnp.sum(post_grad * post_normal, axis=0),
-            jnp.sum(post_grad, axis=0),
-        ],
-        [up_bias_part],
-    )
-
-    head_grads = [
-        attend_back(
-            me_word,
-            apart,
-            slopes,
-            queries,
-            key_rows,
-            values,
-            mixed_own[group],
-            log_totals[group],
-            mixed_grads,
-            group,
+    dense_part = low(dot(mixed_rows, attended_grad, TN))
+    dense_part = low(
+        add_up(
+            scatter_terms(
+                [dense_part[slot * head_cols : (slot + 1) * head_cols] for slot in range(slots)]
+            )
         )
+    )
+    row_sums, up_bias_grad = total_of(row_sums[:4], up_bias_part)
+
+    cols = head_cols // groups
+    pick = lambda array, group: array[:, group * cols : (group + 1) * cols]
+    group_weights = [
+        jnp.concatenate([pick(weight, group) for weight in weights], axis=1)
         for group in range(groups)
     ]
-    proj_grad = jnp.concatenate(
-        [head_grads[group][kind] for kind in range(3) for group in range(groups)], axis=1
-    )
-    far = low(dot(proj_grad[half:], joined, NT))
-    near = low(dot(after(proj_grad[:half], far), joined, NT))
-    normed_grad = scatter_sum(blocks(jnp.concatenate([near, far], axis=0)))
-    proj_late = after(proj_grad, near)
-    joined_part = dot(normed, proj_late, TN)
-    proj_sum = jnp.sum(proj_grad.astype(F32), axis=0)
-    joined_high = joined.astype(F32)
-    shift_part = jnp.sum(joined_high * proj_sum, axis=1)
-    gain_part = (jnp.sum(joined_high * joined_part, axis=1) - shift * shift_part) / gain
-    late = lax.optimization_barrier((low(joined_part), low(dense_part), up_sum, down_sum))
-    joined_sum, dense_sum = lax.psum(late[:2], "dp")
-    input_gain_grad, input_shift_grad, query_bias_grad, value_bias_grad = total_of(
-        [gain_part, shift_part], [proj_sum[:head_cols], proj_sum[2 * head_cols :]]
-    )
-
-    input_normal, input_inverse = norm_stats(layer_input.astype(F32))
-    input_grad = resid_grad + norm_pull(normed_grad * gain, input_normal, input_inverse)
-    joined_sum = joined_sum.astype(F32)
+    head_grads, group_parts, group_sums = [], [], []
+    chain = (up_sum, down_sum)
+    for group in range(groups):
+        grads = mixed_grads if not group else lax.optimization_barrier((*mixed_grads, head_grads[-1]))[:-1]
+        head_grads.append(
+            attend_back(
+                me_word,
+                apart,
+                slopes,
+                queries,
+                key_rows,
+                values,
+                mixed_own[group],
+                log_totals[group],
+                grads,
+                group,
+            )
+        )
+        group_parts.append(dot(normed, head_grads[-1], TN))
+        sending = (low(group_parts[-1]),) + ((dense_part,) if not group else ())
+        sending = lax.optimization_barrier((*sending, *chain))
+        chain = sending[-len(chain) :]
+        sums = lax.psum(sending[: -len(chain)], "dp")
+        if not group:
+            up_sum, down_sum, dense_sum = *chain, sums[1]
+        group_sums.append(sums[0])
+        chain = (sums[0],)
+    far = unproject(head_grads, group_weights, rows, half, 1)
+    near = unproject(head_grads, group_weights, rows, half, 0)
+    normed_terms = scatter_terms([*near, *far])
+
+    shift_part, gain_part, proj_sums = 0.0, 0.0, []
+    for weight, grad, part in zip(group_weights, head_grads, group_parts):
+        proj_sums.append(jnp.sum(grad.astype(F32), axis=0))
+        weight = weight.astype(F32)
+        shift_part = shift_part + jnp.sum(weight * proj_sums[-1], axis=1)
+        gain_part = gain_part + jnp.sum(weight * part, axis=1)
+    gain_part = (gain_part - shift * shift_part) / gain
+    norm_sums, bias_sums = total_of(
+        jnp.stack([gain_part, shift_part]),
+        jnp.concatenate([part[:cols] for part in proj_sums] + [part[2 * cols :] for part in proj_sums]),
+    )
+    weight_grads = [
+        jnp.concatenate([array[:, kind * cols : (kind + 1) * cols] for array in group_sums], axis=1).astype(F32)
+        for kind in range(3)
+    ]
+    input_grad = input_step(normed_terms, layer_input, resid_grad, input_gain)
     return (
         layer_output,
         input_grad,
-        input_gain_grad,
-        input_shift_grad,
-        joined_sum[:, :head_cols],
-        query_bias_grad,
-        joined_sum[:, head_cols : 2 * head_cols],
-        joined_sum[:, 2 * head_cols :],
-        value_bias_grad,
+        norm_sums[0],
+        norm_sums[1],
+        weight_grads[0],
+        bias_sums[:head_cols],
+        weight_grads[1],
+        weight_grads[2],
+        bias_sums[head_cols:],
         dense_sum.astype(F32),
-        dense_bias_grad,
-        post_gain_grad,
-        post_shift_grad,
-        late[2].astype(F32),
+        row_sums[1],
+        row_sums[2],
+        row_sums[3],
+        up_sum.astype(F32),
         up_bias_grad,
-        late[3].astype(F32),
-        down_bias_grad,
+        down_sum.astype(F32),
+        row_sums[0],
     )
 
 
@@ -649,4 +925,4 @@
         P(),
     )
     return jax.shard_map(
-        functools.partial(shards, mesh.shape["tensor"]), mesh=mesh, in_specs=in_specs, out_specs=out_specs, check_vma=False)
+        functools.partial(shards, mesh.shape["tensor"], mesh.shape["dp"]), mesh=mesh, in_specs=in_specs, out_specs=out_specs, check_vma=False)

time: 819 us -> 819 us (level)
  waiting for transfers between devices: 115 us -> 293 us
  blocking collectives: 134 us -> 0 us
  Pallas kernels: 233 us -> 338 us
  matrix products: 140 us -> 60.4 us
  other arithmetic: 75.3 us -> 32 us
  local copies, waits for them, and re-layouts: 80.2 us -> 40.4 us
  starting transfers between devices: 15.4 us -> 29.8 us
    all_gather x2 -> x0, blocking collectives: 134 us -> none  [total_of(): every = lax.all_gather(flat, ('dp', 'tensor'), axis=0)]
    psum x2 -> x3, waiting for transfers between devices: 0.01 us -> 133 us  [the longest x2 133 us: shards(): sums = lax.psum(sending[:-len(chain)], 'dp')]
    pallas_call x1 -> x9, Pallas kernels: 19.9 us -> 125 us  [the longest x2 46.2 us: feed(): pl.pallas_call(functools.partial(feed_kernel, count=count, per=per, held=...]
    dot_general x13 -> x6, matrix products: 140 us -> 60.4 us  [dot(): return lax.dot_general(lhs, rhs, dims, preferred_element_type=F32)]
    ppermute x30 -> x34, waiting for transfers between devices: 115 us -> 153 us  [swap(): return lax.ppermute(array, 'tensor', [(i, i ^ mask) for i in range(slots)])]
    unnamed x151 -> x104, local copies, waits for them, and re-layouts: 45.7 us -> 16 us
    reduce_sum x14 -> x3, other arithmetic: 25.5 us -> 4.96 us  [the longest x2 3.19 us: shards(): proj_sums.append(jnp.sum(grad.astype(F32), axis=0))]
    ppermute x0 -> x6, starting transfers between devices: none -> 10.3 us  [swap_data(): return lax.ppermute(array, 'dp', [(i, i ^ mask) for i in range(streams)])]
  transfers between devices with their start and end apart: 32 -> 43, of which waited for: 4 -> 12; matrix products, arithmetic and copies ran while one was open for 31% -> 16% of each run, Pallas kernels for 29% -> 41%
where the time goes in v3:
time: 819 us; the launch traced here: 810 us
  Pallas kernels  338 us (41%)
  waiting for transfers between devices  293 us (36%)
  matrix products  60.4 us (7%)
  local copies, waits for them, and re-layouts  40.4 us (5%)
  other arithmetic  32 us (4%)
  starting transfers between devices  29.8 us (4%)
  between operations  16 us (2%)
    ppermute x34, waiting for transfers between devices, swap(): return lax.ppermute(array, 'tensor', [(i, i ^ mask) for i in range(slots)])  153 us
    pallas_call x2, Pallas kernels, attend_back(): pl.pallas_call(functools.partial(attend_back_kernel, slots=slots, pair=pa...  140 us
    psum x2, waiting for transfers between devices, shards(): sums = lax.psum(sending[:-len(chain)], 'dp')  133 us
    pallas_call x2, Pallas kernels, attend(): pl.pallas_call(functools.partial(attend_kernel, slots=slots, pair=pair, t...  72.8 us
    dot_general x6, matrix products, dot(): return lax.dot_general(lhs, rhs, dims, preferred_element_type=F32)  60.4 us
    pallas_call x2, Pallas kernels, feed(): pl.pallas_call(functools.partial(feed_kernel, count=count, per=per, held=...  46.2 us
    pallas_call x1, Pallas kernels, post_norm(): pl.pallas_call(functools.partial(post_kernel, slots=slots, groups=groups,...  23 us
    convert_element_type x6, other arithmetic, low(): return array.astype(BF16)  19.9 us
  transfers between devices with their start and end apart: 43, of which 12 were waited for; matrix products, arithmetic and copies ran while one was open for 16% of the time, Pallas kernels for 41%

profile of v3, /device:TPU:0, one launch (start us, length us, event | category | flops | bytes accessed | tf_op | source)
XLA Modules:
  0.0 809.7 jit_solution(2131779420038756072)
XLA Ops:
  7.2 3.0 collective-permute-start
  10.3 45.8 %collective-permute-done.refs_0_.refs_10_ = bf16[1024,1024]{1,0:T(8,128)(2,1)S(1)} collective-permute-done((bf16[1024,1024]{1,0:T(8,128)(2,1)}, bf16[1024,1024]{1,0:T(8,128)(2,1)S(1)}, u32[]{:S(2)}, u32[]{:S(2)}) %collective-permute-start) | collective-permute-done | bytes 2097184 | tf_op jit(solution)/shard_map/ppermute | solution.py:707
  56.1 1.2 broadcast_in_dim.40.refs_7_
  57.4 1.2 broadcast_in_dim.41.refs_8_
  61.1 1.3 broadcast_in_dim.38.refs_2_.refs_5_
  62.4 1.3 broadcast_in_dim.39.refs_3_
  64.3 1.9 fusion.9
  66.1 1.9 fusion.10
  68.0 9.3 %project.2 = (bf16[4096,1024]{1,0:T(8,128)(2,1)}, bf16[4096,256]{1,0:T(8,128)(2,1)}, bf16[4096,256]{1,0:T(8,128)(2,1)}, bf16[4096,256]{1,0:T(8,128)(2,1)}) custom-call(bf16[1024,1024]{1,0:T(8,128)(2,1)} %refs_3_.5, bf16[1024,1024]{1,0:T(8,128)(2,1)} %collective-permute-done.2.refs_1_.refs_9_, bf16[1,1024]{1,0:T(2,128)(2,1)} %broadcast_in_dim.38.refs_2_.refs_5_, ...), custom_call_target="tpu_custom_call" | custom-call | flops 3221225472 | bytes 12582912 | tf_op jit(solution)/shard_map/project/pallas_call | solution.py:390
  77.4 1.8 collective-permute-start.10
  79.4 9.2 %project.3 = (bf16[4096,1024]{1,0:T(8,128)(2,1)}, bf16[4096,256]{1,0:T(8,128)(2,1)}, bf16[4096,256]{1,0:T(8,128)(2,1)}, bf16[4096,256]{1,0:T(8,128)(2,1)}) custom-call(bf16[1024,1024]{1,0:T(8,128)(2,1)} %copy-done.5, ...), custom_call_target="tpu_custom_call", output_to_operand_aliasing={{0}: (9, {}), {1}: (10, {}), {2}: (11, {}), {3}: (12, {})} | custom-call | flops 3221225472 | bytes 12582912 | tf_op jit(solution)/shard_map/project/pallas_call | solution.py:390
  88.6 36.3 %attend.2 = (bf16[4096,128]{1,0:T(8,128)(2,1)}, f32[2,1,4096]{2,1,0:T(1,128)}) custom-call(s32[1]{0:T(128)} %bitcast.me_ref.refs_0_, s32[1]{0:T(128)S(6)} %convert_element_type.125.apart_ref.refs_1_, f32[2]{0:T(128)} %get-tuple-element.170.slope_ref.refs_2_, bf16[4096,256]{1,0:T(8,128)(2,1)} %get-tuple-element.69.q_ref.refs_3_, ...), custom_call_target="tpu_custom_call" | custom-call | flops 36909875200 | bytes 4194304 | tf_op jit(solution)/shard_map/attend/pallas_call | solution.py:181
  125.3 1.7 collective-permute-start.13
  127.2 36.4 %attend.3 = (bf16[4096,128]{1,0:T(8,128)(2,1)}, f32[2,1,4096]{2,1,0:T(1,128)}) custom-call(s32[1]{0:T(128)} %bitcast.me_ref.refs_0_, s32[1]{0:T(128)S(6)} %convert_element_type.125.apart_ref.refs_1_, f32[2]{0:T(128)} %get-tuple-element.169.slope_ref.refs_2_, bf16[4096,256]{1,0:T(8,128)(2,1)} %get-tuple-element.69.q_ref.refs_3_, ...), custom_call_target="tpu_custom_call" | custom-call | flops 36909875200 | bytes 4194304 | tf_op jit(solution)/shard_map/attend/pallas_call | solution.py:181
  167.5 1.7 slice_dynamic-update-slice_fusion.7
  170.7 47.3 %collective-permute-done.6.refs_5_ = bf16[4096,128]{1,0:T(8,128)(2,1)S(1)} collective-permute-done((bf16[4096,128]{1,0:T(8,128)(2,1)}, bf16[4096,128]{1,0:T(8,128)(2,1)S(1)}, u32[]{:S(2)}, u32[]{:S(2)}) %collective-permute-start.6) | collective-permute-done | bytes 1048608 | tf_op jit(solution)/shard_map/ppermute | solution.py:707
  218.5 1.7 slice_dynamic-update-slice_fusion.5
  221.0 1.7 slice_dynamic-update-slice_fusion.3
  225.9 23.0 %post_norm.1 = (bf16[4096,1024]{1,0:T(8,128)(2,1)}, f32[1024,1024]{1,0:T(8,128)}) custom-call(bf16[4096,128]{1,0:T(8,128)(2,1)} %get-tuple-element.72.refs_0_.refs_6_, bf16[4096,128]{1,0:T(8,128)(2,1)} %get-tuple-element.73.refs_1_.refs_6_, bf16[4096,128]{1,0:T(8,128)(2,1)} %collective-permute-done.3.refs_2_, bf16[4096,128]{1,0:T(8,128)(2,1)} %copy-done.25, ...), custom_call_target="tpu_custom_call" | custom-call | flops 8589934592 | bytes 25165824 | tf_op jit(solution)/shard_map/post_norm/pallas_call | solution.py:450
  248.9 23.3 %feed.2 = (bf16[4096,1024]{1,0:T(8,128)(2,1)}, bf16[4096,1024]{1,0:T(8,128)(2,1)}, bf16[4096,1024]{1,0:T(8,128)(2,1)}, f32[1,1024]{1,0:T(1,128)}, bf16[1024,1024...) custom-call(bf16[4096,1024]{1,0:T(8,128)(2,1)} %get-tuple-element.76.refs_0_, ...), custom_call_target="tpu_custom_call" | custom-call | flops 12884901888 | bytes 25165824 | tf_op jit(solution)/shard_map/feed/pallas_call | solution.py:532
  272.6 22.9 %feed.3 = (bf16[4096,1024]{1,0:T(8,128)(2,1)}, bf16[4096,1024]{1,0:T(8,128)(2,1)}, bf16[4096,1024]{1,0:T(8,128)(2,1)}, f32[1,1024]{1,0:T(1,128)}, bf16[1024,1024...) custom-call(bf16[4096,1024]{1,0:T(8,128)(2,1)} %get-tuple-element.76.refs_0_,, ...), custom_call_target="tpu_custom_call", output_to_operand_aliasing={{0}: (6, {}), {1}: (7, {}), {2}: (8, {})} | custom-call | flops 12884901888 | bytes 25165824 | tf_op jit(solution)/shard_map/feed/pallas_call | solution.py:532
  295.4 14.9 %convolution_convert_fusion.2 = bf16[1024,1024]{1,0:T(8,128)(2,1)} fusion(bf16[4096,1024]{1,0:T(8,128)(2,1)} %get-tuple-element.76.refs_0_, bf16[4096,1024]{1,0:T(8,128)(2,1)} %get-tuple-element.103), kind=kOutput, calls=%fused_computation.12 | convolution fusion | flops 8590983168 | bytes 18874368 | tf_op jit(solution)/shard_map/dot_general | solution.py:24
  310.5 11.5 %convolution_convert_fusion = bf16[4096,1024]{1,0:T(8,128)(2,1)S(1)} fusion(bf16[4096,1024]{1,0:T(8,128)(2,1)} %get-tuple-element.81, bf16[1024,1024]{1,0:T(8,128)(2,1)S(1)} %copy-done.38), kind=kOutput, calls=%fused_computation | convolution fusion | flops 8594128896 | bytes 18874368 | tf_op jit(solution)/shard_map/dot_general | solution.py:24
  322.1 2.7 add_convert_fusion.1
  325.1 2.6 fusion.5
  328.5 2.0 copy-done.42
  330.4 12.3 %convolution_convert_fusion.1 = bf16[1024,1024]{1,0:T(8,128)(2,1)} fusion(bf16[4096,1024]{1,0:T(8,128)(2,1)S(1)} %copy-done.42, bf16[4096,1024]{1,0:T(8,128)(2,1)} %get-tuple-element.104), kind=kOutput, calls=%fused_computation.11 | convolution fusion | flops 8590983168 | bytes 18874368 | tf_op jit(solution)/shard_map/dot_general | solution.py:24
  342.8 30.2 %collective-permute-done.20.refs_2_ = bf16[1024,1024]{1,0:T(8,128)(2,1)} collective-permute-done((bf16[1024,1024]{1,0:T(8,128)(2,1)}, bf16[1024,1024]{1,0:T(8,128)(2,1)}, u32[]{:S(2)}, u32[]{:S(2)}) %collective-permute-start.20) | collective-permute-done | bytes 2097184 | tf_op jit(solution)/shard_map/ppermute | solution.py:707
  373.0 11.4 %resid_step.1 = (f32[1024,1024]{1,0:T(8,128)}, bf16[1024,1024]{1,0:T(8,128)(2,1)}, f32[8,1024]{1,0:T(8,128)}, bf16[1024,256]{1,0:T(8,128)(2,1)}, bf16[1024,256]{...) custom-call(bf16[1024,1024]{1,0:T(8,128)(2,1)} %get-tuple-element.83.refs_0_, ...), custom_call_target="tpu_custom_call" | custom-call | flops 2147483648 | bytes 20971520 | tf_op jit(solution)/shard_map/resid_step/pallas_call | solution.py:591
  385.3 4.0 add_convert_fusion.3
  391.8 4.0 convolution_convert_fusion.3
  395.8 19.5 %collective-permute-done.36 = f32[4,1024]{1,0:T(4,128)S(1)} collective-permute-done((f32[4,1024]{1,0:T(4,128)S(1)}, f32[4,1024]{1,0:T(4,128)S(1)}, u32[]{:S(2)}, u32[]{:S(2)}) %collective-permute-start.36) | collective-permute-done | bytes 16416 | tf_op jit(solution)/shard_map/ppermute | solution.py:707
  415.3 1.6 collective-permute-start.37
  417.9 1.4 collective-permute-done.37
  420.3 70.3 %attend_back.2.refs_0_ = bf16[4096,384]{1,0:T(8,128)(2,1)} custom-call(s32[1]{0:T(128)} %bitcast.me_ref.refs_0_, s32[1]{0:T(128)S(6)} %convert_element_type.125.apart_ref.refs_1_, f32[2]{0:T(128)} %get-tuple-element.170.slope_ref.refs_2_, bf16[4096,256]{1,0:T(8,128)(2,1)} %get-tuple-element.69.q_ref.refs_3_, ...), custom_call_target="tpu_custom_call" | custom-call | flops 73819750400 | bytes 8388608 | tf_op jit(solution)/shard_map/attend_back/pallas_call | solution.py:311
  490.6 70.0 %attend_back.3.refs_1_ = bf16[4096,384]{1,0:T(8,128)(2,1)} custom-call(s32[1]{0:T(128)} %bitcast.me_ref.refs_0_, s32[1]{0:T(128)S(6)} %convert_element_type.125.apart_ref.refs_1_, f32[2]{0:T(128)} %get-tuple-element.169.slope_ref.refs_2_, bf16[4096,256]{1,0:T(8,128)(2,1)} %get-tuple-element.69.q_ref.refs_3_, ...), custom_call_target="tpu_custom_call" | custom-call | flops 73819750400 | bytes 8388608 | tf_op jit(solution)/shard_map/attend_back/pallas_call | solution.py:311
  560.6 8.6 %fusion.17 = (bf16[1024,384]{0,1:T(8,128)(2,1)}, f32[1024,384]{0,1:T(8,128)S(1)}) fusion(bf16[4096,1024]{1,0:T(8,128)(2,1)} %get-tuple-element.101, bf16[4096,384]{1,0:T(8,128)(2,1)} %attend_back.3.refs_1_), kind=kOutput, calls=%fused_computation.63 | convolution fusion | flops 3221618688 | bytes 13893632 | tf_op jit(solution)/shard_map/dot_general | solution.py:24
  569.7 9.1 %fusion.18 = (bf16[1024,384]{0,1:T(8,128)(2,1)}, f32[1024,384]{0,1:T(8,128)}) fusion(bf16[4096,1024]{1,0:T(8,128)(2,1)} %get-tuple-element.101, bf16[4096,384]{1,0:T(8,128)(2,1)} %attend_back.2.refs_0_), kind=kOutput, calls=%fused_computation.64 | convolution fusion | flops 3221618688 | bytes 13893632 | tf_op jit(solution)/shard_map/dot_general | solution.py:24
  578.8 1.9 copy.42
  580.7 2.6 convert_reduce_fusion
  584.9 1.8 fusion
  587.2 8.7 %unproject.3 = (bf16[1024,1024]{1,0:T(8,128)(2,1)}, bf16[1024,1024]{1,0:T(8,128)(2,1)}) custom-call(bf16[4096,384]{1,0:T(8,128)(2,1)} %attend_back.2.refs_0_, bf16[4096,384]{1,0:T(8,128)(2,1)} %attend_back.3.refs_1_, bf16[1024,384]{1,0:T(8,128)(2,1)} %get-tuple-element.141.refs_2_, bf16[1024,384]{1,0:T(8,128)(2,1)} %get-tuple-element.177.refs_3_), custom_call_target="tpu_custom_call" | custom-call | flops 3221225472 | bytes 8388608 | tf_op jit(solution)/shard_map/unproject/pallas_call | solution.py:629
  596.0 9.0 %unproject.2 = (bf16[1024,1024]{1,0:T(8,128)(2,1)}, bf16[1024,1024]{1,0:T(8,128)(2,1)}) custom-call(bf16[4096,384]{1,0:T(8,128)(2,1)} %attend_back.2.refs_0_, bf16[4096,384]{1,0:T(8,128)(2,1)} %attend_back.3.refs_1_, bf16[1024,384]{1,0:T(8,128)(2,1)} %get-tuple-element.141.refs_2_, bf16[1024,384]{1,0:T(8,128)(2,1)} %get-tuple-element.177.refs_3_), custom_call_target="tpu_custom_call" | custom-call | flops 3221225472 | bytes 8388608 | tf_op jit(solution)/shard_map/unproject/pallas_call | solution.py:629
  605.7 1.7 collective-permute-start.28
  607.4 1.2 add_convert_fusion.5
  609.4 1.7 collective-permute-start.34
  611.2 1.7 collective-permute-start.38
  612.9 9.5 %collective-permute-done.34 = bf16[256,1024]{1,0:T(8,128)(2,1)S(1)} collective-permute-done((bf16[256,1024]{1,0:T(8,128)(2,1)S(1)}, bf16[256,1024]{1,0:T(8,128)(2,1)S(1)}, u32[]{:S(2)}, u32[]{:S(2)}) %collective-permute-start.34) | collective-permute-done | bytes 524320 | tf_op jit(solution)/shard_map/ppermute | solution.py:707
  623.5 3.9 add_convert_fusion
  627.4 1.5 collective-permute-start.26
  628.9 1.5 collective-permute-start.29
  630.4 2.2 collective-permute-done.29
  632.7 2.8 collective-permute-start.39
  635.5 64.7 %all-reduce.7.cloned.1.call-done = bf16[1024,384]{0,1:T(8,128)(2,1)} async-done(((bf16[1024,384]{0,1:T(8,128)(2,1)}), bf16[1024,384]{0,1:T(8,128)(2,1)}) %all-reduce.7.cloned.1.call-update) | async-done | bytes 786448 | tf_op jit(solution)/shard_map/psum | solution.py:841
  701.0 7.0 add_convert_fusion.2
  708.1 2.0 collective-permute-start.31
  710.7 2.2 collective-permute-done.31
  714.1 2.5 convert_element_type.164
  716.6 2.5 convert_element_type.165
  719.1 68.7 %all-reduce.9.cloned.1.call-done = (bf16[1024,384]{0,1:T(8,128)(2,1)}, bf16[256,1024]{1,0:T(8,128)(2,1)}) async-done(((bf16[1024,384]{0,1:T(8,128)(2,1)}, bf16[256,1024]{1,0:T(8,128)(2,1)}), (bf16[1024,384]{0,1:T(8,128)(2,1)}, bf16[256,1024]{1,0:T(8,128)(2,1)})) %all-reduce.9.cloned.1.call-update) | async-done | bytes 1310736 | tf_op jit(solution)/shard_map/psum | solution.py:841
  789.1 1.3 copy.46
  791.7 1.3 copy.44
  793.0 1.3 copy.45
  794.4 8.4 %input_step.1 = f32[1024,1024]{1,0:T(8,128)} custom-call(bf16[1024,1024]{1,0:T(8,128)(2,1)} %get-tuple-element.96.refs_0_, bf16[1024,1024]{1,0:T(8,128)(2,1)} %collective-permute-done.24.refs_1_, bf16[1024,1024]{1,0:T(8,128)(2,1)} %collective-permute-done.26.refs_2_, bf16[1024,1024]{1,0:T(8,128)(2,1)} %refs_3_.5, f32[1024,1024]{1,0:T(8,128)} %get-tuple-element.100.refs_4_, ...), custom_call_target="tpu_custom_call" | custom-call | flops 20971520 | bytes 16777216 | tf_op jit(solution)/shard_map/input_step/pallas_call | solution.py:661
  (207 shorter events, 30.0 us)
Async XLA Ops:
  7.2 616.2 %all-reduce.11.cloned.1.call-start = ((), (), s32[]{:S(2)}) async-start(), calls=%async_computation.2 | async-start | bytes 8388608 | tf_op jit(solution)/shard_map/psum | solution.py:785
  7.2 48.9 %collective-permute-start = (bf16[1024,1024]{1,0:T(8,128)(2,1)}, bf16[1024,1024]{1,0:T(8,128)(2,1)S(1)}, u32[]{:S(2)}, u32[]{:S(2)}) collective-permute-start(bf16[1024,1024]{1,0:T(8,128)(2,1)} %refs_3_.5), channel_id=1, source_target_pairs={{0,2},{1,3},{2,0},{3,1},{4,6},{5,7},{6,4},{7,5},{8,10},{9,11},{10,... | collective-permute-start | bytes 6291464 | tf_op jit(solution)/shard_map/ppermute | solution.py:707
  10.3 57.7 %collective-permute-start.2 = (bf16[1024,1024]{1,0:T(8,128)(2,1)}, bf16[1024,1024]{1,0:T(8,128)(2,1)}, u32[]{:S(2)}, u32[]{:S(2)}) collective-permute-start(bf16[1024,1024]{1,0:T(8,128)(2,1)} %refs_3_.5), channel_id=1, source_target_pairs={{0,1},{1,0},{2,3},{3,2},{4,5},{5,4},{6,7},{7,6},{8,9},{9,8},{10,11... | collective-permute-start | bytes 6291464 | tf_op jit(solution)/shard_map/ppermute | solution.py:707
  56.1 21.2 %copy-start.5 = (bf16[1024,1024]{1,0:T(8,128)(2,1)}, bf16[1024,1024]{1,0:T(8,128)(2,1)S(1)}, u32[]{:S(2)}) copy-start(bf16[1024,1024]{1,0:T(8,128)(2,1)S(1)} %collective-permute-done.refs_0_.refs_10_) | copy-start | bytes 6291460
  56.1 21.2 %collective-permute-start.1 = (bf16[1024,1024]{1,0:T(8,128)(2,1)S(1)}, bf16[1024,1024]{1,0:T(8,128)(2,1)}, u32[]{:S(2)}, u32[]{:S(2)}) collective-permute-start(bf16[1024,1024]{1,0:T(8,128)(2,1)S(1)} %collective-permute-done.refs_0_.refs_10_), channel_id=1, source_target_pairs={{0,1},{1,0},{2,3},{3,2},{4,5},{5,4},{6,7},{7,6},{8,9},{9,8},{10,11... | collective-permute-start | bytes 6291464 | tf_op jit(solution)/shard_map/ppermute | solution.py:707
  68.0 9.4 %copy-start.20 = (bf16[256,1024]{1,0:T(8,128)(2,1)S(1)}, bf16[256,1024]{1,0:T(8,128)(2,1)}, u32[]{:S(2)}) copy-start(bf16[256,1024]{1,0:T(8,128)(2,1)} %param.27) | copy-start | bytes 1572868
  77.4 49.6 %collective-permute-start.10 = (bf16[256,1024]{1,0:T(8,128)(2,1)S(1)}, bf16[256,1024]{1,0:T(8,128)(2,1)S(1)}, u32[]{:S(2)}, u32[]{:S(2)}) collective-permute-start(bf16[256,1024]{1,0:T(8,128)(2,1)S(1)} %copy-done.20), channel_id=1, source_target_pairs={{0,2},{1,3},{2,0},{3,1},{4,6},{5,7},{6,4},{7,5},{8,10},{9,11},{10,... | collective-permute-start | bytes 1572872 | tf_op jit(solution)/shard_map/ppermute | solution.py:707
  79.2 84.5 %collective-permute-start.9 = (bf16[256,1024]{1,0:T(8,128)(2,1)S(1)}, bf16[256,1024]{1,0:T(8,128)(2,1)S(1)}, u32[]{:S(2)}, u32[]{:S(2)}) collective-permute-start(bf16[256,1024]{1,0:T(8,128)(2,1)S(1)} %copy-done.20), channel_id=1, source_target_pairs={{0,1},{1,0},{2,3},{3,2},{4,5},{5,4},{6,7},{7,6},{8,9},{9,8},{10,11... | collective-permute-start | bytes 1572872 | tf_op jit(solution)/shard_map/ppermute | solution.py:707
  88.6 36.7 %copy-start.11 = (bf16[1024,1024]{1,0:T(8,128)(2,1)S(1)}, bf16[1024,1024]{1,0:T(8,128)(2,1)}, u32[]{:S(2)}) copy-start(bf16[1024,1024]{1,0:T(8,128)(2,1)} %refs_4_.9) | copy-start | bytes 6291460
  124.9 45.1 %collective-permute-start.5 = (bf16[4096,128]{1,0:T(8,128)(2,1)}, bf16[4096,128]{1,0:T(8,128)(2,1)}, u32[]{:S(2)}, u32[]{:S(2)}) collective-permute-start(bf16[4096,128]{1,0:T(8,128)(2,1)} %get-tuple-element.72.refs_0_.refs_6_), channel_id=1, source_target_pairs={{0,2},{1,3},{2,0},{3,1},{4,6},{5,7},{6,4},{7,5},{8,10},{9,11},{10,... | collective-permute-start | bytes 3145736 | tf_op jit(solution)/shard_map/ppermute | solution.py:707
  125.3 92.6 %collective-permute-start.3 = (bf16[4096,128]{1,0:T(8,128)(2,1)}, bf16[4096,128]{1,0:T(8,128)(2,1)}, u32[]{:S(2)}, u32[]{:S(2)}) collective-permute-start(bf16[4096,128]{1,0:T(8,128)(2,1)} %get-tuple-element.72.refs_0_.refs_6_), channel_id=1, source_target_pairs={{0,1},{1,0},{2,3},{3,2},{4,5},{5,4},{6,7},{7,6},{8,9},{9,8},{10,11... | collective-permute-start | bytes 3145736 | tf_op jit(solution)/shard_map/ppermute | solution.py:707
  125.3 93.1 %collective-permute-start.13 = (bf16[1024,1024]{1,0:T(8,128)(2,1)S(1)}, bf16[1024,1024]{1,0:T(8,128)(2,1)}, u32[]{:S(2)}, u32[]{:S(2)}) collective-permute-start(bf16[1024,1024]{1,0:T(8,128)(2,1)S(1)} %copy-done.11), channel_id=1, source_target_pairs={{0,2},{1,3},{2,0},{3,1},{4,6},{5,7},{6,4},{7,5},{8,10},{9,11},{10,... | collective-permute-start | bytes 6291464 | tf_op jit(solution)/shard_map/ppermute | solution.py:707
  127.0 40.4 %collective-permute-start.11 = (bf16[256,1024]{1,0:T(8,128)(2,1)S(1)}, bf16[256,1024]{1,0:T(8,128)(2,1)S(1)}, u32[]{:S(2)}, u32[]{:S(2)}) collective-permute-start(bf16[256,1024]{1,0:T(8,128)(2,1)S(1)} %collective-permute-done.10), channel_id=1, source_target_pairs={{0,1},{1,0},{2,3},{3,2},{4,5},{5,4},{6,7},{7,6},{8,9},{9,8},{10,11... | collective-permute-start | bytes 1572872 | tf_op jit(solution)/shard_map/ppermute | solution.py:707
  127.2 36.9 %copy-start.8 = (bf16[1024,256]{1,0:T(8,128)(2,1)S(1)}, bf16[1024,256]{1,0:T(8,128)(2,1)}, u32[]{:S(2)}) copy-start(bf16[1024,256]{1,0:T(8,128)(2,1)} %refs_6_.3) | copy-start | bytes 1572868
  127.2 37.8 %copy-start.33 = (bf16[1024]{0:T(1024)(128)(2,1)S(1)}, bf16[1024]{0:T(1024)(128)(2,1)}, u32[]{:S(2)}) copy-start(bf16[1024]{0:T(1024)(128)(2,1)} %param.29) | copy-start | bytes 6148
  127.2 38.4 %copy-start.34 = (bf16[1024]{0:T(1024)(128)(2,1)S(1)}, bf16[1024]{0:T(1024)(128)(2,1)}, u32[]{:S(2)}) copy-start(bf16[1024]{0:T(1024)(128)(2,1)} %param.32) | copy-start | bytes 6148
  127.2 39.0 %copy-start.35 = (bf16[1024]{0:T(1024)(128)(2,1)S(1)}, bf16[1024]{0:T(1024)(128)(2,1)}, u32[]{:S(2)}) copy-start(bf16[1024]{0:T(1024)(128)(2,1)} %param.28) | copy-start | bytes 6148
  127.2 39.6 %copy-start.36 = (bf16[1024]{0:T(1024)(128)(2,1)S(1)}, bf16[1024]{0:T(1024)(128)(2,1)}, u32[]{:S(2)}) copy-start(bf16[1024]{0:T(1024)(128)(2,1)} %param.30) | copy-start | bytes 6148
  163.7 54.2 %collective-permute-start.6 = (bf16[4096,128]{1,0:T(8,128)(2,1)}, bf16[4096,128]{1,0:T(8,128)(2,1)S(1)}, u32[]{:S(2)}, u32[]{:S(2)}) collective-permute-start(bf16[4096,128]{1,0:T(8,128)(2,1)} %get-tuple-element.73.refs_1_.refs_6_), channel_id=1, source_target_pairs={{0,2},{1,3},{2,0},{3,1},{4,6},{5,7},{6,4},{7,5},{8,10},{9,11},{10,... | collective-permute-start | bytes 3145736 | tf_op jit(solution)/shard_map/ppermute | solution.py:707
  167.4 52.8 %collective-permute-start.4 = (bf16[4096,128]{1,0:T(8,128)(2,1)S(1)}, bf16[4096,128]{1,0:T(8,128)(2,1)S(1)}, u32[]{:S(2)}, u32[]{:S(2)}) collective-permute-start(bf16[4096,128]{1,0:T(8,128)(2,1)S(1)} %copy-done.23), channel_id=1, source_target_pairs={{0,1},{1,0},{2,3},{3,2},{4,5},{5,4},{6,7},{7,6},{8,9},{9,8},{10,11... | collective-permute-start | bytes 3145736 | tf_op jit(solution)/shard_map/ppermute | solution.py:707
  170.1 53.4 %collective-permute-start.7 = (bf16[4096,128]{1,0:T(8,128)(2,1)}, bf16[4096,128]{1,0:T(8,128)(2,1)S(1)}, u32[]{:S(2)}, u32[]{:S(2)}) collective-permute-start(bf16[4096,128]{1,0:T(8,128)(2,1)} %collective-permute-done.5.refs_4_), channel_id=1, source_target_pairs={{0,1},{1,0},{2,3},{3,2},{4,5},{5,4},{6,7},{7,6},{8,9},{9,8},{10,11... | collective-permute-start | bytes 3145736 | tf_op jit(solution)/shard_map/ppermute | solution.py:707
  170.7 54.9 %copy-start.1 = (bf16[1024,1024]{1,0:T(8,128)(2,1)}, bf16[1024,1024]{1,0:T(8,128)(2,1)S(1)}, u32[]{:S(2)}) copy-start(bf16[1024,1024]{1,0:T(8,128)(2,1)S(1)} %constant_dynamic-update-slice_fusion.refs_12_.refs_6_) | copy-start | bytes 6291460
  217.9 54.6 %collective-permute-start.12 = (bf16[1024,1024]{1,0:T(8,128)(2,1)S(1)}, bf16[1024,1024]{1,0:T(8,128)(2,1)}, u32[]{:S(2)}, u32[]{:S(2)}) collective-permute-start(bf16[1024,1024]{1,0:T(8,128)(2,1)S(1)} %copy-done.11), channel_id=1, source_target_pairs={{0,1},{1,0},{2,3},{3,2},{4,5},{5,4},{6,7},{7,6},{8,9},{9,8},{10,11... | collective-permute-start | bytes 6291464 | tf_op jit(solution)/shard_map/ppermute | solution.py:707
  217.9 6.8 collective-permute-start.8
  218.5 30.4 %collective-permute-start.14 = (bf16[1024,1024]{1,0:T(8,128)(2,1)}, bf16[1024,1024]{1,0:T(8,128)(2,1)}, u32[]{:S(2)}, u32[]{:S(2)}) collective-permute-start(bf16[1024,1024]{1,0:T(8,128)(2,1)} %collective-permute-done.13.refs_1_), channel_id=1, source_target_pairs={{0,1},{1,0},{2,3},{3,2},{4,5},{5,4},{6,7},{7,6},{8,9},{9,8},{10,11... | collective-permute-start | bytes 6291464 | tf_op jit(solution)/shard_map/ppermute | solution.py:707
  272.2 49.9 %collective-permute-start.19 = (bf16[1024,1024]{1,0:T(8,128)(2,1)}, bf16[1024,1024]{1,0:T(8,128)(2,1)S(1)}, u32[]{:S(2)}, u32[]{:S(2)}) collective-permute-start(bf16[1024,1024]{1,0:T(8,128)(2,1)} %get-tuple-element.86), channel_id=1, source_target_pairs={{0,1},{1,0},{2,3},{3,2},{4,5},{5,4},{6,7},{7,6},{8,9},{9,8},{10,11... | collective-permute-start | bytes 6291464 | tf_op jit(solution)/shard_map/ppermute | solution.py:707
  295.4 15.0 %copy-start.38 = (bf16[1024,1024]{1,0:T(8,128)(2,1)S(1)}, bf16[1024,1024]{1,0:T(8,128)(2,1)}, u32[]{:S(2)}) copy-start(bf16[1024,1024]{1,0:T(8,128)(2,1)} %refs_4_.8) | copy-start | bytes 6291460
  310.3 32.4 %collective-permute-start.18 = (bf16[1024,1024]{1,0:T(8,128)(2,1)}, bf16[1024,1024]{1,0:T(8,128)(2,1)}, u32[]{:S(2)}, u32[]{:S(2)}) collective-permute-start(bf16[1024,1024]{1,0:T(8,128)(2,1)} %get-tuple-element.84), channel_id=1, source_target_pairs={{0,1},{1,0},{2,3},{3,2},{4,5},{5,4},{6,7},{7,6},{8,9},{9,8},{10,11... | collective-permute-start | bytes 6291464 | tf_op jit(solution)/shard_map/ppermute | solution.py:707
  310.5 11.6 %copy-start.7 = (bf16[1024,1024]{1,0:T(8,128)(2,1)S(1)}, bf16[1024,1024]{1,0:T(8,128)(2,1)}, u32[]{:S(2)}) copy-start(bf16[1024,1024]{1,0:T(8,128)(2,1)} %get-tuple-element.85) | copy-start | bytes 6291460
  322.0 5.9 copy-start
  324.8 48.2 %collective-permute-start.20 = (bf16[1024,1024]{1,0:T(8,128)(2,1)}, bf16[1024,1024]{1,0:T(8,128)(2,1)}, u32[]{:S(2)}, u32[]{:S(2)}) collective-permute-start(bf16[1024,1024]{1,0:T(8,128)(2,1)} %add_convert_fusion.1), channel_id=1, source_target_pairs={{0,2},{1,3},{2,0},{3,1},{4,6},{5,7},{6,4},{7,5},{8,10},{9,11},{10,... | collective-permute-start | bytes 6291464 | tf_op jit(solution)/shard_map/ppermute | solution.py:707
  327.9 372.3 %collective-permute-start.15 = (bf16[1024,1024]{1,0:T(8,128)(2,1)}, bf16[1024,1024]{1,0:T(8,128)(2,1)}, u32[]{:S(2)}, u32[]{:S(2)}) collective-permute-start(bf16[1024,1024]{1,0:T(8,128)(2,1)} %get-tuple-element.142), channel_id=1, source_target_pairs={{0,1},{1,0},{2,3},{3,2},{4,5},{5,4},{6,7},{7,6},{8,9},{9,8},{10,11... | collective-permute-start | bytes 6291464 | tf_op jit(solution)/shard_map/ppermute | solution.py:707
  328.2 57.1 %collective-permute-start.16 = (bf16[1024,1024]{1,0:T(8,128)(2,1)}, bf16[1024,1024]{1,0:T(8,128)(2,1)S(1)}, u32[]{:S(2)}, u32[]{:S(2)}) collective-permute-start(bf16[1024,1024]{1,0:T(8,128)(2,1)} %get-tuple-element.143), channel_id=1, source_target_pairs={{0,1},{1,0},{2,3},{3,2},{4,5},{5,4},{6,7},{7,6},{8,9},{9,8},{10,11... | collective-permute-start | bytes 6291464 | tf_op jit(solution)/shard_map/ppermute | solution.py:707
  342.7 357.5 %all-reduce.7.cloned.1.call-start = ((), (), s32[]{:S(2)}) async-start(), calls=%async_computation | async-start | bytes 1572864 | tf_op jit(solution)/shard_map/psum | solution.py:841
  385.2 6.0 copy-start.28
  385.2 6.6 copy-start.39
  385.2 6.0 collective-permute-start.35
  389.3 30.9 %collective-permute-start.21 = (bf16[1024,256]{1,0:T(8,128)(2,1)}, bf16[1024,256]{1,0:T(8,128)(2,1)}, u32[]{:S(2)}, u32[]{:S(2)}) collective-permute-start(bf16[1024,256]{1,0:T(8,128)(2,1)} %get-tuple-element.88), channel_id=1, source_target_pairs={{0,1},{1,0},{2,3},{3,2},{4,5},{5,4},{6,7},{7,6},{8,9},{9,8},{10,11... | collective-permute-start | bytes 1572872 | tf_op jit(solution)/shard_map/ppermute | solution.py:707
  389.7 30.6 %collective-permute-start.22 = (bf16[1024,256]{1,0:T(8,128)(2,1)S(1)}, bf16[1024,256]{1,0:T(8,128)(2,1)}, u32[]{:S(2)}, u32[]{:S(2)}) collective-permute-start(bf16[1024,256]{1,0:T(8,128)(2,1)S(1)} %copy-done.41), channel_id=1, source_target_pairs={{0,2},{1,3},{2,0},{3,1},{4,6},{5,7},{6,4},{7,5},{8,10},{9,11},{10,... | collective-permute-start | bytes 1572872 | tf_op jit(solution)/shard_map/ppermute | solution.py:707
  390.0 30.2 %collective-permute-start.23 = (bf16[1024,256]{1,0:T(8,128)(2,1)S(1)}, bf16[1024,256]{1,0:T(8,128)(2,1)}, u32[]{:S(2)}, u32[]{:S(2)}) collective-permute-start(bf16[1024,256]{1,0:T(8,128)(2,1)S(1)} %copy-done.40), channel_id=1, source_target_pairs={{0,3},{1,2},{2,1},{3,0},{4,7},{5,6},{6,5},{7,4},{8,11},{9,10},{10,... | collective-permute-start | bytes 1572872 | tf_op jit(solution)/shard_map/ppermute | solution.py:707
  391.2 24.0 %collective-permute-start.36 = (f32[4,1024]{1,0:T(4,128)S(1)}, f32[4,1024]{1,0:T(4,128)S(1)}, u32[]{:S(2)}, u32[]{:S(2)}) collective-permute-start(f32[4,1024]{1,0:T(4,128)S(1)} %slice_add_fusion), channel_id=1, source_target_pairs={{0,2},{1,3},{2,0},{3,1},{4,6},{5,7},{6,4},{7,5},{8,10},{9,11},{10,... | collective-permute-start | bytes 49160 | tf_op jit(solution)/shard_map/ppermute | solution.py:707
  395.8 94.8 %copy-start.9 = (bf16[1024,1024]{1,0:T(8,128)(2,1)}, bf16[1024,1024]{1,0:T(8,128)(2,1)S(1)}, u32[]{:S(2)}) copy-start(bf16[1024,1024]{1,0:T(8,128)(2,1)S(1)} %convolution_convert_fusion.3) | copy-start | bytes 6291460
  415.3 4.0 collective-permute-start.37
  419.3 281.7 %collective-permute-start.17 = (bf16[1024,1024]{1,0:T(8,128)(2,1)}, bf16[1024,1024]{1,0:T(8,128)(2,1)}, u32[]{:S(2)}, u32[]{:S(2)}) collective-permute-start(bf16[1024,1024]{1,0:T(8,128)(2,1)} %add_convert_fusion.3), channel_id=1, source_target_pairs={{0,2},{1,3},{2,0},{3,1},{4,6},{5,7},{6,4},{7,5},{8,10},{9,11},{10,... | collective-permute-start | bytes 6291464 | tf_op jit(solution)/shard_map/ppermute | solution.py:707
  420.3 185.4 %collective-permute-start.33 = (bf16[256,1024]{1,0:T(8,128)(2,1)}, bf16[256,1024]{1,0:T(8,128)(2,1)}, u32[]{:S(2)}, u32[]{:S(2)}) collective-permute-start(bf16[256,1024]{1,0:T(8,128)(2,1)} %get-tuple-element.145), channel_id=1, source_target_pairs={{0,1},{1,0},{2,3},{3,2},{4,5},{5,4},{6,7},{7,6},{8,9},{9,8},{10,11... | collective-permute-start | bytes 1572872 | tf_op jit(solution)/shard_map/ppermute | solution.py:707
  586.7 18.4 %collective-permute-start.27 = (f32[2,1024]{1,0:T(2,128)S(1)}, f32[2,1024]{1,0:T(2,128)S(1)}, u32[]{:S(2)}, u32[]{:S(2)}) collective-permute-start(f32[2,1024]{1,0:T(2,128)S(1)} %pad_maximum_fusion.3), channel_id=1, source_target_pairs={{0,1},{1,0},{2,3},{3,2},{4,5},{5,4},{6,7},{7,6},{8,9},{9,8},{10,11... | collective-permute-start | bytes 24584 | tf_op jit(solution)/shard_map/ppermute | solution.py:707
  595.9 9.2 %copy-start.21 = (bf16[256,1024]{1,0:T(8,128)(2,1)S(1)}, bf16[256,1024]{1,0:T(8,128)(2,1)}, u32[]{:S(2)}) copy-start(bf16[256,1024]{1,0:T(8,128)(2,1)} %get-tuple-element.144) | copy-start | bytes 1572868
  595.9 11.6 %copy-start.10 = (bf16[1024,1024]{1,0:T(8,128)(2,1)S(1)}, bf16[1024,1024]{1,0:T(8,128)(2,1)}, u32[]{:S(2)}) copy-start(bf16[1024,1024]{1,0:T(8,128)(2,1)} %copy-done.9) | copy-start | bytes 6291460
  595.9 15.3 %copy-start.22 = (f32[5,1024]{1,0:T(8,128)S(1)}, f32[5,1024]{1,0:T(8,128)}, u32[]{:S(2)}) copy-start(f32[5,1024]{1,0:T(8,128)} %add.134) | copy-start | bytes 61444
  595.9 27.6 %collective-permute-start.25 = (bf16[1024,1024]{1,0:T(8,128)(2,1)}, bf16[1024,1024]{1,0:T(8,128)(2,1)}, u32[]{:S(2)}, u32[]{:S(2)}) collective-permute-start(bf16[1024,1024]{1,0:T(8,128)(2,1)} %get-tuple-element.99), channel_id=1, source_target_pairs={{0,1},{1,0},{2,3},{3,2},{4,5},{5,4},{6,7},{7,6},{8,9},{9,8},{10,11... | collective-permute-start | bytes 6291464 | tf_op jit(solution)/shard_map/ppermute | solution.py:707
  605.0 6.1 collective-permute-start.32
  605.7 17.8 %copy-start.6 = (bf16[1024,1024]{1,0:T(8,128)(2,1)S(1)}, bf16[1024,1024]{1,0:T(8,128)(2,1)}, u32[]{:S(2)}) copy-start(bf16[1024,1024]{1,0:T(8,128)(2,1)} %get-tuple-element.98) | copy-start | bytes 6291460
  605.7 3.7 collective-permute-start.28
  609.4 12.9 %collective-permute-start.34 = (bf16[256,1024]{1,0:T(8,128)(2,1)S(1)}, bf16[256,1024]{1,0:T(8,128)(2,1)S(1)}, u32[]{:S(2)}, u32[]{:S(2)}) collective-permute-start(bf16[256,1024]{1,0:T(8,128)(2,1)S(1)} %add_convert_fusion.5), channel_id=1, source_target_pairs={{0,2},{1,3},{2,0},{3,1},{4,6},{5,7},{6,4},{7,5},{8,10},{9,11},{10,... | collective-permute-start | bytes 1572872 | tf_op jit(solution)/shard_map/ppermute | solution.py:707
  611.2 17.7 %collective-permute-start.38 = (f32[5,1024]{1,0:T(8,128)S(1)}, f32[5,1024]{1,0:T(8,128)S(1)}, u32[]{:S(2)}, u32[]{:S(2)}) collective-permute-start(f32[5,1024]{1,0:T(8,128)S(1)} %copy-done.22), channel_id=1, source_target_pairs={{0,8},{4,12},{8,0},{12,4},{16,24},{20,28},{24,16},{28,20},{1,9},{5... | collective-permute-start | bytes 61448 | tf_op jit(solution)/shard_map/ppermute | solution.py:719
  622.3 172.0 %collective-permute-start.24 = (bf16[1024,1024]{1,0:T(8,128)(2,1)}, bf16[1024,1024]{1,0:T(8,128)(2,1)}, u32[]{:S(2)}, u32[]{:S(2)}) collective-permute-start(bf16[1024,1024]{1,0:T(8,128)(2,1)} %get-tuple-element.97), channel_id=1, source_target_pairs={{0,1},{1,0},{2,3},{3,2},{4,5},{5,4},{6,7},{7,6},{8,9},{9,8},{10,11... | collective-permute-start | bytes 6291464 | tf_op jit(solution)/shard_map/ppermute | solution.py:707
  623.4 164.4 %all-reduce.9.cloned.1.call-start = ((), (), s32[]{:S(2)}) async-start(), calls=%async_computation.1 | async-start | bytes 2621440 | tf_op jit(solution)/shard_map/psum | solution.py:841
  623.5 6.9 copy-start.37
  627.4 167.0 %collective-permute-start.26 = (bf16[1024,1024]{1,0:T(8,128)(2,1)}, bf16[1024,1024]{1,0:T(8,128)(2,1)}, u32[]{:S(2)}, u32[]{:S(2)}) collective-permute-start(bf16[1024,1024]{1,0:T(8,128)(2,1)} %add_convert_fusion), channel_id=1, source_target_pairs={{0,2},{1,3},{2,0},{3,1},{4,6},{5,7},{6,4},{7,5},{8,10},{9,11},{10,... | collective-permute-start | bytes 6291464 | tf_op jit(solution)/shard_map/ppermute | solution.py:707
  628.9 3.8 collective-permute-start.29
  632.7 75.3 %collective-permute-start.39 = (f32[5,1024]{1,0:T(8,128)S(1)}, f32[5,1024]{1,0:T(8,128)S(1)}, u32[]{:S(2)}, u32[]{:S(2)}) collective-permute-start(f32[5,1024]{1,0:T(8,128)S(1)} %add.135), channel_id=1, source_target_pairs={{0,16},{4,20},{8,24},{12,28},{16,0},{20,4},{24,8},{28,12},{1,17},{... | collective-permute-start | bytes 61448 | tf_op jit(solution)/shard_map/ppermute | solution.py:719
  700.3 13.8 %copy-start.4 = (bf16[1024,1024]{1,0:T(8,128)(2,1)S(1)}, bf16[1024,1024]{1,0:T(8,128)(2,1)}, u32[]{:S(2)}) copy-start(bf16[1024,1024]{1,0:T(8,128)(2,1)} %get-tuple-element.111) | copy-start | bytes 6291460
  700.3 7.7 collective-permute-start.30
  708.1 4.9 collective-permute-start.31
  (22 other events, 58.1 us)
Sparse Core Ops, SparseCore 0:
  342.9 157.0 all-reduce.10
  623.5 76.6 all-reduce.6
  704.9 82.8 all-reduce.8

commit v4 on v3

v4 whole, which is shorter than its diff:
```python
import functools
import math

import jax
import jax.numpy as jnp
from jax import lax
from jax.experimental import pallas as pl
from jax.experimental.pallas import tpu as pltpu
from jax.sharding import PartitionSpec as P

HEADS = 16
HD = 64
SHORT = 2048
EPSILON = 1e-05
LOG2E = math.log2(math.e)
F32 = jnp.float32
BF16 = jnp.bfloat16
SMALL_COST = pl.CostEstimate(flops=1, transcendentals=0, bytes_accessed=1)
NT = (((1,), (1,)), ((), ()))
NN = (((1,), (0,)), ((), ()))
TN = (((0,), (0,)), ((), ()))


def dot(lhs, rhs, dims=NN):
    return lax.dot_general(lhs, rhs, dims, preferred_element_type=F32)


def low(array):
    return array.astype(BF16)


def norm_stats(rows):
    center = jnp.mean(rows, axis=-1, keepdims=True)
    centered = rows - center
    inverse = lax.rsqrt(jnp.mean(centered * centered, axis=-1, keepdims=True) + EPSILON)
    return centered * inverse, inverse


def norm_pull(grad, normal, inverse):
    grad_mean = jnp.mean(grad, axis=-1, keepdims=True)
    dot_mean = jnp.mean(grad * normal, axis=-1, keepdims=True)
    return inverse * (grad - grad_mean - normal * dot_mean)


def lanes(count):
    return lax.broadcasted_iota(jnp.int32, (count, 128), 1)


def places(count, first):
    return lax.broadcasted_iota(jnp.int32, (count, 128), 0) + first


def widen(head):
    return jnp.concatenate([head.astype(F32), jnp.zeros((head.shape[0], HD), F32)], axis=1)


def split3(value):
    high = low(value).astype(F32)
    middle = low(value - high).astype(F32)
    return high, middle, value - high - middle


def pick3(index, parts):
    return jnp.where(index == 0, parts[0], jnp.where(index == 1, parts[1], parts[2]))


def key_columns(head, first):
    count = head.shape[0]
    lane, place = lanes(count), places(count, first)
    coarse = ((place >> 6) << 6).astype(F32)
    fine = (place & 63).astype(F32)
    wall = jnp.where(place < SHORT, -1e30, 0.0)
    extra = jnp.where(lane < 73, -1.0, jnp.where(lane == 73, wall, 0.0))
    extra = jnp.where(lane < 67, coarse, jnp.where(lane < 70, fine, extra))
    return low(jnp.where(lane < HD, widen(head), extra))


def query_columns(head, first, slope, apart, log_total=None):
    count = head.shape[0]
    lane, place = lanes(count), places(count, first)
    extra = pick3(jnp.where(lane < 67, lane - 64, lane - 67), split3(slope))
    extra = jnp.where(lane < 70, extra, 0.0)
    if log_total is not None:
        extra = jnp.where((lane >= 70) & (lane < 73), pick3(lane - 70, split3(log_total)), extra)
    extra = jnp.where(lane == 73, jnp.where(place >= SHORT, apart, 0.0), extra)
    return low(jnp.where(lane < HD, widen(head), extra))


def ones_columns(head, count):
    lane = lanes(head.shape[0])
    return low(jnp.where(lane < HD, widen(head), jnp.where(lane < HD + count, 1.0, 0.0)))


def grad_columns(head, shift):
    lane = lanes(head.shape[0])
    extra = jnp.where(lane < 67, pick3(lane - 64, split3(shift)), 0.0)
    return low(jnp.where(lane < HD, widen(head), extra))


def each_chunk(me, slots, rows, body):
    chunk = min(rows, 512)
    for slot in range(slots):
        home = (me ^ slot) * rows

        @pl.loop(0, rows // chunk)
        def _(step):
            offset = pl.multiple_of(step * chunk, chunk)
            body(slot, pl.ds(offset, chunk), pl.ds(slot * rows + offset, chunk), home + offset)


def attend_kernel(
    me_ref, apart_ref, slope_ref, q_ref, k_ref, v_ref, o_ref, lse_ref, qa, ka, va, *, slots, pair, tile
):
    me = me_ref[0]
    total = q_ref.shape[0]
    rows = total // slots
    chunk = min(rows, 512)
    apart = apart_ref[0].astype(F32)

    def prepare(slot, inner, spot, place):
        place = pl.multiple_of(place, chunk)
        home = pl.ds(place, chunk)
        for s in range(pair):
            cols = slice(s * HD, (s + 1) * HD)
            qa[s, home, :] = query_columns(q_ref[spot, cols], place, slope_ref[s], apart)
            ka[s, home, :] = key_columns(k_ref[spot, cols], place)
            va[s, home, :] = ones_columns(v_ref[spot, cols], 1)

    each_chunk(me, slots, rows, prepare)
    causal = lax.broadcasted_iota(jnp.int32, (tile, tile), 1) <= lax.broadcasted_iota(
        jnp.int32, (tile, tile), 0
    )
    piece = min(rows, tile)

    def query_tile(index, _):
        first = pl.multiple_of(index * tile, tile)
        queries = [qa[s, pl.ds(first, tile), :] for s in range(pair)]

        def step(at, carry, diagonal):
            after = []
            for s in range(pair):
                top, mix = carry[s]
                scores = dot(queries[s], ka[s, pl.ds(at, tile), :], NT)
                if diagonal:
                    scores = jnp.where(causal, scores, -1e30)
                higher = jnp.maximum(top, jnp.max(scores, axis=1, keepdims=True))
                weights = low(jnp.exp2(scores - higher))
                mix = mix * jnp.exp2(top - higher) + dot(weights, va[s, pl.ds(at, tile), :])
                after.append((higher, mix))
            return tuple(after)

        carry = tuple(
            (jnp.full((tile, 1), -1e38, F32), jnp.zeros((tile, 128), F32)) for _ in range(pair)
        )
        carry = step(first, carry, True)
        carry = lax.fori_loop(
            0, index, lambda at, held: step(pl.multiple_of(at * tile, tile), held, False), carry
        )
        outs = []
        for s in range(pair):
            top, mix = carry[s]
            weight = mix[:, HD : HD + 1]
            outs.append(mix[:, :HD] * (1.0 / weight))
            lse_ref[s, 0, pl.ds(first, tile)] = (top + jnp.log2(weight))[:, 0]
        out = low(jnp.concatenate(outs, axis=1))
        for part in range(tile // piece):
            block = (index * (tile // piece) + part) // (rows // piece)
            offset = first + part * piece - block * rows
            spot = pl.multiple_of((block ^ me) * rows + offset, piece)
            o_ref[pl.ds(spot, piece), :] = out[part * piece : (part + 1) * piece]
        return 0

    lax.fori_loop(0, total // tile, query_tile, 0)


def attend(me, apart, slopes, queries, key_rows, values, slots, group, tile=1024):
    total, width = queries.shape
    pair = min(2, width // HD)
    cols = pair * HD
    spec = pl.BlockSpec((total, cols), lambda g: (0, group))
    scalars = pl.BlockSpec(memory_space=pltpu.SMEM)
    return pl.pallas_call(
        functools.partial(attend_kernel, slots=slots, pair=pair, tile=tile),
        grid=(1,),
        in_specs=[scalars] * 3 + [spec] * 3,
        out_specs=[
            pl.BlockSpec((total, cols), lambda g: (0, 0)),
            pl.BlockSpec((pair, 1, total), lambda g: (0, 0, 0)),
        ],
        out_shape=[
            jax.ShapeDtypeStruct((total, cols), BF16),
            jax.ShapeDtypeStruct((pair, 1, total), F32),
        ],
        scratch_shapes=[pltpu.VMEM((pair, total, 128), BF16)] * 3,
        compiler_params=pltpu.CompilerParams(vmem_limit_bytes=56 << 20),
        cost_estimate=SMALL_COST,
        name="attend",
    )(me, apart, slopes[group * pair : (group + 1) * pair], queries, key_rows, values)


def attend_back_kernel(*refs, slots, pair, tile, key_tile):
    me_ref, apart_ref, slope_ref, q_ref, k_ref, v_ref, o_ref, lse_ref = refs[:8]
    g_refs = refs[8 : 8 + slots]
    out_ref, qa, ka, va, ga, kt, dq_sum = refs[8 + slots :]
    cols = pair * HD
    me = me_ref[0]
    total = q_ref.shape[0]
    rows = total // slots
    chunk = min(rows, 512)
    apart = apart_ref[0].astype(F32)

    def prepare(slot, inner, spot, place):
        place = pl.multiple_of(place, chunk)
        home = pl.ds(place, chunk)
        for s in range(pair):
            mine = slice(s * HD, (s + 1) * HD)
            log_total = lse_ref[s, :, home].T
            qa[s, home, :] = query_columns(q_ref[spot, mine], place, slope_ref[s], apart, log_total)
            keys = key_columns(k_ref[spot, mine], place)
            ka[s, home, :] = keys
            kt[s, :, home] = low(keys.astype(F32).T)
            va[s, home, :] = ones_columns(v_ref[spot, mine], 3)
            grad = g_refs[slot][inner, mine]
            row_dot = jnp.sum(
                grad.astype(F32) * o_ref[spot, mine].astype(F32), axis=1, keepdims=True
            )
            ga[s, home, :] = grad_columns(grad, -row_dot)
            dq_sum[s, :, home] = jnp.zeros((128, chunk), F32)

    each_chunk(me, slots, rows, prepare)
    causal = lax.broadcasted_iota(jnp.int32, (key_tile, key_tile), 0) <= lax.broadcasted_iota(
        jnp.int32, (key_tile, key_tile), 1
    )
    piece = min(rows, key_tile)

    def place_of(place, size):
        block = place // rows
        return pl.multiple_of((block ^ me) * rows + (place - block * rows), size)

    def keys_tile(index, _):
        first = pl.multiple_of(index * key_tile, key_tile)
        here = pl.ds(first, key_tile)

        def step(at, carry, diagonal, width):
            after = []
            for s in range(pair):
                dk, dv = carry[s]
                there = pl.ds(at, width)
                queries, grads = qa[s, there, :], ga[s, there, :]
                probs = jnp.exp2(dot(ka[s, here, :], queries, NT))
                if diagonal:
                    probs = jnp.where(causal, probs, 0.0)
                dv = dv + dot(low(probs), grads)
                score_grad = low(probs * dot(va[s, here, :], grads, NT))
                dk = dk + dot(score_grad, queries)
                dq_sum[s, :, there] += dot(kt[s, :, here], score_grad)
                after.append((dk, dv))
            return tuple(after)

        zeros = jnp.zeros((key_tile, 128), F32)
        carry = step(first, tuple((zeros, zeros) for _ in range(pair)), True, key_tile)
        start = first + key_tile
        short = jnp.minimum((-start) % tile, total - start) // key_tile
        if tile > key_tile:
            carry = lax.fori_loop(
                0,
                short,
                lambda at, held: step(
                    pl.multiple_of(start + at * key_tile, key_tile), held, False, key_tile
                ),
                carry,
            )
            start = start + short * key_tile
        carry = lax.fori_loop(
            0,
            (total - start) // tile,
            lambda at, held: step(
                pl.multiple_of(start + at * tile, min(tile, key_tile)), held, False, tile
            ),
            carry,
        )
        dk = low(jnp.concatenate([held[0][:, :HD] * (1.0 / LOG2E) for held in carry], axis=1))
        dv = low(jnp.concatenate([held[1][:, :HD] for held in carry], axis=1))
        for part in range(key_tile // piece):
            spot = pl.ds(place_of(first + part * piece, piece), piece)
            out_ref[spot, cols : 2 * cols] = dk[part * piece : (part + 1) * piece]
            out_ref[spot, 2 * cols :] = dv[part * piece : (part + 1) * piece]
        return 0

    lax.fori_loop(0, total // key_tile, keys_tile, 0)

    def finish(slot, inner, spot, place):
        home = pl.ds(pl.multiple_of(place, chunk), chunk)
        joined = jnp.concatenate([dq_sum[s, :HD, home] for s in range(pair)], axis=0)
        out_ref[spot, :cols] = low(joined.T * HD**-0.5)

    each_chunk(me, slots, rows, finish)


def attend_back(
    me, apart, slopes, queries, key_rows, values, mixed, log_total, grads, group, tile=1024, key_tile=512
):
    slots = len(grads)
    total, width = queries.shape
    pair = min(2, width // HD)
    cols = pair * HD
    spec = pl.BlockSpec((total, cols), lambda g: (0, group))
    out_spec = pl.BlockSpec((total, cols), lambda g: (0, 0))
    scalars = pl.BlockSpec(memory_space=pltpu.SMEM)
    return pl.pallas_call(
        functools.partial(
            attend_back_kernel, slots=slots, pair=pair, tile=tile, key_tile=key_tile
        ),
        grid=(1,),
        in_specs=[scalars] * 3
        + [spec] * 3
        + [out_spec, pl.BlockSpec((pair, 1, total), lambda g: (0, 0, 0))]
        + [pl.BlockSpec((total // slots, cols), lambda g: (0, group))] * slots,
        out_specs=pl.BlockSpec((total, 3 * cols), lambda g: (0, 0)),
        out_shape=jax.ShapeDtypeStruct((total, 3 * cols), BF16),
        scratch_shapes=[pltpu.VMEM((pair, total, 128), BF16)] * 4
        + [pltpu.VMEM((pair, 128, total), BF16), pltpu.VMEM((pair, 128, total), F32)],
        compiler_params=pltpu.CompilerParams(vmem_limit_bytes=60 << 20),
        cost_estimate=SMALL_COST,
        name="attend_back",
    )(
        me,
        apart,
        slopes[group * pair : (group + 1) * pair],
        queries,
        key_rows,
        values,
        mixed,
        log_total,
        *grads,
    )


def whole(shape):
    return pl.BlockSpec(shape, lambda i: (0,) * len(shape))


def row(ref):
    return ref[...].astype(F32)[None, :]


def choose(slot, refs):
    rows = refs[0][...]
    for at, ref in enumerate(refs[1:], 1):
        rows = jnp.where(slot == at, ref[...], rows)
    return rows


def slot_specs(count, per, block, width, order=lambda i: i):
    return [
        pl.BlockSpec(
            (block, width), lambda i, at=at: (jnp.clip(order(i) - at * per, 0, per - 1), 0)
        )
        for at in range(count)
    ]


def tall_spec(chosen, per, block, width):
    return pl.BlockSpec(
        (block, width),
        lambda i: ((chosen.start + chosen.step * (i // per)) * per + i % per, 0),
    )


def kernel_call(kernel, grid, in_specs, out_specs, out_shape, inputs, held=(), **more):
    return pl.pallas_call(
        kernel,
        grid=grid,
        in_specs=in_specs + [pl.BlockSpec(memory_space=pl.ANY)] * len(held),
        out_specs=out_specs,
        out_shape=out_shape,
        input_output_aliases={len(inputs) + at: at for at in range(len(held))},
        compiler_params=pltpu.CompilerParams(vmem_limit_bytes=56 << 20),
        cost_estimate=SMALL_COST,
        **more,
    )(*inputs, *held)


def shape_of(rows, cols, kind=BF16):
    return jax.ShapeDtypeStruct((rows, cols), kind)


def project_kernel(*refs, count, per):
    x_refs = refs[:count]
    gain_ref, shift_ref, wq_ref, wk_ref, wv_ref, qb_ref, vb_ref = refs[count : count + 7]
    normed_ref, q_ref, k_ref, v_ref = refs[-4:]
    x = choose(pl.program_id(0) // per, x_refs).astype(F32)
    normed = low(norm_stats(x)[0] * row(gain_ref) + row(shift_ref))
    normed_ref[...] = normed
    q_ref[...] = low((dot(normed, wq_ref[...]) + row(qb_ref)) * (LOG2E * HD**-0.5))
    k_ref[...] = low(dot(normed, wk_ref[...]))
    v_ref[...] = low(dot(normed, wv_ref[...]) + row(vb_ref))


def project(x_parts, chosen, slots, vectors, weights, biases, held):
    rows, width = x_parts[0].shape
    block = min(rows, 512)
    per = rows // block
    widths = [width] + [weight.shape[1] for weight in weights]
    return kernel_call(
        functools.partial(project_kernel, count=len(chosen), per=per),
        (len(chosen) * per,),
        slot_specs(len(chosen), per, block, width)
        + [whole(a.shape) for a in (*vectors, *weights, *biases)],
        [tall_spec(chosen, per, block, cols) for cols in widths],
        [shape_of(slots * rows, cols) for cols in widths],
        [*x_parts, *vectors, *weights, *biases],
        held,
        name="project",
    )


def act_grad_kernel(*refs, count, per):
    down_ref, grad_ref, cot_ref = refs[count:]
    cot = choose(pl.program_id(0) // per, refs[:count])
    cot_ref[...] = cot
    grad_ref[...] = low(dot(cot, down_ref[...], NT))


def act_grad_step(cot_parts, down):
    slots = len(cot_parts)
    rows, width = cot_parts[0].shape
    block = min(rows, 1024)
    per = rows // block
    units = down.shape[0]
    return kernel_call(
        functools.partial(act_grad_kernel, count=slots, per=per),
        (slots * per,),
        slot_specs(slots, per, block, width) + [whole(down.shape)],
        [pl.BlockSpec((block, cols), lambda i: (i, 0)) for cols in (units, width)],
        [shape_of(slots * rows, cols) for cols in (units, width)],
        [*cot_parts, down],
        (),
        name="act_grad",
    )


def post_kernel(*refs, slots, groups, per):
    mixed_refs = refs[: slots * groups]
    x_refs = refs[slots * groups : slots * groups + slots]
    weight_refs = refs[slots * groups + slots : slots * groups + 2 * slots]
    bias_ref, gain_ref, shift_ref, post_ref, residual_ref = refs[-5:]
    blocks = pl.num_programs(0)
    at = (pl.program_id(0) + blocks // 2) % blocks
    residual = choose(at // per, x_refs).astype(F32) + row(bias_ref)
    for slot in range(slots):
        mixed = [ref[...] for ref in mixed_refs[slot * groups : (slot + 1) * groups]]
        residual = residual + dot(jnp.concatenate(mixed, axis=1), weight_refs[slot][...])
    normal, _ = norm_stats(residual)
    post_ref[...] = low(normal * row(gain_ref) + row(shift_ref))

    @pl.when(at < per)
    def _():
        residual_ref[...] = residual


def post_norm(mixed, x_parts, weights, bias, gain, shift):
    slots, groups = len(mixed), len(mixed[0])
    rows, width = x_parts[0].shape
    block = min(rows, 512)
    per = rows // block
    blocks = slots * per
    order = lambda i: (i + blocks // 2) % blocks
    specs = [
        pl.BlockSpec(
            (block, part.shape[1]),
            lambda i, slot=slot: (((order(i) // per) ^ slot) * per + order(i) % per, 0),
        )
        for slot in range(slots)
        for part in mixed[slot]
    ]
    return kernel_call(
        functools.partial(post_kernel, slots=slots, groups=groups, per=per),
        (blocks,),
        specs
        + slot_specs(slots, per, block, width, order)
        + [whole(a.shape) for a in (*weights, bias, gain, shift)],
        [
            pl.BlockSpec((block, width), lambda i: (order(i), 0)),
            pl.BlockSpec((block, width), lambda i: (jnp.clip(i - blocks // 2, 0, per - 1), 0)),
        ],
        [shape_of(slots * rows, width), shape_of(rows, width, F32)],
        [*[part for parts in mixed for part in parts], *x_parts, *weights, bias, gain, shift],
        (),
        name="post_norm",
    )


def feed_kernel(*refs, count, per, extras, held):
    post_ref, act_grad_ref, up_ref, bias_ref = refs[:4]
    extra_refs = refs[4 : 4 + extras]
    active_ref, grad_ref, sum_ref = refs[4 + extras + held : 7 + extras + held]
    back_refs = refs[7 + extras + held :]
    slot = pl.program_id(0) // per

    @pl.when(pl.program_id(0) == 0)
    def _():
        sum_ref[...] = jnp.zeros_like(sum_ref)

    post = post_ref[...]
    units = active_ref.shape[1]
    chunk = min(512, units)
    scale, cubic = math.sqrt(2 / math.pi), 0.044715
    for first in range(0, units, chunk):
        cols = slice(first, first + chunk)
        hidden = dot(post, up_ref[:, cols]) + row(bias_ref)[:, cols]
        square = hidden * hidden
        curve = jnp.tanh(hidden * (scale + scale * cubic * square))
        half = 0.5 + 0.5 * curve
        active_ref[:, cols] = low(hidden * half)
        slope = half + (0.5 * hidden) * (1.0 - curve * curve) * (
            scale + 3 * scale * cubic * square
        )
        grad = low(act_grad_ref[:, cols].astype(F32) * slope)
        grad_ref[:, cols] = grad
        sum_ref[:, cols] += jnp.sum(grad.astype(F32), axis=0, keepdims=True)
    back = dot(grad_ref[...], up_ref[...], NT)
    if extras:
        back = back + choose(slot, extra_refs).astype(F32)
    back = low(back)
    for at, back_ref in enumerate(back_refs):

        @pl.when(slot == at)
        def _():
            back_ref[...] = back


def feed(post_all, act_grad, up, up_bias, slots, chosen, extras, held):
    count = len(chosen)
    total, width = post_all.shape
    rows, units = total // slots, up.shape[1]
    block = min(rows, 512)
    per = rows // block
    tall = lambda cols: tall_spec(chosen, per, block, cols)
    active, grad, sums, *backs = kernel_call(
        functools.partial(
            feed_kernel, count=count, per=per, extras=len(extras), held=len(held)
        ),
        (count * per,),
        [tall(width), tall(units), whole(up.shape), whole(up_bias.shape)]
        + slot_specs(len(extras), per, block, width),
        [tall(units), tall(units), whole((1, units))] + slot_specs(count, per, block, width),
        [shape_of(total, units), shape_of(total, units), shape_of(1, units, F32)]
        + [shape_of(rows, width)] * count,
        [post_all, act_grad, up, up_bias, *extras],
        held,
        name="feed",
    )
    return (active, grad), sums, backs


def outer_kernel(left_ref, right_ref, out_ref, total):
    step = pl.program_id(0)

    @pl.when(step == 0)
    def _():
        total[...] = dot(left_ref[...], right_ref[...], TN)

    @pl.when(step > 0)
    def _():
        total[...] += dot(left_ref[...], right_ref[...], TN)

    @pl.when(step == pl.num_programs(0) - 1)
    def _():
        out_ref[...] = low(total[...])


def outer_step(left, right):
    total = left.shape[0]
    block = min(total, 1024)
    shape = (left.shape[1], right.shape[1])
    return kernel_call(
        outer_kernel,
        (total // block,),
        [pl.BlockSpec((block, cols), lambda i: (i, 0)) for cols in shape],
        [whole(shape)],
        [shape_of(*shape)],
        [left, right],
        scratch_shapes=[pltpu.VMEM(shape, F32)],
        name="outer_step",
    )[0]


def pack_kernel(*refs, groups):
    sums_ref, gain_ref, shift_ref = refs[:3]
    row_refs, count_refs = refs[3 : 3 + groups], refs[3 + groups : 3 + 2 * groups]
    unit_refs, (shared_ref, own_ref) = refs[3 + 2 * groups : -2], refs[-2:]
    shared_ref[...] = sums_ref[...]
    rows = row_refs[0][...]
    for ref in row_refs[1:]:
        rows = rows + ref[...]
    shared_ref[4:5, :] = (rows[0:1] - row(shift_ref) * rows[1:2]) / row(gain_ref)
    shared_ref[5:6, :] = rows[1:2]
    own_ref[...] = jnp.zeros_like(own_ref)
    units = unit_refs[0][...]
    for ref in unit_refs[1:]:
        units = units + ref[...]
    own_ref[0:1, : units.shape[1]] = units
    for at, ref in enumerate(count_refs):
        own_ref[1 + at : 2 + at, : ref.shape[1]] = ref[...]


def pack(row_sums, gain, shift, group_rows, group_counts, unit_sums):
    width = row_sums.shape[1]
    inputs = [row_sums, gain, shift, *group_rows, *group_counts, *unit_sums]
    wide = max(a.shape[1] for a in (*group_counts, *unit_sums))
    return kernel_call(
        functools.partial(pack_kernel, groups=len(group_rows)),
        (1,),
        [whole(a.shape) for a in inputs],
        [whole((8, width)), whole((8, wide))],
        [shape_of(8, width, F32), shape_of(8, wide, F32)],
        inputs,
        name="pack",
    )


def resid_kernel(*refs, terms, slots):
    term_refs = refs[:terms]
    residual_ref, cot_ref, gain_ref = refs[terms : terms + 3]
    weight_refs = refs[terms + 3 : terms + 3 + slots]
    grad_ref, low_ref, sums_ref = refs[terms + 3 + slots : terms + 6 + slots]
    part_refs = refs[terms + 6 + slots :]

    @pl.when(pl.program_id(0) == 0)
    def _():
        sums_ref[...] = jnp.zeros_like(sums_ref)

    post_grad = term_refs[0][...].astype(F32)
    for ref in term_refs[1:]:
        post_grad = post_grad + ref[...].astype(F32)
    cot = cot_ref[...].astype(F32)
    normal, inverse = norm_stats(residual_ref[...])
    grad = cot + norm_pull(post_grad * row(gain_ref), normal, inverse)
    grad_ref[...] = grad
    grad_low = low(grad)
    low_ref[...] = grad_low
    for weight_ref, part_ref in zip(weight_refs, part_refs):
        part_ref[...] = low(dot(grad_low, weight_ref[...], NT))
    for at, value in enumerate((cot, grad, post_grad * normal, post_grad)):
        sums_ref[at : at + 1, :] += jnp.sum(value, axis=0, keepdims=True)


def resid_step(terms, residual, cotangent, gain, weights):
    rows, width = residual.shape
    block = min(rows, 256)
    tall = lambda cols: pl.BlockSpec((block, cols), lambda i: (i, 0))
    cols = weights[0].shape[0]
    return kernel_call(
        functools.partial(resid_kernel, terms=len(terms), slots=len(weights)),
        (rows // block,),
        [tall(width)] * (len(terms) + 2) + [whole(a.shape) for a in (gain, *weights)],
        [tall(width), tall(width), whole((8, width))] + [tall(cols)] * len(weights),
        [shape_of(rows, width, F32), shape_of(rows, width), shape_of(8, width, F32)]
        + [shape_of(rows, cols)] * len(weights),
        [*terms, residual, cotangent, gain, *weights],
        (),
        name="resid_step",
    )


def dense_grad_kernel(*refs, slots, groups):
    mixed_refs, grad_ref = refs[: slots * groups], refs[slots * groups]
    out_refs, sum_refs = refs[slots * groups + 1 :][:slots], refs[slots * groups + 1 :][slots:]
    step = pl.program_id(0)
    grad = grad_ref[...]
    for slot in range(slots):
        mixed = [ref[...] for ref in mixed_refs[slot * groups : (slot + 1) * groups]]
        part = dot(jnp.concatenate(mixed, axis=1), grad, TN)
        sum_refs[slot][...] = jnp.where(step == 0, 0.0, sum_refs[slot][...]) + part

    @pl.when(step == pl.num_programs(0) - 1)
    def _():
        for out_ref, sum_ref in zip(out_refs, sum_refs):
            out_ref[...] = low(sum_ref[...])


def dense_grad(mixed, grad):
    slots, groups = len(mixed), len(mixed[0])
    rows, width = grad.shape
    block = min(rows, 512)
    per = rows // block
    cols = sum(part.shape[1] for part in mixed[0])
    return kernel_call(
        functools.partial(dense_grad_kernel, slots=slots, groups=groups),
        (per,),
        [
            pl.BlockSpec((block, part.shape[1]), lambda i, slot=slot: (slot * per + i, 0))
            for slot in range(slots)
            for part in mixed[slot]
        ]
        + [pl.BlockSpec((block, width), lambda i: (i, 0))],
        [whole((cols, width))] * slots,
        [shape_of(cols, width)] * slots,
        [*[part for parts in mixed for part in parts], grad],
        (),
        scratch_shapes=[pltpu.VMEM((cols, width), F32)] * slots,
        name="dense_grad",
    )


def weight_kernel(normed_ref, grad_ref, wq_ref, wk_ref, wv_ref, out_ref, sums_ref, count_ref, total, count):
    step = pl.program_id(0)

    @pl.when(step == 0)
    def _():
        total[...] = jnp.zeros_like(total)
        count[...] = jnp.zeros_like(count)

    grad = grad_ref[...]
    total[...] += dot(normed_ref[...], grad, TN)
    count[...] += jnp.sum(grad.astype(F32), axis=0, keepdims=True)

    @pl.when(step == pl.num_programs(0) - 1)
    def _():
        weight = jnp.concatenate([wq_ref[...], wk_ref[...], wv_ref[...]], axis=1).astype(F32)
        out_ref[...] = low(total[...])
        count_ref[...] = count[...]
        lane = lanes(weight.shape[0])
        cross = jnp.sum(weight * total[...], axis=1, keepdims=True)
        plain = jnp.sum(weight * count[...], axis=1, keepdims=True)
        both = jnp.where(lane == 0, cross, jnp.where(lane == 1, plain, 0.0))
        sums_ref[...] = both.T[:8]


def weight_step(normed, grad, weights, group):
    total, width = normed.shape
    cols = grad.shape[1]
    block = min(total, 1024)
    return kernel_call(
        weight_kernel,
        (total // block,),
        [pl.BlockSpec((block, count), lambda i: (i, 0)) for count in (width, cols)]
        + [pl.BlockSpec((width, cols // 3), lambda i: (0, group))] * 3,
        [whole((width, cols)), whole((8, width)), whole((1, cols))],
        [shape_of(width, cols), shape_of(8, width, F32), shape_of(1, cols, F32)],
        [normed, grad, *weights],
        (),
        scratch_shapes=[pltpu.VMEM((width, cols), F32), pltpu.VMEM((1, cols), F32)],
        name="weight_step",
    )


def unproject_kernel(*refs, groups, per, extras):
    grad_refs, weight_refs = refs[:groups], refs[groups : 4 * groups]
    extra_refs = refs[4 * groups : 4 * groups + extras]
    out_refs = refs[4 * groups + extras : -1]
    joined = refs[-1]
    slot = pl.program_id(0) // per

    @pl.when(pl.program_id(0) == 0)
    def _():
        joined[...] = jnp.concatenate([ref[...] for ref in weight_refs], axis=1)

    total = dot(jnp.concatenate([ref[...] for ref in grad_refs], axis=1), joined[...], NT)
    if extras:
        total = total + choose(slot, extra_refs).astype(F32)
    total = low(total)
    for at, ref in enumerate(out_refs):

        @pl.when(slot == at)
        def _():
            ref[...] = total


def unproject(grads, weights, slots, chosen, extras):
    width = weights[0].shape[0]
    count, groups = len(chosen), len(grads)
    total, cols = grads[0].shape
    rows = total // slots
    block = min(rows, 512)
    per = rows // block
    return kernel_call(
        functools.partial(unproject_kernel, groups=groups, per=per, extras=len(extras)),
        (count * per,),
        [tall_spec(chosen, per, block, cols)] * groups
        + [
            pl.BlockSpec((width, cols // 3), lambda i, group=group: (0, group))
            for group in range(groups)
            for _ in weights
        ]
        + slot_specs(len(extras), per, block, width),
        slot_specs(count, per, block, width),
        [shape_of(rows, width)] * count,
        [*grads, *[weight for _ in grads for weight in weights], *extras],
        (),
        scratch_shapes=[pltpu.VMEM((width, cols * groups), BF16)],
        name="unproject",
    )


def ffn_kernel(*refs, per, extras):
    active_ref, weight_ref = refs[:2]
    slot = pl.program_id(0) // per
    total = dot(active_ref[...], weight_ref[...])
    if extras:
        total = total + choose(slot, refs[2 : 2 + extras]).astype(F32)
    total = low(total)
    for at, ref in enumerate(refs[2 + extras :]):

        @pl.when(slot == at)
        def _():
            ref[...] = total


def ffn_step(active, weight, slots, chosen, extras):
    total, units = active.shape
    width = weight.shape[1]
    rows = total // slots
    block = min(rows, 1024)
    per = rows // block
    count = len(chosen)
    return kernel_call(
        functools.partial(ffn_kernel, per=per, extras=len(extras)),
        (count * per,),
        [tall_spec(chosen, per, block, units), whole(weight.shape)]
        + slot_specs(len(extras), per, block, width),
        slot_specs(count, per, block, width),
        [shape_of(rows, width)] * count,
        [active, weight, *extras],
        name="ffn_step",
    )


def spread_kernel(*refs, groups):
    cols = refs[0].shape[1] // 3
    for kind in range(3):
        for group in range(groups):
            refs[groups + kind][:, group * cols : (group + 1) * cols] = refs[group][
                :, kind * cols : (kind + 1) * cols
            ].astype(F32)


def spread(group_sums):
    width, cols = group_sums[0].shape
    groups = len(group_sums)
    block = min(width, 256)
    return kernel_call(
        functools.partial(spread_kernel, groups=groups),
        (width // block,),
        [pl.BlockSpec((block, cols), lambda i: (i, 0))] * groups,
        [pl.BlockSpec((block, cols // 3 * groups), lambda i: (i, 0))] * 3,
        [shape_of(width, cols // 3 * groups, F32)] * 3,
        list(group_sums),
        name="spread",
    )


def input_kernel(*refs, terms):
    x_ref, resid_ref, gain_ref, out_ref = refs[terms:]
    grad = refs[0][...].astype(F32)
    for ref in refs[1:terms]:
        grad = grad + ref[...].astype(F32)
    normal, inverse = norm_stats(x_ref[...].astype(F32))
    out_ref[...] = resid_ref[...] + norm_pull(grad * row(gain_ref), normal, inverse)


def input_step(terms, layer_input, resid_grad, gain):
    rows, width = resid_grad.shape
    block = min(rows, 256)
    tall = pl.BlockSpec((block, width), lambda i: (i, 0))
    return kernel_call(
        functools.partial(input_kernel, terms=len(terms)),
        (rows // block,),
        [tall] * (len(terms) + 2) + [whole(gain.shape)],
        [tall],
        [shape_of(rows, width, F32)],
        [*terms, layer_input, resid_grad, gain],
        name="input_step",
    )[0]


def shards(
    slots,
    streams,
    layer_input,
    row_ids,
    input_gain,
    input_shift,
    query_weight,
    query_bias,
    key_weight,
    value_weight,
    value_bias,
    dense_weight,
    dense_bias,
    post_gain,
    post_shift,
    up_weight,
    up_bias,
    down_weight,
    down_bias,
    cotangent,
):
    me = lax.axis_index("tensor")
    me_word = me.astype(jnp.int32)[None]
    rows = layer_input.shape[0]
    head_cols = query_weight.shape[1]
    head_count = head_cols // HD
    groups = max(1, head_count // 2)
    bits = [1 << level for level in range(slots.bit_length() - 1)]
    half = slots // 2
    after = lambda array, *others: lax.optimization_barrier((array, *others))[0]

    def swap(array, mask):
        return lax.ppermute(array, "tensor", [(i, i ^ mask) for i in range(slots)])

    def gather(array):
        held = {0: array}
        for bit in reversed(bits):
            held.update({slot ^ bit: swap(part, bit) for slot, part in held.items()})
        return [held[slot] for slot in range(slots)]

    def blocks(array):
        return [array[slot * rows : (slot + 1) * rows] for slot in range(slots)]

    def swap_data(array, mask):
        return lax.ppermute(array, "dp", [(i, i ^ mask) for i in range(streams)])

    def finish_terms(held, terms, levels):
        for bit in levels:
            come = {slot ^ bit: swap(part, bit) for slot, part in held.items() if slot & bit}
            if 0 in come:
                terms.append(come.pop(0))
            held = {
                slot: low(held[slot].astype(F32) + part.astype(F32)) for slot, part in come.items()
            }
        return terms

    def scatter_terms(parts):
        return finish_terms(dict(enumerate(parts)), [parts[0]], bits)

    far_odd = range(half + 1, slots, 2)
    far_even = range(half, slots, 2)
    near_odd = range(1, half, 2)
    near_even = range(0, half, 2)

    def ordered_terms(make):
        far = make(far_odd, (), None)
        far_come = [swap(part, 1) for part in far]
        near = make(near_odd, (), far[-1])
        near_come = [swap(part, 1) for part in near]
        far = make(far_even, far_come, near[-1])
        near = make(near_even, near_come, far[-1])
        held = dict(zip((*far_even, *near_even), (*far, *near)))
        return finish_terms(held, [held.pop(0)], bits[1:])

    def add_up(terms):
        return functools.reduce(
            lambda sum_now, term: sum_now + term.astype(F32), terms[1:], terms[0].astype(F32)
        )

    def total_of(shared, own):
        for bit in bits:
            shared = shared + swap(shared, bit)
        for level in range(streams.bit_length() - 1):
            shared = shared + swap_data(shared, 1 << level)
            own = own + swap_data(own, 1 << level)
        return shared, own

    norm_vectors = (input_gain, input_shift)
    weights = (query_weight, key_weight, value_weight)
    biases = (query_bias, value_bias)
    x_held = {0: layer_input}
    for bit in reversed(bits[1:]):
        x_held.update({slot ^ bit: swap(part, bit) for slot, part in x_held.items()})
    x_held[1] = swap(x_held[0], 1)
    near_parts = [x_held[0], x_held[1]]
    first = range(2)
    held = project(near_parts, first, slots, norm_vectors, weights, biases, ())
    rest = sorted(slot for slot in x_held if slot > 1)
    *arrived, normed = lax.optimization_barrier((*[x_held[slot] for slot in rest], held[0]))
    held = (normed, *held[1:])
    for slot, part in zip(rest, arrived):
        x_held[slot], x_held[slot ^ 1] = part, swap(part, 1)
    x_parts = [x_held[slot] for slot in range(slots)]
    dense_parts = gather(after(dense_weight, arrived[-1]))
    cot_own = after(cotangent, arrived[-1])
    cot_parts = gather(cot_own)
    normed, queries, key_rows, values = project(
        x_parts[2:], range(2, slots), slots, norm_vectors, weights, biases, held
    )

    heads = me * head_count + jnp.arange(head_count)
    slopes = jnp.exp2(-8.0 * (heads + 1).astype(F32) / HEADS) * LOG2E
    apart = (row_ids[:1] != row_ids[SHORT : SHORT + 1]).astype(jnp.int32)

    mixed_own, log_totals, mixed_parts = [], [], []
    for group in range(groups):
        mixed, log_total = attend(
            me_word,
            apart,
            slopes,
            queries if not group else after(queries, cot_parts[half], dense_parts[half], mixed_own[-1]),
            key_rows,
            values,
            slots,
            group,
        )
        mixed_own.append(mixed)
        log_totals.append(log_total)
        if group < groups - 1:
            mixed_parts.append(gather(mixed))
    act_grad, cot_all = act_grad_step(
        lax.optimization_barrier((*cot_parts, mixed_own[-1]))[:-1], down_weight
    )
    came = {0: mixed_own[-1]}
    for bit in reversed(bits[1:]):
        came.update({slot ^ bit: swap(part, bit) for slot, part in came.items()})
    far_slots = sorted(came)[1:]
    *arrived, act_grad = lax.optimization_barrier((*[came[slot] for slot in far_slots], act_grad))
    came.update(zip(far_slots, arrived))
    came.update({slot ^ 1: swap(part, 1) for slot, part in came.items()})
    mixed_parts.append([came[slot] for slot in range(slots)])
    mixed_all = [[mixed_parts[group][slot] for group in range(groups)] for slot in range(slots)]
    post_all, residual = post_norm(
        mixed_all, x_parts, dense_parts, dense_bias, post_gain, post_shift
    )

    fed, up_bias_parts = [()], []

    def make_feed(chosen, extras, gate):
        held, sums, backs = feed(
            post_all, act_grad, up_weight, up_bias, slots, chosen, extras, fed[-1]
        )
        fed.append(held)
        up_bias_parts.append(sums)
        return backs

    post_terms = ordered_terms(make_feed)
    active, hidden_grad = fed[-1]
    up_part = outer_step(post_all, hidden_grad)
    down_part = outer_step(active, after(cot_all, up_part))
    resid_grad, attended_grad, row_sums, *mixed_grads = resid_step(
        [after(post_terms[0], down_part), *post_terms[1:]],
        residual,
        cotangent,
        post_gain,
        dense_parts,
    )
    up_sum, down_sum = lax.psum((up_part, down_part), "dp")
    mixed_grads = [swap(part, slot) if slot else part for slot, part in enumerate(mixed_grads)]
    dense_grads = dense_grad(mixed_all, attended_grad)
    ffn_parts = ffn_step(after(active, dense_grads[-1]), down_weight, slots, range(slots), ())
    *mixed_grads, dense_last, ffn_last = lax.optimization_barrier(
        (*mixed_grads, dense_grads[-1], ffn_parts[-1])
    )
    dense_grads = [*dense_grads[:-1], dense_last]
    dense_terms = [swap(part, slot) if slot else part for slot, part in enumerate(dense_grads)]
    ffn_parts = [*ffn_parts[:-1], ffn_last]
    ffn_come = [swap(part, 1) for part in ffn_parts[1::2]]
    ffn_held = dict(zip(range(0, slots, 2), [
        low(part.astype(F32) + come.astype(F32))
        for part, come in zip(ffn_parts[::2], ffn_come)
    ]))
    ffn_first = ffn_held.pop(0)

    cols = head_cols // groups
    head_grads, group_sums, group_rows, group_counts = [], [], [], []
    for group in range(groups):
        head_grads.append(
            attend_back(
                me_word,
                apart,
                slopes,
                queries,
                key_rows,
                values,
                mixed_own[group],
                log_totals[group],
                mixed_grads,
                group,
            )
        )
        grad = head_grads[-1]
        if not group:
            keys = sorted(ffn_held)
            grad, *parts = lax.optimization_barrier((grad, *[ffn_held[key] for key in keys]))
            ffn_terms = finish_terms(dict(zip(keys, parts)), [ffn_first], bits[1:])
        if group == groups - 1:
            waited = (*ffn_terms, *([group_sums[0], dense_sum] if group else []))
            grad, *waited = lax.optimization_barrier((grad, *waited))
            ffn_terms = waited[: len(ffn_terms)]
            if group:
                group_sums[0], dense_sum = waited[len(ffn_terms) :]
        part, row_part, count_part = weight_step(normed, grad, weights, group)
        group_rows.append(row_part)
        group_counts.append(count_part)
        if not group:
            dense_part = low(add_up(dense_terms))
            part, dense_part, up_sum, down_sum = lax.optimization_barrier(
                (part, dense_part, up_sum, down_sum)
            )
            sums = lax.psum((part, dense_part), "dp")
            dense_sum = sums[1]
            *mixed_grads, _ = lax.optimization_barrier((*mixed_grads, part))
        else:
            sums = lax.psum((part,), "dp")
        group_sums.append(sums[0])
    last = after(head_grads[-1], part)
    normed_terms = ordered_terms(
        lambda chosen, extras, gate: unproject(
            [*head_grads[:-1], last if gate is None else after(last, gate)],
            weights,
            slots,
            chosen,
            extras,
        )
    )
    shared, own = total_of(
        *pack(row_sums, input_gain, input_shift, group_rows, group_counts, up_bias_parts)
    )
    up_bias_grad = own[0, : up_bias.shape[0]]
    counts = own[1 : 1 + groups]
    query_bias_grad = counts[:, :cols].reshape(-1)
    value_bias_grad = counts[:, 2 * cols : 3 * cols].reshape(-1)
    layer_output = low(residual + add_up(ffn_terms) + down_bias.astype(F32))
    weight_grads = spread(group_sums)
    input_grad = input_step(normed_terms, layer_input, resid_grad, input_gain)
    return (
        layer_output,
        input_grad,
        shared[4],
        shared[5],
        weight_grads[0],
        query_bias_grad,
        weight_grads[1],
        weight_grads[2],
        value_bias_grad,
        dense_sum.astype(F32),
        shared[1],
        shared[2],
        shared[3],
        up_sum.astype(F32),
        up_bias_grad,
        down_sum.astype(F32),
        shared[0],
    )


def solution(mesh):
    in_specs = (
        P(("dp", "tensor"), None),
        P("dp"),
        P(),
        P(),
        P(None, "tensor"),
        P("tensor"),
        P(None, "tensor"),
        P(None, "tensor"),
        P("tensor"),
        P("tensor", None),
        P(),
        P(),
        P(),
        P(None, "tensor"),
        P("tensor"),
        P("tensor", None),
        P(),
        P(("dp", "tensor"), None),
    )
    out_specs = (
        P(("dp", "tensor"), None),
        P(("dp", "tensor"), None),
        P(),
        P(),
        P(None, "tensor"),
        P("tensor"),
        P(None, "tensor"),
        P(None, "tensor"),
        P("tensor"),
        P("tensor", None),
        P(),
        P(),
        P(),
        P(None, "tensor"),
        P("tensor"),
        P("tensor", None),
        P(),
    )
    return jax.shard_map(
        functools.partial(shards, mesh.shape["tensor"], mesh.shape["dp"]), mesh=mesh, in_specs=in_specs, out_specs=out_specs, check_vma=False)
```

time: 819 us -> 760 us (0.928)
  Pallas kernels: 338 us -> 431 us
  matrix products: 60.4 us -> 0 us
  waiting for transfers between devices: 293 us -> 236 us
  local copies, waits for them, and re-layouts: 40.4 us -> 14.3 us
  other arithmetic: 32 us -> 23.5 us
    pallas_call x9 -> x22, Pallas kernels: 125 us -> 218 us  [kernel_call(): pl.pallas_call(kernel, grid=grid, in_specs=in_specs + [pl.BlockSpec(memor...]
    psum x2, waiting for transfers between devices: 133 us -> 69.8 us  [the longest x1 57.4 us: shards(): sums = lax.psum((part,), 'dp')]
    dot_general x6 -> x0, matrix products: 60.4 us -> none  [dot(): return lax.dot_general(lhs, rhs, dims, preferred_element_type=F32)]
    psum x1, waiting for transfers between devices: 0.01 us -> 23.2 us  [shards(): up_sum, down_sum = lax.psum((up_part, down_part), 'dp')]
    ppermute x34 -> x32, waiting for transfers between devices: 153 us -> 138 us  [swap(): return lax.ppermute(array, 'tensor', [(i, i ^ mask) for i in range(slots)])]
    slice x11 -> x2, local copies, waits for them, and re-layouts: 12 us -> 1.22 us  [the longest x1 0.62 us: shards(): shared[0]]
    convert_element_type x6 -> x4, other arithmetic: 19.9 us -> 15.9 us  [low(): return array.astype(BF16)]
    ppermute x34 -> x32, starting transfers between devices: 19.3 us -> 21.6 us  [swap(): return lax.ppermute(array, 'tensor', [(i, i ^ mask) for i in range(slots)])]
  transfers between devices with their start and end apart: 43 -> 41, of which waited for: 12 -> 13; matrix products, arithmetic and copies ran while one was open for 16% -> 4% of each run, Pallas kernels for 41% -> 50%
where the time goes in v4:
time: 760 us; the launch traced here: 751 us
  Pallas kernels  431 us (57%)
  waiting for transfers between devices  236 us (31%)
  starting transfers between devices  30.2 us (4%)
  other arithmetic  23.5 us (3%)
  between operations  15.8 us (2%)
  local copies, waits for them, and re-layouts  14.3 us (2%)
    pallas_call x22, Pallas kernels, kernel_call(): pl.pallas_call(kernel, grid=grid, in_specs=in_specs + [pl.BlockSpec(memor...  218 us
    pallas_call x2, Pallas kernels, attend_back(): pl.pallas_call(functools.partial(attend_back_kernel, slots=slots, pair=pa...  140 us
    ppermute x32, waiting for transfers between devices, swap(): return lax.ppermute(array, 'tensor', [(i, i ^ mask) for i in range(slots)])  138 us
    pallas_call x2, Pallas kernels, attend(): pl.pallas_call(functools.partial(attend_kernel, slots=slots, pair=pair, t...  72.9 us
    psum x1, waiting for transfers between devices, shards(): sums = lax.psum((part,), 'dp')  57.4 us
    psum x1, waiting for transfers between devices, shards(): up_sum, down_sum = lax.psum((up_part, down_part), 'dp')  23.2 us
    ppermute x32, starting transfers between devices, swap(): return lax.ppermute(array, 'tensor', [(i, i ^ mask) for i in range(slots)])  21.6 us
    convert_element_type x4, other arithmetic, low(): return array.astype(BF16)  15.9 us
  transfers between devices with their start and end apart: 41, of which 13 were waited for; matrix products, arithmetic and copies ran while one was open for 4% of the time, Pallas kernels for 50%

profile of v4, /device:TPU:0, one launch (start us, length us, event | category | flops | bytes accessed | tf_op | source)
XLA Modules:
  0.0 750.6 jit_solution(15089108280757355333)
XLA Ops:
  7.8 2.6 collective-permute-start
  10.4 1.4 collective-permute-done.1.refs_1_.refs_9_
  11.8 1.3 copy-done.2
  13.1 9.2 %project.2 = (bf16[4096,1024]{1,0:T(8,128)(2,1)}, bf16[4096,256]{1,0:T(8,128)(2,1)}, bf16[4096,256]{1,0:T(8,128)(2,1)}, bf16[4096,256]{1,0:T(8,128)(2,1)}) custom-call(bf16[1024,1024]{1,0:T(8,128)(2,1)} %refs_2_.22, bf16[1024,1024]{1,0:T(8,128)(2,1)} %copy-done.2, bf16[1024]{0:T(1024)(128)(2,1)} %refs_1_.3, bf16[1024]{0:T(1024)(128)(2,1)} %refs_2_.23, ...), custom_call_target="tpu_custom_call" | custom-call | flops 1 | bytes 1 | tf_op jit(solution)/shard_map/project/pallas_call | solution.py:371
  22.3 34.6 %collective-permute-done.refs_0_.refs_10_ = bf16[1024,1024]{1,0:T(8,128)(2,1)} collective-permute-done((bf16[1024,1024]{1,0:T(8,128)(2,1)}, bf16[1024,1024]{1,0:T(8,128)(2,1)}, u32[]{:S(2)}, u32[]{:S(2)}) %collective-permute-start) | collective-permute-done | bytes 2097184 | tf_op jit(solution)/shard_map/ppermute | solution.py:911
  56.9 1.8 collective-permute-start.3
  59.2 45.2 %collective-permute-done.3.refs_2_ = bf16[1024,1024]{1,0:T(8,128)(2,1)} collective-permute-done((bf16[1024,1024]{1,0:T(8,128)(2,1)S(1)}, bf16[1024,1024]{1,0:T(8,128)(2,1)}, u32[]{:S(2)}, u32[]{:S(2)}) %collective-permute-start.3) | collective-permute-done | bytes 2097184 | tf_op jit(solution)/shard_map/ppermute | solution.py:911
  104.4 1.6 collective-permute-start.4
  109.1 9.3 %project.3 = (bf16[4096,1024]{1,0:T(8,128)(2,1)}, bf16[4096,256]{1,0:T(8,128)(2,1)}, bf16[4096,256]{1,0:T(8,128)(2,1)}, bf16[4096,256]{1,0:T(8,128)(2,1)}) custom-call(bf16[1024,1024]{1,0:T(8,128)(2,1)} %collective-permute-done.refs_0_.refs_10_, ...), custom_call_target="tpu_custom_call", output_to_operand_aliasing={{0}: (9, {}), {1}: (10, {}), {2}: (11, {}), {3}: (12, {})} | custom-call | flops 1 | bytes 1 | tf_op jit(solution)/shard_map/project/pallas_call | solution.py:371
  118.4 36.2 %attend.2 = (bf16[4096,128]{1,0:T(8,128)(2,1)}, f32[2,1,4096]{2,1,0:T(1,128)}) custom-call(s32[1]{0:T(128)} %bitcast.me_ref.refs_0_, s32[1]{0:T(128)S(6)} %convert_element_type.60.apart_ref.refs_1_, f32[2]{0:T(128)} %get-tuple-element.226.slope_ref.refs_2_, bf16[4096,256]{1,0:T(8,128)(2,1)} %get-tuple-element.126.q_ref.refs_3_, ...), custom_call_target="tpu_custom_call" | custom-call | flops 1 | bytes 1 | tf_op jit(solution)/shard_map/attend/pallas_call | solution.py:182
  155.0 36.7 %attend.3 = (bf16[4096,128]{1,0:T(8,128)(2,1)}, f32[2,1,4096]{2,1,0:T(1,128)}) custom-call(s32[1]{0:T(128)} %bitcast.me_ref.refs_0_, s32[1]{0:T(128)S(6)} %convert_element_type.60.apart_ref.refs_1_, f32[2]{0:T(128)} %get-tuple-element.225.slope_ref.refs_2_, bf16[4096,256]{1,0:T(8,128)(2,1)} %get-tuple-element.126.q_ref.refs_3_, ...), custom_call_target="tpu_custom_call" | custom-call | flops 1 | bytes 1 | tf_op jit(solution)/shard_map/attend/pallas_call | solution.py:182
  191.7 1.6 collective-permute-start.8
  194.4 15.3 %act_grad.1 = (bf16[4096,1024]{1,0:T(8,128)(2,1)}, bf16[4096,1024]{1,0:T(8,128)(2,1)}) custom-call(bf16[1024,1024]{1,0:T(8,128)(2,1)} %refs_3_.17, bf16[1024,1024]{1,0:T(8,128)(2,1)} %collective-permute-done.9.refs_1_, bf16[1024,1024]{1,0:T(8,128)(2,1)} %collective-permute-done.3.refs_2_, bf16[1024,1024]{1,0:T(8,128)(2,1)} %collective-permute-done.10.refs_3_, ...), custom_call_target="tpu_custom_call" | custom-call | flops 1 | bytes 1 | tf_op jit(solution)/shard_map/act_grad/pallas_call | solution.py:371
  209.6 7.3 collective-permute-done.8.refs_5_
  217.5 3.1 collective-permute-done.14.refs_15_.refs_8_
  223.4 22.8 %post_norm.1 = (bf16[4096,1024]{1,0:T(8,128)(2,1)}, f32[1024,1024]{1,0:T(8,128)}) custom-call(bf16[4096,128]{1,0:T(8,128)(2,1)} %get-tuple-element.123.refs_0_.refs_6_, bf16[4096,128]{1,0:T(8,128)(2,1)} %get-tuple-element.127.refs_1_.refs_6_, bf16[4096,128]{1,0:T(8,128)(2,1)} %copy-done.5, bf16[4096,128]{1,0:T(8,128)(2,1)} %copy-done.6, ...), custom_call_target="tpu_custom_call" | custom-call | flops 1 | bytes 1 | tf_op jit(solution)/shard_map/post_norm/pallas_call | solution.py:371
  246.2 11.7 %feed.4 = (bf16[4096,1024]{1,0:T(8,128)(2,1)}, bf16[4096,1024]{1,0:T(8,128)(2,1)}, f32[1,1024]{1,0:T(1,128)}, bf16[1024,1024]{1,0:T(8,128)(2,1)}) custom-call(bf16[4096,1024]{1,0:T(8,128)(2,1)} %get-tuple-element.136.refs_0_.left_ref, bf16[4096,1024]{1,0:T(8,128)(2,1)} %get-tuple-element.137.refs_1_, bf16[1024,1024]{1,0:T(8,128)(2,1)} %refs_2_.17, ...), custom_call_target="tpu_custom_call" | custom-call | flops 1 | bytes 1 | tf_op jit(solution)/shard_map/feed/pallas_call | solution.py:371
  258.0 11.6 %feed.5 = (bf16[4096,1024]{1,0:T(8,128)(2,1)}, bf16[4096,1024]{1,0:T(8,128)(2,1)}, f32[1,1024]{1,0:T(1,128)}, bf16[1024,1024]{1,0:T(8,128)(2,1)}) custom-call(bf16[4096,1024]{1,0:T(8,128)(2,1)} %get-tuple-element.136.refs_0_.left_ref, bf16[4096,1024]{1,0:T(8,128)(2,1)} %get-tuple-element.137.refs_1_, ...), custom_call_target="tpu_custom_call", output_to_operand_aliasing={{0}: (4, {}), {1}: (5, {})} | custom-call | flops 1 | bytes 1 | tf_op jit(solution)/shard_map/feed/pallas_call | solution.py:371
  270.0 1.3 copy-done.13
  271.3 12.6 %feed.6 = (bf16[4096,1024]{1,0:T(8,128)(2,1)}, bf16[4096,1024]{1,0:T(8,128)(2,1)}, f32[1,1024]{1,0:T(1,128)}, bf16[1024,1024]{1,0:T(8,128)(2,1)}) custom-call(bf16[4096,1024]{1,0:T(8,128)(2,1)} %get-tuple-element.136.refs_0_.left_ref, bf16[4096,1024]{1,0:T(8,128)(2,1)} %get-tuple-element.137.refs_1_, ...), custom_call_target="tpu_custom_call", output_to_operand_aliasing={{0}: (5, {}), {1}: (6, {})} | custom-call | flops 1 | bytes 1 | tf_op jit(solution)/shard_map/feed/pallas_call | solution.py:371
  283.9 1.6 collective-permute-start.17
  285.5 1.3 copy-done.12
  286.8 12.8 %feed.7 = (bf16[4096,1024]{1,0:T(8,128)(2,1)}, bf16[4096,1024]{1,0:T(8,128)(2,1)}, f32[1,1024]{1,0:T(1,128)}, bf16[1024,1024]{1,0:T(8,128)(2,1)}) custom-call(bf16[4096,1024]{1,0:T(8,128)(2,1)} %get-tuple-element.136.refs_0_.left_ref, bf16[4096,1024]{1,0:T(8,128)(2,1)} %get-tuple-element.137.refs_1_, ...), custom_call_target="tpu_custom_call", output_to_operand_aliasing={{0}: (5, {}), {1}: (6, {})} | custom-call | flops 1 | bytes 1 | tf_op jit(solution)/shard_map/feed/pallas_call | solution.py:371
  299.6 13.3 %outer_step.2 = bf16[1024,1024]{1,0:T(8,128)(2,1)} custom-call(bf16[4096,1024]{1,0:T(8,128)(2,1)} %get-tuple-element.136.refs_0_.left_ref, bf16[4096,1024]{1,0:T(8,128)(2,1)} %get-tuple-element.149.right_ref), custom_call_target="tpu_custom_call" | custom-call | flops 1 | bytes 1 | tf_op jit(solution)/shard_map/outer_step/pallas_call | solution.py:371
  312.9 13.3 %outer_step.3 = bf16[1024,1024]{1,0:T(8,128)(2,1)} custom-call(bf16[4096,1024]{1,0:T(8,128)(2,1)} %get-tuple-element.159.left_ref.refs_0_, bf16[4096,1024]{1,0:T(8,128)(2,1)} %get-tuple-element.150.right_ref), custom_call_target="tpu_custom_call" | custom-call | flops 1 | bytes 1 | tf_op jit(solution)/shard_map/outer_step/pallas_call | solution.py:371
  326.3 5.5 collective-permute-done.17.refs_1_
  331.8 1.3 copy-done.17
  333.1 10.6 %resid_step.1 = (f32[1024,1024]{1,0:T(8,128)}, bf16[1024,1024]{1,0:T(8,128)(2,1)}, f32[8,1024]{1,0:T(8,128)}, bf16[1024,256]{1,0:T(8,128)(2,1)}, bf16[1024,256]{...) custom-call(bf16[1024,1024]{1,0:T(8,128)(2,1)} %get-tuple-element.151.refs_0_, ...), custom_call_target="tpu_custom_call" | custom-call | flops 1 | bytes 1 | tf_op jit(solution)/shard_map/resid_step/pallas_call | solution.py:371
  343.8 1.7 collective-permute-start.19
  345.6 5.9 dense_grad.1
  351.5 15.8 %ffn_step.1 = (bf16[1024,1024]{1,0:T(8,128)(2,1)}, bf16[1024,1024]{1,0:T(8,128)(2,1)}, bf16[1024,1024]{1,0:T(8,128)(2,1)}, bf16[1024,1024]{1,0:T(8,128)(2,1)}) custom-call(bf16[4096,1024]{1,0:T(8,128)(2,1)} %get-tuple-element.159.left_ref.refs_0_, bf16[1024,1024]{1,0:T(8,128)(2,1)} %refs_1_.2), custom_call_target="tpu_custom_call" | custom-call | flops 1 | bytes 1 | tf_op jit(solution)/shard_map/ffn_step/pallas_call | solution.py:371
  367.4 1.7 collective-permute-done.20.refs_11_
  369.8 1.7 collective-permute-start.23
  372.0 70.0 %attend_back.2.grad_ref.refs_0_ = bf16[4096,384]{1,0:T(8,128)(2,1)} custom-call(s32[1]{0:T(128)} %bitcast.me_ref.refs_0_, s32[1]{0:T(128)S(6)} %convert_element_type.60.apart_ref.refs_1_, f32[2]{0:T(128)} %get-tuple-element.226.slope_ref.refs_2_, bf16[4096,256]{1,0:T(8,128)(2,1)} %get-tuple-element.126.q_ref.refs_3_, ...), custom_call_target="tpu_custom_call" | custom-call | flops 1 | bytes 1 | tf_op jit(solution)/shard_map/attend_back/pallas_call | solution.py:310
  442.0 4.6 add_convert_fusion.2
  446.6 1.6 collective-permute-start.26
  448.3 2.6 add_convert_fusion.3
  450.8 9.4 %weight_step.2 = (bf16[1024,384]{1,0:T(8,128)(2,1)}, f32[8,1024]{1,0:T(8,128)}, f32[1,384]{1,0:T(1,128)}) custom-call(bf16[4096,1024]{1,0:T(8,128)(2,1)} %get-tuple-element.165.normed_ref, bf16[4096,384]{1,0:T(8,128)(2,1)} %attend_back.2.grad_ref.refs_0_, bf16[1024,256]{1,0:T(8,128)(2,1)} %refs_5_.12, bf16[1024,256]{1,0:T(8,128)(2,1)} %refs_6_.11, ...), custom_call_target="tpu_custom_call" | custom-call | flops 1 | bytes 1 | tf_op jit(solution)/shard_map/weight_step/pallas_call | solution.py:371
  460.2 23.2 %all-reduce.10.cloned.1.call-done = (bf16[1024,1024]{1,0:T(8,128)(2,1)}, bf16[1024,1024]{1,0:T(8,128)(2,1)}) async-done(((bf16[1024,1024]{1,0:T(8,128)(2,1)}, bf16[1024,1024]{1,0:T(8,128)(2,1)}), (bf16[1024,1024]{1,0:T(8,128)(2,1)}, bf16[1024,1024]{1,0:T(8,128)(2,1)})) %all-reduce.10.cloned.1.call-update) | async-done | bytes 4194320 | tf_op jit(solution)/shard_map/psum | solution.py:1046
  483.4 1.3 copy-done.11
  484.7 3.2 add_convert_fusion.1
  487.9 70.1 %attend_back.3.grad_ref.refs_1_ = bf16[4096,384]{1,0:T(8,128)(2,1)} custom-call(s32[1]{0:T(128)} %bitcast.me_ref.refs_0_, s32[1]{0:T(128)S(6)} %convert_element_type.60.apart_ref.refs_1_, f32[2]{0:T(128)} %get-tuple-element.225.slope_ref.refs_2_, bf16[4096,256]{1,0:T(8,128)(2,1)} %get-tuple-element.126.q_ref.refs_3_, ...), custom_call_target="tpu_custom_call" | custom-call | flops 1 | bytes 1 | tf_op jit(solution)/shard_map/attend_back/pallas_call | solution.py:310
  558.0 12.3 %all-reduce.8.cloned.1.call-done = (bf16[1024,384]{1,0:T(8,128)(2,1)}, bf16[256,1024]{1,0:T(8,128)(2,1)}) async-done(((bf16[1024,384]{1,0:T(8,128)(2,1)}, bf16[256,1024]{1,0:T(8,128)(2,1)}), (bf16[1024,384]{1,0:T(8,128)(2,1)}, bf16[256,1024]{1,0:T(8,128)(2,1)})) %all-reduce.8.cloned.1.call-update) | async-done | bytes 1310736 | tf_op jit(solution)/shard_map/psum | solution.py:1099
  570.4 9.6 %weight_step.3 = (bf16[1024,384]{1,0:T(8,128)(2,1)}, f32[8,1024]{1,0:T(8,128)}, f32[1,384]{1,0:T(1,128)}) custom-call(bf16[4096,1024]{1,0:T(8,128)(2,1)} %get-tuple-element.165.normed_ref, bf16[4096,384]{1,0:T(8,128)(2,1)} %attend_back.3.grad_ref.refs_1_, bf16[1024,256]{1,0:T(8,128)(2,1)} %refs_5_.12, bf16[1024,256]{1,0:T(8,128)(2,1)} %refs_6_.11, ...), custom_call_target="tpu_custom_call" | custom-call | flops 1 | bytes 1 | tf_op jit(solution)/shard_map/weight_step/pallas_call | solution.py:371
  579.9 5.1 unproject.4
  585.1 5.1 unproject.5
  590.7 1.3 copy-done.18
  592.1 5.5 unproject.6
  597.6 1.5 collective-permute-start.29
  599.0 1.5 pack.1
  600.6 1.5 collective-permute-start.35
  603.4 1.3 collective-permute-done.35
  606.7 39.4 %collective-permute-done.31 = f32[8,1024]{1,0:T(8,128)S(1)} collective-permute-done((f32[8,1024]{1,0:T(8,128)S(1)}, f32[8,1024]{1,0:T(8,128)S(1)}, u32[]{:S(2)}, u32[]{:S(2)}) %collective-permute-start.31) | collective-permute-done | bytes 32800 | tf_op jit(solution)/shard_map/ppermute | solution.py:911
  646.1 1.5 collective-permute-start.32
  647.6 2.5 convert_element_type.78
  650.1 2.5 convert_element_type.79
  652.6 1.6 collective-permute-start.37
  654.8 5.5 add_convert_fusion
  661.4 2.1 collective-permute-start.34
  664.7 3.7 collective-permute-done.34
  669.0 57.4 %all-reduce.6.cloned.1.call-done.refs_1_ = bf16[1024,384]{1,0:T(8,128)(2,1)} async-done(((bf16[1024,384]{1,0:T(8,128)(2,1)}), bf16[1024,384]{1,0:T(8,128)(2,1)}) %all-reduce.6.cloned.1.call-update) | async-done | bytes 786448 | tf_op jit(solution)/shard_map/psum | solution.py:1103
  726.5 3.9 spread.1
  730.4 5.5 unproject.7.refs_0_
  735.9 7.7 %input_step.1 = f32[1024,1024]{1,0:T(8,128)} custom-call(bf16[1024,1024]{1,0:T(8,128)(2,1)} %unproject.7.refs_0_, bf16[1024,1024]{1,0:T(8,128)(2,1)} %collective-permute-done.29.refs_1_, bf16[1024,1024]{1,0:T(8,128)(2,1)} %refs_2_.22, f32[1024,1024]{1,0:T(8,128)} %get-tuple-element.192.refs_3_, bf16[1024]{0:T(1024)(128)(2,1)} %refs_1_.3), custom_call_target="tpu_custom_call" | custom-call | flops 1 | bytes 1 | tf_op jit(solution)/shard_map/input_step/pallas_call | solution.py:371
  (117 shorter events, 17.1 us)
Async XLA Ops:
  7.2 49.7 %copy-start.1 = (bf16[1024,1024]{1,0:T(8,128)(2,1)S(1)}, bf16[1024,1024]{1,0:T(8,128)(2,1)}, u32[]{:S(2)}) copy-start(bf16[1024,1024]{1,0:T(8,128)(2,1)} %refs_3_.17) | copy-start | bytes 6291460
  7.2 97.2 %copy-start.19 = (bf16[256,1024]{1,0:T(8,128)(2,1)S(1)}, bf16[256,1024]{1,0:T(8,128)(2,1)}, u32[]{:S(2)}) copy-start(bf16[256,1024]{1,0:T(8,128)(2,1)} %refs_5_.8) | copy-start | bytes 1572868
  7.2 476.1 %all-reduce.10.cloned.1.call-start = ((), (), s32[]{:S(2)}) async-start(), calls=%async_computation.2 | async-start | bytes 8388608 | tf_op jit(solution)/shard_map/psum | solution.py:1046
  7.3 4.5 collective-permute-start.1
  7.8 49.1 %collective-permute-start = (bf16[1024,1024]{1,0:T(8,128)(2,1)}, bf16[1024,1024]{1,0:T(8,128)(2,1)}, u32[]{:S(2)}, u32[]{:S(2)}) collective-permute-start(bf16[1024,1024]{1,0:T(8,128)(2,1)} %refs_2_.22), channel_id=1, source_target_pairs={{0,2},{1,3},{2,0},{3,1},{4,6},{5,7},{6,4},{7,5},{8,10},{9,11},{10,... | collective-permute-start | bytes 6291464 | tf_op jit(solution)/shard_map/ppermute | solution.py:911
  11.8 1.3 copy-start.2
  56.9 47.5 %collective-permute-start.3 = (bf16[1024,1024]{1,0:T(8,128)(2,1)S(1)}, bf16[1024,1024]{1,0:T(8,128)(2,1)}, u32[]{:S(2)}, u32[]{:S(2)}) collective-permute-start(bf16[1024,1024]{1,0:T(8,128)(2,1)S(1)} %copy-done.1), channel_id=1, source_target_pairs={{0,2},{1,3},{2,0},{3,1},{4,6},{5,7},{6,4},{7,5},{8,10},{9,11},{10,... | collective-permute-start | bytes 6291464 | tf_op jit(solution)/shard_map/ppermute | solution.py:911
  58.7 50.4 %collective-permute-start.2 = (bf16[1024,1024]{1,0:T(8,128)(2,1)}, bf16[1024,1024]{1,0:T(8,128)(2,1)}, u32[]{:S(2)}, u32[]{:S(2)}) collective-permute-start(bf16[1024,1024]{1,0:T(8,128)(2,1)} %collective-permute-done.refs_0_.refs_10_), channel_id=1, source_target_pairs={{0,1},{1,0},{2,3},{3,2},{4,5},{5,4},{6,7},{7,6},{8,9},{9,8},{10,11... | collective-permute-start | bytes 6291464 | tf_op jit(solution)/shard_map/ppermute | solution.py:911
  58.7 134.7 %collective-permute-start.9 = (bf16[1024,1024]{1,0:T(8,128)(2,1)S(1)}, bf16[1024,1024]{1,0:T(8,128)(2,1)}, u32[]{:S(2)}, u32[]{:S(2)}) collective-permute-start(bf16[1024,1024]{1,0:T(8,128)(2,1)S(1)} %copy-done.1), channel_id=1, source_target_pairs={{0,1},{1,0},{2,3},{3,2},{4,5},{5,4},{6,7},{7,6},{8,9},{9,8},{10,11... | collective-permute-start | bytes 6291464 | tf_op jit(solution)/shard_map/ppermute | solution.py:911
  104.4 89.5 %collective-permute-start.10 = (bf16[1024,1024]{1,0:T(8,128)(2,1)}, bf16[1024,1024]{1,0:T(8,128)(2,1)}, u32[]{:S(2)}, u32[]{:S(2)}) collective-permute-start(bf16[1024,1024]{1,0:T(8,128)(2,1)} %collective-permute-done.3.refs_2_), channel_id=1, source_target_pairs={{0,1},{1,0},{2,3},{3,2},{4,5},{5,4},{6,7},{7,6},{8,9},{9,8},{10,11... | collective-permute-start | bytes 6291464 | tf_op jit(solution)/shard_map/ppermute | solution.py:911
  104.4 50.6 %collective-permute-start.4 = (bf16[256,1024]{1,0:T(8,128)(2,1)S(1)}, bf16[256,1024]{1,0:T(8,128)(2,1)}, u32[]{:S(2)}, u32[]{:S(2)}) collective-permute-start(bf16[256,1024]{1,0:T(8,128)(2,1)S(1)} %copy-done.19), channel_id=1, source_target_pairs={{0,2},{1,3},{2,0},{3,1},{4,6},{5,7},{6,4},{7,5},{8,10},{9,11},{10,... | collective-permute-start | bytes 1572872 | tf_op jit(solution)/shard_map/ppermute | solution.py:911
  154.6 39.3 %collective-permute-start.7 = (bf16[4096,128]{1,0:T(8,128)(2,1)}, bf16[4096,128]{1,0:T(8,128)(2,1)S(1)}, u32[]{:S(2)}, u32[]{:S(2)}) collective-permute-start(bf16[4096,128]{1,0:T(8,128)(2,1)} %get-tuple-element.123.refs_0_.refs_6_), channel_id=1, source_target_pairs={{0,2},{1,3},{2,0},{3,1},{4,6},{5,7},{6,4},{7,5},{8,10},{9,11},{10,... | collective-permute-start | bytes 3145736 | tf_op jit(solution)/shard_map/ppermute | solution.py:911
  155.0 38.3 %copy-start = (bf16[4096,128]{1,0:T(8,128)(2,1)S(1)}, bf16[4096,128]{1,0:T(8,128)(2,1)}, u32[]{:S(2)}) copy-start(bf16[4096,128]{1,0:T(8,128)(2,1)} %get-tuple-element.123.refs_0_.refs_6_) | copy-start | bytes 3145732
  191.7 25.2 %collective-permute-start.8 = (bf16[4096,128]{1,0:T(8,128)(2,1)}, bf16[4096,128]{1,0:T(8,128)(2,1)S(1)}, u32[]{:S(2)}, u32[]{:S(2)}) collective-permute-start(bf16[4096,128]{1,0:T(8,128)(2,1)} %get-tuple-element.127.refs_1_.refs_6_), channel_id=1, source_target_pairs={{0,2},{1,3},{2,0},{3,1},{4,6},{5,7},{6,4},{7,5},{8,10},{9,11},{10,... | collective-permute-start | bytes 3145736 | tf_op jit(solution)/shard_map/ppermute | solution.py:911
  193.3 23.7 %collective-permute-start.13 = (bf16[256,1024]{1,0:T(8,128)(2,1)S(1)}, bf16[256,1024]{1,0:T(8,128)(2,1)}, u32[]{:S(2)}, u32[]{:S(2)}) collective-permute-start(bf16[256,1024]{1,0:T(8,128)(2,1)S(1)} %copy-done.19), channel_id=1, source_target_pairs={{0,1},{1,0},{2,3},{3,2},{4,5},{5,4},{6,7},{7,6},{8,9},{9,8},{10,11... | collective-permute-start | bytes 1572872 | tf_op jit(solution)/shard_map/ppermute | solution.py:911
  193.3 27.3 %collective-permute-start.5 = (bf16[4096,128]{1,0:T(8,128)(2,1)S(1)}, bf16[4096,128]{1,0:T(8,128)(2,1)S(1)}, u32[]{:S(2)}, u32[]{:S(2)}) collective-permute-start(bf16[4096,128]{1,0:T(8,128)(2,1)S(1)} %copy-done), channel_id=1, source_target_pairs={{0,1},{1,0},{2,3},{3,2},{4,5},{5,4},{6,7},{7,6},{8,9},{9,8},{10,11... | collective-permute-start | bytes 3145736 | tf_op jit(solution)/shard_map/ppermute | solution.py:911
  193.8 15.8 %copy-start.3 = (bf16[4096,128]{1,0:T(8,128)(2,1)}, bf16[4096,128]{1,0:T(8,128)(2,1)S(1)}, u32[]{:S(2)}) copy-start(bf16[4096,128]{1,0:T(8,128)(2,1)S(1)} %collective-permute-done.7.refs_4_) | copy-start | bytes 3145732
  193.8 26.8 %collective-permute-start.6 = (bf16[4096,128]{1,0:T(8,128)(2,1)}, bf16[4096,128]{1,0:T(8,128)(2,1)S(1)}, u32[]{:S(2)}, u32[]{:S(2)}) collective-permute-start(bf16[4096,128]{1,0:T(8,128)(2,1)} %get-tuple-element.127.refs_1_.refs_6_), channel_id=1, source_target_pairs={{0,1},{1,0},{2,3},{3,2},{4,5},{5,4},{6,7},{7,6},{8,9},{9,8},{10,11... | collective-permute-start | bytes 3145736 | tf_op jit(solution)/shard_map/ppermute | solution.py:911
  193.9 26.7 %collective-permute-start.11 = (bf16[4096,128]{1,0:T(8,128)(2,1)S(1)}, bf16[4096,128]{1,0:T(8,128)(2,1)S(1)}, u32[]{:S(2)}, u32[]{:S(2)}) collective-permute-start(bf16[4096,128]{1,0:T(8,128)(2,1)S(1)} %collective-permute-done.7.refs_4_), channel_id=1, source_target_pairs={{0,1},{1,0},{2,3},{3,2},{4,5},{5,4},{6,7},{7,6},{8,9},{9,8},{10,11... | collective-permute-start | bytes 3145736 | tf_op jit(solution)/shard_map/ppermute | solution.py:911
  217.0 3.7 copy-start.4
  217.0 3.7 collective-permute-start.12
  217.0 3.6 collective-permute-start.14
  220.6 1.1 copy-start.5
  220.6 1.5 copy-start.6
  220.6 1.8 copy-start.7
  222.5 1.0 copy-start.8
  257.9 12.1 %collective-permute-start.16 = (bf16[1024,1024]{1,0:T(8,128)(2,1)}, bf16[1024,1024]{1,0:T(8,128)(2,1)S(1)}, u32[]{:S(2)}, u32[]{:S(2)}) collective-permute-start(bf16[1024,1024]{1,0:T(8,128)(2,1)} %get-tuple-element.141), channel_id=1, source_target_pairs={{0,1},{1,0},{2,3},{3,2},{4,5},{5,4},{6,7},{7,6},{8,9},{9,8},{10,11... | collective-permute-start | bytes 6291464 | tf_op jit(solution)/shard_map/ppermute | solution.py:911
  269.6 15.9 %collective-permute-start.15 = (bf16[1024,1024]{1,0:T(8,128)(2,1)}, bf16[1024,1024]{1,0:T(8,128)(2,1)S(1)}, u32[]{:S(2)}, u32[]{:S(2)}) collective-permute-start(bf16[1024,1024]{1,0:T(8,128)(2,1)} %get-tuple-element.140), channel_id=1, source_target_pairs={{0,1},{1,0},{2,3},{3,2},{4,5},{5,4},{6,7},{7,6},{8,9},{9,8},{10,11... | collective-permute-start | bytes 6291464 | tf_op jit(solution)/shard_map/ppermute | solution.py:911
  270.0 1.3 copy-start.13
  283.9 47.9 %collective-permute-start.17 = (bf16[1024,1024]{1,0:T(8,128)(2,1)}, bf16[1024,1024]{1,0:T(8,128)(2,1)S(1)}, u32[]{:S(2)}, u32[]{:S(2)}) collective-permute-start(bf16[1024,1024]{1,0:T(8,128)(2,1)} %get-tuple-element.152), channel_id=1, source_target_pairs={{0,2},{1,3},{2,0},{3,1},{4,6},{5,7},{6,4},{7,5},{8,10},{9,11},{10,... | collective-permute-start | bytes 6291464 | tf_op jit(solution)/shard_map/ppermute | solution.py:911
  285.5 1.3 copy-start.12
  326.2 244.1 %all-reduce.8.cloned.1.call-start = ((), (), s32[]{:S(2)}) async-start(), calls=%async_computation.1 | async-start | bytes 2621440 | tf_op jit(solution)/shard_map/psum | solution.py:1099
  331.8 1.3 copy-start.17
  343.7 23.7 %collective-permute-start.18 = (bf16[1024,256]{1,0:T(8,128)(2,1)}, bf16[1024,256]{1,0:T(8,128)(2,1)S(1)}, u32[]{:S(2)}, u32[]{:S(2)}) collective-permute-start(bf16[1024,256]{1,0:T(8,128)(2,1)} %get-tuple-element.154), channel_id=1, source_target_pairs={{0,1},{1,0},{2,3},{3,2},{4,5},{5,4},{6,7},{7,6},{8,9},{9,8},{10,11... | collective-permute-start | bytes 1572872 | tf_op jit(solution)/shard_map/ppermute | solution.py:911
  343.8 23.6 %collective-permute-start.19 = (bf16[1024,256]{1,0:T(8,128)(2,1)}, bf16[1024,256]{1,0:T(8,128)(2,1)S(1)}, u32[]{:S(2)}, u32[]{:S(2)}) collective-permute-start(bf16[1024,256]{1,0:T(8,128)(2,1)} %get-tuple-element.155), channel_id=1, source_target_pairs={{0,2},{1,3},{2,0},{3,1},{4,6},{5,7},{6,4},{7,5},{8,10},{9,11},{10,... | collective-permute-start | bytes 1572872 | tf_op jit(solution)/shard_map/ppermute | solution.py:911
  345.5 23.6 %collective-permute-start.20 = (bf16[1024,256]{1,0:T(8,128)(2,1)}, bf16[1024,256]{1,0:T(8,128)(2,1)S(1)}, u32[]{:S(2)}, u32[]{:S(2)}) collective-permute-start(bf16[1024,256]{1,0:T(8,128)(2,1)} %get-tuple-element.156), channel_id=1, source_target_pairs={{0,3},{1,2},{2,1},{3,0},{4,7},{5,6},{6,5},{7,4},{8,11},{9,10},{10,... | collective-permute-start | bytes 1572872 | tf_op jit(solution)/shard_map/ppermute | solution.py:911
  367.4 4.6 copy-start.14
  367.4 4.6 copy-start.15
  369.1 2.9 copy-start.16
  369.1 72.9 %collective-permute-start.21 = (bf16[1024,1024]{1,0:T(8,128)(2,1)}, bf16[1024,1024]{1,0:T(8,128)(2,1)}, u32[]{:S(2)}, u32[]{:S(2)}) collective-permute-start(bf16[1024,1024]{1,0:T(8,128)(2,1)} %get-tuple-element.168), channel_id=1, source_target_pairs={{0,1},{1,0},{2,3},{3,2},{4,5},{5,4},{6,7},{7,6},{8,9},{9,8},{10,11... | collective-permute-start | bytes 6291464 | tf_op jit(solution)/shard_map/ppermute | solution.py:911
  369.8 78.5 %collective-permute-start.23 = (bf16[256,1024]{1,0:T(8,128)(2,1)}, bf16[256,1024]{1,0:T(8,128)(2,1)}, u32[]{:S(2)}, u32[]{:S(2)}) collective-permute-start(bf16[256,1024]{1,0:T(8,128)(2,1)} %get-tuple-element.173), channel_id=1, source_target_pairs={{0,2},{1,3},{2,0},{3,1},{4,6},{5,7},{6,4},{7,5},{8,10},{9,11},{10,... | collective-permute-start | bytes 1572872 | tf_op jit(solution)/shard_map/ppermute | solution.py:911
  371.5 76.8 %collective-permute-start.22 = (bf16[256,1024]{1,0:T(8,128)(2,1)}, bf16[256,1024]{1,0:T(8,128)(2,1)}, u32[]{:S(2)}, u32[]{:S(2)}) collective-permute-start(bf16[256,1024]{1,0:T(8,128)(2,1)} %get-tuple-element.172), channel_id=1, source_target_pairs={{0,1},{1,0},{2,3},{3,2},{4,5},{5,4},{6,7},{7,6},{8,9},{9,8},{10,11... | collective-permute-start | bytes 1572872 | tf_op jit(solution)/shard_map/ppermute | solution.py:911
  371.5 112.0 %collective-permute-start.25 = (bf16[1024,1024]{1,0:T(8,128)(2,1)}, bf16[1024,1024]{1,0:T(8,128)(2,1)S(1)}, u32[]{:S(2)}, u32[]{:S(2)}) collective-permute-start(bf16[1024,1024]{1,0:T(8,128)(2,1)} %get-tuple-element.181), channel_id=1, source_target_pairs={{0,1},{1,0},{2,3},{3,2},{4,5},{5,4},{6,7},{7,6},{8,9},{9,8},{10,11... | collective-permute-start | bytes 6291464 | tf_op jit(solution)/shard_map/ppermute | solution.py:911
  372.0 76.3 %collective-permute-start.24 = (bf16[256,1024]{1,0:T(8,128)(2,1)}, bf16[256,1024]{1,0:T(8,128)(2,1)}, u32[]{:S(2)}, u32[]{:S(2)}) collective-permute-start(bf16[256,1024]{1,0:T(8,128)(2,1)} %get-tuple-element.174), channel_id=1, source_target_pairs={{0,3},{1,2},{2,1},{3,0},{4,7},{5,6},{6,5},{7,4},{8,11},{9,10},{10,... | collective-permute-start | bytes 1572872 | tf_op jit(solution)/shard_map/ppermute | solution.py:911
  442.0 6.2 copy-start.22
  446.6 123.7 %collective-permute-start.26 = (bf16[1024,1024]{1,0:T(8,128)(2,1)}, bf16[1024,1024]{1,0:T(8,128)(2,1)}, u32[]{:S(2)}, u32[]{:S(2)}) collective-permute-start(bf16[1024,1024]{1,0:T(8,128)(2,1)} %add_convert_fusion.2), channel_id=1, source_target_pairs={{0,2},{1,3},{2,0},{3,1},{4,6},{5,7},{6,4},{7,5},{8,10},{9,11},{10,... | collective-permute-start | bytes 6291464 | tf_op jit(solution)/shard_map/ppermute | solution.py:911
  483.4 243.1 %all-reduce.6.cloned.1.call-start = ((), (), s32[]{:S(2)}) async-start(), calls=%async_computation | async-start | bytes 1572864 | tf_op jit(solution)/shard_map/psum | solution.py:1103
  483.4 1.3 copy-start.11
  585.0 5.7 collective-permute-start.27
  590.2 57.3 %copy-start.23 = (bf16[1024]{0:T(1024)(128)(2,1)S(1)}, bf16[1024]{0:T(1024)(128)(2,1)}, u32[]{:S(2)}) copy-start(bf16[1024]{0:T(1024)(128)(2,1)} %param.34) | copy-start | bytes 6148
  590.2 57.3 %copy-start.10 = (bf16[1024,1024]{1,0:T(8,128)(2,1)S(1)}, bf16[1024,1024]{1,0:T(8,128)(2,1)}, u32[]{:S(2)}) copy-start(bf16[1024,1024]{1,0:T(8,128)(2,1)} %get-tuple-element.209) | copy-start | bytes 6291460
  590.2 140.1 %collective-permute-start.28 = (bf16[1024,1024]{1,0:T(8,128)(2,1)}, bf16[1024,1024]{1,0:T(8,128)(2,1)}, u32[]{:S(2)}, u32[]{:S(2)}) collective-permute-start(bf16[1024,1024]{1,0:T(8,128)(2,1)} %unproject.5), channel_id=1, source_target_pairs={{0,1},{1,0},{2,3},{3,2},{4,5},{5,4},{6,7},{7,6},{8,9},{9,8},{10,11... | collective-permute-start | bytes 6291464 | tf_op jit(solution)/shard_map/ppermute | solution.py:911
  590.7 1.3 copy-start.18
  597.6 138.4 %collective-permute-start.29 = (bf16[1024,1024]{1,0:T(8,128)(2,1)}, bf16[1024,1024]{1,0:T(8,128)(2,1)}, u32[]{:S(2)}, u32[]{:S(2)}) collective-permute-start(bf16[1024,1024]{1,0:T(8,128)(2,1)} %unproject.6), channel_id=1, source_target_pairs={{0,2},{1,3},{2,0},{3,1},{4,6},{5,7},{6,4},{7,5},{8,10},{9,11},{10,... | collective-permute-start | bytes 6291464 | tf_op jit(solution)/shard_map/ppermute | solution.py:911
  600.6 1.5 collective-permute-start.30
  600.6 4.2 collective-permute-start.35
  602.9 43.2 %collective-permute-start.31 = (f32[8,1024]{1,0:T(8,128)S(1)}, f32[8,1024]{1,0:T(8,128)S(1)}, u32[]{:S(2)}, u32[]{:S(2)}) collective-permute-start(f32[8,1024]{1,0:T(8,128)S(1)} %add.84), channel_id=1, source_target_pairs={{0,2},{1,3},{2,0},{3,1},{4,6},{5,7},{6,4},{7,5},{8,10},{9,11},{10,... | collective-permute-start | bytes 98312 | tf_op jit(solution)/shard_map/ppermute | solution.py:911
  605.5 47.0 %collective-permute-start.36 = (f32[8,1024]{1,0:T(8,128)S(1)}, f32[8,1024]{1,0:T(8,128)S(1)}, u32[]{:S(2)}, u32[]{:S(2)}) collective-permute-start(f32[8,1024]{1,0:T(8,128)S(1)} %add.89), channel_id=1, source_target_pairs={{0,8},{4,12},{8,0},{12,4},{16,24},{20,28},{24,16},{28,20},{1,9},{5... | collective-permute-start | bytes 98312 | tf_op jit(solution)/shard_map/ppermute | solution.py:923
  646.1 8.1 %collective-permute-start.32 = (f32[8,1024]{1,0:T(8,128)S(1)}, f32[8,1024]{1,0:T(8,128)S(1)}, u32[]{:S(2)}, u32[]{:S(2)}) collective-permute-start(f32[8,1024]{1,0:T(8,128)S(1)} %add.85), channel_id=1, source_target_pairs={{0,4},{4,0},{8,12},{12,8},{16,20},{20,16},{24,28},{28,24},{1,5},{5... | collective-permute-start | bytes 98312 | tf_op jit(solution)/shard_map/ppermute | solution.py:923
  647.6 2.5 copy-start.9
  652.6 8.8 %collective-permute-start.37 = (f32[8,1024]{1,0:T(8,128)S(1)}, f32[8,1024]{1,0:T(8,128)S(1)}, u32[]{:S(2)}, u32[]{:S(2)}) collective-permute-start(f32[8,1024]{1,0:T(8,128)S(1)} %add.90), channel_id=1, source_target_pairs={{0,16},{4,20},{8,24},{12,28},{16,0},{20,4},{24,8},{28,12},{1,17},{... | collective-permute-start | bytes 98312 | tf_op jit(solution)/shard_map/ppermute | solution.py:923
  654.2 6.1 copy-start.21
  654.2 7.2 collective-permute-start.33
  661.4 7.0 collective-permute-start.34
  (1 other events, 0.8 us)
Sparse Core Ops, SparseCore 0:
  326.4 156.9 all-reduce.9
  487.5 82.7 all-reduce.7
  652.7 73.7 all-reduce.5

commit v5 on v4

--- a/solution.py
+++ b/solution.py
@@ -193,7 +193,9 @@
         ],
         scratch_shapes=[pltpu.VMEM((pair, total, 128), BF16)] * 3,
         compiler_params=pltpu.CompilerParams(vmem_limit_bytes=56 << 20),
-        cost_estimate=SMALL_COST,
+        cost_estimate=pl.CostEstimate(
+            flops=pair * 1200 * total * total, transcendentals=0, bytes_accessed=8 * total * cols
+        ),
         name="attend",
     )(me, apart, slopes[group * pair : (group + 1) * pair], queries, key_rows, values)
 
@@ -321,7 +323,9 @@
         scratch_shapes=[pltpu.VMEM((pair, total, 128), BF16)] * 4
         + [pltpu.VMEM((pair, 128, total), BF16), pltpu.VMEM((pair, 128, total), F32)],
         compiler_params=pltpu.CompilerParams(vmem_limit_bytes=60 << 20),
-        cost_estimate=SMALL_COST,
+        cost_estimate=pl.CostEstimate(
+            flops=pair * 2400 * total * total, transcendentals=0, bytes_accessed=16 * total * cols
+        ),
         name="attend_back",
     )(
         me,
@@ -554,7 +558,15 @@
     return (active, grad), sums, backs
 
 
-def outer_kernel(left_ref, right_ref, out_ref, total):
+def split_rows(total, me, keep_ref, send_ref, streams):
+    rows = total.shape[0] // streams
+    for slot in range(streams):
+        part = low(total[pl.ds(pl.multiple_of((me ^ slot) * rows, rows), rows), :])
+        ref = send_ref if slot % 2 else keep_ref
+        ref[slot // 2 * rows : (slot // 2 + 1) * rows, :] = part
+
+
+def outer_kernel(me_ref, left_ref, right_ref, keep_ref, send_ref, total, *, streams):
     step = pl.program_id(0)
 
     @pl.when(step == 0)
@@ -567,57 +579,190 @@
 
     @pl.when(step == pl.num_programs(0) - 1)
     def _():
-        out_ref[...] = low(total[...])
-
-
-def outer_step(left, right):
+        split_rows(total, me_ref[0], keep_ref, send_ref, streams)
+
+
+def outer_step(left, right, me, streams):
     total = left.shape[0]
     block = min(total, 1024)
     shape = (left.shape[1], right.shape[1])
-    return kernel_call(
-        outer_kernel,
+    half = (shape[0] // 2, shape[1])
+    return kernel_call(
+        functools.partial(outer_kernel, streams=streams),
         (total // block,),
-        [pl.BlockSpec((block, cols), lambda i: (i, 0)) for cols in shape],
-        [whole(shape)],
-        [shape_of(*shape)],
-        [left, right],
+        [pl.BlockSpec(memory_space=pltpu.SMEM)]
+        + [pl.BlockSpec((block, cols), lambda i: (i, 0)) for cols in shape],
+        [whole(half)] * 2,
+        [shape_of(*half)] * 2,
+        [me, left, right],
         scratch_shapes=[pltpu.VMEM(shape, F32)],
         name="outer_step",
+    )
+
+
+def join_kernel(me_ref, *refs, early, streams):
+    parts, (keep_ref, send_ref) = refs[:-2], refs[-2:]
+    rows = parts[0].shape[0] // streams
+    for slot in range(streams):
+        home = pl.ds(pl.multiple_of((me_ref[0] ^ slot) * rows, rows), rows)
+        out = send_ref if slot % 2 else keep_ref
+        here = slice(slot // 2 * rows, (slot // 2 + 1) * rows)
+        at = 0
+        for part in parts[:early]:
+            out[here, at : at + part.shape[1]] = part[home, :]
+            at += part.shape[1]
+        total = parts[early][home, :].astype(F32)
+        for part in parts[early + 1 :]:
+            total = total + part[home, :].astype(F32)
+        out[here, at:] = low(total)
+
+
+def join_step(early, terms, me, streams):
+    inputs = [*early, *terms]
+    cols = sum(part.shape[1] for part in early) + terms[0].shape[1]
+    half = (terms[0].shape[0] // 2, cols)
+    return kernel_call(
+        functools.partial(join_kernel, early=len(early), streams=streams),
+        (1,),
+        [pl.BlockSpec(memory_space=pltpu.SMEM)] + [whole(a.shape) for a in inputs],
+        [whole(half)] * 2,
+        [shape_of(*half)] * 2,
+        [me, *inputs],
+        name="join_step",
+    )
+
+
+def late_kernel(*refs):
+    (keep, come, keep_late, come_late), outs = refs[:4], refs[4:]
+    rows, cols = outs[0].shape[0], keep.shape[1]
+    for slot, out in enumerate(outs):
+        here = slice(slot * rows, (slot + 1) * rows)
+        out[:, :cols] = low(keep[here, :].astype(F32) + come[here, :].astype(F32))
+        out[:, cols:] = low(keep_late[here, :].astype(F32) + come_late[here, :].astype(F32))
+
+
+def late_step(pairs, slots):
+    inputs = [array for pair in pairs for array in pair]
+    shape = (inputs[0].shape[0] // slots, inputs[0].shape[1] + inputs[2].shape[1])
+    return kernel_call(
+        late_kernel,
+        (1,),
+        [whole(a.shape) for a in inputs],
+        [whole(shape)] * slots,
+        [shape_of(*shape)] * slots,
+        inputs,
+        name="late_step",
+    )
+
+
+def pair_kernel(*refs, count):
+    parts, outs = refs[: 2 * count], refs[2 * count :]
+    rows = outs[0].shape[0] // count
+    for at in range(count):
+        keep, come = parts[2 * at : 2 * at + 2]
+        for slot, out in enumerate(outs):
+            here = slice(slot * rows, (slot + 1) * rows)
+            out[at * rows : (at + 1) * rows, :] = low(
+                keep[here, :].astype(F32) + come[here, :].astype(F32)
+            )
+
+
+def pair_step(pairs, slots):
+    inputs = [array for pair in pairs for array in pair]
+    rows, cols = inputs[0].shape
+    shape = (rows // slots * len(pairs), cols)
+    return kernel_call(
+        functools.partial(pair_kernel, count=len(pairs)),
+        (1,),
+        [whole(a.shape) for a in inputs],
+        [whole(shape)] * slots,
+        [shape_of(*shape)] * slots,
+        inputs,
+        name="pair_step",
+    )
+
+
+def stack_kernel(*refs):
+    rows = refs[0].shape[0]
+    for at, ref in enumerate(refs[:-1]):
+        refs[-1][at * rows : (at + 1) * rows, :] = ref[...]
+
+
+def stack_step(parts):
+    rows, cols = parts[0].shape
+    return kernel_call(
+        stack_kernel,
+        (1,),
+        [whole((rows, cols))] * len(parts),
+        [whole((rows * len(parts), cols))],
+        [shape_of(rows * len(parts), cols)],
+        list(parts),
+        name="stack_step",
     )[0]
+
+
+def shard_views(even_ref, odd_ref, streams):
+    rows = even_ref.shape[0] // (streams // 2)
+    return [
+        (slot, ref.at[slot // 2 * rows : (slot // 2 + 1) * rows])
+        for slot, ref in enumerate([even_ref, odd_ref] * (streams // 2))
+    ]
+
+
+def feed_grads_kernel(me_ref, even_ref, odd_ref, up_ref, down_ref, up_rows, *, streams):
+    rows = even_ref.shape[0] // streams
+    for slot, part in shard_views(even_ref, odd_ref, streams):
+        home = pl.ds(pl.multiple_of((me_ref[0] ^ slot) * rows, rows), rows)
+        up_rows[home, :] = part[:rows, :].astype(F32)
+        down_ref[home, :] = part[rows:, :].astype(F32)
+    up_ref[...] = up_rows[...].T
+
+
+def feed_grads(even, odd, me, streams):
+    units, width = even.shape
+    return kernel_call(
+        functools.partial(feed_grads_kernel, streams=streams),
+        (1,),
+        [pl.BlockSpec(memory_space=pltpu.SMEM)] + [whole(even.shape)] * 2,
+        [whole((width, units)), whole((units, width))],
+        [shape_of(width, units, F32), shape_of(units, width, F32)],
+        [me, even, odd],
+        scratch_shapes=[pltpu.VMEM((units, width), F32)],
+        name="feed_grads",
+    )
 
 
 def pack_kernel(*refs, groups):
     sums_ref, gain_ref, shift_ref = refs[:3]
     row_refs, count_refs = refs[3 : 3 + groups], refs[3 + groups : 3 + 2 * groups]
-    unit_refs, (shared_ref, own_ref) = refs[3 + 2 * groups : -2], refs[-2:]
-    shared_ref[...] = sums_ref[...]
+    unit_refs, out_ref = refs[3 + 2 * groups : -1], refs[-1]
+    out_ref[...] = jnp.zeros_like(out_ref)
+    out_ref[:4, : sums_ref.shape[1]] = sums_ref[:4, :]
     rows = row_refs[0][...]
     for ref in row_refs[1:]:
         rows = rows + ref[...]
-    shared_ref[4:5, :] = (rows[0:1] - row(shift_ref) * rows[1:2]) / row(gain_ref)
-    shared_ref[5:6, :] = rows[1:2]
-    own_ref[...] = jnp.zeros_like(own_ref)
+    out_ref[4:5, : rows.shape[1]] = (rows[0:1] - row(shift_ref) * rows[1:2]) / row(gain_ref)
+    out_ref[5:6, : rows.shape[1]] = rows[1:2]
     units = unit_refs[0][...]
     for ref in unit_refs[1:]:
         units = units + ref[...]
-    own_ref[0:1, : units.shape[1]] = units
+    out_ref[8:9, : units.shape[1]] = units
     for at, ref in enumerate(count_refs):
-        own_ref[1 + at : 2 + at, : ref.shape[1]] = ref[...]
+        out_ref[9 + at : 10 + at, : ref.shape[1]] = ref[...]
 
 
 def pack(row_sums, gain, shift, group_rows, group_counts, unit_sums):
-    width = row_sums.shape[1]
     inputs = [row_sums, gain, shift, *group_rows, *group_counts, *unit_sums]
-    wide = max(a.shape[1] for a in (*group_counts, *unit_sums))
+    wide = max(a.shape[1] for a in (row_sums, *group_counts, *unit_sums))
     return kernel_call(
         functools.partial(pack_kernel, groups=len(group_rows)),
         (1,),
         [whole(a.shape) for a in inputs],
-        [whole((8, width)), whole((8, wide))],
-        [shape_of(8, width, F32), shape_of(8, wide, F32)],
+        [whole((16, wide))],
+        [shape_of(16, wide, F32)],
         inputs,
         name="pack",
-    )
+    )[0]
 
 
 def resid_kernel(*refs, terms, slots):
@@ -666,18 +811,20 @@
 
 def dense_grad_kernel(*refs, slots, groups):
     mixed_refs, grad_ref = refs[: slots * groups], refs[slots * groups]
-    out_refs, sum_refs = refs[slots * groups + 1 :][:slots], refs[slots * groups + 1 :][slots:]
+    even_ref, odd_ref, *sum_refs = refs[slots * groups + 1 :]
     step = pl.program_id(0)
     grad = grad_ref[...]
     for slot in range(slots):
         mixed = [ref[...] for ref in mixed_refs[slot * groups : (slot + 1) * groups]]
-        part = dot(jnp.concatenate(mixed, axis=1), grad, TN)
+        part = dot(grad, jnp.concatenate(mixed, axis=1), TN)
         sum_refs[slot][...] = jnp.where(step == 0, 0.0, sum_refs[slot][...]) + part
 
     @pl.when(step == pl.num_programs(0) - 1)
     def _():
-        for out_ref, sum_ref in zip(out_refs, sum_refs):
-            out_ref[...] = low(sum_ref[...])
+        rows = sum_refs[0].shape[0]
+        for slot, sum_ref in enumerate(sum_refs):
+            out_ref = odd_ref if slot % 2 else even_ref
+            out_ref[slot // 2 * rows : (slot // 2 + 1) * rows, :] = low(sum_ref[...])
 
 
 def dense_grad(mixed, grad):
@@ -695,16 +842,17 @@
             for part in mixed[slot]
         ]
         + [pl.BlockSpec((block, width), lambda i: (i, 0))],
-        [whole((cols, width))] * slots,
-        [shape_of(cols, width)] * slots,
+        [whole((width * slots // 2, cols))] * 2,
+        [shape_of(width * slots // 2, cols)] * 2,
         [*[part for parts in mixed for part in parts], grad],
         (),
-        scratch_shapes=[pltpu.VMEM((cols, width), F32)] * slots,
+        scratch_shapes=[pltpu.VMEM((width, cols), F32)] * slots,
         name="dense_grad",
     )
 
 
-def weight_kernel(normed_ref, grad_ref, wq_ref, wk_ref, wv_ref, out_ref, sums_ref, count_ref, total, count):
+def weight_kernel(me_ref, normed_ref, grad_ref, wq_ref, wk_ref, wv_ref, *refs, streams):
+    *out_refs, sums_ref, count_ref, total, count = refs
     step = pl.program_id(0)
 
     @pl.when(step == 0)
@@ -719,7 +867,10 @@
     @pl.when(step == pl.num_programs(0) - 1)
     def _():
         weight = jnp.concatenate([wq_ref[...], wk_ref[...], wv_ref[...]], axis=1).astype(F32)
-        out_ref[...] = low(total[...])
+        if streams:
+            split_rows(total, me_ref[0], *out_refs, streams)
+        else:
+            out_refs[0][...] = low(total[...])
         count_ref[...] = count[...]
         lane = lanes(weight.shape[0])
         cross = jnp.sum(weight * total[...], axis=1, keepdims=True)
@@ -728,22 +879,24 @@
         sums_ref[...] = both.T[:8]
 
 
-def weight_step(normed, grad, weights, group):
+def weight_step(normed, grad, weights, group, me, streams):
     total, width = normed.shape
     cols = grad.shape[1]
     block = min(total, 1024)
-    return kernel_call(
-        weight_kernel,
+    outs = [(width // 2, cols)] * 2 if streams else [(width, cols)]
+    *parts, sums, count = kernel_call(
+        functools.partial(weight_kernel, streams=streams),
         (total // block,),
-        [pl.BlockSpec((block, count), lambda i: (i, 0)) for count in (width, cols)]
+        [pl.BlockSpec(memory_space=pltpu.SMEM)]
+        + [pl.BlockSpec((block, count), lambda i: (i, 0)) for count in (width, cols)]
         + [pl.BlockSpec((width, cols // 3), lambda i: (0, group))] * 3,
-        [whole((width, cols)), whole((8, width)), whole((1, cols))],
-        [shape_of(width, cols), shape_of(8, width, F32), shape_of(1, cols, F32)],
-        [normed, grad, *weights],
-        (),
+        [whole(shape) for shape in outs] + [whole((8, width)), whole((1, cols))],
+        [shape_of(*shape) for shape in outs] + [shape_of(8, width, F32), shape_of(1, cols, F32)],
+        [me, normed, grad, *weights],
         scratch_shapes=[pltpu.VMEM((width, cols), F32), pltpu.VMEM((1, cols), F32)],
         name="weight_step",
     )
+    return parts, sums, count
 
 
 def unproject_kernel(*refs, groups, per, extras):
@@ -794,59 +947,78 @@
     )
 
 
-def ffn_kernel(*refs, per, extras):
-    active_ref, weight_ref = refs[:2]
-    slot = pl.program_id(0) // per
-    total = dot(active_ref[...], weight_ref[...])
-    if extras:
-        total = total + choose(slot, refs[2 : 2 + extras]).astype(F32)
-    total = low(total)
-    for at, ref in enumerate(refs[2 + extras :]):
-
-        @pl.when(slot == at)
-        def _():
-            ref[...] = total
-
-
-def ffn_step(active, weight, slots, chosen, extras):
+def ffn_kernel(active_ref, weight_ref, even_ref, odd_ref, *, per):
+    total = low(dot(active_ref[...], weight_ref[...]))
+    odd = pl.program_id(0) // per % 2
+
+    @pl.when(odd == 0)
+    def _():
+        even_ref[...] = total
+
+    @pl.when(odd == 1)
+    def _():
+        odd_ref[...] = total
+
+
+def ffn_step(active, weight, slots):
     total, units = active.shape
     width = weight.shape[1]
     rows = total // slots
     block = min(rows, 1024)
     per = rows // block
-    count = len(chosen)
-    return kernel_call(
-        functools.partial(ffn_kernel, per=per, extras=len(extras)),
-        (count * per,),
-        [tall_spec(chosen, per, block, units), whole(weight.shape)]
-        + slot_specs(len(extras), per, block, width),
-        slot_specs(count, per, block, width),
-        [shape_of(rows, width)] * count,
-        [active, weight, *extras],
+    half = (total // 2, width)
+
+    def half_spec(odd):
+        def place(i):
+            slot, step = i // per, i % per
+            now = slot // 2 * per
+            if odd:
+                return (jnp.where(slot % 2 == 1, now + step, jnp.maximum(now - 1, 0)), 0)
+            return (jnp.where(slot % 2 == 0, now + step, now + per - 1), 0)
+
+        return pl.BlockSpec((block, width), place)
+
+    return kernel_call(
+        functools.partial(ffn_kernel, per=per),
+        (slots * per,),
+        [pl.BlockSpec((block, units), lambda i: (i, 0)), whole(weight.shape)],
+        [half_spec(0), half_spec(1)],
+        [shape_of(*half)] * 2,
+        [active, weight],
         name="ffn_step",
     )
 
 
-def spread_kernel(*refs, groups):
-    cols = refs[0].shape[1] // 3
-    for kind in range(3):
+def spread_kernel(me_ref, even_ref, odd_ref, *refs, groups, streams):
+    *out_refs, dense_ref, dense_rows = refs
+    cols = out_refs[0].shape[1] // groups
+    heads = dense_ref.shape[0]
+    rows = even_ref.shape[0] * 2 // streams
+    for slot, part in shard_views(even_ref, odd_ref, streams):
+        home = pl.ds(pl.multiple_of((me_ref[0] ^ slot) * rows, rows), rows)
         for group in range(groups):
-            refs[groups + kind][:, group * cols : (group + 1) * cols] = refs[group][
-                :, kind * cols : (kind + 1) * cols
-            ].astype(F32)
-
-
-def spread(group_sums):
-    width, cols = group_sums[0].shape
-    groups = len(group_sums)
-    block = min(width, 256)
-    return kernel_call(
-        functools.partial(spread_kernel, groups=groups),
-        (width // block,),
-        [pl.BlockSpec((block, cols), lambda i: (i, 0))] * groups,
-        [pl.BlockSpec((block, cols // 3 * groups), lambda i: (i, 0))] * 3,
-        [shape_of(width, cols // 3 * groups, F32)] * 3,
-        list(group_sums),
+            first = group * 3 * cols + (heads if group == groups - 1 else 0)
+            for kind in range(3):
+                at = first + kind * cols
+                out_refs[kind][home, group * cols : (group + 1) * cols] = part[
+                    :, at : at + cols
+                ].astype(F32)
+        first = (groups - 1) * 3 * cols
+        dense_rows[home, :] = part[:, first : first + heads].astype(F32)
+    dense_ref[...] = dense_rows[...].T
+
+
+def spread(even, odd, me, streams, groups, heads):
+    width = even.shape[0] * 2
+    shapes = [(width, heads)] * 3 + [(heads, width)]
+    return kernel_call(
+        functools.partial(spread_kernel, groups=groups, streams=streams),
+        (1,),
+        [pl.BlockSpec(memory_space=pltpu.SMEM)] + [whole(even.shape)] * 2,
+        [whole(shape) for shape in shapes],
+        [shape_of(*shape, F32) for shape in shapes],
+        [me, even, odd],
+        scratch_shapes=[pltpu.VMEM((width, heads), F32)],
         name="spread",
     )
 
@@ -899,6 +1071,7 @@
 ):
     me = lax.axis_index("tensor")
     me_word = me.astype(jnp.int32)[None]
+    stream = lax.axis_index("dp").astype(jnp.int32)[None]
     rows = layer_input.shape[0]
     head_cols = query_weight.shape[1]
     head_count = head_cols // HD
@@ -955,13 +1128,13 @@
             lambda sum_now, term: sum_now + term.astype(F32), terms[1:], terms[0].astype(F32)
         )
 
-    def total_of(shared, own):
-        for bit in bits:
-            shared = shared + swap(shared, bit)
-        for level in range(streams.bit_length() - 1):
-            shared = shared + swap_data(shared, 1 << level)
-            own = own + swap_data(own, 1 << level)
-        return shared, own
+    far_streams = range(2, streams, 2)
+
+    def exchange(parts):
+        return low(add_up([parts[0], *[swap_data(parts[k // 2], k) for k in far_streams]]))
+
+    def collect_far(shard):
+        return [shard, *[swap_data(shard, k) for k in far_streams]]
 
     norm_vectors = (input_gain, input_shift)
     weights = (query_weight, key_weight, value_weight)
@@ -981,7 +1154,9 @@
     x_parts = [x_held[slot] for slot in range(slots)]
     dense_parts = gather(after(dense_weight, arrived[-1]))
     cot_own = after(cotangent, arrived[-1])
-    cot_parts = gather(cot_own)
+    cot_held = {0: cot_own}
+    for bit in reversed(bits[1:]):
+        cot_held.update({slot ^ bit: swap(part, bit) for slot, part in cot_held.items()})
     normed, queries, key_rows, values = project(
         x_parts[2:], range(2, slots), slots, norm_vectors, weights, biases, held
     )
@@ -996,7 +1171,7 @@
             me_word,
             apart,
             slopes,
-            queries if not group else after(queries, cot_parts[half], dense_parts[half], mixed_own[-1]),
+            queries if not group else after(queries, cot_held[half], mixed_own[-1]),
             key_rows,
             values,
             slots,
@@ -1004,10 +1179,16 @@
         )
         mixed_own.append(mixed)
         log_totals.append(log_total)
+        if not group:
+            keys = sorted(cot_held)
+            held = lax.optimization_barrier((*[cot_held[key] for key in keys], mixed))[:-1]
+            cot_held.update(zip(keys, held))
+            cot_held.update({slot ^ 1: swap(part, 1) for slot, part in cot_held.items()})
+            cot_parts = [cot_held[slot] for slot in range(slots)]
         if group < groups - 1:
             mixed_parts.append(gather(mixed))
     act_grad, cot_all = act_grad_step(
-        lax.optimization_barrier((*cot_parts, mixed_own[-1]))[:-1], down_weight
+        lax.optimization_barrier((*cot_parts, mixed_own[-1], *dense_parts[2:]))[:slots], down_weight
     )
     came = {0: mixed_own[-1]}
     for bit in reversed(bits[1:]):
@@ -1034,94 +1215,131 @@
 
     post_terms = ordered_terms(make_feed)
     active, hidden_grad = fed[-1]
-    up_part = outer_step(post_all, hidden_grad)
-    down_part = outer_step(active, after(cot_all, up_part))
+    up_keep, up_send = outer_step(hidden_grad, post_all, stream, streams)
+    down_keep, down_send = outer_step(active, after(cot_all, up_keep), stream, streams)
+    up_come, down_come = swap_data(up_send, 1), swap_data(down_send, 1)
     resid_grad, attended_grad, row_sums, *mixed_grads = resid_step(
-        [after(post_terms[0], down_part), *post_terms[1:]],
+        [after(post_terms[0], down_keep), *post_terms[1:]],
         residual,
         cotangent,
         post_gain,
         dense_parts,
     )
-    up_sum, down_sum = lax.psum((up_part, down_part), "dp")
     mixed_grads = [swap(part, slot) if slot else part for slot, part in enumerate(mixed_grads)]
-    dense_grads = dense_grad(mixed_all, attended_grad)
-    ffn_parts = ffn_step(after(active, dense_grads[-1]), down_weight, slots, range(slots), ())
-    *mixed_grads, dense_last, ffn_last = lax.optimization_barrier(
-        (*mixed_grads, dense_grads[-1], ffn_parts[-1])
-    )
-    dense_grads = [*dense_grads[:-1], dense_last]
-    dense_terms = [swap(part, slot) if slot else part for slot, part in enumerate(dense_grads)]
-    ffn_parts = [*ffn_parts[:-1], ffn_last]
-    ffn_come = [swap(part, 1) for part in ffn_parts[1::2]]
-    ffn_held = dict(zip(range(0, slots, 2), [
-        low(part.astype(F32) + come.astype(F32))
-        for part, come in zip(ffn_parts[::2], ffn_come)
-    ]))
-    ffn_first = ffn_held.pop(0)
+    dense_even, dense_odd = dense_grad(mixed_all, attended_grad)
+    ffn_even, ffn_odd = ffn_step(after(active, dense_odd), down_weight, slots)
+    feed_parts = pair_step(
+        [(after(up_keep, ffn_odd), up_come), (down_keep, down_come)], streams // 2
+    )
+    moved = lax.optimization_barrier((*mixed_grads, dense_odd, ffn_odd, *feed_parts))
+    mixed_grads, (dense_odd, ffn_odd), feed_parts = (
+        moved[:slots],
+        moved[slots : slots + 2],
+        moved[slots + 2 :],
+    )
+    dense_come, ffn_come = swap(dense_odd, 1), swap(ffn_odd, 1)
+
+    def partner_sums(even, come):
+        size = even.shape[0] * 2 // slots
+        cuts = [slice(at * size, (at + 1) * size) for at in range(slots // 2)]
+        return [low(even[cut].astype(F32) + come[cut].astype(F32)) for cut in cuts]
 
     cols = head_cols // groups
-    head_grads, group_sums, group_rows, group_counts = [], [], [], []
-    for group in range(groups):
-        head_grads.append(
-            attend_back(
-                me_word,
-                apart,
-                slopes,
-                queries,
-                key_rows,
-                values,
-                mixed_own[group],
-                log_totals[group],
-                mixed_grads,
-                group,
-            )
+    head_grads, early_parts, group_rows, group_counts = [], [], [], []
+
+    def backward(group):
+        return attend_back(
+            me_word,
+            apart,
+            slopes,
+            queries,
+            key_rows,
+            values,
+            mixed_own[group],
+            log_totals[group],
+            mixed_grads,
+            group,
         )
+
+    dense_sums = partner_sums(dense_even, dense_come)
+    for group in range(groups - 1):
+        head_grads.append(backward(group))
         grad = head_grads[-1]
-        if not group:
-            keys = sorted(ffn_held)
-            grad, *parts = lax.optimization_barrier((grad, *[ffn_held[key] for key in keys]))
-            ffn_terms = finish_terms(dict(zip(keys, parts)), [ffn_first], bits[1:])
-        if group == groups - 1:
-            waited = (*ffn_terms, *([group_sums[0], dense_sum] if group else []))
-            grad, *waited = lax.optimization_barrier((grad, *waited))
-            ffn_terms = waited[: len(ffn_terms)]
-            if group:
-                group_sums[0], dense_sum = waited[len(ffn_terms) :]
-        part, row_part, count_part = weight_step(normed, grad, weights, group)
+        if group == groups - 2:
+            grad, *dense_sums = lax.optimization_barrier((grad, *dense_sums))
+        parts, row_part, count_part = weight_step(normed, grad, weights, group, stream, 0)
+        early_parts += parts
         group_rows.append(row_part)
         group_counts.append(count_part)
-        if not group:
-            dense_part = low(add_up(dense_terms))
-            part, dense_part, up_sum, down_sum = lax.optimization_barrier(
-                (part, dense_part, up_sum, down_sum)
-            )
-            sums = lax.psum((part, dense_part), "dp")
-            dense_sum = sums[1]
-            *mixed_grads, _ = lax.optimization_barrier((*mixed_grads, part))
-        else:
-            sums = lax.psum((part,), "dp")
-        group_sums.append(sums[0])
-    last = after(head_grads[-1], part)
-    normed_terms = ordered_terms(
-        lambda chosen, extras, gate: unproject(
-            [*head_grads[:-1], last if gate is None else after(last, gate)],
-            weights,
-            slots,
-            chosen,
-            extras,
+        mixed_grads = lax.optimization_barrier((*mixed_grads, parts[-1]))[:-1]
+    even_slots = range(2, slots, 2)
+    dense_terms = finish_terms(dict(zip(even_slots, dense_sums[1:])), [dense_sums[0]], bits[1:])
+    early_keep, early_send = join_step(early_parts, dense_terms, stream, streams)
+    moved = lax.optimization_barrier(
+        (*mixed_grads, early_send, exchange(feed_parts), *partner_sums(ffn_even, ffn_come))
+    )
+    mixed_grads, (early_send, feed_shard), ffn_sums = (
+        moved[:slots],
+        moved[slots : slots + 2],
+        moved[slots + 2 :],
+    )
+    early_come = swap_data(early_send, 1)
+    feed_shards = collect_far(feed_shard)
+    ffn_terms = finish_terms(dict(zip(even_slots, ffn_sums[1:])), [ffn_sums[0]], bits[1:])
+    head_grads.append(backward(groups - 1))
+    grad, early_come, *arrived = lax.optimization_barrier(
+        (head_grads[-1], early_come, *feed_shards, *ffn_terms)
+    )
+    feed_shards, ffn_terms = arrived[: len(feed_shards)], arrived[len(feed_shards) :]
+    (late_keep, late_send), row_part, count_part = weight_step(
+        normed, grad, weights, groups - 1, stream, streams
+    )
+    group_rows.append(row_part)
+    group_counts.append(count_part)
+    late_come = swap_data(late_send, 1)
+    vectors = pack(row_sums, input_gain, input_shift, group_rows, group_counts, up_bias_parts)
+    feed_even = stack_step([*feed_shards[:-1], after(feed_shards[-1], vectors)])
+    summed = vectors + swap_data(vectors, 1)
+    feed_odd = swap_data(after(feed_even, late_come, summed), 1)
+    seen = []
+
+    def make_unproject(chosen, extras, gate):
+        gates = [feed_even if gate is None else gate]
+        if not seen:
+            gates += [late_come, summed]
+        seen.append(0)
+        return unproject(
+            [*head_grads[:-1], after(head_grads[-1], *gates)], weights, slots, chosen, extras
         )
-    )
-    shared, own = total_of(
-        *pack(row_sums, input_gain, input_shift, group_rows, group_counts, up_bias_parts)
-    )
+
+    normed_terms = ordered_terms(make_unproject)
+    late_parts = late_step(
+        [(early_keep, early_come), (after(late_keep, normed_terms[0]), late_come)], streams // 2
+    )
+    layer_output = low(residual + add_up(ffn_terms) + down_bias.astype(F32))
+    *late_shards, feed_odd, layer_output = lax.optimization_barrier(
+        (*collect_far(exchange(late_parts)), feed_odd, layer_output)
+    )
+    late_even = stack_step(late_shards)
+    late_odd = swap_data(late_even, 1)
+    for level in range(1, streams.bit_length() - 1):
+        summed = summed + swap_data(summed, 1 << level)
+    own = summed[8:]
+    shared = after(summed, normed_terms[-1])[:8]
+    for bit in reversed(bits):
+        shared = shared + swap(shared, bit)
+    shared = shared[:, : resid_grad.shape[1]]
+    up_grad, down_grad = feed_grads(after(feed_even, late_even), feed_odd, stream, streams)
     up_bias_grad = own[0, : up_bias.shape[0]]
     counts = own[1 : 1 + groups]
     query_bias_grad = counts[:, :cols].reshape(-1)
     value_bias_grad = counts[:, 2 * cols : 3 * cols].reshape(-1)
-    layer_output = low(residual + add_up(ffn_terms) + down_bias.astype(F32))
-    weight_grads = spread(group_sums)
+    normed_terms[-1] = after(normed_terms[-1], feed_odd)
     input_grad = input_step(normed_terms, layer_input, resid_grad, input_gain)
+    late_even = after(late_even, input_grad)
+    *weight_grads, dense_weight_grad = spread(
+        late_even, late_odd, stream, streams, groups, head_cols
+    )
     return (
         layer_output,
         input_grad,
@@ -1132,13 +1350,13 @@
         weight_grads[1],
         weight_grads[2],
         value_bias_grad,
-        dense_sum.astype(F32),
+        dense_weight_grad,
         shared[1],
         shared[2],
         shared[3],
-        up_sum.astype(F32),
+        up_grad,
         up_bias_grad,
-        down_sum.astype(F32),
+        down_grad,
         shared[0],
     )
 

time: 760 us -> 641 us (0.84)
  waiting for transfers between devices: 236 us -> 98.4 us
  Pallas kernels: 431 us -> 451 us
  starting transfers between devices: 30.2 us -> 49.8 us
  between operations: 15.8 us -> 2.81 us
  other arithmetic: 23.5 us -> 12.4 us
    psum x3 -> x0, waiting for transfers between devices: 92.9 us -> none  [the longest x1 57.4 us: shards(): sums = lax.psum((part,), 'dp')]
    ppermute x32 -> x30, waiting for transfers between devices: 138 us -> 56.1 us  [swap(): return lax.ppermute(array, 'tensor', [(i, i ^ mask) for i in range(slots)])]
    ppermute x6 -> x21, waiting for transfers between devices: 5.02 us -> 42.3 us  [swap_data(): return lax.ppermute(array, 'dp', [(i, i ^ mask) for i in range(streams)])]
    ppermute x6 -> x21, starting transfers between devices: 8.51 us -> 31.6 us  [swap_data(): return lax.ppermute(array, 'dp', [(i, i ^ mask) for i in range(streams)])]
    pallas_call x22 -> x28, Pallas kernels: 218 us -> 238 us  [kernel_call(): pl.pallas_call(kernel, grid=grid, in_specs=in_specs + [pl.BlockSpec(memor...]
    convert_element_type x4 -> x5, other arithmetic: 15.9 us -> 12.4 us  [low(): return array.astype(BF16)]
    ppermute x32 -> x30, starting transfers between devices: 21.6 us -> 18.1 us  [swap(): return lax.ppermute(array, 'tensor', [(i, i ^ mask) for i in range(slots)])]
  transfers between devices with their start and end apart: 41 -> 51, of which waited for: 13 -> 16; matrix products, arithmetic and copies ran while one was open for 4% -> 2% of each run, Pallas kernels for 50% -> 64%
where the time goes in v5:
time: 641 us; the launch traced here: 632 us
  Pallas kernels  451 us (70%)
  waiting for transfers between devices  98.4 us (15%)
  starting transfers between devices  49.8 us (8%)
  local copies, waits for them, and re-layouts  17.6 us (3%)
  other arithmetic  12.4 us (2%)
    pallas_call x28, Pallas kernels, kernel_call(): pl.pallas_call(kernel, grid=grid, in_specs=in_specs + [pl.BlockSpec(memor...  238 us
    pallas_call x2, Pallas kernels, attend_back(): pl.pallas_call(functools.partial(attend_back_kernel, slots=slots, pair=pa...  140 us
    pallas_call x2, Pallas kernels, attend(): pl.pallas_call(functools.partial(attend_kernel, slots=slots, pair=pair, t...  72.9 us
    ppermute x30, waiting for transfers between devices, swap(): return lax.ppermute(array, 'tensor', [(i, i ^ mask) for i in range(slots)])  56.1 us
    ppermute x21, waiting for transfers between devices, swap_data(): return lax.ppermute(array, 'dp', [(i, i ^ mask) for i in range(streams)])  42.3 us
    ppermute x21, starting transfers between devices, swap_data(): return lax.ppermute(array, 'dp', [(i, i ^ mask) for i in range(streams)])  31.6 us
    ppermute x30, starting transfers between devices, swap(): return lax.ppermute(array, 'tensor', [(i, i ^ mask) for i in range(slots)])  18.1 us
    unnamed x72, local copies, waits for them, and re-layouts  14.1 us
  transfers between devices with their start and end apart: 51, of which 16 were waited for; matrix products, arithmetic and copies ran while one was open for 2% of the time, Pallas kernels for 64%

profile of v5, /device:TPU:0, one launch (start us, length us, event | category | flops | bytes accessed | tf_op | source)
XLA Modules:
  0.0 632.4 jit_solution(11563020793359023275)
XLA Ops:
  1.2 2.6 collective-permute-start
  3.8 1.4 collective-permute-done.1.refs_1_.refs_9_
  6.5 9.2 %project.2 = (bf16[4096,1024]{1,0:T(8,128)(2,1)}, bf16[4096,256]{1,0:T(8,128)(2,1)}, bf16[4096,256]{1,0:T(8,128)(2,1)}, bf16[4096,256]{1,0:T(8,128)(2,1)}) custom-call(bf16[1024,1024]{1,0:T(8,128)(2,1)} %refs_2_.23, bf16[1024,1024]{1,0:T(8,128)(2,1)} %copy-done.2, bf16[1024]{0:T(1024)(128)(2,1)} %refs_4_.17, bf16[1024]{0:T(1024)(128)(2,1)} %refs_2_.18, ...), custom_call_target="tpu_custom_call" | custom-call | flops 1 | bytes 1 | tf_op jit(solution)/shard_map/project/pallas_call | solution.py:375
  15.8 34.6 %collective-permute-done.refs_0_.refs_10_ = bf16[1024,1024]{1,0:T(8,128)(2,1)} collective-permute-done((bf16[1024,1024]{1,0:T(8,128)(2,1)}, bf16[1024,1024]{1,0:T(8,128)(2,1)}, u32[]{:S(2)}, u32[]{:S(2)}) %collective-permute-start) | collective-permute-done | bytes 2097184 | tf_op jit(solution)/shard_map/ppermute | solution.py:1084
  53.5 1.8 collective-permute-start.3
  55.5 9.3 %project.3 = (bf16[4096,1024]{1,0:T(8,128)(2,1)}, bf16[4096,256]{1,0:T(8,128)(2,1)}, bf16[4096,256]{1,0:T(8,128)(2,1)}, bf16[4096,256]{1,0:T(8,128)(2,1)}) custom-call(bf16[1024,1024]{1,0:T(8,128)(2,1)} %collective-permute-done.refs_0_.refs_10_, ...), custom_call_target="tpu_custom_call", output_to_operand_aliasing={{0}: (9, {}), {1}: (10, {}), {2}: (11, {}), {3}: (12, {})} | custom-call | flops 1 | bytes 1 | tf_op jit(solution)/shard_map/project/pallas_call | solution.py:375
  64.8 36.2 %attend.2 = (bf16[4096,128]{1,0:T(8,128)(2,1)}, f32[2,1,4096]{2,1,0:T(1,128)}) custom-call(s32[1]{0:T(128)} %bitcast.1.me_ref.refs_0_, s32[1]{0:T(128)S(6)} %convert_element_type.84.apart_ref.refs_1_, f32[2]{0:T(128)} %get-tuple-element.306.slope_ref.refs_2_, bf16[4096,256]{1,0:T(8,128)(2,1)} %get-tuple-element.168.q_ref.refs_3_, ...), custom_call_target="tpu_custom_call" | custom-call | flops 40265318400 | bytes 4194304 | tf_op jit(solution)/shard_map/attend/pallas_call | solution.py:182
  100.9 1.8 collective-permute-start.6
  103.2 36.7 %attend.3 = (bf16[4096,128]{1,0:T(8,128)(2,1)}, f32[2,1,4096]{2,1,0:T(1,128)}) custom-call(s32[1]{0:T(128)} %bitcast.1.me_ref.refs_0_, s32[1]{0:T(128)S(6)} %convert_element_type.84.apart_ref.refs_1_, f32[2]{0:T(128)} %get-tuple-element.305.slope_ref.refs_2_, bf16[4096,256]{1,0:T(8,128)(2,1)} %get-tuple-element.168.q_ref.refs_3_, ...), custom_call_target="tpu_custom_call" | custom-call | flops 40265318400 | bytes 4194304 | tf_op jit(solution)/shard_map/attend/pallas_call | solution.py:182
  143.7 15.3 %act_grad.1 = (bf16[4096,1024]{1,0:T(8,128)(2,1)}, bf16[4096,1024]{1,0:T(8,128)(2,1)}) custom-call(bf16[1024,1024]{1,0:T(8,128)(2,1)} %refs_3_.17, bf16[1024,1024]{1,0:T(8,128)(2,1)} %collective-permute-done.8.refs_1_, bf16[1024,1024]{1,0:T(8,128)(2,1)} %collective-permute-done.3.refs_2_, bf16[1024,1024]{1,0:T(8,128)(2,1)} %collective-permute-done.9.refs_3_, ...), custom_call_target="tpu_custom_call" | custom-call | flops 1 | bytes 1 | tf_op jit(solution)/shard_map/act_grad/pallas_call | solution.py:375
  159.0 6.2 collective-permute-done.7.refs_5_
  165.7 2.7 collective-permute-done.14.refs_13_.refs_6_
  171.4 22.8 %post_norm.1 = (bf16[4096,1024]{1,0:T(8,128)(2,1)}, f32[1024,1024]{1,0:T(8,128)}) custom-call(bf16[4096,128]{1,0:T(8,128)(2,1)} %get-tuple-element.164.refs_0_.refs_6_, bf16[4096,128]{1,0:T(8,128)(2,1)} %get-tuple-element.169.refs_1_.refs_6_, bf16[4096,128]{1,0:T(8,128)(2,1)} %copy-done.7, bf16[4096,128]{1,0:T(8,128)(2,1)} %copy-done.8, ...), custom_call_target="tpu_custom_call" | custom-call | flops 1 | bytes 1 | tf_op jit(solution)/shard_map/post_norm/pallas_call | solution.py:375
  194.1 11.7 %feed.4 = (bf16[4096,1024]{1,0:T(8,128)(2,1)}, bf16[4096,1024]{1,0:T(8,128)(2,1)}, f32[1,1024]{1,0:T(1,128)}, bf16[1024,1024]{1,0:T(8,128)(2,1)}) custom-call(bf16[4096,1024]{1,0:T(8,128)(2,1)} %get-tuple-element.178.refs_0_.right_ref, bf16[4096,1024]{1,0:T(8,128)(2,1)} %get-tuple-element.179.refs_1_, bf16[1024,1024]{1,0:T(8,128)(2,1)} %refs_2_.17, ...), custom_call_target="tpu_custom_call" | custom-call | flops 1 | bytes 1 | tf_op jit(solution)/shard_map/feed/pallas_call | solution.py:375
  206.2 11.6 %feed.5 = (bf16[4096,1024]{1,0:T(8,128)(2,1)}, bf16[4096,1024]{1,0:T(8,128)(2,1)}, f32[1,1024]{1,0:T(1,128)}, bf16[1024,1024]{1,0:T(8,128)(2,1)}) custom-call(bf16[4096,1024]{1,0:T(8,128)(2,1)} %get-tuple-element.178.refs_0_.right_ref, bf16[4096,1024]{1,0:T(8,128)(2,1)} %get-tuple-element.179.refs_1_, ...), custom_call_target="tpu_custom_call", output_to_operand_aliasing={{0}: (4, {}), {1}: (5, {})} | custom-call | flops 1 | bytes 1 | tf_op jit(solution)/shard_map/feed/pallas_call | solution.py:375
  217.9 1.3 copy-done.12
  219.2 12.6 %feed.6 = (bf16[4096,1024]{1,0:T(8,128)(2,1)}, bf16[4096,1024]{1,0:T(8,128)(2,1)}, f32[1,1024]{1,0:T(1,128)}, bf16[1024,1024]{1,0:T(8,128)(2,1)}) custom-call(bf16[4096,1024]{1,0:T(8,128)(2,1)} %get-tuple-element.178.refs_0_.right_ref, bf16[4096,1024]{1,0:T(8,128)(2,1)} %get-tuple-element.179.refs_1_, ...), custom_call_target="tpu_custom_call", output_to_operand_aliasing={{0}: (5, {}), {1}: (6, {})} | custom-call | flops 1 | bytes 1 | tf_op jit(solution)/shard_map/feed/pallas_call | solution.py:375
  234.2 12.8 %feed.7 = (bf16[4096,1024]{1,0:T(8,128)(2,1)}, bf16[4096,1024]{1,0:T(8,128)(2,1)}, f32[1,1024]{1,0:T(1,128)}, bf16[1024,1024]{1,0:T(8,128)(2,1)}) custom-call(bf16[4096,1024]{1,0:T(8,128)(2,1)} %get-tuple-element.178.refs_0_.right_ref, bf16[4096,1024]{1,0:T(8,128)(2,1)} %get-tuple-element.179.refs_1_, ...), custom_call_target="tpu_custom_call", output_to_operand_aliasing={{0}: (5, {}), {1}: (6, {})} | custom-call | flops 1 | bytes 1 | tf_op jit(solution)/shard_map/feed/pallas_call | solution.py:375
  247.0 13.3 %outer_step.2 = (bf16[512,1024]{1,0:T(8,128)(2,1)}, bf16[512,1024]{1,0:T(8,128)(2,1)}) custom-call(s32[1]{0:T(128)} %bitcast.me_ref, bf16[4096,1024]{1,0:T(8,128)(2,1)} %get-tuple-element.191.left_ref, bf16[4096,1024]{1,0:T(8,128)(2,1)} %get-tuple-element.178.refs_0_.right_ref), custom_call_target="tpu_custom_call" | custom-call | flops 1 | bytes 1 | tf_op jit(solution)/shard_map/outer_step/pallas_call | solution.py:375
  260.3 1.5 collective-permute-start.21
  261.8 13.3 %outer_step.3 = (bf16[512,1024]{1,0:T(8,128)(2,1)}, bf16[512,1024]{1,0:T(8,128)(2,1)}) custom-call(s32[1]{0:T(128)} %bitcast.me_ref, bf16[4096,1024]{1,0:T(8,128)(2,1)} %get-tuple-element.204.left_ref.active_ref, bf16[4096,1024]{1,0:T(8,128)(2,1)} %get-tuple-element.193.right_ref), custom_call_target="tpu_custom_call" | custom-call | flops 1 | bytes 1 | tf_op jit(solution)/shard_map/outer_step/pallas_call | solution.py:375
  275.6 4.4 collective-permute-done.17.refs_1_
  280.1 10.2 %resid_step.1 = (f32[1024,1024]{1,0:T(8,128)}, bf16[1024,1024]{1,0:T(8,128)(2,1)}, f32[8,1024]{1,0:T(8,128)}, bf16[1024,256]{1,0:T(8,128)(2,1)}, bf16[1024,256]{...) custom-call(bf16[1024,1024]{1,0:T(8,128)(2,1)} %get-tuple-element.195.refs_0_, ...), custom_call_target="tpu_custom_call" | custom-call | flops 1 | bytes 1 | tf_op jit(solution)/shard_map/resid_step/pallas_call | solution.py:375
  292.2 6.3 %dense_grad.1 = (bf16[2048,256]{1,0:T(8,128)(2,1)}, bf16[2048,256]{1,0:T(8,128)(2,1)}) custom-call(bf16[4096,128]{1,0:T(8,128)(2,1)} %get-tuple-element.164.refs_0_.refs_6_, bf16[4096,128]{1,0:T(8,128)(2,1)} %get-tuple-element.169.refs_1_.refs_6_, bf16[4096,128]{1,0:T(8,128)(2,1)} %copy-done.7, bf16[4096,128]{1,0:T(8,128)(2,1)} %copy-done.8, ...), custom_call_target="tpu_custom_call" | custom-call | flops 1 | bytes 1 | tf_op jit(solution)/shard_map/dense_grad/pallas_call | solution.py:375
  298.5 14.5 %ffn_step.1 = (bf16[2048,1024]{1,0:T(8,128)(2,1)}, bf16[2048,1024]{1,0:T(8,128)(2,1)}) custom-call(bf16[4096,1024]{1,0:T(8,128)(2,1)} %get-tuple-element.204.left_ref.active_ref, bf16[1024,1024]{1,0:T(8,128)(2,1)} %weight_ref.1), custom_call_target="tpu_custom_call" | custom-call | flops 1 | bytes 1 | tf_op jit(solution)/shard_map/ffn_step/pallas_call | solution.py:375
  315.0 3.7 pair_step.1
  319.1 3.6 collective-permute-start.27
  323.5 70.2 %attend_back.2.grad_ref.refs_0_ = bf16[4096,384]{1,0:T(8,128)(2,1)} custom-call(s32[1]{0:T(128)} %bitcast.1.me_ref.refs_0_, s32[1]{0:T(128)S(6)} %convert_element_type.84.apart_ref.refs_1_, f32[2]{0:T(128)} %get-tuple-element.306.slope_ref.refs_2_, bf16[4096,256]{1,0:T(8,128)(2,1)} %get-tuple-element.168.q_ref.refs_3_, ...), custom_call_target="tpu_custom_call" | custom-call | flops 80530636800 | bytes 8388608 | tf_op jit(solution)/shard_map/attend_back/pallas_call | solution.py:312
  396.0 1.4 add_convert_fusion.3.refs_0_
  397.4 9.6 %weight_step.2 = (bf16[1024,384]{1,0:T(8,128)(2,1)}, f32[8,1024]{1,0:T(8,128)}, f32[1,384]{1,0:T(1,128)}) custom-call(s32[1]{0:T(128)} %bitcast.me_ref, bf16[4096,1024]{1,0:T(8,128)(2,1)} %get-tuple-element.160.normed_ref, bf16[4096,384]{1,0:T(8,128)(2,1)} %attend_back.2.grad_ref.refs_0_, bf16[1024,256]{1,0:T(8,128)(2,1)} %refs_5_.12, ...), custom_call_target="tpu_custom_call" | custom-call | flops 1 | bytes 1 | tf_op jit(solution)/shard_map/weight_step/pallas_call | solution.py:375
  407.0 2.4 collective-permute-done.24.refs_2_
  410.3 2.6 join_step.1
  413.0 4.6 add_convert_fusion.1
  418.8 2.9 collective-permute-start.31
  421.9 1.5 collective-permute-start.29
  424.5 70.0 %attend_back.3.grad_ref.refs_1_ = bf16[4096,384]{1,0:T(8,128)(2,1)} custom-call(s32[1]{0:T(128)} %bitcast.1.me_ref.refs_0_, s32[1]{0:T(128)S(6)} %convert_element_type.84.apart_ref.refs_1_, f32[2]{0:T(128)} %get-tuple-element.305.slope_ref.refs_2_, bf16[4096,256]{1,0:T(8,128)(2,1)} %get-tuple-element.168.q_ref.refs_3_, ...), custom_call_target="tpu_custom_call" | custom-call | flops 80530636800 | bytes 8388608 | tf_op jit(solution)/shard_map/attend_back/pallas_call | solution.py:312
  494.6 10.0 %weight_step.3 = (bf16[512,384]{1,0:T(8,128)(2,1)}, bf16[512,384]{1,0:T(8,128)(2,1)}, f32[8,1024]{1,0:T(8,128)}, f32[1,384]{1,0:T(1,128)}) custom-call(s32[1]{0:T(128)} %bitcast.me_ref, bf16[4096,1024]{1,0:T(8,128)(2,1)} %get-tuple-element.160.normed_ref, bf16[4096,384]{1,0:T(8,128)(2,1)} %attend_back.3.grad_ref.refs_1_, bf16[1024,256]{1,0:T(8,128)(2,1)} %refs_5_.12, ...), custom_call_target="tpu_custom_call" | custom-call | flops 1 | bytes 1 | tf_op jit(solution)/shard_map/weight_step/pallas_call | solution.py:375
  505.1 1.5 pack.1
  506.7 1.5 collective-permute-start.35
  508.2 3.1 stack_step.2.even_ref
  511.2 4.4 collective-permute-done.35
  515.6 5.2 unproject.4
  520.8 5.1 unproject.5
  528.2 5.5 unproject.6
  534.7 5.7 unproject.7.refs_0_
  540.4 2.5 late_step.1
  542.9 3.5 collective-permute-start.40
  547.3 7.0 %collective-permute-done.40 = bf16[128,1024]{1,0:T(8,128)(2,1)S(1)} collective-permute-done((bf16[128,1024]{1,0:T(8,128)(2,1)}, bf16[128,1024]{1,0:T(8,128)(2,1)S(1)}, u32[]{:S(2)}, u32[]{:S(2)}) %collective-permute-start.40) | collective-permute-done | bytes 262176 | tf_op jit(solution)/shard_map/ppermute | solution.py:1096
  554.3 13.4 %collective-permute-done.39 = bf16[128,1024]{1,0:T(8,128)(2,1)S(1)} collective-permute-done((bf16[128,1024]{1,0:T(8,128)(2,1)}, bf16[128,1024]{1,0:T(8,128)(2,1)S(1)}, u32[]{:S(2)}, u32[]{:S(2)}) %collective-permute-start.39) | collective-permute-done | bytes 262176 | tf_op jit(solution)/shard_map/ppermute | solution.py:1096
  568.9 2.9 collective-permute-start.42
  571.8 1.5 collective-permute-start.43
  573.3 4.1 add_convert_fusion
  577.4 2.7 collective-permute-done.41.refs_1_
  580.0 10.3 %collective-permute-done.42.refs_2_ = bf16[128,1024]{1,0:T(8,128)(2,1)S(1)} collective-permute-done((bf16[128,1024]{1,0:T(8,128)(2,1)S(1)}, bf16[128,1024]{1,0:T(8,128)(2,1)S(1)}, u32[]{:S(2)}, u32[]{:S(2)}) %collective-permute-start.42) | collective-permute-done | bytes 262176 | tf_op jit(solution)/shard_map/ppermute | solution.py:1096
  591.8 2.2 stack_step.3.even_ref
  594.0 1.5 collective-permute-start.50
  595.5 3.1 collective-permute-start.46
  598.6 2.2 collective-permute-done.46
  600.8 3.3 collective-permute-start.47
  604.2 2.2 collective-permute-done.47
  607.6 2.9 collective-permute-done.48
  611.6 7.1 %feed_grads.1 = (f32[1024,1024]{1,0:T(8,128)}, f32[1024,1024]{1,0:T(8,128)}) custom-call(s32[1]{0:T(128)} %bitcast.me_ref, bf16[1024,1024]{1,0:T(8,128)(2,1)} %stack_step.2.even_ref, bf16[1024,1024]{1,0:T(8,128)(2,1)} %collective-permute-done.44.odd_ref), custom_call_target="tpu_custom_call" | custom-call | flops 1 | bytes 1 | tf_op jit(solution)/shard_map/feed_grads/pallas_call | solution.py:375
  618.7 7.7 %input_step.1 = f32[1024,1024]{1,0:T(8,128)} custom-call(bf16[1024,1024]{1,0:T(8,128)(2,1)} %unproject.7.refs_0_, bf16[1024,1024]{1,0:T(8,128)(2,1)} %collective-permute-done.45.refs_1_, bf16[1024,1024]{1,0:T(8,128)(2,1)} %refs_2_.23, f32[1024,1024]{1,0:T(8,128)} %get-tuple-element.277.refs_3_, bf16[1024]{0:T(1024)(128)(2,1)} %refs_4_.17), custom_call_target="tpu_custom_call" | custom-call | flops 1 | bytes 1 | tf_op jit(solution)/shard_map/input_step/pallas_call | solution.py:375
  627.4 4.0 spread.1
  (160 shorter events, 37.0 us)
Async XLA Ops:
  0.7 52.8 %copy-start.1 = (bf16[1024,1024]{1,0:T(8,128)(2,1)S(1)}, bf16[1024,1024]{1,0:T(8,128)(2,1)}, u32[]{:S(2)}) copy-start(bf16[1024,1024]{1,0:T(8,128)(2,1)} %refs_3_.17) | copy-start | bytes 6291460
  0.7 54.6 %copy-start.15 = (bf16[256,1024]{1,0:T(8,128)(2,1)S(1)}, bf16[256,1024]{1,0:T(8,128)(2,1)}, u32[]{:S(2)}) copy-start(bf16[256,1024]{1,0:T(8,128)(2,1)} %refs_5_.8) | copy-start | bytes 1572868
  0.7 4.5 collective-permute-start.1
  1.2 49.1 %collective-permute-start = (bf16[1024,1024]{1,0:T(8,128)(2,1)}, bf16[1024,1024]{1,0:T(8,128)(2,1)}, u32[]{:S(2)}, u32[]{:S(2)}) collective-permute-start(bf16[1024,1024]{1,0:T(8,128)(2,1)} %refs_2_.23), channel_id=1, source_target_pairs={{0,2},{1,3},{2,0},{3,1},{4,6},{5,7},{6,4},{7,5},{8,10},{9,11},{10,... | collective-permute-start | bytes 6291464 | tf_op jit(solution)/shard_map/ppermute | solution.py:1084
  50.3 5.2 collective-permute-start.2
  53.5 49.2 %collective-permute-start.3 = (bf16[1024,1024]{1,0:T(8,128)(2,1)S(1)}, bf16[1024,1024]{1,0:T(8,128)(2,1)}, u32[]{:S(2)}, u32[]{:S(2)}) collective-permute-start(bf16[1024,1024]{1,0:T(8,128)(2,1)S(1)} %copy-done.1), channel_id=1, source_target_pairs={{0,2},{1,3},{2,0},{3,1},{4,6},{5,7},{6,4},{7,5},{8,10},{9,11},{10,... | collective-permute-start | bytes 6291464 | tf_op jit(solution)/shard_map/ppermute | solution.py:1084
  55.2 85.8 %collective-permute-start.10 = (bf16[256,1024]{1,0:T(8,128)(2,1)S(1)}, bf16[256,1024]{1,0:T(8,128)(2,1)S(1)}, u32[]{:S(2)}, u32[]{:S(2)}) collective-permute-start(bf16[256,1024]{1,0:T(8,128)(2,1)S(1)} %copy-done.15), channel_id=1, source_target_pairs={{0,2},{1,3},{2,0},{3,1},{4,6},{5,7},{6,4},{7,5},{8,10},{9,11},{10,... | collective-permute-start | bytes 1572872 | tf_op jit(solution)/shard_map/ppermute | solution.py:1084
  100.9 42.2 %collective-permute-start.6 = (bf16[4096,128]{1,0:T(8,128)(2,1)}, bf16[4096,128]{1,0:T(8,128)(2,1)S(1)}, u32[]{:S(2)}, u32[]{:S(2)}) collective-permute-start(bf16[4096,128]{1,0:T(8,128)(2,1)} %get-tuple-element.164.refs_0_.refs_6_), channel_id=1, source_target_pairs={{0,2},{1,3},{2,0},{3,1},{4,6},{5,7},{6,4},{7,5},{8,10},{9,11},{10,... | collective-permute-start | bytes 3145736 | tf_op jit(solution)/shard_map/ppermute | solution.py:1084
  102.7 41.0 %collective-permute-start.9 = (bf16[1024,1024]{1,0:T(8,128)(2,1)}, bf16[1024,1024]{1,0:T(8,128)(2,1)}, u32[]{:S(2)}, u32[]{:S(2)}) collective-permute-start(bf16[1024,1024]{1,0:T(8,128)(2,1)} %collective-permute-done.3.refs_2_), channel_id=1, source_target_pairs={{0,1},{1,0},{2,3},{3,2},{4,5},{5,4},{6,7},{7,6},{8,9},{9,8},{10,11... | collective-permute-start | bytes 6291464 | tf_op jit(solution)/shard_map/ppermute | solution.py:1084
  102.7 40.9 %collective-permute-start.8 = (bf16[1024,1024]{1,0:T(8,128)(2,1)S(1)}, bf16[1024,1024]{1,0:T(8,128)(2,1)}, u32[]{:S(2)}, u32[]{:S(2)}) collective-permute-start(bf16[1024,1024]{1,0:T(8,128)(2,1)S(1)} %copy-done.1), channel_id=1, source_target_pairs={{0,1},{1,0},{2,3},{3,2},{4,5},{5,4},{6,7},{7,6},{8,9},{9,8},{10,11... | collective-permute-start | bytes 6291464 | tf_op jit(solution)/shard_map/ppermute | solution.py:1084
  103.2 39.8 %copy-start.4 = (bf16[4096,128]{1,0:T(8,128)(2,1)S(1)}, bf16[4096,128]{1,0:T(8,128)(2,1)}, u32[]{:S(2)}) copy-start(bf16[4096,128]{1,0:T(8,128)(2,1)} %get-tuple-element.164.refs_0_.refs_6_) | copy-start | bytes 3145732
  139.9 25.3 %collective-permute-start.7 = (bf16[4096,128]{1,0:T(8,128)(2,1)}, bf16[4096,128]{1,0:T(8,128)(2,1)S(1)}, u32[]{:S(2)}, u32[]{:S(2)}) collective-permute-start(bf16[4096,128]{1,0:T(8,128)(2,1)} %get-tuple-element.169.refs_1_.refs_6_), channel_id=1, source_target_pairs={{0,2},{1,3},{2,0},{3,1},{4,6},{5,7},{6,4},{7,5},{8,10},{9,11},{10,... | collective-permute-start | bytes 3145736 | tf_op jit(solution)/shard_map/ppermute | solution.py:1084
  141.0 2.0 collective-permute-start.11
  143.0 25.4 %collective-permute-start.4 = (bf16[4096,128]{1,0:T(8,128)(2,1)S(1)}, bf16[4096,128]{1,0:T(8,128)(2,1)S(1)}, u32[]{:S(2)}, u32[]{:S(2)}) collective-permute-start(bf16[4096,128]{1,0:T(8,128)(2,1)S(1)} %copy-done.4), channel_id=1, source_target_pairs={{0,1},{1,0},{2,3},{3,2},{4,5},{5,4},{6,7},{7,6},{8,9},{9,8},{10,11... | collective-permute-start | bytes 3145736 | tf_op jit(solution)/shard_map/ppermute | solution.py:1084
  143.2 15.8 %copy-start.5 = (bf16[4096,128]{1,0:T(8,128)(2,1)}, bf16[4096,128]{1,0:T(8,128)(2,1)S(1)}, u32[]{:S(2)}) copy-start(bf16[4096,128]{1,0:T(8,128)(2,1)S(1)} %collective-permute-done.6.refs_4_) | copy-start | bytes 3145732
  143.2 25.3 %collective-permute-start.5 = (bf16[4096,128]{1,0:T(8,128)(2,1)}, bf16[4096,128]{1,0:T(8,128)(2,1)S(1)}, u32[]{:S(2)}, u32[]{:S(2)}) collective-permute-start(bf16[4096,128]{1,0:T(8,128)(2,1)} %get-tuple-element.169.refs_1_.refs_6_), channel_id=1, source_target_pairs={{0,1},{1,0},{2,3},{3,2},{4,5},{5,4},{6,7},{7,6},{8,9},{9,8},{10,11... | collective-permute-start | bytes 3145736 | tf_op jit(solution)/shard_map/ppermute | solution.py:1084
  143.6 24.9 %collective-permute-start.12 = (bf16[4096,128]{1,0:T(8,128)(2,1)S(1)}, bf16[4096,128]{1,0:T(8,128)(2,1)S(1)}, u32[]{:S(2)}, u32[]{:S(2)}) collective-permute-start(bf16[4096,128]{1,0:T(8,128)(2,1)S(1)} %collective-permute-done.6.refs_4_), channel_id=1, source_target_pairs={{0,1},{1,0},{2,3},{3,2},{4,5},{5,4},{6,7},{7,6},{8,9},{9,8},{10,11... | collective-permute-start | bytes 3145736 | tf_op jit(solution)/shard_map/ppermute | solution.py:1084
  165.2 3.4 collective-permute-start.13
  165.2 3.2 collective-permute-start.14
  205.8 12.1 %collective-permute-start.16 = (bf16[1024,1024]{1,0:T(8,128)(2,1)}, bf16[1024,1024]{1,0:T(8,128)(2,1)S(1)}, u32[]{:S(2)}, u32[]{:S(2)}) collective-permute-start(bf16[1024,1024]{1,0:T(8,128)(2,1)} %get-tuple-element.183), channel_id=1, source_target_pairs={{0,1},{1,0},{2,3},{3,2},{4,5},{5,4},{6,7},{7,6},{8,9},{9,8},{10,11... | collective-permute-start | bytes 6291464 | tf_op jit(solution)/shard_map/ppermute | solution.py:1084
  217.8 15.0 %collective-permute-start.15 = (bf16[1024,1024]{1,0:T(8,128)(2,1)}, bf16[1024,1024]{1,0:T(8,128)(2,1)S(1)}, u32[]{:S(2)}, u32[]{:S(2)}) collective-permute-start(bf16[1024,1024]{1,0:T(8,128)(2,1)} %get-tuple-element.182), channel_id=1, source_target_pairs={{0,1},{1,0},{2,3},{3,2},{4,5},{5,4},{6,7},{7,6},{8,9},{9,8},{10,11... | collective-permute-start | bytes 6291464 | tf_op jit(solution)/shard_map/ppermute | solution.py:1084
  231.8 48.3 %collective-permute-start.17 = (bf16[1024,1024]{1,0:T(8,128)(2,1)}, bf16[1024,1024]{1,0:T(8,128)(2,1)}, u32[]{:S(2)}, u32[]{:S(2)}) collective-permute-start(bf16[1024,1024]{1,0:T(8,128)(2,1)} %get-tuple-element.196), channel_id=1, source_target_pairs={{0,2},{1,3},{2,0},{3,1},{4,6},{5,7},{6,4},{7,5},{8,10},{9,11},{10,... | collective-permute-start | bytes 6291464 | tf_op jit(solution)/shard_map/ppermute | solution.py:1084
  260.3 52.8 %collective-permute-start.21 = (bf16[512,1024]{1,0:T(8,128)(2,1)}, bf16[512,1024]{1,0:T(8,128)(2,1)S(1)}, u32[]{:S(2)}, u32[]{:S(2)}) collective-permute-start(bf16[512,1024]{1,0:T(8,128)(2,1)} %get-tuple-element.207), channel_id=1, source_target_pairs={{0,4},{4,0},{8,12},{12,8},{16,20},{20,16},{24,28},{28,24},{1,5},{5... | collective-permute-start | bytes 3145736 | tf_op jit(solution)/shard_map/ppermute | solution.py:1096
  275.1 37.9 %collective-permute-start.22 = (bf16[512,1024]{1,0:T(8,128)(2,1)}, bf16[512,1024]{1,0:T(8,128)(2,1)S(1)}, u32[]{:S(2)}, u32[]{:S(2)}) collective-permute-start(bf16[512,1024]{1,0:T(8,128)(2,1)} %get-tuple-element.208), channel_id=1, source_target_pairs={{0,4},{4,0},{8,12},{12,8},{16,20},{20,16},{24,28},{28,24},{1,5},{5... | collective-permute-start | bytes 3145736 | tf_op jit(solution)/shard_map/ppermute | solution.py:1096
  290.2 28.4 %collective-permute-start.18 = (bf16[1024,256]{1,0:T(8,128)(2,1)}, bf16[1024,256]{1,0:T(8,128)(2,1)S(1)}, u32[]{:S(2)}, u32[]{:S(2)}) collective-permute-start(bf16[1024,256]{1,0:T(8,128)(2,1)} %get-tuple-element.199), channel_id=1, source_target_pairs={{0,1},{1,0},{2,3},{3,2},{4,5},{5,4},{6,7},{7,6},{8,9},{9,8},{10,11... | collective-permute-start | bytes 1572872 | tf_op jit(solution)/shard_map/ppermute | solution.py:1084
  290.3 28.3 %collective-permute-start.19 = (bf16[1024,256]{1,0:T(8,128)(2,1)}, bf16[1024,256]{1,0:T(8,128)(2,1)S(1)}, u32[]{:S(2)}, u32[]{:S(2)}) collective-permute-start(bf16[1024,256]{1,0:T(8,128)(2,1)} %get-tuple-element.200), channel_id=1, source_target_pairs={{0,2},{1,3},{2,0},{3,1},{4,6},{5,7},{6,4},{7,5},{8,10},{9,11},{10,... | collective-permute-start | bytes 1572872 | tf_op jit(solution)/shard_map/ppermute | solution.py:1084
  291.4 27.2 %collective-permute-start.20 = (bf16[1024,256]{1,0:T(8,128)(2,1)}, bf16[1024,256]{1,0:T(8,128)(2,1)S(1)}, u32[]{:S(2)}, u32[]{:S(2)}) collective-permute-start(bf16[1024,256]{1,0:T(8,128)(2,1)} %get-tuple-element.201), channel_id=1, source_target_pairs={{0,3},{1,2},{2,1},{3,0},{4,7},{5,6},{6,5},{7,4},{8,11},{9,10},{10,... | collective-permute-start | bytes 1572872 | tf_op jit(solution)/shard_map/ppermute | solution.py:1084
  318.7 75.0 %collective-permute-start.23 = (bf16[2048,256]{1,0:T(8,128)(2,1)}, bf16[2048,256]{1,0:T(8,128)(2,1)S(1)}, u32[]{:S(2)}, u32[]{:S(2)}) collective-permute-start(bf16[2048,256]{1,0:T(8,128)(2,1)} %get-tuple-element.218), channel_id=1, source_target_pairs={{0,1},{1,0},{2,3},{3,2},{4,5},{5,4},{6,7},{7,6},{8,9},{9,8},{10,11... | collective-permute-start | bytes 3145736 | tf_op jit(solution)/shard_map/ppermute | solution.py:1084
  319.1 76.9 %collective-permute-start.27 = (bf16[256,1024]{1,0:T(8,128)(2,1)}, bf16[256,1024]{1,0:T(8,128)(2,1)S(1)}, u32[]{:S(2)}, u32[]{:S(2)}) collective-permute-start(bf16[256,1024]{1,0:T(8,128)(2,1)} %get-tuple-element.233), channel_id=1, source_target_pairs={{0,24},{4,28},{8,16},{12,20},{16,8},{20,12},{24,0},{28,4},{1,25},{... | collective-permute-start | bytes 1572872 | tf_op jit(solution)/shard_map/ppermute | solution.py:1096
  322.7 73.3 %collective-permute-start.26 = (bf16[256,1024]{1,0:T(8,128)(2,1)}, bf16[256,1024]{1,0:T(8,128)(2,1)S(1)}, u32[]{:S(2)}, u32[]{:S(2)}) collective-permute-start(bf16[256,1024]{1,0:T(8,128)(2,1)} %get-tuple-element.232), channel_id=1, source_target_pairs={{0,16},{4,20},{8,24},{12,28},{16,0},{20,4},{24,8},{28,12},{1,17},{... | collective-permute-start | bytes 1572872 | tf_op jit(solution)/shard_map/ppermute | solution.py:1096
  322.7 73.3 %collective-permute-start.25 = (bf16[256,1024]{1,0:T(8,128)(2,1)}, bf16[256,1024]{1,0:T(8,128)(2,1)}, u32[]{:S(2)}, u32[]{:S(2)}) collective-permute-start(bf16[256,1024]{1,0:T(8,128)(2,1)} %get-tuple-element.231), channel_id=1, source_target_pairs={{0,8},{4,12},{8,0},{12,4},{16,24},{20,28},{24,16},{28,20},{1,9},{5... | collective-permute-start | bytes 1572872 | tf_op jit(solution)/shard_map/ppermute | solution.py:1096
  323.5 89.5 %collective-permute-start.28 = (bf16[2048,1024]{1,0:T(8,128)(2,1)}, bf16[2048,1024]{1,0:T(8,128)(2,1)}, u32[]{:S(2)}, u32[]{:S(2)}) collective-permute-start(bf16[2048,1024]{1,0:T(8,128)(2,1)} %get-tuple-element.235), channel_id=1, source_target_pairs={{0,1},{1,0},{2,3},{3,2},{4,5},{5,4},{6,7},{7,6},{8,9},{9,8},{10,11... | collective-permute-start | bytes 12582920 | tf_op jit(solution)/shard_map/ppermute | solution.py:1084
  323.5 70.2 %copy-start.18 = (bf16[2048,256]{1,0:T(8,128)(2,1)S(1)}, bf16[2048,256]{1,0:T(8,128)(2,1)}, u32[]{:S(2)}) copy-start(bf16[2048,256]{1,0:T(8,128)(2,1)} %get-tuple-element.217) | copy-start | bytes 3145732
  394.9 14.5 %collective-permute-start.24 = (bf16[1024,256]{1,0:T(8,128)(2,1)}, bf16[1024,256]{1,0:T(8,128)(2,1)S(1)}, u32[]{:S(2)}, u32[]{:S(2)}) collective-permute-start(bf16[1024,256]{1,0:T(8,128)(2,1)} %get-tuple-element.222), channel_id=1, source_target_pairs={{0,2},{1,3},{2,0},{3,1},{4,6},{5,7},{6,4},{7,5},{8,10},{9,11},{10,... | collective-permute-start | bytes 1572872 | tf_op jit(solution)/shard_map/ppermute | solution.py:1084
  397.4 24.3 %copy-start.14 = (bf16[256,1024]{1,0:T(8,128)(2,1)}, bf16[256,1024]{1,0:T(8,128)(2,1)S(1)}, u32[]{:S(2)}) copy-start(bf16[256,1024]{1,0:T(8,128)(2,1)S(1)} %add_convert_fusion.3.refs_0_) | copy-start | bytes 1572868
  397.4 15.5 %copy-start.3 = (bf16[2048,1024]{1,0:T(8,128)(2,1)S(1)}, bf16[2048,1024]{1,0:T(8,128)(2,1)}, u32[]{:S(2)}) copy-start(bf16[2048,1024]{1,0:T(8,128)(2,1)} %get-tuple-element.234) | copy-start | bytes 12582916
  417.5 77.0 %collective-permute-start.30 = (bf16[256,1024]{1,0:T(8,128)(2,1)S(1)}, bf16[256,1024]{1,0:T(8,128)(2,1)S(1)}, u32[]{:S(2)}, u32[]{:S(2)}) collective-permute-start(bf16[256,1024]{1,0:T(8,128)(2,1)S(1)} %add_convert_fusion.3.refs_0_), channel_id=1, source_target_pairs={{0,8},{4,12},{8,0},{12,4},{16,24},{20,28},{24,16},{28,20},{1,9},{5... | collective-permute-start | bytes 1572872 | tf_op jit(solution)/shard_map/ppermute | solution.py:1096
  418.8 75.7 %collective-permute-start.31 = (bf16[256,1024]{1,0:T(8,128)(2,1)S(1)}, bf16[256,1024]{1,0:T(8,128)(2,1)}, u32[]{:S(2)}, u32[]{:S(2)}) collective-permute-start(bf16[256,1024]{1,0:T(8,128)(2,1)S(1)} %add_convert_fusion.3.refs_0_), channel_id=1, source_target_pairs={{0,16},{4,20},{8,24},{12,28},{16,0},{20,4},{24,8},{28,12},{1,17},{... | collective-permute-start | bytes 1572872 | tf_op jit(solution)/shard_map/ppermute | solution.py:1096
  421.7 72.8 %collective-permute-start.32 = (bf16[256,1024]{1,0:T(8,128)(2,1)S(1)}, bf16[256,1024]{1,0:T(8,128)(2,1)}, u32[]{:S(2)}, u32[]{:S(2)}) collective-permute-start(bf16[256,1024]{1,0:T(8,128)(2,1)S(1)} %add_convert_fusion.3.refs_0_), channel_id=1, source_target_pairs={{0,24},{4,28},{8,16},{12,20},{16,8},{20,12},{24,0},{28,4},{1,25},{... | collective-permute-start | bytes 1572872 | tf_op jit(solution)/shard_map/ppermute | solution.py:1096
  421.9 72.6 %collective-permute-start.29 = (bf16[512,640]{1,0:T(8,128)(2,1)}, bf16[512,640]{1,0:T(8,128)(2,1)S(1)}, u32[]{:S(2)}, u32[]{:S(2)}) collective-permute-start(bf16[512,640]{1,0:T(8,128)(2,1)} %get-tuple-element.240), channel_id=1, source_target_pairs={{0,4},{4,0},{8,12},{12,8},{16,20},{20,16},{24,28},{28,24},{1,5},{5... | collective-permute-start | bytes 1966088 | tf_op jit(solution)/shard_map/ppermute | solution.py:1096
  423.4 71.1 %collective-permute-start.33 = (bf16[1024,1024]{1,0:T(8,128)(2,1)}, bf16[1024,1024]{1,0:T(8,128)(2,1)}, u32[]{:S(2)}, u32[]{:S(2)}) collective-permute-start(bf16[1024,1024]{1,0:T(8,128)(2,1)} %get-tuple-element.243), channel_id=1, source_target_pairs={{0,2},{1,3},{2,0},{3,1},{4,6},{5,7},{6,4},{7,5},{8,10},{9,11},{10,... | collective-permute-start | bytes 6291464 | tf_op jit(solution)/shard_map/ppermute | solution.py:1084
  494.5 10.0 %copy-start.26 = (bf16[256,1024]{1,0:T(8,128)(2,1)}, bf16[256,1024]{1,0:T(8,128)(2,1)S(1)}, u32[]{:S(2)}) copy-start(bf16[256,1024]{1,0:T(8,128)(2,1)S(1)} %collective-permute-done.30.refs_1_) | copy-start | bytes 1572868
  494.5 10.0 %copy-start.23 = (bf16[512,640]{1,0:T(8,128)(2,1)}, bf16[512,640]{1,0:T(8,128)(2,1)S(1)}, u32[]{:S(2)}) copy-start(bf16[512,640]{1,0:T(8,128)(2,1)S(1)} %collective-permute-done.29.refs_1_) | copy-start | bytes 1966084
  504.5 11.1 %collective-permute-start.34 = (bf16[512,384]{1,0:T(8,128)(2,1)}, bf16[512,384]{1,0:T(8,128)(2,1)S(1)}, u32[]{:S(2)}, u32[]{:S(2)}) collective-permute-start(bf16[512,384]{1,0:T(8,128)(2,1)} %get-tuple-element.261), channel_id=1, source_target_pairs={{0,4},{4,0},{8,12},{12,8},{16,20},{20,16},{24,28},{28,24},{1,5},{5... | collective-permute-start | bytes 1179656 | tf_op jit(solution)/shard_map/ppermute | solution.py:1096
  506.7 8.9 %copy-start.28 = (f32[16,1024]{1,0:T(8,128)S(1)}, f32[16,1024]{1,0:T(8,128)}, u32[]{:S(2)}) copy-start(f32[16,1024]{1,0:T(8,128)} %pack.1) | copy-start | bytes 196612
  506.7 8.9 %collective-permute-start.35 = (f32[16,1024]{1,0:T(8,128)}, f32[16,1024]{1,0:T(8,128)S(1)}, u32[]{:S(2)}, u32[]{:S(2)}) collective-permute-start(f32[16,1024]{1,0:T(8,128)} %pack.1), channel_id=1, source_target_pairs={{0,4},{4,0},{8,12},{12,8},{16,20},{20,16},{24,28},{28,24},{1,5},{5... | collective-permute-start | bytes 196616 | tf_op jit(solution)/shard_map/ppermute | solution.py:1096
  520.8 6.1 collective-permute-start.36
  525.9 8.8 %collective-permute-start.37 = (bf16[1024,1024]{1,0:T(8,128)(2,1)}, bf16[1024,1024]{1,0:T(8,128)(2,1)}, u32[]{:S(2)}, u32[]{:S(2)}) collective-permute-start(bf16[1024,1024]{1,0:T(8,128)(2,1)} %unproject.5), channel_id=1, source_target_pairs={{0,1},{1,0},{2,3},{3,2},{4,5},{5,4},{6,7},{7,6},{8,9},{9,8},{10,11... | collective-permute-start | bytes 6291464 | tf_op jit(solution)/shard_map/ppermute | solution.py:1084
  526.4 51.0 %collective-permute-start.44 = (bf16[1024,1024]{1,0:T(8,128)(2,1)}, bf16[1024,1024]{1,0:T(8,128)(2,1)}, u32[]{:S(2)}, u32[]{:S(2)}) collective-permute-start(bf16[1024,1024]{1,0:T(8,128)(2,1)} %stack_step.2.even_ref), channel_id=1, source_target_pairs={{0,4},{4,0},{8,12},{12,8},{16,20},{20,16},{24,28},{28,24},{1,5},{5... | collective-permute-start | bytes 6291464 | tf_op jit(solution)/shard_map/ppermute | solution.py:1096
  533.7 72.7 %collective-permute-start.45 = (bf16[1024,1024]{1,0:T(8,128)(2,1)}, bf16[1024,1024]{1,0:T(8,128)(2,1)}, u32[]{:S(2)}, u32[]{:S(2)}) collective-permute-start(bf16[1024,1024]{1,0:T(8,128)(2,1)} %unproject.6), channel_id=1, source_target_pairs={{0,2},{1,3},{2,0},{3,1},{4,6},{5,7},{6,4},{7,5},{8,10},{9,11},{10,... | collective-permute-start | bytes 6291464 | tf_op jit(solution)/shard_map/ppermute | solution.py:1084
  534.7 38.6 %copy-start = (f32[1024,1024]{1,0:T(8,128)S(1)}, f32[1024,1024]{1,0:T(8,128)}, u32[]{:S(2)}) copy-start(f32[1024,1024]{1,0:T(8,128)} %get-tuple-element.197.refs_2_) | copy-start | bytes 12582916
  542.9 11.4 %collective-permute-start.40 = (bf16[128,1024]{1,0:T(8,128)(2,1)}, bf16[128,1024]{1,0:T(8,128)(2,1)S(1)}, u32[]{:S(2)}, u32[]{:S(2)}) collective-permute-start(bf16[128,1024]{1,0:T(8,128)(2,1)} %get-tuple-element.270), channel_id=1, source_target_pairs={{0,24},{4,28},{8,16},{12,20},{16,8},{20,12},{24,0},{28,4},{1,25},{... | collective-permute-start | bytes 786440 | tf_op jit(solution)/shard_map/ppermute | solution.py:1096
  546.5 21.2 %collective-permute-start.39 = (bf16[128,1024]{1,0:T(8,128)(2,1)}, bf16[128,1024]{1,0:T(8,128)(2,1)S(1)}, u32[]{:S(2)}, u32[]{:S(2)}) collective-permute-start(bf16[128,1024]{1,0:T(8,128)(2,1)} %get-tuple-element.269), channel_id=1, source_target_pairs={{0,16},{4,20},{8,24},{12,28},{16,0},{20,4},{24,8},{28,12},{1,17},{... | collective-permute-start | bytes 786440 | tf_op jit(solution)/shard_map/ppermute | solution.py:1096
  546.5 21.2 %collective-permute-start.38 = (bf16[128,1024]{1,0:T(8,128)(2,1)}, bf16[128,1024]{1,0:T(8,128)(2,1)S(1)}, u32[]{:S(2)}, u32[]{:S(2)}) collective-permute-start(bf16[128,1024]{1,0:T(8,128)(2,1)} %get-tuple-element.268), channel_id=1, source_target_pairs={{0,8},{4,12},{8,0},{12,4},{16,24},{20,28},{24,16},{28,20},{1,9},{5... | collective-permute-start | bytes 786440 | tf_op jit(solution)/shard_map/ppermute | solution.py:1096
  568.8 8.5 %copy-start.22 = (bf16[128,1024]{1,0:T(8,128)(2,1)}, bf16[128,1024]{1,0:T(8,128)(2,1)S(1)}, u32[]{:S(2)}) copy-start(bf16[128,1024]{1,0:T(8,128)(2,1)S(1)} %add_convert_fusion.6.refs_0_) | copy-start | bytes 786436
  568.8 11.2 %collective-permute-start.41 = (bf16[128,1024]{1,0:T(8,128)(2,1)S(1)}, bf16[128,1024]{1,0:T(8,128)(2,1)S(1)}, u32[]{:S(2)}, u32[]{:S(2)}) collective-permute-start(bf16[128,1024]{1,0:T(8,128)(2,1)S(1)} %add_convert_fusion.6.refs_0_), channel_id=1, source_target_pairs={{0,8},{4,12},{8,0},{12,4},{16,24},{20,28},{24,16},{28,20},{1,9},{5... | collective-permute-start | bytes 786440 | tf_op jit(solution)/shard_map/ppermute | solution.py:1096
  568.9 21.4 %collective-permute-start.42 = (bf16[128,1024]{1,0:T(8,128)(2,1)S(1)}, bf16[128,1024]{1,0:T(8,128)(2,1)S(1)}, u32[]{:S(2)}, u32[]{:S(2)}) collective-permute-start(bf16[128,1024]{1,0:T(8,128)(2,1)S(1)} %add_convert_fusion.6.refs_0_), channel_id=1, source_target_pairs={{0,16},{4,20},{8,24},{12,28},{16,0},{20,4},{24,8},{28,12},{1,17},{... | collective-permute-start | bytes 786440 | tf_op jit(solution)/shard_map/ppermute | solution.py:1096
  571.8 18.5 %collective-permute-start.43 = (bf16[128,1024]{1,0:T(8,128)(2,1)S(1)}, bf16[128,1024]{1,0:T(8,128)(2,1)S(1)}, u32[]{:S(2)}, u32[]{:S(2)}) collective-permute-start(bf16[128,1024]{1,0:T(8,128)(2,1)S(1)} %add_convert_fusion.6.refs_0_), channel_id=1, source_target_pairs={{0,24},{4,28},{8,16},{12,20},{16,8},{20,12},{24,0},{28,4},{1,25},{... | collective-permute-start | bytes 786440 | tf_op jit(solution)/shard_map/ppermute | solution.py:1096
  580.0 10.3 %copy-start.29 = (bf16[128,1024]{1,0:T(8,128)(2,1)}, bf16[128,1024]{1,0:T(8,128)(2,1)S(1)}, u32[]{:S(2)}) copy-start(bf16[128,1024]{1,0:T(8,128)(2,1)S(1)} %collective-permute-done.41.refs_1_) | copy-start | bytes 786436
  594.0 32.4 %collective-permute-start.50 = (bf16[512,1024]{1,0:T(8,128)(2,1)}, bf16[512,1024]{1,0:T(8,128)(2,1)S(1)}, u32[]{:S(2)}, u32[]{:S(2)}) collective-permute-start(bf16[512,1024]{1,0:T(8,128)(2,1)} %stack_step.3.even_ref), channel_id=1, source_target_pairs={{0,4},{4,0},{8,12},{12,8},{16,20},{20,16},{24,28},{28,24},{1,5},{5... | collective-permute-start | bytes 3145736 | tf_op jit(solution)/shard_map/ppermute | solution.py:1096
  595.5 5.3 collective-permute-start.46
  600.8 5.6 collective-permute-start.47
  606.4 4.0 collective-permute-start.48
  610.4 20.9 %collective-permute-start.49 = (f32[8,1024]{1,0:T(8,128)S(1)}, f32[8,1024]{1,0:T(8,128)S(1)}, u32[]{:S(2)}, u32[]{:S(2)}) collective-permute-start(f32[8,1024]{1,0:T(8,128)S(1)} %slice_add_fusion), channel_id=1, source_target_pairs={{0,1},{1,0},{2,3},{3,2},{4,5},{5,4},{6,7},{7,6},{8,9},{9,8},{10,11... | collective-permute-start | bytes 98312 | tf_op jit(solution)/shard_map/ppermute | solution.py:1084
  (23 other events, 49.9 us)

commit v6 on v5

--- a/solution.py
+++ b/solution.py
@@ -1317,8 +1317,15 @@
         [(early_keep, early_come), (after(late_keep, normed_terms[0]), late_come)], streams // 2
     )
     layer_output = low(residual + add_up(ffn_terms) + down_bias.astype(F32))
-    *late_shards, feed_odd, layer_output = lax.optimization_barrier(
-        (*collect_far(exchange(late_parts)), feed_odd, layer_output)
+    up_grad, down_grad = feed_grads(feed_even, feed_odd, stream, streams)
+    input_grad = input_step(
+        [*normed_terms[:-1], after(normed_terms[-1], up_grad)],
+        layer_input,
+        resid_grad,
+        input_gain,
+    )
+    *late_shards, layer_output, input_grad = lax.optimization_barrier(
+        (*collect_far(exchange(late_parts)), layer_output, input_grad)
     )
     late_even = stack_step(late_shards)
     late_odd = swap_data(late_even, 1)
@@ -1329,14 +1336,10 @@
     for bit in reversed(bits):
         shared = shared + swap(shared, bit)
     shared = shared[:, : resid_grad.shape[1]]
-    up_grad, down_grad = feed_grads(after(feed_even, late_even), feed_odd, stream, streams)
     up_bias_grad = own[0, : up_bias.shape[0]]
     counts = own[1 : 1 + groups]
     query_bias_grad = counts[:, :cols].reshape(-1)
     value_bias_grad = counts[:, 2 * cols : 3 * cols].reshape(-1)
-    normed_terms[-1] = after(normed_terms[-1], feed_odd)
-    input_grad = input_step(normed_terms, layer_input, resid_grad, input_gain)
-    late_even = after(late_even, input_grad)
     *weight_grads, dense_weight_grad = spread(
         late_even, late_odd, stream, streams, groups, head_cols
     )

time: 641 us -> 633 us (0.988)
  transfers between devices with their start and end apart: 51 -> 51, of which waited for: 16 -> 15; matrix products, arithmetic and copies ran while one was open for 2% -> 2% of each run, Pallas kernels for 64% -> 63%
where the time goes in v6:
time: 633 us; the launch traced here: 624 us
  Pallas kernels  451 us (71%)
  waiting for transfers between devices  93.6 us (15%)
  starting transfers between devices  46.4 us (7%)
  local copies, waits for them, and re-layouts  17.7 us (3%)
  other arithmetic  12.4 us (2%)
    pallas_call x28, Pallas kernels, kernel_call(): pl.pallas_call(kernel, grid=grid, in_specs=in_specs + [pl.BlockSpec(memor...  238 us
    pallas_call x2, Pallas kernels, attend_back(): pl.pallas_call(functools.partial(attend_back_kernel, slots=slots, pair=pa...  140 us
    pallas_call x2, Pallas kernels, attend(): pl.pallas_call(functools.partial(attend_kernel, slots=slots, pair=pair, t...  72.9 us
    ppermute x30, waiting for transfers between devices, swap(): return lax.ppermute(array, 'tensor', [(i, i ^ mask) for i in range(slots)])  56.1 us
    ppermute x21, waiting for transfers between devices, swap_data(): return lax.ppermute(array, 'dp', [(i, i ^ mask) for i in range(streams)])  37.5 us
    ppermute x21, starting transfers between devices, swap_data(): return lax.ppermute(array, 'dp', [(i, i ^ mask) for i in range(streams)])  28.3 us
    ppermute x30, starting transfers between devices, swap(): return lax.ppermute(array, 'tensor', [(i, i ^ mask) for i in range(slots)])  18.1 us
    unnamed x72, local copies, waits for them, and re-layouts  14.1 us
  transfers between devices with their start and end apart: 51, of which 15 were waited for; matrix products, arithmetic and copies ran while one was open for 2% of the time, Pallas kernels for 63%

profile of v6, /device:TPU:0, one launch (start us, length us, event | category | flops | bytes accessed | tf_op | source)
XLA Modules:
  0.0 624.3 jit_solution(6751359150705227270)
XLA Ops:
  1.2 2.6 collective-permute-start
  3.8 1.4 collective-permute-done.1.refs_1_.refs_9_
  6.5 9.2 %project.2 = (bf16[4096,1024]{1,0:T(8,128)(2,1)}, bf16[4096,256]{1,0:T(8,128)(2,1)}, bf16[4096,256]{1,0:T(8,128)(2,1)}, bf16[4096,256]{1,0:T(8,128)(2,1)}) custom-call(bf16[1024,1024]{1,0:T(8,128)(2,1)} %refs_2_.23, bf16[1024,1024]{1,0:T(8,128)(2,1)} %copy-done.2, bf16[1024]{0:T(1024)(128)(2,1)} %refs_4_.17, bf16[1024]{0:T(1024)(128)(2,1)} %refs_2_.18, ...), custom_call_target="tpu_custom_call" | custom-call | flops 1 | bytes 1 | tf_op jit(solution)/shard_map/project/pallas_call | solution.py:375
  15.8 34.6 %collective-permute-done.refs_0_.refs_10_ = bf16[1024,1024]{1,0:T(8,128)(2,1)} collective-permute-done((bf16[1024,1024]{1,0:T(8,128)(2,1)}, bf16[1024,1024]{1,0:T(8,128)(2,1)}, u32[]{:S(2)}, u32[]{:S(2)}) %collective-permute-start) | collective-permute-done | bytes 2097184 | tf_op jit(solution)/shard_map/ppermute | solution.py:1084
  53.5 1.8 collective-permute-start.3
  55.5 9.3 %project.3 = (bf16[4096,1024]{1,0:T(8,128)(2,1)}, bf16[4096,256]{1,0:T(8,128)(2,1)}, bf16[4096,256]{1,0:T(8,128)(2,1)}, bf16[4096,256]{1,0:T(8,128)(2,1)}) custom-call(bf16[1024,1024]{1,0:T(8,128)(2,1)} %collective-permute-done.refs_0_.refs_10_, ...), custom_call_target="tpu_custom_call", output_to_operand_aliasing={{0}: (9, {}), {1}: (10, {}), {2}: (11, {}), {3}: (12, {})} | custom-call | flops 1 | bytes 1 | tf_op jit(solution)/shard_map/project/pallas_call | solution.py:375
  64.8 36.2 %attend.2 = (bf16[4096,128]{1,0:T(8,128)(2,1)}, f32[2,1,4096]{2,1,0:T(1,128)}) custom-call(s32[1]{0:T(128)} %bitcast.1.me_ref.refs_0_, s32[1]{0:T(128)S(6)} %convert_element_type.84.apart_ref.refs_1_, f32[2]{0:T(128)} %get-tuple-element.302.slope_ref.refs_2_, bf16[4096,256]{1,0:T(8,128)(2,1)} %get-tuple-element.166.q_ref.refs_3_, ...), custom_call_target="tpu_custom_call" | custom-call | flops 40265318400 | bytes 4194304 | tf_op jit(solution)/shard_map/attend/pallas_call | solution.py:182
  100.9 1.8 collective-permute-start.6
  103.2 36.7 %attend.3 = (bf16[4096,128]{1,0:T(8,128)(2,1)}, f32[2,1,4096]{2,1,0:T(1,128)}) custom-call(s32[1]{0:T(128)} %bitcast.1.me_ref.refs_0_, s32[1]{0:T(128)S(6)} %convert_element_type.84.apart_ref.refs_1_, f32[2]{0:T(128)} %get-tuple-element.301.slope_ref.refs_2_, bf16[4096,256]{1,0:T(8,128)(2,1)} %get-tuple-element.166.q_ref.refs_3_, ...), custom_call_target="tpu_custom_call" | custom-call | flops 40265318400 | bytes 4194304 | tf_op jit(solution)/shard_map/attend/pallas_call | solution.py:182
  143.7 15.3 %act_grad.1 = (bf16[4096,1024]{1,0:T(8,128)(2,1)}, bf16[4096,1024]{1,0:T(8,128)(2,1)}) custom-call(bf16[1024,1024]{1,0:T(8,128)(2,1)} %refs_3_.17, bf16[1024,1024]{1,0:T(8,128)(2,1)} %collective-permute-done.8.refs_1_, bf16[1024,1024]{1,0:T(8,128)(2,1)} %collective-permute-done.3.refs_2_, bf16[1024,1024]{1,0:T(8,128)(2,1)} %collective-permute-done.9.refs_3_, ...), custom_call_target="tpu_custom_call" | custom-call | flops 1 | bytes 1 | tf_op jit(solution)/shard_map/act_grad/pallas_call | solution.py:375
  159.0 6.2 collective-permute-done.7.refs_5_
  165.7 2.7 collective-permute-done.14.refs_13_.refs_6_
  171.4 22.8 %post_norm.1 = (bf16[4096,1024]{1,0:T(8,128)(2,1)}, f32[1024,1024]{1,0:T(8,128)}) custom-call(bf16[4096,128]{1,0:T(8,128)(2,1)} %get-tuple-element.162.refs_0_.refs_6_, bf16[4096,128]{1,0:T(8,128)(2,1)} %get-tuple-element.167.refs_1_.refs_6_, bf16[4096,128]{1,0:T(8,128)(2,1)} %copy-done.7, bf16[4096,128]{1,0:T(8,128)(2,1)} %copy-done.8, ...), custom_call_target="tpu_custom_call" | custom-call | flops 1 | bytes 1 | tf_op jit(solution)/shard_map/post_norm/pallas_call | solution.py:375
  194.1 11.7 %feed.4 = (bf16[4096,1024]{1,0:T(8,128)(2,1)}, bf16[4096,1024]{1,0:T(8,128)(2,1)}, f32[1,1024]{1,0:T(1,128)}, bf16[1024,1024]{1,0:T(8,128)(2,1)}) custom-call(bf16[4096,1024]{1,0:T(8,128)(2,1)} %get-tuple-element.176.refs_0_.right_ref, bf16[4096,1024]{1,0:T(8,128)(2,1)} %get-tuple-element.177.refs_1_, bf16[1024,1024]{1,0:T(8,128)(2,1)} %refs_2_.17, ...), custom_call_target="tpu_custom_call" | custom-call | flops 1 | bytes 1 | tf_op jit(solution)/shard_map/feed/pallas_call | solution.py:375
  206.2 11.6 %feed.5 = (bf16[4096,1024]{1,0:T(8,128)(2,1)}, bf16[4096,1024]{1,0:T(8,128)(2,1)}, f32[1,1024]{1,0:T(1,128)}, bf16[1024,1024]{1,0:T(8,128)(2,1)}) custom-call(bf16[4096,1024]{1,0:T(8,128)(2,1)} %get-tuple-element.176.refs_0_.right_ref, bf16[4096,1024]{1,0:T(8,128)(2,1)} %get-tuple-element.177.refs_1_, ...), custom_call_target="tpu_custom_call", output_to_operand_aliasing={{0}: (4, {}), {1}: (5, {})} | custom-call | flops 1 | bytes 1 | tf_op jit(solution)/shard_map/feed/pallas_call | solution.py:375
  217.9 1.3 copy-done.12
  219.2 12.6 %feed.6 = (bf16[4096,1024]{1,0:T(8,128)(2,1)}, bf16[4096,1024]{1,0:T(8,128)(2,1)}, f32[1,1024]{1,0:T(1,128)}, bf16[1024,1024]{1,0:T(8,128)(2,1)}) custom-call(bf16[4096,1024]{1,0:T(8,128)(2,1)} %get-tuple-element.176.refs_0_.right_ref, bf16[4096,1024]{1,0:T(8,128)(2,1)} %get-tuple-element.177.refs_1_, ...), custom_call_target="tpu_custom_call", output_to_operand_aliasing={{0}: (5, {}), {1}: (6, {})} | custom-call | flops 1 | bytes 1 | tf_op jit(solution)/shard_map/feed/pallas_call | solution.py:375
  232.9 1.3 copy-done.11
  234.2 12.8 %feed.7 = (bf16[4096,1024]{1,0:T(8,128)(2,1)}, bf16[4096,1024]{1,0:T(8,128)(2,1)}, f32[1,1024]{1,0:T(1,128)}, bf16[1024,1024]{1,0:T(8,128)(2,1)}) custom-call(bf16[4096,1024]{1,0:T(8,128)(2,1)} %get-tuple-element.176.refs_0_.right_ref, bf16[4096,1024]{1,0:T(8,128)(2,1)} %get-tuple-element.177.refs_1_, ...), custom_call_target="tpu_custom_call", output_to_operand_aliasing={{0}: (5, {}), {1}: (6, {})} | custom-call | flops 1 | bytes 1 | tf_op jit(solution)/shard_map/feed/pallas_call | solution.py:375
  247.0 13.3 %outer_step.2 = (bf16[512,1024]{1,0:T(8,128)(2,1)}, bf16[512,1024]{1,0:T(8,128)(2,1)}) custom-call(s32[1]{0:T(128)} %bitcast.me_ref, bf16[4096,1024]{1,0:T(8,128)(2,1)} %get-tuple-element.189.left_ref, bf16[4096,1024]{1,0:T(8,128)(2,1)} %get-tuple-element.176.refs_0_.right_ref), custom_call_target="tpu_custom_call" | custom-call | flops 1 | bytes 1 | tf_op jit(solution)/shard_map/outer_step/pallas_call | solution.py:375
  260.3 1.5 collective-permute-start.21
  261.8 13.3 %outer_step.3 = (bf16[512,1024]{1,0:T(8,128)(2,1)}, bf16[512,1024]{1,0:T(8,128)(2,1)}) custom-call(s32[1]{0:T(128)} %bitcast.me_ref, bf16[4096,1024]{1,0:T(8,128)(2,1)} %get-tuple-element.202.left_ref.active_ref, bf16[4096,1024]{1,0:T(8,128)(2,1)} %get-tuple-element.191.right_ref), custom_call_target="tpu_custom_call" | custom-call | flops 1 | bytes 1 | tf_op jit(solution)/shard_map/outer_step/pallas_call | solution.py:375
  275.6 4.4 collective-permute-done.17.refs_1_
  280.1 10.2 %resid_step.1 = (f32[1024,1024]{1,0:T(8,128)}, bf16[1024,1024]{1,0:T(8,128)(2,1)}, f32[8,1024]{1,0:T(8,128)}, bf16[1024,256]{1,0:T(8,128)(2,1)}, bf16[1024,256]{...) custom-call(bf16[1024,1024]{1,0:T(8,128)(2,1)} %get-tuple-element.193.refs_0_, ...), custom_call_target="tpu_custom_call" | custom-call | flops 1 | bytes 1 | tf_op jit(solution)/shard_map/resid_step/pallas_call | solution.py:375
  292.2 6.3 %dense_grad.1 = (bf16[2048,256]{1,0:T(8,128)(2,1)}, bf16[2048,256]{1,0:T(8,128)(2,1)}) custom-call(bf16[4096,128]{1,0:T(8,128)(2,1)} %get-tuple-element.162.refs_0_.refs_6_, bf16[4096,128]{1,0:T(8,128)(2,1)} %get-tuple-element.167.refs_1_.refs_6_, bf16[4096,128]{1,0:T(8,128)(2,1)} %copy-done.7, bf16[4096,128]{1,0:T(8,128)(2,1)} %copy-done.8, ...), custom_call_target="tpu_custom_call" | custom-call | flops 1 | bytes 1 | tf_op jit(solution)/shard_map/dense_grad/pallas_call | solution.py:375
  298.5 14.5 %ffn_step.1 = (bf16[2048,1024]{1,0:T(8,128)(2,1)}, bf16[2048,1024]{1,0:T(8,128)(2,1)}) custom-call(bf16[4096,1024]{1,0:T(8,128)(2,1)} %get-tuple-element.202.left_ref.active_ref, bf16[1024,1024]{1,0:T(8,128)(2,1)} %weight_ref.1), custom_call_target="tpu_custom_call" | custom-call | flops 1 | bytes 1 | tf_op jit(solution)/shard_map/ffn_step/pallas_call | solution.py:375
  315.0 3.7 pair_step.1
  319.1 3.6 collective-permute-start.27
  323.5 70.2 %attend_back.2.grad_ref.refs_0_ = bf16[4096,384]{1,0:T(8,128)(2,1)} custom-call(s32[1]{0:T(128)} %bitcast.1.me_ref.refs_0_, s32[1]{0:T(128)S(6)} %convert_element_type.84.apart_ref.refs_1_, f32[2]{0:T(128)} %get-tuple-element.302.slope_ref.refs_2_, bf16[4096,256]{1,0:T(8,128)(2,1)} %get-tuple-element.166.q_ref.refs_3_, ...), custom_call_target="tpu_custom_call" | custom-call | flops 80530636800 | bytes 8388608 | tf_op jit(solution)/shard_map/attend_back/pallas_call | solution.py:312
  396.0 1.4 add_convert_fusion.3.refs_0_
  397.4 9.6 %weight_step.2 = (bf16[1024,384]{1,0:T(8,128)(2,1)}, f32[8,1024]{1,0:T(8,128)}, f32[1,384]{1,0:T(1,128)}) custom-call(s32[1]{0:T(128)} %bitcast.me_ref, bf16[4096,1024]{1,0:T(8,128)(2,1)} %get-tuple-element.158.normed_ref, bf16[4096,384]{1,0:T(8,128)(2,1)} %attend_back.2.grad_ref.refs_0_, bf16[1024,256]{1,0:T(8,128)(2,1)} %refs_5_.12, ...), custom_call_target="tpu_custom_call" | custom-call | flops 1 | bytes 1 | tf_op jit(solution)/shard_map/weight_step/pallas_call | solution.py:375
  407.0 2.4 collective-permute-done.24.refs_2_
  410.3 2.6 join_step.1
  413.0 4.6 add_convert_fusion.1
  418.8 2.9 collective-permute-start.31
  421.9 1.5 collective-permute-start.29
  424.5 70.0 %attend_back.3.grad_ref.refs_1_ = bf16[4096,384]{1,0:T(8,128)(2,1)} custom-call(s32[1]{0:T(128)} %bitcast.1.me_ref.refs_0_, s32[1]{0:T(128)S(6)} %convert_element_type.84.apart_ref.refs_1_, f32[2]{0:T(128)} %get-tuple-element.301.slope_ref.refs_2_, bf16[4096,256]{1,0:T(8,128)(2,1)} %get-tuple-element.166.q_ref.refs_3_, ...), custom_call_target="tpu_custom_call" | custom-call | flops 80530636800 | bytes 8388608 | tf_op jit(solution)/shard_map/attend_back/pallas_call | solution.py:312
  494.6 10.0 %weight_step.3 = (bf16[512,384]{1,0:T(8,128)(2,1)}, bf16[512,384]{1,0:T(8,128)(2,1)}, f32[8,1024]{1,0:T(8,128)}, f32[1,384]{1,0:T(1,128)}) custom-call(s32[1]{0:T(128)} %bitcast.me_ref, bf16[4096,1024]{1,0:T(8,128)(2,1)} %get-tuple-element.158.normed_ref, bf16[4096,384]{1,0:T(8,128)(2,1)} %attend_back.3.grad_ref.refs_1_, bf16[1024,256]{1,0:T(8,128)(2,1)} %refs_5_.12, ...), custom_call_target="tpu_custom_call" | custom-call | flops 1 | bytes 1 | tf_op jit(solution)/shard_map/weight_step/pallas_call | solution.py:375
  505.1 1.5 pack.1
  506.7 1.5 collective-permute-start.35
  508.2 3.1 stack_step.2.even_ref
  511.2 4.4 collective-permute-done.35
  515.6 5.2 unproject.4
  520.8 5.1 unproject.5
  526.9 1.3 copy-done.13
  528.2 5.5 unproject.6
  534.7 5.7 unproject.7.refs_0_
  540.4 2.5 late_step.1
  542.9 3.5 collective-permute-start.40
  547.3 7.0 %collective-permute-done.40 = bf16[128,1024]{1,0:T(8,128)(2,1)S(1)} collective-permute-done((bf16[128,1024]{1,0:T(8,128)(2,1)}, bf16[128,1024]{1,0:T(8,128)(2,1)S(1)}, u32[]{:S(2)}, u32[]{:S(2)}) %collective-permute-start.40) | collective-permute-done | bytes 262176 | tf_op jit(solution)/shard_map/ppermute | solution.py:1096
  554.3 13.4 %collective-permute-done.39 = bf16[128,1024]{1,0:T(8,128)(2,1)S(1)} collective-permute-done((bf16[128,1024]{1,0:T(8,128)(2,1)}, bf16[128,1024]{1,0:T(8,128)(2,1)S(1)}, u32[]{:S(2)}, u32[]{:S(2)}) %collective-permute-start.39) | collective-permute-done | bytes 262176 | tf_op jit(solution)/shard_map/ppermute | solution.py:1096
  568.9 2.9 collective-permute-start.42
  571.9 1.5 collective-permute-start.43
  573.3 4.1 add_convert_fusion
  577.4 7.1 %feed_grads.1 = (f32[1024,1024]{1,0:T(8,128)}, f32[1024,1024]{1,0:T(8,128)}) custom-call(s32[1]{0:T(128)} %bitcast.me_ref, bf16[1024,1024]{1,0:T(8,128)(2,1)} %stack_step.2.even_ref, bf16[1024,1024]{1,0:T(8,128)(2,1)} %collective-permute-done.45.odd_ref), custom_call_target="tpu_custom_call" | custom-call | flops 1 | bytes 1 | tf_op jit(solution)/shard_map/feed_grads/pallas_call | solution.py:375
  584.5 7.7 %input_step.1 = f32[1024,1024]{1,0:T(8,128)} custom-call(bf16[1024,1024]{1,0:T(8,128)(2,1)} %unproject.7.refs_0_, bf16[1024,1024]{1,0:T(8,128)(2,1)} %collective-permute-done.44.refs_1_, bf16[1024,1024]{1,0:T(8,128)(2,1)} %refs_2_.23, f32[1024,1024]{1,0:T(8,128)} %get-tuple-element.274.refs_3_, bf16[1024]{0:T(1024)(128)(2,1)} %refs_4_.17), custom_call_target="tpu_custom_call" | custom-call | flops 1 | bytes 1 | tf_op jit(solution)/shard_map/input_step/pallas_call | solution.py:375
  593.7 2.2 stack_step.3.even_ref
  595.9 1.5 collective-permute-start.50
  598.6 3.8 collective-permute-done.46
  602.4 1.8 collective-permute-start.47
  604.2 4.1 collective-permute-done.47
  609.4 2.9 collective-permute-done.48
  614.2 4.8 collective-permute-done.50.odd_ref
  619.9 4.0 spread.1
  (160 shorter events, 35.7 us)
Async XLA Ops:
  0.7 52.8 %copy-start.1 = (bf16[1024,1024]{1,0:T(8,128)(2,1)S(1)}, bf16[1024,1024]{1,0:T(8,128)(2,1)}, u32[]{:S(2)}) copy-start(bf16[1024,1024]{1,0:T(8,128)(2,1)} %refs_3_.17) | copy-start | bytes 6291460
  0.7 54.6 %copy-start.15 = (bf16[256,1024]{1,0:T(8,128)(2,1)S(1)}, bf16[256,1024]{1,0:T(8,128)(2,1)}, u32[]{:S(2)}) copy-start(bf16[256,1024]{1,0:T(8,128)(2,1)} %refs_5_.8) | copy-start | bytes 1572868
  0.7 4.5 collective-permute-start.1
  1.2 49.1 %collective-permute-start = (bf16[1024,1024]{1,0:T(8,128)(2,1)}, bf16[1024,1024]{1,0:T(8,128)(2,1)}, u32[]{:S(2)}, u32[]{:S(2)}) collective-permute-start(bf16[1024,1024]{1,0:T(8,128)(2,1)} %refs_2_.23), channel_id=1, source_target_pairs={{0,2},{1,3},{2,0},{3,1},{4,6},{5,7},{6,4},{7,5},{8,10},{9,11},{10,... | collective-permute-start | bytes 6291464 | tf_op jit(solution)/shard_map/ppermute | solution.py:1084
  50.3 5.2 collective-permute-start.2
  53.5 49.2 %collective-permute-start.3 = (bf16[1024,1024]{1,0:T(8,128)(2,1)S(1)}, bf16[1024,1024]{1,0:T(8,128)(2,1)}, u32[]{:S(2)}, u32[]{:S(2)}) collective-permute-start(bf16[1024,1024]{1,0:T(8,128)(2,1)S(1)} %copy-done.1), channel_id=1, source_target_pairs={{0,2},{1,3},{2,0},{3,1},{4,6},{5,7},{6,4},{7,5},{8,10},{9,11},{10,... | collective-permute-start | bytes 6291464 | tf_op jit(solution)/shard_map/ppermute | solution.py:1084
  55.2 85.8 %collective-permute-start.10 = (bf16[256,1024]{1,0:T(8,128)(2,1)S(1)}, bf16[256,1024]{1,0:T(8,128)(2,1)S(1)}, u32[]{:S(2)}, u32[]{:S(2)}) collective-permute-start(bf16[256,1024]{1,0:T(8,128)(2,1)S(1)} %copy-done.15), channel_id=1, source_target_pairs={{0,2},{1,3},{2,0},{3,1},{4,6},{5,7},{6,4},{7,5},{8,10},{9,11},{10,... | collective-permute-start | bytes 1572872 | tf_op jit(solution)/shard_map/ppermute | solution.py:1084
  100.9 42.2 %collective-permute-start.6 = (bf16[4096,128]{1,0:T(8,128)(2,1)}, bf16[4096,128]{1,0:T(8,128)(2,1)S(1)}, u32[]{:S(2)}, u32[]{:S(2)}) collective-permute-start(bf16[4096,128]{1,0:T(8,128)(2,1)} %get-tuple-element.162.refs_0_.refs_6_), channel_id=1, source_target_pairs={{0,2},{1,3},{2,0},{3,1},{4,6},{5,7},{6,4},{7,5},{8,10},{9,11},{10,... | collective-permute-start | bytes 3145736 | tf_op jit(solution)/shard_map/ppermute | solution.py:1084
  102.7 41.0 %collective-permute-start.9 = (bf16[1024,1024]{1,0:T(8,128)(2,1)}, bf16[1024,1024]{1,0:T(8,128)(2,1)}, u32[]{:S(2)}, u32[]{:S(2)}) collective-permute-start(bf16[1024,1024]{1,0:T(8,128)(2,1)} %collective-permute-done.3.refs_2_), channel_id=1, source_target_pairs={{0,1},{1,0},{2,3},{3,2},{4,5},{5,4},{6,7},{7,6},{8,9},{9,8},{10,11... | collective-permute-start | bytes 6291464 | tf_op jit(solution)/shard_map/ppermute | solution.py:1084
  102.7 40.9 %collective-permute-start.8 = (bf16[1024,1024]{1,0:T(8,128)(2,1)S(1)}, bf16[1024,1024]{1,0:T(8,128)(2,1)}, u32[]{:S(2)}, u32[]{:S(2)}) collective-permute-start(bf16[1024,1024]{1,0:T(8,128)(2,1)S(1)} %copy-done.1), channel_id=1, source_target_pairs={{0,1},{1,0},{2,3},{3,2},{4,5},{5,4},{6,7},{7,6},{8,9},{9,8},{10,11... | collective-permute-start | bytes 6291464 | tf_op jit(solution)/shard_map/ppermute | solution.py:1084
  103.2 39.8 %copy-start.4 = (bf16[4096,128]{1,0:T(8,128)(2,1)S(1)}, bf16[4096,128]{1,0:T(8,128)(2,1)}, u32[]{:S(2)}) copy-start(bf16[4096,128]{1,0:T(8,128)(2,1)} %get-tuple-element.162.refs_0_.refs_6_) | copy-start | bytes 3145732
  139.9 25.3 %collective-permute-start.7 = (bf16[4096,128]{1,0:T(8,128)(2,1)}, bf16[4096,128]{1,0:T(8,128)(2,1)S(1)}, u32[]{:S(2)}, u32[]{:S(2)}) collective-permute-start(bf16[4096,128]{1,0:T(8,128)(2,1)} %get-tuple-element.167.refs_1_.refs_6_), channel_id=1, source_target_pairs={{0,2},{1,3},{2,0},{3,1},{4,6},{5,7},{6,4},{7,5},{8,10},{9,11},{10,... | collective-permute-start | bytes 3145736 | tf_op jit(solution)/shard_map/ppermute | solution.py:1084
  141.0 2.0 collective-permute-start.11
  143.0 25.4 %collective-permute-start.4 = (bf16[4096,128]{1,0:T(8,128)(2,1)S(1)}, bf16[4096,128]{1,0:T(8,128)(2,1)S(1)}, u32[]{:S(2)}, u32[]{:S(2)}) collective-permute-start(bf16[4096,128]{1,0:T(8,128)(2,1)S(1)} %copy-done.4), channel_id=1, source_target_pairs={{0,1},{1,0},{2,3},{3,2},{4,5},{5,4},{6,7},{7,6},{8,9},{9,8},{10,11... | collective-permute-start | bytes 3145736 | tf_op jit(solution)/shard_map/ppermute | solution.py:1084
  143.2 15.8 %copy-start.5 = (bf16[4096,128]{1,0:T(8,128)(2,1)}, bf16[4096,128]{1,0:T(8,128)(2,1)S(1)}, u32[]{:S(2)}) copy-start(bf16[4096,128]{1,0:T(8,128)(2,1)S(1)} %collective-permute-done.6.refs_4_) | copy-start | bytes 3145732
  143.2 25.3 %collective-permute-start.5 = (bf16[4096,128]{1,0:T(8,128)(2,1)}, bf16[4096,128]{1,0:T(8,128)(2,1)S(1)}, u32[]{:S(2)}, u32[]{:S(2)}) collective-permute-start(bf16[4096,128]{1,0:T(8,128)(2,1)} %get-tuple-element.167.refs_1_.refs_6_), channel_id=1, source_target_pairs={{0,1},{1,0},{2,3},{3,2},{4,5},{5,4},{6,7},{7,6},{8,9},{9,8},{10,11... | collective-permute-start | bytes 3145736 | tf_op jit(solution)/shard_map/ppermute | solution.py:1084
  143.6 24.9 %collective-permute-start.12 = (bf16[4096,128]{1,0:T(8,128)(2,1)S(1)}, bf16[4096,128]{1,0:T(8,128)(2,1)S(1)}, u32[]{:S(2)}, u32[]{:S(2)}) collective-permute-start(bf16[4096,128]{1,0:T(8,128)(2,1)S(1)} %collective-permute-done.6.refs_4_), channel_id=1, source_target_pairs={{0,1},{1,0},{2,3},{3,2},{4,5},{5,4},{6,7},{7,6},{8,9},{9,8},{10,11... | collective-permute-start | bytes 3145736 | tf_op jit(solution)/shard_map/ppermute | solution.py:1084
  165.2 3.4 collective-permute-start.13
  165.2 3.2 collective-permute-start.14
  205.8 12.1 %collective-permute-start.16 = (bf16[1024,1024]{1,0:T(8,128)(2,1)}, bf16[1024,1024]{1,0:T(8,128)(2,1)S(1)}, u32[]{:S(2)}, u32[]{:S(2)}) collective-permute-start(bf16[1024,1024]{1,0:T(8,128)(2,1)} %get-tuple-element.181), channel_id=1, source_target_pairs={{0,1},{1,0},{2,3},{3,2},{4,5},{5,4},{6,7},{7,6},{8,9},{9,8},{10,11... | collective-permute-start | bytes 6291464 | tf_op jit(solution)/shard_map/ppermute | solution.py:1084
  217.8 15.0 %collective-permute-start.15 = (bf16[1024,1024]{1,0:T(8,128)(2,1)}, bf16[1024,1024]{1,0:T(8,128)(2,1)S(1)}, u32[]{:S(2)}, u32[]{:S(2)}) collective-permute-start(bf16[1024,1024]{1,0:T(8,128)(2,1)} %get-tuple-element.180), channel_id=1, source_target_pairs={{0,1},{1,0},{2,3},{3,2},{4,5},{5,4},{6,7},{7,6},{8,9},{9,8},{10,11... | collective-permute-start | bytes 6291464 | tf_op jit(solution)/shard_map/ppermute | solution.py:1084
  231.8 48.3 %collective-permute-start.17 = (bf16[1024,1024]{1,0:T(8,128)(2,1)}, bf16[1024,1024]{1,0:T(8,128)(2,1)}, u32[]{:S(2)}, u32[]{:S(2)}) collective-permute-start(bf16[1024,1024]{1,0:T(8,128)(2,1)} %get-tuple-element.194), channel_id=1, source_target_pairs={{0,2},{1,3},{2,0},{3,1},{4,6},{5,7},{6,4},{7,5},{8,10},{9,11},{10,... | collective-permute-start | bytes 6291464 | tf_op jit(solution)/shard_map/ppermute | solution.py:1084
  260.3 52.8 %collective-permute-start.21 = (bf16[512,1024]{1,0:T(8,128)(2,1)}, bf16[512,1024]{1,0:T(8,128)(2,1)S(1)}, u32[]{:S(2)}, u32[]{:S(2)}) collective-permute-start(bf16[512,1024]{1,0:T(8,128)(2,1)} %get-tuple-element.205), channel_id=1, source_target_pairs={{0,4},{4,0},{8,12},{12,8},{16,20},{20,16},{24,28},{28,24},{1,5},{5... | collective-permute-start | bytes 3145736 | tf_op jit(solution)/shard_map/ppermute | solution.py:1096
  275.1 37.9 %collective-permute-start.22 = (bf16[512,1024]{1,0:T(8,128)(2,1)}, bf16[512,1024]{1,0:T(8,128)(2,1)S(1)}, u32[]{:S(2)}, u32[]{:S(2)}) collective-permute-start(bf16[512,1024]{1,0:T(8,128)(2,1)} %get-tuple-element.206), channel_id=1, source_target_pairs={{0,4},{4,0},{8,12},{12,8},{16,20},{20,16},{24,28},{28,24},{1,5},{5... | collective-permute-start | bytes 3145736 | tf_op jit(solution)/shard_map/ppermute | solution.py:1096
  290.2 28.4 %collective-permute-start.18 = (bf16[1024,256]{1,0:T(8,128)(2,1)}, bf16[1024,256]{1,0:T(8,128)(2,1)S(1)}, u32[]{:S(2)}, u32[]{:S(2)}) collective-permute-start(bf16[1024,256]{1,0:T(8,128)(2,1)} %get-tuple-element.197), channel_id=1, source_target_pairs={{0,1},{1,0},{2,3},{3,2},{4,5},{5,4},{6,7},{7,6},{8,9},{9,8},{10,11... | collective-permute-start | bytes 1572872 | tf_op jit(solution)/shard_map/ppermute | solution.py:1084
  290.3 28.3 %collective-permute-start.19 = (bf16[1024,256]{1,0:T(8,128)(2,1)}, bf16[1024,256]{1,0:T(8,128)(2,1)S(1)}, u32[]{:S(2)}, u32[]{:S(2)}) collective-permute-start(bf16[1024,256]{1,0:T(8,128)(2,1)} %get-tuple-element.198), channel_id=1, source_target_pairs={{0,2},{1,3},{2,0},{3,1},{4,6},{5,7},{6,4},{7,5},{8,10},{9,11},{10,... | collective-permute-start | bytes 1572872 | tf_op jit(solution)/shard_map/ppermute | solution.py:1084
  291.4 27.2 %collective-permute-start.20 = (bf16[1024,256]{1,0:T(8,128)(2,1)}, bf16[1024,256]{1,0:T(8,128)(2,1)S(1)}, u32[]{:S(2)}, u32[]{:S(2)}) collective-permute-start(bf16[1024,256]{1,0:T(8,128)(2,1)} %get-tuple-element.199), channel_id=1, source_target_pairs={{0,3},{1,2},{2,1},{3,0},{4,7},{5,6},{6,5},{7,4},{8,11},{9,10},{10,... | collective-permute-start | bytes 1572872 | tf_op jit(solution)/shard_map/ppermute | solution.py:1084
  318.7 75.0 %collective-permute-start.23 = (bf16[2048,256]{1,0:T(8,128)(2,1)}, bf16[2048,256]{1,0:T(8,128)(2,1)S(1)}, u32[]{:S(2)}, u32[]{:S(2)}) collective-permute-start(bf16[2048,256]{1,0:T(8,128)(2,1)} %get-tuple-element.216), channel_id=1, source_target_pairs={{0,1},{1,0},{2,3},{3,2},{4,5},{5,4},{6,7},{7,6},{8,9},{9,8},{10,11... | collective-permute-start | bytes 3145736 | tf_op jit(solution)/shard_map/ppermute | solution.py:1084
  319.1 76.9 %collective-permute-start.27 = (bf16[256,1024]{1,0:T(8,128)(2,1)}, bf16[256,1024]{1,0:T(8,128)(2,1)S(1)}, u32[]{:S(2)}, u32[]{:S(2)}) collective-permute-start(bf16[256,1024]{1,0:T(8,128)(2,1)} %get-tuple-element.231), channel_id=1, source_target_pairs={{0,24},{4,28},{8,16},{12,20},{16,8},{20,12},{24,0},{28,4},{1,25},{... | collective-permute-start | bytes 1572872 | tf_op jit(solution)/shard_map/ppermute | solution.py:1096
  322.7 73.3 %collective-permute-start.26 = (bf16[256,1024]{1,0:T(8,128)(2,1)}, bf16[256,1024]{1,0:T(8,128)(2,1)S(1)}, u32[]{:S(2)}, u32[]{:S(2)}) collective-permute-start(bf16[256,1024]{1,0:T(8,128)(2,1)} %get-tuple-element.230), channel_id=1, source_target_pairs={{0,16},{4,20},{8,24},{12,28},{16,0},{20,4},{24,8},{28,12},{1,17},{... | collective-permute-start | bytes 1572872 | tf_op jit(solution)/shard_map/ppermute | solution.py:1096
  322.7 73.3 %collective-permute-start.25 = (bf16[256,1024]{1,0:T(8,128)(2,1)}, bf16[256,1024]{1,0:T(8,128)(2,1)}, u32[]{:S(2)}, u32[]{:S(2)}) collective-permute-start(bf16[256,1024]{1,0:T(8,128)(2,1)} %get-tuple-element.229), channel_id=1, source_target_pairs={{0,8},{4,12},{8,0},{12,4},{16,24},{20,28},{24,16},{28,20},{1,9},{5... | collective-permute-start | bytes 1572872 | tf_op jit(solution)/shard_map/ppermute | solution.py:1096
  323.5 89.5 %collective-permute-start.28 = (bf16[2048,1024]{1,0:T(8,128)(2,1)}, bf16[2048,1024]{1,0:T(8,128)(2,1)}, u32[]{:S(2)}, u32[]{:S(2)}) collective-permute-start(bf16[2048,1024]{1,0:T(8,128)(2,1)} %get-tuple-element.233), channel_id=1, source_target_pairs={{0,1},{1,0},{2,3},{3,2},{4,5},{5,4},{6,7},{7,6},{8,9},{9,8},{10,11... | collective-permute-start | bytes 12582920 | tf_op jit(solution)/shard_map/ppermute | solution.py:1084
  323.5 70.2 %copy-start.18 = (bf16[2048,256]{1,0:T(8,128)(2,1)S(1)}, bf16[2048,256]{1,0:T(8,128)(2,1)}, u32[]{:S(2)}) copy-start(bf16[2048,256]{1,0:T(8,128)(2,1)} %get-tuple-element.215) | copy-start | bytes 3145732
  394.9 14.5 %collective-permute-start.24 = (bf16[1024,256]{1,0:T(8,128)(2,1)}, bf16[1024,256]{1,0:T(8,128)(2,1)S(1)}, u32[]{:S(2)}, u32[]{:S(2)}) collective-permute-start(bf16[1024,256]{1,0:T(8,128)(2,1)} %get-tuple-element.220), channel_id=1, source_target_pairs={{0,2},{1,3},{2,0},{3,1},{4,6},{5,7},{6,4},{7,5},{8,10},{9,11},{10,... | collective-permute-start | bytes 1572872 | tf_op jit(solution)/shard_map/ppermute | solution.py:1084
  397.4 24.3 %copy-start.14 = (bf16[256,1024]{1,0:T(8,128)(2,1)}, bf16[256,1024]{1,0:T(8,128)(2,1)S(1)}, u32[]{:S(2)}) copy-start(bf16[256,1024]{1,0:T(8,128)(2,1)S(1)} %add_convert_fusion.3.refs_0_) | copy-start | bytes 1572868
  397.4 15.5 %copy-start.3 = (bf16[2048,1024]{1,0:T(8,128)(2,1)S(1)}, bf16[2048,1024]{1,0:T(8,128)(2,1)}, u32[]{:S(2)}) copy-start(bf16[2048,1024]{1,0:T(8,128)(2,1)} %get-tuple-element.232) | copy-start | bytes 12582916
  417.5 77.0 %collective-permute-start.30 = (bf16[256,1024]{1,0:T(8,128)(2,1)S(1)}, bf16[256,1024]{1,0:T(8,128)(2,1)S(1)}, u32[]{:S(2)}, u32[]{:S(2)}) collective-permute-start(bf16[256,1024]{1,0:T(8,128)(2,1)S(1)} %add_convert_fusion.3.refs_0_), channel_id=1, source_target_pairs={{0,8},{4,12},{8,0},{12,4},{16,24},{20,28},{24,16},{28,20},{1,9},{5... | collective-permute-start | bytes 1572872 | tf_op jit(solution)/shard_map/ppermute | solution.py:1096
  418.8 75.7 %collective-permute-start.31 = (bf16[256,1024]{1,0:T(8,128)(2,1)S(1)}, bf16[256,1024]{1,0:T(8,128)(2,1)}, u32[]{:S(2)}, u32[]{:S(2)}) collective-permute-start(bf16[256,1024]{1,0:T(8,128)(2,1)S(1)} %add_convert_fusion.3.refs_0_), channel_id=1, source_target_pairs={{0,16},{4,20},{8,24},{12,28},{16,0},{20,4},{24,8},{28,12},{1,17},{... | collective-permute-start | bytes 1572872 | tf_op jit(solution)/shard_map/ppermute | solution.py:1096
  421.7 72.8 %collective-permute-start.32 = (bf16[256,1024]{1,0:T(8,128)(2,1)S(1)}, bf16[256,1024]{1,0:T(8,128)(2,1)}, u32[]{:S(2)}, u32[]{:S(2)}) collective-permute-start(bf16[256,1024]{1,0:T(8,128)(2,1)S(1)} %add_convert_fusion.3.refs_0_), channel_id=1, source_target_pairs={{0,24},{4,28},{8,16},{12,20},{16,8},{20,12},{24,0},{28,4},{1,25},{... | collective-permute-start | bytes 1572872 | tf_op jit(solution)/shard_map/ppermute | solution.py:1096
  421.9 72.6 %collective-permute-start.29 = (bf16[512,640]{1,0:T(8,128)(2,1)}, bf16[512,640]{1,0:T(8,128)(2,1)S(1)}, u32[]{:S(2)}, u32[]{:S(2)}) collective-permute-start(bf16[512,640]{1,0:T(8,128)(2,1)} %get-tuple-element.238), channel_id=1, source_target_pairs={{0,4},{4,0},{8,12},{12,8},{16,20},{20,16},{24,28},{28,24},{1,5},{5... | collective-permute-start | bytes 1966088 | tf_op jit(solution)/shard_map/ppermute | solution.py:1096
  423.4 71.1 %collective-permute-start.33 = (bf16[1024,1024]{1,0:T(8,128)(2,1)}, bf16[1024,1024]{1,0:T(8,128)(2,1)}, u32[]{:S(2)}, u32[]{:S(2)}) collective-permute-start(bf16[1024,1024]{1,0:T(8,128)(2,1)} %get-tuple-element.241), channel_id=1, source_target_pairs={{0,2},{1,3},{2,0},{3,1},{4,6},{5,7},{6,4},{7,5},{8,10},{9,11},{10,... | collective-permute-start | bytes 6291464 | tf_op jit(solution)/shard_map/ppermute | solution.py:1084
  494.5 10.0 %copy-start.26 = (bf16[256,1024]{1,0:T(8,128)(2,1)}, bf16[256,1024]{1,0:T(8,128)(2,1)S(1)}, u32[]{:S(2)}) copy-start(bf16[256,1024]{1,0:T(8,128)(2,1)S(1)} %collective-permute-done.30.refs_1_) | copy-start | bytes 1572868
  494.5 10.0 %copy-start.23 = (bf16[512,640]{1,0:T(8,128)(2,1)}, bf16[512,640]{1,0:T(8,128)(2,1)S(1)}, u32[]{:S(2)}) copy-start(bf16[512,640]{1,0:T(8,128)(2,1)S(1)} %collective-permute-done.29.refs_1_) | copy-start | bytes 1966084
  504.5 11.1 %collective-permute-start.34 = (bf16[512,384]{1,0:T(8,128)(2,1)}, bf16[512,384]{1,0:T(8,128)(2,1)S(1)}, u32[]{:S(2)}, u32[]{:S(2)}) collective-permute-start(bf16[512,384]{1,0:T(8,128)(2,1)} %get-tuple-element.259), channel_id=1, source_target_pairs={{0,4},{4,0},{8,12},{12,8},{16,20},{20,16},{24,28},{28,24},{1,5},{5... | collective-permute-start | bytes 1179656 | tf_op jit(solution)/shard_map/ppermute | solution.py:1096
  506.7 8.9 %copy-start.28 = (f32[16,1024]{1,0:T(8,128)S(1)}, f32[16,1024]{1,0:T(8,128)}, u32[]{:S(2)}) copy-start(f32[16,1024]{1,0:T(8,128)} %pack.1) | copy-start | bytes 196612
  506.7 8.9 %collective-permute-start.35 = (f32[16,1024]{1,0:T(8,128)}, f32[16,1024]{1,0:T(8,128)S(1)}, u32[]{:S(2)}, u32[]{:S(2)}) collective-permute-start(f32[16,1024]{1,0:T(8,128)} %pack.1), channel_id=1, source_target_pairs={{0,4},{4,0},{8,12},{12,8},{16,20},{20,16},{24,28},{28,24},{1,5},{5... | collective-permute-start | bytes 196616 | tf_op jit(solution)/shard_map/ppermute | solution.py:1096
  520.8 6.1 collective-permute-start.36
  525.9 8.8 %collective-permute-start.37 = (bf16[1024,1024]{1,0:T(8,128)(2,1)}, bf16[1024,1024]{1,0:T(8,128)(2,1)}, u32[]{:S(2)}, u32[]{:S(2)}) collective-permute-start(bf16[1024,1024]{1,0:T(8,128)(2,1)} %unproject.5), channel_id=1, source_target_pairs={{0,1},{1,0},{2,3},{3,2},{4,5},{5,4},{6,7},{7,6},{8,9},{9,8},{10,11... | collective-permute-start | bytes 6291464 | tf_op jit(solution)/shard_map/ppermute | solution.py:1084
  526.4 51.0 %collective-permute-start.45 = (bf16[1024,1024]{1,0:T(8,128)(2,1)}, bf16[1024,1024]{1,0:T(8,128)(2,1)}, u32[]{:S(2)}, u32[]{:S(2)}) collective-permute-start(bf16[1024,1024]{1,0:T(8,128)(2,1)} %stack_step.2.even_ref), channel_id=1, source_target_pairs={{0,4},{4,0},{8,12},{12,8},{16,20},{20,16},{24,28},{28,24},{1,5},{5... | collective-permute-start | bytes 6291464 | tf_op jit(solution)/shard_map/ppermute | solution.py:1096
  533.7 50.8 %collective-permute-start.44 = (bf16[1024,1024]{1,0:T(8,128)(2,1)}, bf16[1024,1024]{1,0:T(8,128)(2,1)}, u32[]{:S(2)}, u32[]{:S(2)}) collective-permute-start(bf16[1024,1024]{1,0:T(8,128)(2,1)} %unproject.6), channel_id=1, source_target_pairs={{0,2},{1,3},{2,0},{3,1},{4,6},{5,7},{6,4},{7,5},{8,10},{9,11},{10,... | collective-permute-start | bytes 6291464 | tf_op jit(solution)/shard_map/ppermute | solution.py:1084
  534.7 38.6 %copy-start = (f32[1024,1024]{1,0:T(8,128)S(1)}, f32[1024,1024]{1,0:T(8,128)}, u32[]{:S(2)}) copy-start(f32[1024,1024]{1,0:T(8,128)} %get-tuple-element.195.refs_2_) | copy-start | bytes 12582916
  540.4 6.9 %copy-start.32 = (bf16[1024]{0:T(1024)(128)(2,1)S(1)}, bf16[1024]{0:T(1024)(128)(2,1)}, u32[]{:S(2)}) copy-start(bf16[1024]{0:T(1024)(128)(2,1)} %param.34) | copy-start | bytes 6148
  542.9 11.3 %collective-permute-start.40 = (bf16[128,1024]{1,0:T(8,128)(2,1)}, bf16[128,1024]{1,0:T(8,128)(2,1)S(1)}, u32[]{:S(2)}, u32[]{:S(2)}) collective-permute-start(bf16[128,1024]{1,0:T(8,128)(2,1)} %get-tuple-element.268), channel_id=1, source_target_pairs={{0,24},{4,28},{8,16},{12,20},{16,8},{20,12},{24,0},{28,4},{1,25},{... | collective-permute-start | bytes 786440 | tf_op jit(solution)/shard_map/ppermute | solution.py:1096
  546.5 21.2 %collective-permute-start.39 = (bf16[128,1024]{1,0:T(8,128)(2,1)}, bf16[128,1024]{1,0:T(8,128)(2,1)S(1)}, u32[]{:S(2)}, u32[]{:S(2)}) collective-permute-start(bf16[128,1024]{1,0:T(8,128)(2,1)} %get-tuple-element.267), channel_id=1, source_target_pairs={{0,16},{4,20},{8,24},{12,28},{16,0},{20,4},{24,8},{28,12},{1,17},{... | collective-permute-start | bytes 786440 | tf_op jit(solution)/shard_map/ppermute | solution.py:1096
  546.5 21.2 %collective-permute-start.38 = (bf16[128,1024]{1,0:T(8,128)(2,1)}, bf16[128,1024]{1,0:T(8,128)(2,1)S(1)}, u32[]{:S(2)}, u32[]{:S(2)}) collective-permute-start(bf16[128,1024]{1,0:T(8,128)(2,1)} %get-tuple-element.266), channel_id=1, source_target_pairs={{0,8},{4,12},{8,0},{12,4},{16,24},{20,28},{24,16},{28,20},{1,9},{5... | collective-permute-start | bytes 786440 | tf_op jit(solution)/shard_map/ppermute | solution.py:1096
  568.8 8.5 %copy-start.22 = (bf16[128,1024]{1,0:T(8,128)(2,1)}, bf16[128,1024]{1,0:T(8,128)(2,1)S(1)}, u32[]{:S(2)}) copy-start(bf16[128,1024]{1,0:T(8,128)(2,1)S(1)} %add_convert_fusion.6.refs_0_) | copy-start | bytes 786436
  568.9 23.3 %collective-permute-start.41 = (bf16[128,1024]{1,0:T(8,128)(2,1)S(1)}, bf16[128,1024]{1,0:T(8,128)(2,1)S(1)}, u32[]{:S(2)}, u32[]{:S(2)}) collective-permute-start(bf16[128,1024]{1,0:T(8,128)(2,1)S(1)} %add_convert_fusion.6.refs_0_), channel_id=1, source_target_pairs={{0,8},{4,12},{8,0},{12,4},{16,24},{20,28},{24,16},{28,20},{1,9},{5... | collective-permute-start | bytes 786440 | tf_op jit(solution)/shard_map/ppermute | solution.py:1096
  568.9 23.2 %collective-permute-start.42 = (bf16[128,1024]{1,0:T(8,128)(2,1)S(1)}, bf16[128,1024]{1,0:T(8,128)(2,1)S(1)}, u32[]{:S(2)}, u32[]{:S(2)}) collective-permute-start(bf16[128,1024]{1,0:T(8,128)(2,1)S(1)} %add_convert_fusion.6.refs_0_), channel_id=1, source_target_pairs={{0,16},{4,20},{8,24},{12,28},{16,0},{20,4},{24,8},{28,12},{1,17},{... | collective-permute-start | bytes 786440 | tf_op jit(solution)/shard_map/ppermute | solution.py:1096
  571.9 20.3 %collective-permute-start.43 = (bf16[128,1024]{1,0:T(8,128)(2,1)S(1)}, bf16[128,1024]{1,0:T(8,128)(2,1)S(1)}, u32[]{:S(2)}, u32[]{:S(2)}) collective-permute-start(bf16[128,1024]{1,0:T(8,128)(2,1)S(1)} %add_convert_fusion.6.refs_0_), channel_id=1, source_target_pairs={{0,24},{4,28},{8,16},{12,20},{16,8},{20,12},{24,0},{28,4},{1,25},{... | collective-permute-start | bytes 786440 | tf_op jit(solution)/shard_map/ppermute | solution.py:1096
  595.9 23.0 %collective-permute-start.50 = (bf16[512,1024]{1,0:T(8,128)(2,1)}, bf16[512,1024]{1,0:T(8,128)(2,1)S(1)}, u32[]{:S(2)}, u32[]{:S(2)}) collective-permute-start(bf16[512,1024]{1,0:T(8,128)(2,1)} %stack_step.3.even_ref), channel_id=1, source_target_pairs={{0,4},{4,0},{8,12},{12,8},{16,20},{20,16},{24,28},{28,24},{1,5},{5... | collective-permute-start | bytes 3145736 | tf_op jit(solution)/shard_map/ppermute | solution.py:1096
  597.4 5.0 collective-permute-start.46
  602.4 5.9 collective-permute-start.47
  608.3 4.0 collective-permute-start.48
  612.3 1.2 collective-permute-start.49
  (23 other events, 43.7 us)

commit v7 on v6

--- a/solution.py
+++ b/solution.py
@@ -1301,34 +1301,37 @@
     feed_even = stack_step([*feed_shards[:-1], after(feed_shards[-1], vectors)])
     summed = vectors + swap_data(vectors, 1)
     feed_odd = swap_data(after(feed_even, late_come, summed), 1)
+    late_parts = late_step(
+        [(early_keep, early_come), (after(late_keep, feed_even), late_come)], streams // 2
+    )
+    late_shard = exchange(late_parts)
     seen = []
 
     def make_unproject(chosen, extras, gate):
         gates = [feed_even if gate is None else gate]
         if not seen:
-            gates += [late_come, summed]
+            gates += [late_parts[-1], summed]
+        if len(seen) == 2:
+            gates.append(late_shard)
         seen.append(0)
         return unproject(
             [*head_grads[:-1], after(head_grads[-1], *gates)], weights, slots, chosen, extras
         )
 
     normed_terms = ordered_terms(make_unproject)
-    late_parts = late_step(
-        [(early_keep, early_come), (after(late_keep, normed_terms[0]), late_come)], streams // 2
-    )
     layer_output = low(residual + add_up(ffn_terms) + down_bias.astype(F32))
-    up_grad, down_grad = feed_grads(feed_even, feed_odd, stream, streams)
+    up_grad, down_grad = feed_grads(after(feed_even, normed_terms[0]), feed_odd, stream, streams)
+    *late_shards, layer_output, up_grad = lax.optimization_barrier(
+        (*collect_far(late_shard), layer_output, up_grad)
+    )
+    late_even = stack_step(late_shards)
+    late_odd = swap_data(late_even, 1)
     input_grad = input_step(
-        [*normed_terms[:-1], after(normed_terms[-1], up_grad)],
+        [*normed_terms[:-1], after(normed_terms[-1], late_even)],
         layer_input,
         resid_grad,
         input_gain,
     )
-    *late_shards, layer_output, input_grad = lax.optimization_barrier(
-        (*collect_far(exchange(late_parts)), layer_output, input_grad)
-    )
-    late_even = stack_step(late_shards)
-    late_odd = swap_data(late_even, 1)
     for level in range(1, streams.bit_length() - 1):
         summed = summed + swap_data(summed, 1 << level)
     own = summed[8:]
@@ -1341,7 +1344,7 @@
     query_bias_grad = counts[:, :cols].reshape(-1)
     value_bias_grad = counts[:, 2 * cols : 3 * cols].reshape(-1)
     *weight_grads, dense_weight_grad = spread(
-        late_even, late_odd, stream, streams, groups, head_cols
+        after(late_even, input_grad), late_odd, stream, streams, groups, head_cols
     )
     return (
         layer_output,

time: 633 us -> 642 us (1.014)
  starting transfers between devices: 46.4 us -> 59.3 us
    ppermute x21, starting transfers between devices: 28.3 us -> 41.3 us  [swap_data(): return lax.ppermute(array, 'dp', [(i, i ^ mask) for i in range(streams)])]
    ppermute x21, waiting for transfers between devices: 37.5 us -> 26.1 us  [swap_data(): return lax.ppermute(array, 'dp', [(i, i ^ mask) for i in range(streams)])]
    ppermute x30, waiting for transfers between devices: 56.1 us -> 65.6 us  [swap(): return lax.ppermute(array, 'tensor', [(i, i ^ mask) for i in range(slots)])]
    unnamed x72 -> x78, local copies, waits for them, and re-layouts: 14.1 us -> 12.8 us
  transfers between devices with their start and end apart: 51 -> 51, of which waited for: 15 -> 17; matrix products, arithmetic and copies ran while one was open for 2% -> 2% of each run, Pallas kernels for 63% -> 63%
where the time goes in v7:
time: 642 us; the launch traced here: 633 us
  Pallas kernels  451 us (70%)
  waiting for transfers between devices  91.7 us (14%)
  starting transfers between devices  59.3 us (9%)
  local copies, waits for them, and re-layouts  16.4 us (3%)
  other arithmetic  11.5 us (2%)
    pallas_call x28, Pallas kernels, kernel_call(): pl.pallas_call(kernel, grid=grid, in_specs=in_specs + [pl.BlockSpec(memor...  238 us
    pallas_call x2, Pallas kernels, attend_back(): pl.pallas_call(functools.partial(attend_back_kernel, slots=slots, pair=pa...  140 us
    pallas_call x2, Pallas kernels, attend(): pl.pallas_call(functools.partial(attend_kernel, slots=slots, pair=pair, t...  72.9 us
    ppermute x30, waiting for transfers between devices, swap(): return lax.ppermute(array, 'tensor', [(i, i ^ mask) for i in range(slots)])  65.6 us
    ppermute x21, starting transfers between devices, swap_data(): return lax.ppermute(array, 'dp', [(i, i ^ mask) for i in range(streams)])  41.3 us
    ppermute x21, waiting for transfers between devices, swap_data(): return lax.ppermute(array, 'dp', [(i, i ^ mask) for i in range(streams)])  26.1 us
    ppermute x30, starting transfers between devices, swap(): return lax.ppermute(array, 'tensor', [(i, i ^ mask) for i in range(slots)])  18 us
  transfers between devices with their start and end apart: 51, of which 17 were waited for; matrix products, arithmetic and copies ran while one was open for 2% of the time, Pallas kernels for 63%

profile of v7, /device:TPU:0, one launch (start us, length us, event | category | flops | bytes accessed | tf_op | source)
XLA Modules:
  0.0 633.1 jit_solution(6996221370226170110)
XLA Ops:
  1.2 2.6 collective-permute-start
  3.8 1.4 collective-permute-done.1.refs_1_.refs_9_
  6.5 9.3 %project.2 = (bf16[4096,1024]{1,0:T(8,128)(2,1)}, bf16[4096,256]{1,0:T(8,128)(2,1)}, bf16[4096,256]{1,0:T(8,128)(2,1)}, bf16[4096,256]{1,0:T(8,128)(2,1)}) custom-call(bf16[1024,1024]{1,0:T(8,128)(2,1)} %refs_2_.23, bf16[1024,1024]{1,0:T(8,128)(2,1)} %copy-done.2, bf16[1024]{0:T(1024)(128)(2,1)} %refs_4_.17, bf16[1024]{0:T(1024)(128)(2,1)} %refs_2_.18, ...), custom_call_target="tpu_custom_call" | custom-call | flops 1 | bytes 1 | tf_op jit(solution)/shard_map/project/pallas_call | solution.py:375
  15.8 34.6 %collective-permute-done.refs_0_.refs_10_ = bf16[1024,1024]{1,0:T(8,128)(2,1)} collective-permute-done((bf16[1024,1024]{1,0:T(8,128)(2,1)}, bf16[1024,1024]{1,0:T(8,128)(2,1)}, u32[]{:S(2)}, u32[]{:S(2)}) %collective-permute-start) | collective-permute-done | bytes 2097184 | tf_op jit(solution)/shard_map/ppermute | solution.py:1084
  53.5 1.8 collective-permute-start.3
  55.5 9.3 %project.3 = (bf16[4096,1024]{1,0:T(8,128)(2,1)}, bf16[4096,256]{1,0:T(8,128)(2,1)}, bf16[4096,256]{1,0:T(8,128)(2,1)}, bf16[4096,256]{1,0:T(8,128)(2,1)}) custom-call(bf16[1024,1024]{1,0:T(8,128)(2,1)} %collective-permute-done.refs_0_.refs_10_, ...), custom_call_target="tpu_custom_call", output_to_operand_aliasing={{0}: (9, {}), {1}: (10, {}), {2}: (11, {}), {3}: (12, {})} | custom-call | flops 1 | bytes 1 | tf_op jit(solution)/shard_map/project/pallas_call | solution.py:375
  64.8 36.2 %attend.2 = (bf16[4096,128]{1,0:T(8,128)(2,1)}, f32[2,1,4096]{2,1,0:T(1,128)}) custom-call(s32[1]{0:T(128)} %bitcast.1.me_ref.refs_0_, s32[1]{0:T(128)S(6)} %convert_element_type.84.apart_ref.refs_1_, f32[2]{0:T(128)} %get-tuple-element.306.slope_ref.refs_2_, bf16[4096,256]{1,0:T(8,128)(2,1)} %get-tuple-element.168.q_ref.refs_3_, ...), custom_call_target="tpu_custom_call" | custom-call | flops 40265318400 | bytes 4194304 | tf_op jit(solution)/shard_map/attend/pallas_call | solution.py:182
  100.9 1.8 collective-permute-start.6
  103.2 36.7 %attend.3 = (bf16[4096,128]{1,0:T(8,128)(2,1)}, f32[2,1,4096]{2,1,0:T(1,128)}) custom-call(s32[1]{0:T(128)} %bitcast.1.me_ref.refs_0_, s32[1]{0:T(128)S(6)} %convert_element_type.84.apart_ref.refs_1_, f32[2]{0:T(128)} %get-tuple-element.305.slope_ref.refs_2_, bf16[4096,256]{1,0:T(8,128)(2,1)} %get-tuple-element.168.q_ref.refs_3_, ...), custom_call_target="tpu_custom_call" | custom-call | flops 40265318400 | bytes 4194304 | tf_op jit(solution)/shard_map/attend/pallas_call | solution.py:182
  143.7 15.3 %act_grad.1 = (bf16[4096,1024]{1,0:T(8,128)(2,1)}, bf16[4096,1024]{1,0:T(8,128)(2,1)}) custom-call(bf16[1024,1024]{1,0:T(8,128)(2,1)} %refs_3_.17, bf16[1024,1024]{1,0:T(8,128)(2,1)} %collective-permute-done.8.refs_1_, bf16[1024,1024]{1,0:T(8,128)(2,1)} %collective-permute-done.3.refs_2_, bf16[1024,1024]{1,0:T(8,128)(2,1)} %collective-permute-done.9.refs_3_, ...), custom_call_target="tpu_custom_call" | custom-call | flops 1 | bytes 1 | tf_op jit(solution)/shard_map/act_grad/pallas_call | solution.py:375
  159.0 6.2 collective-permute-done.7.refs_5_
  165.7 2.7 collective-permute-done.14.refs_13_.refs_6_
  171.3 22.8 %post_norm.1 = (bf16[4096,1024]{1,0:T(8,128)(2,1)}, f32[1024,1024]{1,0:T(8,128)}) custom-call(bf16[4096,128]{1,0:T(8,128)(2,1)} %get-tuple-element.164.refs_0_.refs_6_, bf16[4096,128]{1,0:T(8,128)(2,1)} %get-tuple-element.169.refs_1_.refs_6_, bf16[4096,128]{1,0:T(8,128)(2,1)} %copy-done.7, bf16[4096,128]{1,0:T(8,128)(2,1)} %copy-done.8, ...), custom_call_target="tpu_custom_call" | custom-call | flops 1 | bytes 1 | tf_op jit(solution)/shard_map/post_norm/pallas_call | solution.py:375
  194.1 11.7 %feed.4 = (bf16[4096,1024]{1,0:T(8,128)(2,1)}, bf16[4096,1024]{1,0:T(8,128)(2,1)}, f32[1,1024]{1,0:T(1,128)}, bf16[1024,1024]{1,0:T(8,128)(2,1)}) custom-call(bf16[4096,1024]{1,0:T(8,128)(2,1)} %get-tuple-element.178.refs_0_.right_ref, bf16[4096,1024]{1,0:T(8,128)(2,1)} %get-tuple-element.179.refs_1_, bf16[1024,1024]{1,0:T(8,128)(2,1)} %refs_2_.17, ...), custom_call_target="tpu_custom_call" | custom-call | flops 1 | bytes 1 | tf_op jit(solution)/shard_map/feed/pallas_call | solution.py:375
  206.2 11.6 %feed.5 = (bf16[4096,1024]{1,0:T(8,128)(2,1)}, bf16[4096,1024]{1,0:T(8,128)(2,1)}, f32[1,1024]{1,0:T(1,128)}, bf16[1024,1024]{1,0:T(8,128)(2,1)}) custom-call(bf16[4096,1024]{1,0:T(8,128)(2,1)} %get-tuple-element.178.refs_0_.right_ref, bf16[4096,1024]{1,0:T(8,128)(2,1)} %get-tuple-element.179.refs_1_, ...), custom_call_target="tpu_custom_call", output_to_operand_aliasing={{0}: (4, {}), {1}: (5, {})} | custom-call | flops 1 | bytes 1 | tf_op jit(solution)/shard_map/feed/pallas_call | solution.py:375
  217.9 1.3 copy-done.12
  219.2 12.6 %feed.6 = (bf16[4096,1024]{1,0:T(8,128)(2,1)}, bf16[4096,1024]{1,0:T(8,128)(2,1)}, f32[1,1024]{1,0:T(1,128)}, bf16[1024,1024]{1,0:T(8,128)(2,1)}) custom-call(bf16[4096,1024]{1,0:T(8,128)(2,1)} %get-tuple-element.178.refs_0_.right_ref, bf16[4096,1024]{1,0:T(8,128)(2,1)} %get-tuple-element.179.refs_1_, ...), custom_call_target="tpu_custom_call", output_to_operand_aliasing={{0}: (5, {}), {1}: (6, {})} | custom-call | flops 1 | bytes 1 | tf_op jit(solution)/shard_map/feed/pallas_call | solution.py:375
  234.2 12.8 %feed.7 = (bf16[4096,1024]{1,0:T(8,128)(2,1)}, bf16[4096,1024]{1,0:T(8,128)(2,1)}, f32[1,1024]{1,0:T(1,128)}, bf16[1024,1024]{1,0:T(8,128)(2,1)}) custom-call(bf16[4096,1024]{1,0:T(8,128)(2,1)} %get-tuple-element.178.refs_0_.right_ref, bf16[4096,1024]{1,0:T(8,128)(2,1)} %get-tuple-element.179.refs_1_, ...), custom_call_target="tpu_custom_call", output_to_operand_aliasing={{0}: (5, {}), {1}: (6, {})} | custom-call | flops 1 | bytes 1 | tf_op jit(solution)/shard_map/feed/pallas_call | solution.py:375
  247.0 13.3 %outer_step.2 = (bf16[512,1024]{1,0:T(8,128)(2,1)}, bf16[512,1024]{1,0:T(8,128)(2,1)}) custom-call(s32[1]{0:T(128)} %bitcast.me_ref, bf16[4096,1024]{1,0:T(8,128)(2,1)} %get-tuple-element.191.left_ref, bf16[4096,1024]{1,0:T(8,128)(2,1)} %get-tuple-element.178.refs_0_.right_ref), custom_call_target="tpu_custom_call" | custom-call | flops 1 | bytes 1 | tf_op jit(solution)/shard_map/outer_step/pallas_call | solution.py:375
  260.3 1.5 collective-permute-start.21
  261.8 13.3 %outer_step.3 = (bf16[512,1024]{1,0:T(8,128)(2,1)}, bf16[512,1024]{1,0:T(8,128)(2,1)}) custom-call(s32[1]{0:T(128)} %bitcast.me_ref, bf16[4096,1024]{1,0:T(8,128)(2,1)} %get-tuple-element.204.left_ref.active_ref, bf16[4096,1024]{1,0:T(8,128)(2,1)} %get-tuple-element.193.right_ref), custom_call_target="tpu_custom_call" | custom-call | flops 1 | bytes 1 | tf_op jit(solution)/shard_map/outer_step/pallas_call | solution.py:375
  275.6 4.4 collective-permute-done.17.refs_1_
  280.0 10.2 %resid_step.1 = (f32[1024,1024]{1,0:T(8,128)}, bf16[1024,1024]{1,0:T(8,128)(2,1)}, f32[8,1024]{1,0:T(8,128)}, bf16[1024,256]{1,0:T(8,128)(2,1)}, bf16[1024,256]{...) custom-call(bf16[1024,1024]{1,0:T(8,128)(2,1)} %get-tuple-element.195.refs_0_, ...), custom_call_target="tpu_custom_call" | custom-call | flops 1 | bytes 1 | tf_op jit(solution)/shard_map/resid_step/pallas_call | solution.py:375
  292.1 6.3 %dense_grad.1 = (bf16[2048,256]{1,0:T(8,128)(2,1)}, bf16[2048,256]{1,0:T(8,128)(2,1)}) custom-call(bf16[4096,128]{1,0:T(8,128)(2,1)} %get-tuple-element.164.refs_0_.refs_6_, bf16[4096,128]{1,0:T(8,128)(2,1)} %get-tuple-element.169.refs_1_.refs_6_, bf16[4096,128]{1,0:T(8,128)(2,1)} %copy-done.7, bf16[4096,128]{1,0:T(8,128)(2,1)} %copy-done.8, ...), custom_call_target="tpu_custom_call" | custom-call | flops 1 | bytes 1 | tf_op jit(solution)/shard_map/dense_grad/pallas_call | solution.py:375
  298.5 14.5 %ffn_step.1 = (bf16[2048,1024]{1,0:T(8,128)(2,1)}, bf16[2048,1024]{1,0:T(8,128)(2,1)}) custom-call(bf16[4096,1024]{1,0:T(8,128)(2,1)} %get-tuple-element.204.left_ref.active_ref, bf16[1024,1024]{1,0:T(8,128)(2,1)} %weight_ref.1), custom_call_target="tpu_custom_call" | custom-call | flops 1 | bytes 1 | tf_op jit(solution)/shard_map/ffn_step/pallas_call | solution.py:375
  314.9 3.7 pair_step.1
  319.1 3.6 collective-permute-start.27
  323.5 70.2 %attend_back.2.grad_ref.refs_0_ = bf16[4096,384]{1,0:T(8,128)(2,1)} custom-call(s32[1]{0:T(128)} %bitcast.1.me_ref.refs_0_, s32[1]{0:T(128)S(6)} %convert_element_type.84.apart_ref.refs_1_, f32[2]{0:T(128)} %get-tuple-element.306.slope_ref.refs_2_, bf16[4096,256]{1,0:T(8,128)(2,1)} %get-tuple-element.168.q_ref.refs_3_, ...), custom_call_target="tpu_custom_call" | custom-call | flops 80530636800 | bytes 8388608 | tf_op jit(solution)/shard_map/attend_back/pallas_call | solution.py:312
  396.0 1.4 add_convert_fusion.3.refs_0_
  397.4 9.6 %weight_step.2 = (bf16[1024,384]{1,0:T(8,128)(2,1)}, f32[8,1024]{1,0:T(8,128)}, f32[1,384]{1,0:T(1,128)}) custom-call(s32[1]{0:T(128)} %bitcast.me_ref, bf16[4096,1024]{1,0:T(8,128)(2,1)} %get-tuple-element.160.normed_ref, bf16[4096,384]{1,0:T(8,128)(2,1)} %attend_back.2.grad_ref.refs_0_, bf16[1024,256]{1,0:T(8,128)(2,1)} %refs_5_.12, ...), custom_call_target="tpu_custom_call" | custom-call | flops 1 | bytes 1 | tf_op jit(solution)/shard_map/weight_step/pallas_call | solution.py:375
  407.0 2.4 collective-permute-done.24.refs_2_
  410.3 2.6 join_step.1
  412.9 4.6 add_convert_fusion.1
  418.7 2.9 collective-permute-start.31
  421.9 1.5 collective-permute-start.29
  424.4 70.0 %attend_back.3.grad_ref.refs_1_ = bf16[4096,384]{1,0:T(8,128)(2,1)} custom-call(s32[1]{0:T(128)} %bitcast.1.me_ref.refs_0_, s32[1]{0:T(128)S(6)} %convert_element_type.84.apart_ref.refs_1_, f32[2]{0:T(128)} %get-tuple-element.305.slope_ref.refs_2_, bf16[4096,256]{1,0:T(8,128)(2,1)} %get-tuple-element.168.q_ref.refs_3_, ...), custom_call_target="tpu_custom_call" | custom-call | flops 80530636800 | bytes 8388608 | tf_op jit(solution)/shard_map/attend_back/pallas_call | solution.py:312
  494.5 10.0 %weight_step.3 = (bf16[512,384]{1,0:T(8,128)(2,1)}, bf16[512,384]{1,0:T(8,128)(2,1)}, f32[8,1024]{1,0:T(8,128)}, f32[1,384]{1,0:T(1,128)}) custom-call(s32[1]{0:T(128)} %bitcast.me_ref, bf16[4096,1024]{1,0:T(8,128)(2,1)} %get-tuple-element.160.normed_ref, bf16[4096,384]{1,0:T(8,128)(2,1)} %attend_back.3.grad_ref.refs_1_, bf16[1024,256]{1,0:T(8,128)(2,1)} %refs_5_.12, ...), custom_call_target="tpu_custom_call" | custom-call | flops 1 | bytes 1 | tf_op jit(solution)/shard_map/weight_step/pallas_call | solution.py:375
  505.1 1.5 pack.1
  506.6 1.5 collective-permute-start.41
  508.1 3.0 stack_step.2.even_ref
  511.1 4.4 collective-permute-done.41
  516.3 2.6 late_step.1
  518.9 5.1 unproject.4
  524.1 5.2 unproject.5
  529.6 3.5 collective-permute-start.37
  533.7 7.0 %collective-permute-done.37 = bf16[128,1024]{1,0:T(8,128)(2,1)S(1)} collective-permute-done((bf16[128,1024]{1,0:T(8,128)(2,1)S(1)}, bf16[128,1024]{1,0:T(8,128)(2,1)S(1)}, u32[]{:S(2)}, u32[]{:S(2)}) %collective-permute-start.37) | collective-permute-done | bytes 262176 | tf_op jit(solution)/shard_map/ppermute | solution.py:1096
  540.7 9.9 %collective-permute-start.35 = (bf16[128,1024]{1,0:T(8,128)(2,1)S(1)}, bf16[128,1024]{1,0:T(8,128)(2,1)S(1)}, u32[]{:S(2)}, u32[]{:S(2)}) collective-permute-start(bf16[128,1024]{1,0:T(8,128)(2,1)S(1)} %copy-done.36), channel_id=1, source_target_pairs={{0,8},{4,12},{8,0},{12,4},{16,24},{20,28},{24,16},{28,20},{1,9},{5... | collective-permute-start | bytes 786440 | tf_op jit(solution)/shard_map/ppermute | solution.py:1096
  550.6 4.4 collective-permute-done.36
  555.0 5.5 collective-permute-done.35
  560.7 5.7 unproject.6
  567.4 2.9 collective-permute-start.39
  570.3 1.5 collective-permute-start.40
  571.8 4.1 add_convert_fusion
  575.8 5.5 unproject.7.refs_0_
  581.3 7.1 %feed_grads.1 = (f32[1024,1024]{1,0:T(8,128)}, f32[1024,1024]{1,0:T(8,128)}) custom-call(s32[1]{0:T(128)} %bitcast.me_ref, bf16[1024,1024]{1,0:T(8,128)(2,1)} %stack_step.2.even_ref, bf16[1024,1024]{1,0:T(8,128)(2,1)} %collective-permute-done.44.odd_ref), custom_call_target="tpu_custom_call" | custom-call | flops 1 | bytes 1 | tf_op jit(solution)/shard_map/feed_grads/pallas_call | solution.py:375
  589.6 2.3 stack_step.3.even_ref
  592.4 5.0 collective-permute-start.46
  597.4 2.2 collective-permute-done.46
  599.6 3.0 collective-permute-start.47
  602.6 2.2 collective-permute-done.47
  604.9 9.5 %collective-permute-done.45.refs_1_ = bf16[1024,1024]{1,0:T(8,128)(2,1)} collective-permute-done((bf16[1024,1024]{1,0:T(8,128)(2,1)}, bf16[1024,1024]{1,0:T(8,128)(2,1)}, u32[]{:S(2)}, u32[]{:S(2)}) %collective-permute-start.45) | collective-permute-done | bytes 2097184 | tf_op jit(solution)/shard_map/ppermute | solution.py:1084
  615.3 2.9 collective-permute-done.48
  619.5 7.7 %input_step.1 = f32[1024,1024]{1,0:T(8,128)} custom-call(bf16[1024,1024]{1,0:T(8,128)(2,1)} %unproject.7.refs_0_, bf16[1024,1024]{1,0:T(8,128)(2,1)} %collective-permute-done.45.refs_1_, bf16[1024,1024]{1,0:T(8,128)(2,1)} %refs_2_.23, f32[1024,1024]{1,0:T(8,128)} %get-tuple-element.282.refs_3_, bf16[1024]{0:T(1024)(128)(2,1)} %refs_4_.17), custom_call_target="tpu_custom_call" | custom-call | flops 1 | bytes 1 | tf_op jit(solution)/shard_map/input_step/pallas_call | solution.py:375
  628.1 4.0 spread.1
  (166 shorter events, 34.7 us)
Async XLA Ops:
  0.7 52.8 %copy-start.1 = (bf16[1024,1024]{1,0:T(8,128)(2,1)S(1)}, bf16[1024,1024]{1,0:T(8,128)(2,1)}, u32[]{:S(2)}) copy-start(bf16[1024,1024]{1,0:T(8,128)(2,1)} %refs_3_.17) | copy-start | bytes 6291460
  0.7 54.6 %copy-start.14 = (bf16[256,1024]{1,0:T(8,128)(2,1)S(1)}, bf16[256,1024]{1,0:T(8,128)(2,1)}, u32[]{:S(2)}) copy-start(bf16[256,1024]{1,0:T(8,128)(2,1)} %refs_5_.8) | copy-start | bytes 1572868
  0.7 4.5 collective-permute-start.1
  1.2 49.1 %collective-permute-start = (bf16[1024,1024]{1,0:T(8,128)(2,1)}, bf16[1024,1024]{1,0:T(8,128)(2,1)}, u32[]{:S(2)}, u32[]{:S(2)}) collective-permute-start(bf16[1024,1024]{1,0:T(8,128)(2,1)} %refs_2_.23), channel_id=1, source_target_pairs={{0,2},{1,3},{2,0},{3,1},{4,6},{5,7},{6,4},{7,5},{8,10},{9,11},{10,... | collective-permute-start | bytes 6291464 | tf_op jit(solution)/shard_map/ppermute | solution.py:1084
  50.3 5.2 collective-permute-start.2
  53.5 49.2 %collective-permute-start.3 = (bf16[1024,1024]{1,0:T(8,128)(2,1)S(1)}, bf16[1024,1024]{1,0:T(8,128)(2,1)}, u32[]{:S(2)}, u32[]{:S(2)}) collective-permute-start(bf16[1024,1024]{1,0:T(8,128)(2,1)S(1)} %copy-done.1), channel_id=1, source_target_pairs={{0,2},{1,3},{2,0},{3,1},{4,6},{5,7},{6,4},{7,5},{8,10},{9,11},{10,... | collective-permute-start | bytes 6291464 | tf_op jit(solution)/shard_map/ppermute | solution.py:1084
  55.2 85.8 %collective-permute-start.10 = (bf16[256,1024]{1,0:T(8,128)(2,1)S(1)}, bf16[256,1024]{1,0:T(8,128)(2,1)S(1)}, u32[]{:S(2)}, u32[]{:S(2)}) collective-permute-start(bf16[256,1024]{1,0:T(8,128)(2,1)S(1)} %copy-done.14), channel_id=1, source_target_pairs={{0,2},{1,3},{2,0},{3,1},{4,6},{5,7},{6,4},{7,5},{8,10},{9,11},{10,... | collective-permute-start | bytes 1572872 | tf_op jit(solution)/shard_map/ppermute | solution.py:1084
  100.9 42.3 %collective-permute-start.6 = (bf16[4096,128]{1,0:T(8,128)(2,1)}, bf16[4096,128]{1,0:T(8,128)(2,1)S(1)}, u32[]{:S(2)}, u32[]{:S(2)}) collective-permute-start(bf16[4096,128]{1,0:T(8,128)(2,1)} %get-tuple-element.164.refs_0_.refs_6_), channel_id=1, source_target_pairs={{0,2},{1,3},{2,0},{3,1},{4,6},{5,7},{6,4},{7,5},{8,10},{9,11},{10,... | collective-permute-start | bytes 3145736 | tf_op jit(solution)/shard_map/ppermute | solution.py:1084
  102.7 41.0 %collective-permute-start.9 = (bf16[1024,1024]{1,0:T(8,128)(2,1)}, bf16[1024,1024]{1,0:T(8,128)(2,1)}, u32[]{:S(2)}, u32[]{:S(2)}) collective-permute-start(bf16[1024,1024]{1,0:T(8,128)(2,1)} %collective-permute-done.3.refs_2_), channel_id=1, source_target_pairs={{0,1},{1,0},{2,3},{3,2},{4,5},{5,4},{6,7},{7,6},{8,9},{9,8},{10,11... | collective-permute-start | bytes 6291464 | tf_op jit(solution)/shard_map/ppermute | solution.py:1084
  102.7 40.9 %collective-permute-start.8 = (bf16[1024,1024]{1,0:T(8,128)(2,1)S(1)}, bf16[1024,1024]{1,0:T(8,128)(2,1)}, u32[]{:S(2)}, u32[]{:S(2)}) collective-permute-start(bf16[1024,1024]{1,0:T(8,128)(2,1)S(1)} %copy-done.1), channel_id=1, source_target_pairs={{0,1},{1,0},{2,3},{3,2},{4,5},{5,4},{6,7},{7,6},{8,9},{9,8},{10,11... | collective-permute-start | bytes 6291464 | tf_op jit(solution)/shard_map/ppermute | solution.py:1084
  103.2 39.8 %copy-start.4 = (bf16[4096,128]{1,0:T(8,128)(2,1)S(1)}, bf16[4096,128]{1,0:T(8,128)(2,1)}, u32[]{:S(2)}) copy-start(bf16[4096,128]{1,0:T(8,128)(2,1)} %get-tuple-element.164.refs_0_.refs_6_) | copy-start | bytes 3145732
  139.9 25.3 %collective-permute-start.7 = (bf16[4096,128]{1,0:T(8,128)(2,1)}, bf16[4096,128]{1,0:T(8,128)(2,1)S(1)}, u32[]{:S(2)}, u32[]{:S(2)}) collective-permute-start(bf16[4096,128]{1,0:T(8,128)(2,1)} %get-tuple-element.169.refs_1_.refs_6_), channel_id=1, source_target_pairs={{0,2},{1,3},{2,0},{3,1},{4,6},{5,7},{6,4},{7,5},{8,10},{9,11},{10,... | collective-permute-start | bytes 3145736 | tf_op jit(solution)/shard_map/ppermute | solution.py:1084
  141.0 2.0 collective-permute-start.11
  143.0 25.4 %collective-permute-start.4 = (bf16[4096,128]{1,0:T(8,128)(2,1)S(1)}, bf16[4096,128]{1,0:T(8,128)(2,1)S(1)}, u32[]{:S(2)}, u32[]{:S(2)}) collective-permute-start(bf16[4096,128]{1,0:T(8,128)(2,1)S(1)} %copy-done.4), channel_id=1, source_target_pairs={{0,1},{1,0},{2,3},{3,2},{4,5},{5,4},{6,7},{7,6},{8,9},{9,8},{10,11... | collective-permute-start | bytes 3145736 | tf_op jit(solution)/shard_map/ppermute | solution.py:1084
  143.2 15.8 %copy-start.5 = (bf16[4096,128]{1,0:T(8,128)(2,1)}, bf16[4096,128]{1,0:T(8,128)(2,1)S(1)}, u32[]{:S(2)}) copy-start(bf16[4096,128]{1,0:T(8,128)(2,1)S(1)} %collective-permute-done.6.refs_4_) | copy-start | bytes 3145732
  143.2 25.3 %collective-permute-start.5 = (bf16[4096,128]{1,0:T(8,128)(2,1)}, bf16[4096,128]{1,0:T(8,128)(2,1)S(1)}, u32[]{:S(2)}, u32[]{:S(2)}) collective-permute-start(bf16[4096,128]{1,0:T(8,128)(2,1)} %get-tuple-element.169.refs_1_.refs_6_), channel_id=1, source_target_pairs={{0,1},{1,0},{2,3},{3,2},{4,5},{5,4},{6,7},{7,6},{8,9},{9,8},{10,11... | collective-permute-start | bytes 3145736 | tf_op jit(solution)/shard_map/ppermute | solution.py:1084
  143.6 24.9 %collective-permute-start.12 = (bf16[4096,128]{1,0:T(8,128)(2,1)S(1)}, bf16[4096,128]{1,0:T(8,128)(2,1)S(1)}, u32[]{:S(2)}, u32[]{:S(2)}) collective-permute-start(bf16[4096,128]{1,0:T(8,128)(2,1)S(1)} %collective-permute-done.6.refs_4_), channel_id=1, source_target_pairs={{0,1},{1,0},{2,3},{3,2},{4,5},{5,4},{6,7},{7,6},{8,9},{9,8},{10,11... | collective-permute-start | bytes 3145736 | tf_op jit(solution)/shard_map/ppermute | solution.py:1084
  165.2 3.4 collective-permute-start.13
  165.2 3.2 collective-permute-start.14
  205.8 12.1 %collective-permute-start.16 = (bf16[1024,1024]{1,0:T(8,128)(2,1)}, bf16[1024,1024]{1,0:T(8,128)(2,1)S(1)}, u32[]{:S(2)}, u32[]{:S(2)}) collective-permute-start(bf16[1024,1024]{1,0:T(8,128)(2,1)} %get-tuple-element.183), channel_id=1, source_target_pairs={{0,1},{1,0},{2,3},{3,2},{4,5},{5,4},{6,7},{7,6},{8,9},{9,8},{10,11... | collective-permute-start | bytes 6291464 | tf_op jit(solution)/shard_map/ppermute | solution.py:1084
  217.8 15.1 %collective-permute-start.15 = (bf16[1024,1024]{1,0:T(8,128)(2,1)}, bf16[1024,1024]{1,0:T(8,128)(2,1)S(1)}, u32[]{:S(2)}, u32[]{:S(2)}) collective-permute-start(bf16[1024,1024]{1,0:T(8,128)(2,1)} %get-tuple-element.182), channel_id=1, source_target_pairs={{0,1},{1,0},{2,3},{3,2},{4,5},{5,4},{6,7},{7,6},{8,9},{9,8},{10,11... | collective-permute-start | bytes 6291464 | tf_op jit(solution)/shard_map/ppermute | solution.py:1084
  231.8 48.2 %collective-permute-start.17 = (bf16[1024,1024]{1,0:T(8,128)(2,1)}, bf16[1024,1024]{1,0:T(8,128)(2,1)}, u32[]{:S(2)}, u32[]{:S(2)}) collective-permute-start(bf16[1024,1024]{1,0:T(8,128)(2,1)} %get-tuple-element.196), channel_id=1, source_target_pairs={{0,2},{1,3},{2,0},{3,1},{4,6},{5,7},{6,4},{7,5},{8,10},{9,11},{10,... | collective-permute-start | bytes 6291464 | tf_op jit(solution)/shard_map/ppermute | solution.py:1084
  260.3 52.7 %collective-permute-start.21 = (bf16[512,1024]{1,0:T(8,128)(2,1)}, bf16[512,1024]{1,0:T(8,128)(2,1)S(1)}, u32[]{:S(2)}, u32[]{:S(2)}) collective-permute-start(bf16[512,1024]{1,0:T(8,128)(2,1)} %get-tuple-element.207), channel_id=1, source_target_pairs={{0,4},{4,0},{8,12},{12,8},{16,20},{20,16},{24,28},{28,24},{1,5},{5... | collective-permute-start | bytes 3145736 | tf_op jit(solution)/shard_map/ppermute | solution.py:1096
  275.1 37.9 %collective-permute-start.22 = (bf16[512,1024]{1,0:T(8,128)(2,1)}, bf16[512,1024]{1,0:T(8,128)(2,1)S(1)}, u32[]{:S(2)}, u32[]{:S(2)}) collective-permute-start(bf16[512,1024]{1,0:T(8,128)(2,1)} %get-tuple-element.208), channel_id=1, source_target_pairs={{0,4},{4,0},{8,12},{12,8},{16,20},{20,16},{24,28},{28,24},{1,5},{5... | collective-permute-start | bytes 3145736 | tf_op jit(solution)/shard_map/ppermute | solution.py:1096
  290.2 28.4 %collective-permute-start.18 = (bf16[1024,256]{1,0:T(8,128)(2,1)}, bf16[1024,256]{1,0:T(8,128)(2,1)S(1)}, u32[]{:S(2)}, u32[]{:S(2)}) collective-permute-start(bf16[1024,256]{1,0:T(8,128)(2,1)} %get-tuple-element.199), channel_id=1, source_target_pairs={{0,1},{1,0},{2,3},{3,2},{4,5},{5,4},{6,7},{7,6},{8,9},{9,8},{10,11... | collective-permute-start | bytes 1572872 | tf_op jit(solution)/shard_map/ppermute | solution.py:1084
  290.3 28.3 %collective-permute-start.19 = (bf16[1024,256]{1,0:T(8,128)(2,1)}, bf16[1024,256]{1,0:T(8,128)(2,1)S(1)}, u32[]{:S(2)}, u32[]{:S(2)}) collective-permute-start(bf16[1024,256]{1,0:T(8,128)(2,1)} %get-tuple-element.200), channel_id=1, source_target_pairs={{0,2},{1,3},{2,0},{3,1},{4,6},{5,7},{6,4},{7,5},{8,10},{9,11},{10,... | collective-permute-start | bytes 1572872 | tf_op jit(solution)/shard_map/ppermute | solution.py:1084
  291.4 27.2 %collective-permute-start.20 = (bf16[1024,256]{1,0:T(8,128)(2,1)}, bf16[1024,256]{1,0:T(8,128)(2,1)S(1)}, u32[]{:S(2)}, u32[]{:S(2)}) collective-permute-start(bf16[1024,256]{1,0:T(8,128)(2,1)} %get-tuple-element.201), channel_id=1, source_target_pairs={{0,3},{1,2},{2,1},{3,0},{4,7},{5,6},{6,5},{7,4},{8,11},{9,10},{10,... | collective-permute-start | bytes 1572872 | tf_op jit(solution)/shard_map/ppermute | solution.py:1084
  318.6 75.0 %collective-permute-start.23 = (bf16[2048,256]{1,0:T(8,128)(2,1)}, bf16[2048,256]{1,0:T(8,128)(2,1)S(1)}, u32[]{:S(2)}, u32[]{:S(2)}) collective-permute-start(bf16[2048,256]{1,0:T(8,128)(2,1)} %get-tuple-element.218), channel_id=1, source_target_pairs={{0,1},{1,0},{2,3},{3,2},{4,5},{5,4},{6,7},{7,6},{8,9},{9,8},{10,11... | collective-permute-start | bytes 3145736 | tf_op jit(solution)/shard_map/ppermute | solution.py:1084
  319.1 76.9 %collective-permute-start.27 = (bf16[256,1024]{1,0:T(8,128)(2,1)}, bf16[256,1024]{1,0:T(8,128)(2,1)S(1)}, u32[]{:S(2)}, u32[]{:S(2)}) collective-permute-start(bf16[256,1024]{1,0:T(8,128)(2,1)} %get-tuple-element.233), channel_id=1, source_target_pairs={{0,24},{4,28},{8,16},{12,20},{16,8},{20,12},{24,0},{28,4},{1,25},{... | collective-permute-start | bytes 1572872 | tf_op jit(solution)/shard_map/ppermute | solution.py:1096
  322.7 73.3 %collective-permute-start.26 = (bf16[256,1024]{1,0:T(8,128)(2,1)}, bf16[256,1024]{1,0:T(8,128)(2,1)S(1)}, u32[]{:S(2)}, u32[]{:S(2)}) collective-permute-start(bf16[256,1024]{1,0:T(8,128)(2,1)} %get-tuple-element.232), channel_id=1, source_target_pairs={{0,16},{4,20},{8,24},{12,28},{16,0},{20,4},{24,8},{28,12},{1,17},{... | collective-permute-start | bytes 1572872 | tf_op jit(solution)/shard_map/ppermute | solution.py:1096
  322.7 73.3 %collective-permute-start.25 = (bf16[256,1024]{1,0:T(8,128)(2,1)}, bf16[256,1024]{1,0:T(8,128)(2,1)}, u32[]{:S(2)}, u32[]{:S(2)}) collective-permute-start(bf16[256,1024]{1,0:T(8,128)(2,1)} %get-tuple-element.231), channel_id=1, source_target_pairs={{0,8},{4,12},{8,0},{12,4},{16,24},{20,28},{24,16},{28,20},{1,9},{5... | collective-permute-start | bytes 1572872 | tf_op jit(solution)/shard_map/ppermute | solution.py:1096
  323.4 89.4 %collective-permute-start.28 = (bf16[2048,1024]{1,0:T(8,128)(2,1)}, bf16[2048,1024]{1,0:T(8,128)(2,1)}, u32[]{:S(2)}, u32[]{:S(2)}) collective-permute-start(bf16[2048,1024]{1,0:T(8,128)(2,1)} %get-tuple-element.235), channel_id=1, source_target_pairs={{0,1},{1,0},{2,3},{3,2},{4,5},{5,4},{6,7},{7,6},{8,9},{9,8},{10,11... | collective-permute-start | bytes 12582920 | tf_op jit(solution)/shard_map/ppermute | solution.py:1084
  323.5 70.2 %copy-start.17 = (bf16[2048,256]{1,0:T(8,128)(2,1)S(1)}, bf16[2048,256]{1,0:T(8,128)(2,1)}, u32[]{:S(2)}) copy-start(bf16[2048,256]{1,0:T(8,128)(2,1)} %get-tuple-element.217) | copy-start | bytes 3145732
  394.9 14.5 %collective-permute-start.24 = (bf16[1024,256]{1,0:T(8,128)(2,1)}, bf16[1024,256]{1,0:T(8,128)(2,1)S(1)}, u32[]{:S(2)}, u32[]{:S(2)}) collective-permute-start(bf16[1024,256]{1,0:T(8,128)(2,1)} %get-tuple-element.222), channel_id=1, source_target_pairs={{0,2},{1,3},{2,0},{3,1},{4,6},{5,7},{6,4},{7,5},{8,10},{9,11},{10,... | collective-permute-start | bytes 1572872 | tf_op jit(solution)/shard_map/ppermute | solution.py:1084
  397.4 24.2 %copy-start.13 = (bf16[256,1024]{1,0:T(8,128)(2,1)}, bf16[256,1024]{1,0:T(8,128)(2,1)S(1)}, u32[]{:S(2)}) copy-start(bf16[256,1024]{1,0:T(8,128)(2,1)S(1)} %add_convert_fusion.3.refs_0_) | copy-start | bytes 1572868
  397.4 15.5 %copy-start.3 = (bf16[2048,1024]{1,0:T(8,128)(2,1)S(1)}, bf16[2048,1024]{1,0:T(8,128)(2,1)}, u32[]{:S(2)}) copy-start(bf16[2048,1024]{1,0:T(8,128)(2,1)} %get-tuple-element.234) | copy-start | bytes 12582916
  417.5 77.0 %collective-permute-start.30 = (bf16[256,1024]{1,0:T(8,128)(2,1)S(1)}, bf16[256,1024]{1,0:T(8,128)(2,1)S(1)}, u32[]{:S(2)}, u32[]{:S(2)}) collective-permute-start(bf16[256,1024]{1,0:T(8,128)(2,1)S(1)} %add_convert_fusion.3.refs_0_), channel_id=1, source_target_pairs={{0,8},{4,12},{8,0},{12,4},{16,24},{20,28},{24,16},{28,20},{1,9},{5... | collective-permute-start | bytes 1572872 | tf_op jit(solution)/shard_map/ppermute | solution.py:1096
  418.7 75.7 %collective-permute-start.31 = (bf16[256,1024]{1,0:T(8,128)(2,1)S(1)}, bf16[256,1024]{1,0:T(8,128)(2,1)}, u32[]{:S(2)}, u32[]{:S(2)}) collective-permute-start(bf16[256,1024]{1,0:T(8,128)(2,1)S(1)} %add_convert_fusion.3.refs_0_), channel_id=1, source_target_pairs={{0,16},{4,20},{8,24},{12,28},{16,0},{20,4},{24,8},{28,12},{1,17},{... | collective-permute-start | bytes 1572872 | tf_op jit(solution)/shard_map/ppermute | solution.py:1096
  421.6 72.8 %collective-permute-start.32 = (bf16[256,1024]{1,0:T(8,128)(2,1)S(1)}, bf16[256,1024]{1,0:T(8,128)(2,1)}, u32[]{:S(2)}, u32[]{:S(2)}) collective-permute-start(bf16[256,1024]{1,0:T(8,128)(2,1)S(1)} %add_convert_fusion.3.refs_0_), channel_id=1, source_target_pairs={{0,24},{4,28},{8,16},{12,20},{16,8},{20,12},{24,0},{28,4},{1,25},{... | collective-permute-start | bytes 1572872 | tf_op jit(solution)/shard_map/ppermute | solution.py:1096
  421.9 72.6 %collective-permute-start.29 = (bf16[512,640]{1,0:T(8,128)(2,1)}, bf16[512,640]{1,0:T(8,128)(2,1)S(1)}, u32[]{:S(2)}, u32[]{:S(2)}) collective-permute-start(bf16[512,640]{1,0:T(8,128)(2,1)} %get-tuple-element.240), channel_id=1, source_target_pairs={{0,4},{4,0},{8,12},{12,8},{16,20},{20,16},{24,28},{28,24},{1,5},{5... | collective-permute-start | bytes 1966088 | tf_op jit(solution)/shard_map/ppermute | solution.py:1096
  423.3 71.1 %collective-permute-start.33 = (bf16[1024,1024]{1,0:T(8,128)(2,1)}, bf16[1024,1024]{1,0:T(8,128)(2,1)}, u32[]{:S(2)}, u32[]{:S(2)}) collective-permute-start(bf16[1024,1024]{1,0:T(8,128)(2,1)} %get-tuple-element.243), channel_id=1, source_target_pairs={{0,2},{1,3},{2,0},{3,1},{4,6},{5,7},{6,4},{7,5},{8,10},{9,11},{10,... | collective-permute-start | bytes 6291464 | tf_op jit(solution)/shard_map/ppermute | solution.py:1084
  494.4 10.0 %copy-start.25 = (bf16[256,1024]{1,0:T(8,128)(2,1)}, bf16[256,1024]{1,0:T(8,128)(2,1)S(1)}, u32[]{:S(2)}) copy-start(bf16[256,1024]{1,0:T(8,128)(2,1)S(1)} %collective-permute-done.30.refs_1_) | copy-start | bytes 1572868
  494.5 10.0 %copy-start.22 = (bf16[512,640]{1,0:T(8,128)(2,1)}, bf16[512,640]{1,0:T(8,128)(2,1)S(1)}, u32[]{:S(2)}) copy-start(bf16[512,640]{1,0:T(8,128)(2,1)S(1)} %collective-permute-done.29.refs_1_) | copy-start | bytes 1966084
  504.5 11.1 %collective-permute-start.34 = (bf16[512,384]{1,0:T(8,128)(2,1)}, bf16[512,384]{1,0:T(8,128)(2,1)S(1)}, u32[]{:S(2)}, u32[]{:S(2)}) collective-permute-start(bf16[512,384]{1,0:T(8,128)(2,1)} %get-tuple-element.262), channel_id=1, source_target_pairs={{0,4},{4,0},{8,12},{12,8},{16,20},{20,16},{24,28},{28,24},{1,5},{5... | collective-permute-start | bytes 1179656 | tf_op jit(solution)/shard_map/ppermute | solution.py:1096
  506.6 8.9 %collective-permute-start.41 = (f32[16,1024]{1,0:T(8,128)}, f32[16,1024]{1,0:T(8,128)S(1)}, u32[]{:S(2)}, u32[]{:S(2)}) collective-permute-start(f32[16,1024]{1,0:T(8,128)} %pack.1), channel_id=1, source_target_pairs={{0,4},{4,0},{8,12},{12,8},{16,20},{20,16},{24,28},{28,24},{1,5},{5... | collective-permute-start | bytes 196616 | tf_op jit(solution)/shard_map/ppermute | solution.py:1096
  524.0 9.7 %copy-start.37 = (bf16[128,1024]{1,0:T(8,128)(2,1)S(1)}, bf16[128,1024]{1,0:T(8,128)(2,1)}, u32[]{:S(2)}) copy-start(bf16[128,1024]{1,0:T(8,128)(2,1)} %get-tuple-element.265) | copy-start | bytes 786436
  524.0 16.7 %copy-start.36 = (bf16[128,1024]{1,0:T(8,128)(2,1)S(1)}, bf16[128,1024]{1,0:T(8,128)(2,1)}, u32[]{:S(2)}) copy-start(bf16[128,1024]{1,0:T(8,128)(2,1)} %get-tuple-element.264) | copy-start | bytes 786436
  524.0 36.5 %copy-start.27 = (bf16[128,1024]{1,0:T(8,128)(2,1)S(1)}, bf16[128,1024]{1,0:T(8,128)(2,1)}, u32[]{:S(2)}) copy-start(bf16[128,1024]{1,0:T(8,128)(2,1)} %get-tuple-element.263) | copy-start | bytes 786436
  524.0 36.7 %collective-permute-start.42 = (bf16[1024,1024]{1,0:T(8,128)(2,1)}, bf16[1024,1024]{1,0:T(8,128)(2,1)}, u32[]{:S(2)}, u32[]{:S(2)}) collective-permute-start(bf16[1024,1024]{1,0:T(8,128)(2,1)} %unproject.4), channel_id=1, source_target_pairs={{0,1},{1,0},{2,3},{3,2},{4,5},{5,4},{6,7},{7,6},{8,9},{9,8},{10,11... | collective-permute-start | bytes 6291464 | tf_op jit(solution)/shard_map/ppermute | solution.py:1084
  529.3 41.0 %collective-permute-start.43 = (bf16[1024,1024]{1,0:T(8,128)(2,1)}, bf16[1024,1024]{1,0:T(8,128)(2,1)}, u32[]{:S(2)}, u32[]{:S(2)}) collective-permute-start(bf16[1024,1024]{1,0:T(8,128)(2,1)} %unproject.5), channel_id=1, source_target_pairs={{0,1},{1,0},{2,3},{3,2},{4,5},{5,4},{6,7},{7,6},{8,9},{9,8},{10,11... | collective-permute-start | bytes 6291464 | tf_op jit(solution)/shard_map/ppermute | solution.py:1084
  529.6 11.1 %collective-permute-start.37 = (bf16[128,1024]{1,0:T(8,128)(2,1)S(1)}, bf16[128,1024]{1,0:T(8,128)(2,1)S(1)}, u32[]{:S(2)}, u32[]{:S(2)}) collective-permute-start(bf16[128,1024]{1,0:T(8,128)(2,1)S(1)} %copy-done.38), channel_id=1, source_target_pairs={{0,24},{4,28},{8,16},{12,20},{16,8},{20,12},{24,0},{28,4},{1,25},{... | collective-permute-start | bytes 786440 | tf_op jit(solution)/shard_map/ppermute | solution.py:1096
  533.2 48.1 %collective-permute-start.44 = (bf16[1024,1024]{1,0:T(8,128)(2,1)}, bf16[1024,1024]{1,0:T(8,128)(2,1)}, u32[]{:S(2)}, u32[]{:S(2)}) collective-permute-start(bf16[1024,1024]{1,0:T(8,128)(2,1)} %stack_step.2.even_ref), channel_id=1, source_target_pairs={{0,4},{4,0},{8,12},{12,8},{16,20},{20,16},{24,28},{28,24},{1,5},{5... | collective-permute-start | bytes 6291464 | tf_op jit(solution)/shard_map/ppermute | solution.py:1096
  533.7 21.2 %collective-permute-start.36 = (bf16[128,1024]{1,0:T(8,128)(2,1)S(1)}, bf16[128,1024]{1,0:T(8,128)(2,1)S(1)}, u32[]{:S(2)}, u32[]{:S(2)}) collective-permute-start(bf16[128,1024]{1,0:T(8,128)(2,1)S(1)} %copy-done.37), channel_id=1, source_target_pairs={{0,16},{4,20},{8,24},{12,28},{16,0},{20,4},{24,8},{28,12},{1,17},{... | collective-permute-start | bytes 786440 | tf_op jit(solution)/shard_map/ppermute | solution.py:1096
  540.7 19.8 %collective-permute-start.35 = (bf16[128,1024]{1,0:T(8,128)(2,1)S(1)}, bf16[128,1024]{1,0:T(8,128)(2,1)S(1)}, u32[]{:S(2)}, u32[]{:S(2)}) collective-permute-start(bf16[128,1024]{1,0:T(8,128)(2,1)S(1)} %copy-done.36), channel_id=1, source_target_pairs={{0,8},{4,12},{8,0},{12,4},{16,24},{20,28},{24,16},{28,20},{1,9},{5... | collective-permute-start | bytes 786440 | tf_op jit(solution)/shard_map/ppermute | solution.py:1096
  560.7 11.1 %copy-start = (f32[1024,1024]{1,0:T(8,128)S(1)}, f32[1024,1024]{1,0:T(8,128)}, u32[]{:S(2)}) copy-start(f32[1024,1024]{1,0:T(8,128)} %get-tuple-element.197.refs_2_) | copy-start | bytes 12582916
  566.4 48.0 %collective-permute-start.45 = (bf16[1024,1024]{1,0:T(8,128)(2,1)}, bf16[1024,1024]{1,0:T(8,128)(2,1)}, u32[]{:S(2)}, u32[]{:S(2)}) collective-permute-start(bf16[1024,1024]{1,0:T(8,128)(2,1)} %unproject.6), channel_id=1, source_target_pairs={{0,2},{1,3},{2,0},{3,1},{4,6},{5,7},{6,4},{7,5},{8,10},{9,11},{10,... | collective-permute-start | bytes 6291464 | tf_op jit(solution)/shard_map/ppermute | solution.py:1084
  567.4 21.1 %collective-permute-start.38 = (bf16[128,1024]{1,0:T(8,128)(2,1)S(1)}, bf16[128,1024]{1,0:T(8,128)(2,1)S(1)}, u32[]{:S(2)}, u32[]{:S(2)}) collective-permute-start(bf16[128,1024]{1,0:T(8,128)(2,1)S(1)} %add_convert_fusion.6.refs_0_), channel_id=1, source_target_pairs={{0,8},{4,12},{8,0},{12,4},{16,24},{20,28},{24,16},{28,20},{1,9},{5... | collective-permute-start | bytes 786440 | tf_op jit(solution)/shard_map/ppermute | solution.py:1096
  567.4 21.4 %collective-permute-start.39 = (bf16[128,1024]{1,0:T(8,128)(2,1)S(1)}, bf16[128,1024]{1,0:T(8,128)(2,1)S(1)}, u32[]{:S(2)}, u32[]{:S(2)}) collective-permute-start(bf16[128,1024]{1,0:T(8,128)(2,1)S(1)} %add_convert_fusion.6.refs_0_), channel_id=1, source_target_pairs={{0,16},{4,20},{8,24},{12,28},{16,0},{20,4},{24,8},{28,12},{1,17},{... | collective-permute-start | bytes 786440 | tf_op jit(solution)/shard_map/ppermute | solution.py:1096
  570.3 18.5 %collective-permute-start.40 = (bf16[128,1024]{1,0:T(8,128)(2,1)S(1)}, bf16[128,1024]{1,0:T(8,128)(2,1)S(1)}, u32[]{:S(2)}, u32[]{:S(2)}) collective-permute-start(bf16[128,1024]{1,0:T(8,128)(2,1)S(1)} %add_convert_fusion.6.refs_0_), channel_id=1, source_target_pairs={{0,24},{4,28},{8,16},{12,20},{16,8},{20,12},{24,0},{28,4},{1,25},{... | collective-permute-start | bytes 786440 | tf_op jit(solution)/shard_map/ppermute | solution.py:1096
  591.8 35.3 %collective-permute-start.50 = (bf16[512,1024]{1,0:T(8,128)(2,1)}, bf16[512,1024]{1,0:T(8,128)(2,1)S(1)}, u32[]{:S(2)}, u32[]{:S(2)}) collective-permute-start(bf16[512,1024]{1,0:T(8,128)(2,1)} %stack_step.3.even_ref), channel_id=1, source_target_pairs={{0,4},{4,0},{8,12},{12,8},{16,20},{20,16},{24,28},{28,24},{1,5},{5... | collective-permute-start | bytes 3145736 | tf_op jit(solution)/shard_map/ppermute | solution.py:1096
  592.4 7.2 %collective-permute-start.46 = (f32[16,1024]{1,0:T(8,128)S(1)}, f32[16,1024]{1,0:T(8,128)S(1)}, u32[]{:S(2)}, u32[]{:S(2)}) collective-permute-start(f32[16,1024]{1,0:T(8,128)S(1)} %add.85), channel_id=1, source_target_pairs={{0,8},{4,12},{8,0},{12,4},{16,24},{20,28},{24,16},{28,20},{1,9},{5... | collective-permute-start | bytes 196616 | tf_op jit(solution)/shard_map/ppermute | solution.py:1096
  599.6 5.2 collective-permute-start.47
  614.4 3.9 collective-permute-start.48
  618.3 13.8 %collective-permute-start.49 = (f32[8,1024]{1,0:T(8,128)S(1)}, f32[8,1024]{1,0:T(8,128)S(1)}, u32[]{:S(2)}, u32[]{:S(2)}) collective-permute-start(f32[8,1024]{1,0:T(8,128)S(1)} %slice_add_fusion), channel_id=1, source_target_pairs={{0,1},{1,0},{2,3},{3,2},{4,5},{5,4},{6,7},{7,6},{8,9},{9,8},{10,11... | collective-permute-start | bytes 98312 | tf_op jit(solution)/shard_map/ppermute | solution.py:1084
  (26 other events, 68.9 us)

commit v8 on v6

--- a/solution.py
+++ b/solution.py
@@ -108,18 +108,14 @@
             body(slot, pl.ds(offset, chunk), pl.ds(slot * rows + offset, chunk), home + offset)
 
 
-def attend_kernel(
-    me_ref, apart_ref, slope_ref, q_ref, k_ref, v_ref, o_ref, lse_ref, qa, ka, va, *, slots, pair, tile
-):
-    me = me_ref[0]
-    total = q_ref.shape[0]
-    rows = total // slots
+def attend_columns(slot_map, refs, scratch, pair, slope_ref, apart, first=0):
+    (q_ref, k_ref, v_ref), (qa, ka, va) = refs, scratch
+    me, slots, rows = slot_map
     chunk = min(rows, 512)
-    apart = apart_ref[0].astype(F32)
 
     def prepare(slot, inner, spot, place):
         place = pl.multiple_of(place, chunk)
-        home = pl.ds(place, chunk)
+        home = pl.ds(pl.multiple_of(place - first, chunk), chunk)
         for s in range(pair):
             cols = slice(s * HD, (s + 1) * HD)
             qa[s, home, :] = query_columns(q_ref[spot, cols], place, slope_ref[s], apart)
@@ -127,35 +123,137 @@
             va[s, home, :] = ones_columns(v_ref[spot, cols], 1)
 
     each_chunk(me, slots, rows, prepare)
-    causal = lax.broadcasted_iota(jnp.int32, (tile, tile), 1) <= lax.broadcasted_iota(
+
+
+def attend_step(queries, carry, keys, values, mask):
+    after = []
+    for query, (top, mix), key, value in zip(queries, carry, keys, values):
+        scores = dot(query, key, NT)
+        if mask is not None:
+            scores = jnp.where(mask, scores, -1e30)
+        higher = jnp.maximum(top, jnp.max(scores, axis=1, keepdims=True))
+        weights = low(jnp.exp2(scores - higher))
+        mix = mix * jnp.exp2(top - higher) + dot(weights, value)
+        after.append((higher, mix))
+    return tuple(after)
+
+
+def attend_start(tile, pair):
+    return tuple(
+        (jnp.full((tile, 1), -1e38, F32), jnp.zeros((tile, 128), F32)) for _ in range(pair)
+    )
+
+
+def causal_mask(tile):
+    return lax.broadcasted_iota(jnp.int32, (tile, tile), 1) <= lax.broadcasted_iota(
         jnp.int32, (tile, tile), 0
     )
+
+
+def tiles_of(ref, pair, at, tile):
+    return [ref[s, pl.ds(pl.multiple_of(at, tile), tile), :] for s in range(pair)]
+
+
+def attend_own_kernel(
+    me_ref, apart_ref, slope_ref, q_ref, k_ref, v_ref, state_ref, qa, ka, va, *, pair, tile
+):
+    me = me_ref[0]
+    total = q_ref.shape[0]
+    rows = total // 2
+    apart = apart_ref[0].astype(F32)
+    attend_columns(
+        (me, 2, rows), (q_ref, k_ref, v_ref), (qa, ka, va), pair, slope_ref, apart,
+        me // 2 * total,
+    )
+    mask = causal_mask(tile)
+    lane = lanes(tile)
+
+    def query_tile(index, _):
+        first = index * tile
+        queries = tiles_of(qa, pair, first, tile)
+
+        def step(at, carry, mask):
+            keys, values = tiles_of(ka, pair, at, tile), tiles_of(va, pair, at, tile)
+            return attend_step(queries, carry, keys, values, mask)
+
+        carry = step(first, attend_start(tile, pair), mask)
+        carry = lax.fori_loop(0, index, lambda at, held: step(at * tile, held, None), carry)
+        for s, (top, mix) in enumerate(carry):
+            state_ref[s, pl.ds(pl.multiple_of(first, tile), tile), :] = jnp.where(
+                lane == HD + 1, top, mix
+            )
+        return 0
+
+    lax.fori_loop(0, total // tile, query_tile, 0)
+
+
+def attend_own(me, apart, slopes, queries, key_rows, values, rows, group, tile=1024):
+    width = queries.shape[1]
+    pair = min(2, width // HD)
+    spec = pl.BlockSpec((2 * rows, pair * HD), lambda g: (0, group))
+    scalars = pl.BlockSpec(memory_space=pltpu.SMEM)
+    shape = (pair, 2 * rows, 128)
+    return pl.pallas_call(
+        functools.partial(attend_own_kernel, pair=pair, tile=tile),
+        grid=(1,),
+        in_specs=[scalars] * 3 + [spec] * 3,
+        out_specs=pl.BlockSpec(shape, lambda g: (0, 0, 0)),
+        out_shape=jax.ShapeDtypeStruct(shape, F32),
+        scratch_shapes=[pltpu.VMEM(shape, BF16)] * 3,
+        compiler_params=pltpu.CompilerParams(vmem_limit_bytes=56 << 20),
+        cost_estimate=SMALL_COST,
+        name="attend_own",
+    )(me, apart, slopes[group * pair : (group + 1) * pair], queries, key_rows, values)
+
+
+def attend_kernel(*refs, slots, pair, tile, own):
+    me_ref, apart_ref, slope_ref, q_ref, k_ref, v_ref = refs[:6]
+    own_ref = refs[6] if own else None
+    o_ref, lse_ref, qa, ka, va, state = refs[-6:]
+    me = me_ref[0]
+    total = q_ref.shape[0]
+    rows = total // slots
+    apart = apart_ref[0].astype(F32)
+    attend_columns(
+        (me, slots, rows), (q_ref, k_ref, v_ref), (qa, ka, va), pair, slope_ref, apart
+    )
+    mask = causal_mask(tile)
     piece = min(rows, tile)
+    part_tiles = 2 * rows // tile if own else 0
+    own_first = me // 2 * part_tiles
 
     def query_tile(index, _):
         first = pl.multiple_of(index * tile, tile)
-        queries = [qa[s, pl.ds(first, tile), :] for s in range(pair)]
-
-        def step(at, carry, diagonal):
-            after = []
-            for s in range(pair):
-                top, mix = carry[s]
-                scores = dot(queries[s], ka[s, pl.ds(at, tile), :], NT)
-                if diagonal:
-                    scores = jnp.where(causal, scores, -1e30)
-                higher = jnp.maximum(top, jnp.max(scores, axis=1, keepdims=True))
-                weights = low(jnp.exp2(scores - higher))
-                mix = mix * jnp.exp2(top - higher) + dot(weights, va[s, pl.ds(at, tile), :])
-                after.append((higher, mix))
-            return tuple(after)
-
-        carry = tuple(
-            (jnp.full((tile, 1), -1e38, F32), jnp.zeros((tile, 128), F32)) for _ in range(pair)
-        )
-        carry = step(first, carry, True)
-        carry = lax.fori_loop(
-            0, index, lambda at, held: step(pl.multiple_of(at * tile, tile), held, False), carry
-        )
+        queries = tiles_of(qa, pair, first, tile)
+
+        def step(at, carry, mask):
+            keys, values = tiles_of(ka, pair, at, tile), tiles_of(va, pair, at, tile)
+            return attend_step(queries, carry, keys, values, mask)
+
+        def begin():
+            return step(first, attend_start(tile, pair), mask)
+
+        count = index
+        if own:
+            inside = (index >= own_first) & (index < own_first + part_tiles)
+            lane = lanes(tile)
+
+            @pl.when(inside)
+            def _():
+                spot = pl.multiple_of((index - own_first) * tile, tile)
+                for s in range(pair):
+                    state[s] = own_ref[s, pl.ds(spot, tile), :]
+
+            @pl.when(jnp.logical_not(inside))
+            def _():
+                for s, (top, mix) in enumerate(begin()):
+                    state[s] = jnp.where(lane == HD + 1, top, mix)
+
+            carry = tuple((state[s, :, HD + 1 : HD + 2], state[s]) for s in range(pair))
+            count = jnp.where(inside, own_first, index)
+        else:
+            carry = begin()
+        carry = lax.fori_loop(0, count, lambda at, held: step(at * tile, held, None), carry)
         outs = []
         for s in range(pair):
             top, mix = carry[s]
@@ -173,16 +271,18 @@
     lax.fori_loop(0, total // tile, query_tile, 0)
 
 
-def attend(me, apart, slopes, queries, key_rows, values, slots, group, tile=1024):
+def attend(me, apart, slopes, queries, key_rows, values, slots, group, own, tile=1024):
     total, width = queries.shape
     pair = min(2, width // HD)
     cols = pair * HD
     spec = pl.BlockSpec((total, cols), lambda g: (0, group))
     scalars = pl.BlockSpec(memory_space=pltpu.SMEM)
     return pl.pallas_call(
-        functools.partial(attend_kernel, slots=slots, pair=pair, tile=tile),
+        functools.partial(attend_kernel, slots=slots, pair=pair, tile=tile, own=bool(own)),
         grid=(1,),
-        in_specs=[scalars] * 3 + [spec] * 3,
+        in_specs=[scalars] * 3
+        + [spec] * 3
+        + [pl.BlockSpec(state.shape, lambda g: (0, 0, 0)) for state in own],
         out_specs=[
             pl.BlockSpec((total, cols), lambda g: (0, 0)),
             pl.BlockSpec((pair, 1, total), lambda g: (0, 0, 0)),
@@ -191,13 +291,14 @@
             jax.ShapeDtypeStruct((total, cols), BF16),
             jax.ShapeDtypeStruct((pair, 1, total), F32),
         ],
-        scratch_shapes=[pltpu.VMEM((pair, total, 128), BF16)] * 3,
+        scratch_shapes=[pltpu.VMEM((pair, total, 128), BF16)] * 3
+        + [pltpu.VMEM((pair, tile, 128), F32)],
         compiler_params=pltpu.CompilerParams(vmem_limit_bytes=56 << 20),
         cost_estimate=pl.CostEstimate(
             flops=pair * 1200 * total * total, transcendentals=0, bytes_accessed=8 * total * cols
         ),
         name="attend",
-    )(me, apart, slopes[group * pair : (group + 1) * pair], queries, key_rows, values)
+    )(me, apart, slopes[group * pair : (group + 1) * pair], queries, key_rows, values, *own)
 
 
 def attend_back_kernel(*refs, slots, pair, tile, key_tile):
@@ -1146,9 +1247,21 @@
     near_parts = [x_held[0], x_held[1]]
     first = range(2)
     held = project(near_parts, first, slots, norm_vectors, weights, biases, ())
+    heads = me * head_count + jnp.arange(head_count)
+    slopes = jnp.exp2(-8.0 * (heads + 1).astype(F32) / HEADS) * LOG2E
+    apart = (row_ids[:1] != row_ids[SHORT : SHORT + 1]).astype(jnp.int32)
+    own_states = [()] * groups
+    if slots > 2 and 2 * rows % 1024 == 0:
+        own_states = [
+            (attend_own(me_word, apart, slopes, *held[1:], rows, group),) for group in range(groups)
+        ]
     rest = sorted(slot for slot in x_held if slot > 1)
-    *arrived, normed = lax.optimization_barrier((*[x_held[slot] for slot in rest], held[0]))
-    held = (normed, *held[1:])
+    moved = lax.optimization_barrier(
+        (*[x_held[slot] for slot in rest], *held, *[state for own in own_states for state in own])
+    )
+    arrived, held = moved[: len(rest)], moved[len(rest) : len(rest) + 4]
+    if own_states[0]:
+        own_states = [(state,) for state in moved[len(rest) + 4 :]]
     for slot, part in zip(rest, arrived):
         x_held[slot], x_held[slot ^ 1] = part, swap(part, 1)
     x_parts = [x_held[slot] for slot in range(slots)]
@@ -1160,10 +1273,6 @@
     normed, queries, key_rows, values = project(
         x_parts[2:], range(2, slots), slots, norm_vectors, weights, biases, held
     )
-
-    heads = me * head_count + jnp.arange(head_count)
-    slopes = jnp.exp2(-8.0 * (heads + 1).astype(F32) / HEADS) * LOG2E
-    apart = (row_ids[:1] != row_ids[SHORT : SHORT + 1]).astype(jnp.int32)
 
     mixed_own, log_totals, mixed_parts = [], [], []
     for group in range(groups):
@@ -1176,6 +1285,7 @@
             values,
             slots,
             group,
+            own_states[group],
         )
         mixed_own.append(mixed)
         log_totals.append(log_total)

time: 633 us -> 638 us (level)
  Pallas kernels: 451 us -> 482 us
  waiting for transfers between devices: 93.6 us -> 69.4 us
    pallas_call x0 -> x2, Pallas kernels: none -> 25.6 us  [attend_own(): pl.pallas_call(functools.partial(attend_own_kernel, pair=pair, tile=tile)...]
    ppermute x30, waiting for transfers between devices: 56.1 us -> 31.9 us  [swap(): return lax.ppermute(array, 'tensor', [(i, i ^ mask) for i in range(slots)])]
    unnamed x72 -> x74, local copies, waits for them, and re-layouts: 14.1 us -> 15.5 us
  transfers between devices with their start and end apart: 51 -> 51, of which waited for: 15 -> 14; matrix products, arithmetic and copies ran while one was open for 2% -> 2% of each run, Pallas kernels for 63% -> 68%
where the time goes in v8:
time: 638 us; the launch traced here: 630 us
  Pallas kernels  482 us (76%)
  waiting for transfers between devices  69.4 us (11%)
  starting transfers between devices  44.2 us (7%)
  local copies, waits for them, and re-layouts  19.1 us (3%)
  other arithmetic  12.4 us (2%)
    pallas_call x28, Pallas kernels, kernel_call(): pl.pallas_call(kernel, grid=grid, in_specs=in_specs + [pl.BlockSpec(memor...  238 us
    pallas_call x2, Pallas kernels, attend_back(): pl.pallas_call(functools.partial(attend_back_kernel, slots=slots, pair=pa...  140 us
    pallas_call x2, Pallas kernels, attend(): pl.pallas_call(functools.partial(attend_kernel, slots=slots, pair=pair, t...  78.3 us
    ppermute x21, waiting for transfers between devices, swap_data(): return lax.ppermute(array, 'dp', [(i, i ^ mask) for i in range(streams)])  37.5 us
    ppermute x30, waiting for transfers between devices, swap(): return lax.ppermute(array, 'tensor', [(i, i ^ mask) for i in range(slots)])  31.9 us
    ppermute x21, starting transfers between devices, swap_data(): return lax.ppermute(array, 'dp', [(i, i ^ mask) for i in range(streams)])  28.2 us
    pallas_call x2, Pallas kernels, attend_own(): pl.pallas_call(functools.partial(attend_own_kernel, pair=pair, tile=tile)...  25.6 us
    ppermute x30, starting transfers between devices, swap(): return lax.ppermute(array, 'tensor', [(i, i ^ mask) for i in range(slots)])  16 us
  transfers between devices with their start and end apart: 51, of which 14 were waited for; matrix products, arithmetic and copies ran while one was open for 2% of the time, Pallas kernels for 68%

profile of v8, /device:TPU:0, one launch (start us, length us, event | category | flops | bytes accessed | tf_op | source)
XLA Modules:
  0.0 630.2 jit_solution(3017612877191716717)
XLA Ops:
  1.2 2.6 collective-permute-start
  8.2 9.2 %project.2 = (bf16[4096,1024]{1,0:T(8,128)(2,1)}, bf16[4096,256]{1,0:T(8,128)(2,1)}, bf16[4096,256]{1,0:T(8,128)(2,1)}, bf16[4096,256]{1,0:T(8,128)(2,1)}) custom-call(bf16[1024,1024]{1,0:T(8,128)(2,1)} %refs_2_.23, bf16[1024,1024]{1,0:T(8,128)(2,1)} %copy-done.3, bf16[1024]{0:T(1024)(128)(2,1)} %refs_4_.17, bf16[1024]{0:T(1024)(128)(2,1)} %refs_2_.18, ...), custom_call_target="tpu_custom_call" | custom-call | flops 1 | bytes 1 | tf_op jit(solution)/shard_map/project/pallas_call | solution.py:476
  17.4 12.6 %attend_own.2.refs_6_ = f32[2,2048,128]{2,1,0:T(8,128)} custom-call(s32[1]{0:T(128)} %bitcast.1.me_ref.refs_0_, s32[1]{0:T(128)S(6)} %convert_element_type.84.apart_ref.refs_1_, f32[2]{0:T(128)} %get-tuple-element.312.slope_ref.refs_2_, bf16[4096,256]{1,0:T(8,128)(2,1)} %get-tuple-element.163.q_ref.refs_10_, ...), custom_call_target="tpu_custom_call" | custom-call | flops 1 | bytes 1 | tf_op jit(solution)/shard_map/attend_own/pallas_call | solution.py:196
  30.1 13.0 %attend_own.3.refs_6_ = f32[2,2048,128]{2,1,0:T(8,128)} custom-call(s32[1]{0:T(128)} %bitcast.1.me_ref.refs_0_, s32[1]{0:T(128)S(6)} %convert_element_type.84.apart_ref.refs_1_, f32[2]{0:T(128)} %get-tuple-element.311.slope_ref.refs_2_, bf16[4096,256]{1,0:T(8,128)(2,1)} %get-tuple-element.163.q_ref.refs_10_, ...), custom_call_target="tpu_custom_call" | custom-call | flops 1 | bytes 1 | tf_op jit(solution)/shard_map/attend_own/pallas_call | solution.py:196
  43.1 7.2 %collective-permute-done.refs_0_.refs_10_ = bf16[1024,1024]{1,0:T(8,128)(2,1)} collective-permute-done((bf16[1024,1024]{1,0:T(8,128)(2,1)}, bf16[1024,1024]{1,0:T(8,128)(2,1)}, u32[]{:S(2)}, u32[]{:S(2)}) %collective-permute-start) | collective-permute-done | bytes 2097184 | tf_op jit(solution)/shard_map/ppermute | solution.py:1185
  50.3 1.8 collective-permute-start.3
  52.3 2.3 collective-permute-done.2.refs_1_.refs_11_
  56.0 9.2 %project.3 = (bf16[4096,1024]{1,0:T(8,128)(2,1)}, bf16[4096,256]{1,0:T(8,128)(2,1)}, bf16[4096,256]{1,0:T(8,128)(2,1)}, bf16[4096,256]{1,0:T(8,128)(2,1)}) custom-call(bf16[1024,1024]{1,0:T(8,128)(2,1)} %collective-permute-done.refs_0_.refs_10_, ...), custom_call_target="tpu_custom_call", output_to_operand_aliasing={{0}: (9, {}), {1}: (10, {}), {2}: (11, {}), {3}: (12, {})} | custom-call | flops 1 | bytes 1 | tf_op jit(solution)/shard_map/project/pallas_call | solution.py:476
  65.2 39.1 %attend.2 = (bf16[4096,128]{1,0:T(8,128)(2,1)}, f32[2,1,4096]{2,1,0:T(1,128)}) custom-call(s32[1]{0:T(128)} %bitcast.1.me_ref.refs_0_, s32[1]{0:T(128)S(6)} %convert_element_type.84.apart_ref.refs_1_, f32[2]{0:T(128)} %get-tuple-element.312.slope_ref.refs_2_, bf16[4096,256]{1,0:T(8,128)(2,1)} %get-tuple-element.175.refs_3_, ...), custom_call_target="tpu_custom_call" | custom-call | flops 40265318400 | bytes 4194304 | tf_op jit(solution)/shard_map/attend/pallas_call | solution.py:280
  104.3 2.0 collective-permute-start.6
  106.8 39.3 %attend.3 = (bf16[4096,128]{1,0:T(8,128)(2,1)}, f32[2,1,4096]{2,1,0:T(1,128)}) custom-call(s32[1]{0:T(128)} %bitcast.1.me_ref.refs_0_, s32[1]{0:T(128)S(6)} %convert_element_type.84.apart_ref.refs_1_, f32[2]{0:T(128)} %get-tuple-element.311.slope_ref.refs_2_, bf16[4096,256]{1,0:T(8,128)(2,1)} %get-tuple-element.175.refs_3_, ...), custom_call_target="tpu_custom_call" | custom-call | flops 40265318400 | bytes 4194304 | tf_op jit(solution)/shard_map/attend/pallas_call | solution.py:280
  149.1 15.3 %act_grad.1 = (bf16[4096,1024]{1,0:T(8,128)(2,1)}, bf16[4096,1024]{1,0:T(8,128)(2,1)}) custom-call(bf16[1024,1024]{1,0:T(8,128)(2,1)} %refs_3_.17, bf16[1024,1024]{1,0:T(8,128)(2,1)} %collective-permute-done.8.refs_1_, bf16[1024,1024]{1,0:T(8,128)(2,1)} %collective-permute-done.3.refs_2_, bf16[1024,1024]{1,0:T(8,128)(2,1)} %collective-permute-done.9.refs_3_, ...), custom_call_target="tpu_custom_call" | custom-call | flops 1 | bytes 1 | tf_op jit(solution)/shard_map/act_grad/pallas_call | solution.py:476
  164.4 6.9 %collective-permute-done.7.refs_5_ = bf16[4096,128]{1,0:T(8,128)(2,1)S(1)} collective-permute-done((bf16[4096,128]{1,0:T(8,128)(2,1)}, bf16[4096,128]{1,0:T(8,128)(2,1)S(1)}, u32[]{:S(2)}, u32[]{:S(2)}) %collective-permute-start.7) | collective-permute-done | bytes 1048608 | tf_op jit(solution)/shard_map/ppermute | solution.py:1185
  171.9 2.9 collective-permute-done.14.refs_13_.refs_6_
  177.7 22.8 %post_norm.1 = (bf16[4096,1024]{1,0:T(8,128)(2,1)}, f32[1024,1024]{1,0:T(8,128)}) custom-call(bf16[4096,128]{1,0:T(8,128)(2,1)} %get-tuple-element.171.refs_0_.refs_6_, bf16[4096,128]{1,0:T(8,128)(2,1)} %get-tuple-element.177.refs_1_.refs_6_, bf16[4096,128]{1,0:T(8,128)(2,1)} %copy-done.8, bf16[4096,128]{1,0:T(8,128)(2,1)} %copy-done.9, ...), custom_call_target="tpu_custom_call" | custom-call | flops 1 | bytes 1 | tf_op jit(solution)/shard_map/post_norm/pallas_call | solution.py:476
  200.4 11.7 %feed.4 = (bf16[4096,1024]{1,0:T(8,128)(2,1)}, bf16[4096,1024]{1,0:T(8,128)(2,1)}, f32[1,1024]{1,0:T(1,128)}, bf16[1024,1024]{1,0:T(8,128)(2,1)}) custom-call(bf16[4096,1024]{1,0:T(8,128)(2,1)} %get-tuple-element.186.refs_0_.right_ref, bf16[4096,1024]{1,0:T(8,128)(2,1)} %get-tuple-element.187.refs_1_, bf16[1024,1024]{1,0:T(8,128)(2,1)} %refs_2_.17, ...), custom_call_target="tpu_custom_call" | custom-call | flops 1 | bytes 1 | tf_op jit(solution)/shard_map/feed/pallas_call | solution.py:476
  212.2 11.6 %feed.5 = (bf16[4096,1024]{1,0:T(8,128)(2,1)}, bf16[4096,1024]{1,0:T(8,128)(2,1)}, f32[1,1024]{1,0:T(1,128)}, bf16[1024,1024]{1,0:T(8,128)(2,1)}) custom-call(bf16[4096,1024]{1,0:T(8,128)(2,1)} %get-tuple-element.186.refs_0_.right_ref, bf16[4096,1024]{1,0:T(8,128)(2,1)} %get-tuple-element.187.refs_1_, ...), custom_call_target="tpu_custom_call", output_to_operand_aliasing={{0}: (4, {}), {1}: (5, {})} | custom-call | flops 1 | bytes 1 | tf_op jit(solution)/shard_map/feed/pallas_call | solution.py:476
  225.5 12.6 %feed.6 = (bf16[4096,1024]{1,0:T(8,128)(2,1)}, bf16[4096,1024]{1,0:T(8,128)(2,1)}, f32[1,1024]{1,0:T(1,128)}, bf16[1024,1024]{1,0:T(8,128)(2,1)}) custom-call(bf16[4096,1024]{1,0:T(8,128)(2,1)} %get-tuple-element.186.refs_0_.right_ref, bf16[4096,1024]{1,0:T(8,128)(2,1)} %get-tuple-element.187.refs_1_, ...), custom_call_target="tpu_custom_call", output_to_operand_aliasing={{0}: (5, {}), {1}: (6, {})} | custom-call | flops 1 | bytes 1 | tf_op jit(solution)/shard_map/feed/pallas_call | solution.py:476
  239.9 12.8 %feed.7 = (bf16[4096,1024]{1,0:T(8,128)(2,1)}, bf16[4096,1024]{1,0:T(8,128)(2,1)}, f32[1,1024]{1,0:T(1,128)}, bf16[1024,1024]{1,0:T(8,128)(2,1)}) custom-call(bf16[4096,1024]{1,0:T(8,128)(2,1)} %get-tuple-element.186.refs_0_.right_ref, bf16[4096,1024]{1,0:T(8,128)(2,1)} %get-tuple-element.187.refs_1_, ...), custom_call_target="tpu_custom_call", output_to_operand_aliasing={{0}: (5, {}), {1}: (6, {})} | custom-call | flops 1 | bytes 1 | tf_op jit(solution)/shard_map/feed/pallas_call | solution.py:476
  252.7 13.3 %outer_step.2 = (bf16[512,1024]{1,0:T(8,128)(2,1)}, bf16[512,1024]{1,0:T(8,128)(2,1)}) custom-call(s32[1]{0:T(128)} %bitcast.me_ref, bf16[4096,1024]{1,0:T(8,128)(2,1)} %get-tuple-element.199.left_ref, bf16[4096,1024]{1,0:T(8,128)(2,1)} %get-tuple-element.186.refs_0_.right_ref), custom_call_target="tpu_custom_call" | custom-call | flops 1 | bytes 1 | tf_op jit(solution)/shard_map/outer_step/pallas_call | solution.py:476
  266.0 1.5 collective-permute-start.21
  267.5 13.3 %outer_step.3 = (bf16[512,1024]{1,0:T(8,128)(2,1)}, bf16[512,1024]{1,0:T(8,128)(2,1)}) custom-call(s32[1]{0:T(128)} %bitcast.me_ref, bf16[4096,1024]{1,0:T(8,128)(2,1)} %get-tuple-element.212.left_ref.active_ref, bf16[4096,1024]{1,0:T(8,128)(2,1)} %get-tuple-element.201.right_ref), custom_call_target="tpu_custom_call" | custom-call | flops 1 | bytes 1 | tf_op jit(solution)/shard_map/outer_step/pallas_call | solution.py:476
  281.4 4.7 collective-permute-done.17.refs_1_
  286.1 10.2 %resid_step.1 = (f32[1024,1024]{1,0:T(8,128)}, bf16[1024,1024]{1,0:T(8,128)(2,1)}, f32[8,1024]{1,0:T(8,128)}, bf16[1024,256]{1,0:T(8,128)(2,1)}, bf16[1024,256]{...) custom-call(bf16[1024,1024]{1,0:T(8,128)(2,1)} %get-tuple-element.203.refs_0_, ...), custom_call_target="tpu_custom_call" | custom-call | flops 1 | bytes 1 | tf_op jit(solution)/shard_map/resid_step/pallas_call | solution.py:476
  298.2 6.3 %dense_grad.1 = (bf16[2048,256]{1,0:T(8,128)(2,1)}, bf16[2048,256]{1,0:T(8,128)(2,1)}) custom-call(bf16[4096,128]{1,0:T(8,128)(2,1)} %get-tuple-element.171.refs_0_.refs_6_, bf16[4096,128]{1,0:T(8,128)(2,1)} %get-tuple-element.177.refs_1_.refs_6_, bf16[4096,128]{1,0:T(8,128)(2,1)} %copy-done.8, bf16[4096,128]{1,0:T(8,128)(2,1)} %copy-done.9, ...), custom_call_target="tpu_custom_call" | custom-call | flops 1 | bytes 1 | tf_op jit(solution)/shard_map/dense_grad/pallas_call | solution.py:476
  304.5 14.5 %ffn_step.1 = (bf16[2048,1024]{1,0:T(8,128)(2,1)}, bf16[2048,1024]{1,0:T(8,128)(2,1)}) custom-call(bf16[4096,1024]{1,0:T(8,128)(2,1)} %get-tuple-element.212.left_ref.active_ref, bf16[1024,1024]{1,0:T(8,128)(2,1)} %weight_ref.1), custom_call_target="tpu_custom_call" | custom-call | flops 1 | bytes 1 | tf_op jit(solution)/shard_map/ffn_step/pallas_call | solution.py:476
  321.0 3.7 pair_step.1
  325.1 3.6 collective-permute-start.27
  329.5 70.2 %attend_back.2.grad_ref.refs_0_ = bf16[4096,384]{1,0:T(8,128)(2,1)} custom-call(s32[1]{0:T(128)} %bitcast.1.me_ref.refs_0_, s32[1]{0:T(128)S(6)} %convert_element_type.84.apart_ref.refs_1_, f32[2]{0:T(128)} %get-tuple-element.312.slope_ref.refs_2_, bf16[4096,256]{1,0:T(8,128)(2,1)} %get-tuple-element.175.refs_3_, ...), custom_call_target="tpu_custom_call" | custom-call | flops 80530636800 | bytes 8388608 | tf_op jit(solution)/shard_map/attend_back/pallas_call | solution.py:413
  401.4 1.4 add_convert_fusion.3.refs_0_
  402.8 9.6 %weight_step.2 = (bf16[1024,384]{1,0:T(8,128)(2,1)}, f32[8,1024]{1,0:T(8,128)}, f32[1,384]{1,0:T(1,128)}) custom-call(s32[1]{0:T(128)} %bitcast.me_ref, bf16[4096,1024]{1,0:T(8,128)(2,1)} %get-tuple-element.166.normed_ref, bf16[4096,384]{1,0:T(8,128)(2,1)} %attend_back.2.grad_ref.refs_0_, bf16[1024,256]{1,0:T(8,128)(2,1)} %refs_5_.12, ...), custom_call_target="tpu_custom_call" | custom-call | flops 1 | bytes 1 | tf_op jit(solution)/shard_map/weight_step/pallas_call | solution.py:476
  412.4 3.0 collective-permute-done.24.refs_2_
  416.3 2.6 join_step.1
  418.9 4.6 add_convert_fusion.1
  424.7 2.9 collective-permute-start.31
  427.9 1.5 collective-permute-start.29
  429.9 70.0 %attend_back.3.grad_ref.refs_1_ = bf16[4096,384]{1,0:T(8,128)(2,1)} custom-call(s32[1]{0:T(128)} %bitcast.1.me_ref.refs_0_, s32[1]{0:T(128)S(6)} %convert_element_type.84.apart_ref.refs_1_, f32[2]{0:T(128)} %get-tuple-element.311.slope_ref.refs_2_, bf16[4096,256]{1,0:T(8,128)(2,1)} %get-tuple-element.175.refs_3_, ...), custom_call_target="tpu_custom_call" | custom-call | flops 80530636800 | bytes 8388608 | tf_op jit(solution)/shard_map/attend_back/pallas_call | solution.py:413
  500.0 10.0 %weight_step.3 = (bf16[512,384]{1,0:T(8,128)(2,1)}, bf16[512,384]{1,0:T(8,128)(2,1)}, f32[8,1024]{1,0:T(8,128)}, f32[1,384]{1,0:T(1,128)}) custom-call(s32[1]{0:T(128)} %bitcast.me_ref, bf16[4096,1024]{1,0:T(8,128)(2,1)} %get-tuple-element.166.normed_ref, bf16[4096,384]{1,0:T(8,128)(2,1)} %attend_back.3.grad_ref.refs_1_, bf16[1024,256]{1,0:T(8,128)(2,1)} %refs_5_.12, ...), custom_call_target="tpu_custom_call" | custom-call | flops 1 | bytes 1 | tf_op jit(solution)/shard_map/weight_step/pallas_call | solution.py:476
  510.5 1.5 pack.1
  512.1 1.5 collective-permute-start.35
  513.6 3.1 stack_step.2.even_ref
  516.6 4.4 collective-permute-done.35
  521.1 5.2 unproject.4
  526.3 5.1 unproject.5
  533.6 5.5 unproject.6
  539.1 1.6 collective-permute-start.44
  540.7 5.6 unproject.7.refs_0_
  546.4 2.5 late_step.1
  548.9 3.5 collective-permute-start.40
  553.3 7.0 %collective-permute-done.40 = bf16[128,1024]{1,0:T(8,128)(2,1)S(1)} collective-permute-done((bf16[128,1024]{1,0:T(8,128)(2,1)}, bf16[128,1024]{1,0:T(8,128)(2,1)S(1)}, u32[]{:S(2)}, u32[]{:S(2)}) %collective-permute-start.40) | collective-permute-done | bytes 262176 | tf_op jit(solution)/shard_map/ppermute | solution.py:1197
  560.2 13.4 %collective-permute-done.39 = bf16[128,1024]{1,0:T(8,128)(2,1)S(1)} collective-permute-done((bf16[128,1024]{1,0:T(8,128)(2,1)}, bf16[128,1024]{1,0:T(8,128)(2,1)S(1)}, u32[]{:S(2)}, u32[]{:S(2)}) %collective-permute-start.39) | collective-permute-done | bytes 262176 | tf_op jit(solution)/shard_map/ppermute | solution.py:1197
  574.9 2.9 collective-permute-start.42
  577.8 1.5 collective-permute-start.43
  579.3 4.1 add_convert_fusion
  583.3 7.1 %feed_grads.1 = (f32[1024,1024]{1,0:T(8,128)}, f32[1024,1024]{1,0:T(8,128)}) custom-call(s32[1]{0:T(128)} %bitcast.me_ref, bf16[1024,1024]{1,0:T(8,128)(2,1)} %stack_step.2.even_ref, bf16[1024,1024]{1,0:T(8,128)(2,1)} %collective-permute-done.45.odd_ref), custom_call_target="tpu_custom_call" | custom-call | flops 1 | bytes 1 | tf_op jit(solution)/shard_map/feed_grads/pallas_call | solution.py:476
  590.5 7.7 %input_step.1 = f32[1024,1024]{1,0:T(8,128)} custom-call(bf16[1024,1024]{1,0:T(8,128)(2,1)} %unproject.7.refs_0_, bf16[1024,1024]{1,0:T(8,128)(2,1)} %collective-permute-done.44.refs_1_, bf16[1024,1024]{1,0:T(8,128)(2,1)} %refs_2_.23, f32[1024,1024]{1,0:T(8,128)} %get-tuple-element.284.refs_3_, bf16[1024]{0:T(1024)(128)(2,1)} %refs_4_.17), custom_call_target="tpu_custom_call" | custom-call | flops 1 | bytes 1 | tf_op jit(solution)/shard_map/input_step/pallas_call | solution.py:476
  599.6 2.2 stack_step.3.even_ref
  601.9 1.5 collective-permute-start.50
  604.6 3.8 collective-permute-done.46
  608.3 1.8 collective-permute-start.47
  610.1 4.1 collective-permute-done.47
  614.9 3.4 collective-permute-done.48
  620.1 4.8 collective-permute-done.50.odd_ref
  625.8 4.0 spread.1
  (164 shorter events, 36.9 us)
Async XLA Ops:
  0.7 6.2 collective-permute-start.1
  1.2 49.1 %collective-permute-start = (bf16[1024,1024]{1,0:T(8,128)(2,1)}, bf16[1024,1024]{1,0:T(8,128)(2,1)}, u32[]{:S(2)}, u32[]{:S(2)}) collective-permute-start(bf16[1024,1024]{1,0:T(8,128)(2,1)} %refs_2_.23), channel_id=1, source_target_pairs={{0,2},{1,3},{2,0},{3,1},{4,6},{5,7},{6,4},{7,5},{8,10},{9,11},{10,... | collective-permute-start | bytes 6291464 | tf_op jit(solution)/shard_map/ppermute | solution.py:1185
  30.1 20.2 %copy-start.1 = (bf16[1024,1024]{1,0:T(8,128)(2,1)S(1)}, bf16[1024,1024]{1,0:T(8,128)(2,1)}, u32[]{:S(2)}) copy-start(bf16[1024,1024]{1,0:T(8,128)(2,1)} %refs_3_.17) | copy-start | bytes 6291460
  30.1 22.0 %copy-start.16 = (bf16[256,1024]{1,0:T(8,128)(2,1)S(1)}, bf16[256,1024]{1,0:T(8,128)(2,1)}, u32[]{:S(2)}) copy-start(bf16[256,1024]{1,0:T(8,128)(2,1)} %refs_5_.8) | copy-start | bytes 1572868
  50.3 4.4 collective-permute-start.2
  50.3 56.0 %collective-permute-start.3 = (bf16[1024,1024]{1,0:T(8,128)(2,1)S(1)}, bf16[1024,1024]{1,0:T(8,128)(2,1)}, u32[]{:S(2)}, u32[]{:S(2)}) collective-permute-start(bf16[1024,1024]{1,0:T(8,128)(2,1)S(1)} %copy-done.1), channel_id=1, source_target_pairs={{0,2},{1,3},{2,0},{3,1},{4,6},{5,7},{6,4},{7,5},{8,10},{9,11},{10,... | collective-permute-start | bytes 6291464 | tf_op jit(solution)/shard_map/ppermute | solution.py:1185
  52.1 94.3 %collective-permute-start.10 = (bf16[256,1024]{1,0:T(8,128)(2,1)S(1)}, bf16[256,1024]{1,0:T(8,128)(2,1)S(1)}, u32[]{:S(2)}, u32[]{:S(2)}) collective-permute-start(bf16[256,1024]{1,0:T(8,128)(2,1)S(1)} %copy-done.16), channel_id=1, source_target_pairs={{0,2},{1,3},{2,0},{3,1},{4,6},{5,7},{6,4},{7,5},{8,10},{9,11},{10,... | collective-permute-start | bytes 1572872 | tf_op jit(solution)/shard_map/ppermute | solution.py:1185
  104.3 44.2 %copy-start.5 = (bf16[4096,128]{1,0:T(8,128)(2,1)S(1)}, bf16[4096,128]{1,0:T(8,128)(2,1)}, u32[]{:S(2)}) copy-start(bf16[4096,128]{1,0:T(8,128)(2,1)} %get-tuple-element.171.refs_0_.refs_6_) | copy-start | bytes 3145732
  104.3 44.3 %collective-permute-start.6 = (bf16[4096,128]{1,0:T(8,128)(2,1)}, bf16[4096,128]{1,0:T(8,128)(2,1)S(1)}, u32[]{:S(2)}, u32[]{:S(2)}) collective-permute-start(bf16[4096,128]{1,0:T(8,128)(2,1)} %get-tuple-element.171.refs_0_.refs_6_), channel_id=1, source_target_pairs={{0,2},{1,3},{2,0},{3,1},{4,6},{5,7},{6,4},{7,5},{8,10},{9,11},{10,... | collective-permute-start | bytes 3145736 | tf_op jit(solution)/shard_map/ppermute | solution.py:1185
  106.3 42.8 %collective-permute-start.9 = (bf16[1024,1024]{1,0:T(8,128)(2,1)}, bf16[1024,1024]{1,0:T(8,128)(2,1)}, u32[]{:S(2)}, u32[]{:S(2)}) collective-permute-start(bf16[1024,1024]{1,0:T(8,128)(2,1)} %collective-permute-done.3.refs_2_), channel_id=1, source_target_pairs={{0,1},{1,0},{2,3},{3,2},{4,5},{5,4},{6,7},{7,6},{8,9},{9,8},{10,11... | collective-permute-start | bytes 6291464 | tf_op jit(solution)/shard_map/ppermute | solution.py:1185
  106.3 42.7 %collective-permute-start.8 = (bf16[1024,1024]{1,0:T(8,128)(2,1)S(1)}, bf16[1024,1024]{1,0:T(8,128)(2,1)}, u32[]{:S(2)}, u32[]{:S(2)}) collective-permute-start(bf16[1024,1024]{1,0:T(8,128)(2,1)S(1)} %copy-done.1), channel_id=1, source_target_pairs={{0,1},{1,0},{2,3},{3,2},{4,5},{5,4},{6,7},{7,6},{8,9},{9,8},{10,11... | collective-permute-start | bytes 6291464 | tf_op jit(solution)/shard_map/ppermute | solution.py:1185
  146.1 25.3 %collective-permute-start.7 = (bf16[4096,128]{1,0:T(8,128)(2,1)}, bf16[4096,128]{1,0:T(8,128)(2,1)S(1)}, u32[]{:S(2)}, u32[]{:S(2)}) collective-permute-start(bf16[4096,128]{1,0:T(8,128)(2,1)} %get-tuple-element.177.refs_1_.refs_6_), channel_id=1, source_target_pairs={{0,2},{1,3},{2,0},{3,1},{4,6},{5,7},{6,4},{7,5},{8,10},{9,11},{10,... | collective-permute-start | bytes 3145736 | tf_op jit(solution)/shard_map/ppermute | solution.py:1185
  146.4 2.0 collective-permute-start.11
  148.5 26.3 %collective-permute-start.4 = (bf16[4096,128]{1,0:T(8,128)(2,1)S(1)}, bf16[4096,128]{1,0:T(8,128)(2,1)S(1)}, u32[]{:S(2)}, u32[]{:S(2)}) collective-permute-start(bf16[4096,128]{1,0:T(8,128)(2,1)S(1)} %copy-done.5), channel_id=1, source_target_pairs={{0,1},{1,0},{2,3},{3,2},{4,5},{5,4},{6,7},{7,6},{8,9},{9,8},{10,11... | collective-permute-start | bytes 3145736 | tf_op jit(solution)/shard_map/ppermute | solution.py:1185
  148.6 15.8 %copy-start.6 = (bf16[4096,128]{1,0:T(8,128)(2,1)}, bf16[4096,128]{1,0:T(8,128)(2,1)S(1)}, u32[]{:S(2)}) copy-start(bf16[4096,128]{1,0:T(8,128)(2,1)S(1)} %collective-permute-done.6.refs_4_) | copy-start | bytes 3145732
  148.6 26.2 %collective-permute-start.5 = (bf16[4096,128]{1,0:T(8,128)(2,1)}, bf16[4096,128]{1,0:T(8,128)(2,1)S(1)}, u32[]{:S(2)}, u32[]{:S(2)}) collective-permute-start(bf16[4096,128]{1,0:T(8,128)(2,1)} %get-tuple-element.177.refs_1_.refs_6_), channel_id=1, source_target_pairs={{0,1},{1,0},{2,3},{3,2},{4,5},{5,4},{6,7},{7,6},{8,9},{9,8},{10,11... | collective-permute-start | bytes 3145736 | tf_op jit(solution)/shard_map/ppermute | solution.py:1185
  149.0 25.8 %collective-permute-start.12 = (bf16[4096,128]{1,0:T(8,128)(2,1)S(1)}, bf16[4096,128]{1,0:T(8,128)(2,1)S(1)}, u32[]{:S(2)}, u32[]{:S(2)}) collective-permute-start(bf16[4096,128]{1,0:T(8,128)(2,1)S(1)} %collective-permute-done.6.refs_4_), channel_id=1, source_target_pairs={{0,1},{1,0},{2,3},{3,2},{4,5},{5,4},{6,7},{7,6},{8,9},{9,8},{10,11... | collective-permute-start | bytes 3145736 | tf_op jit(solution)/shard_map/ppermute | solution.py:1185
  171.4 4.2 collective-permute-start.13
  171.4 3.4 collective-permute-start.14
  212.1 12.1 %collective-permute-start.16 = (bf16[1024,1024]{1,0:T(8,128)(2,1)}, bf16[1024,1024]{1,0:T(8,128)(2,1)S(1)}, u32[]{:S(2)}, u32[]{:S(2)}) collective-permute-start(bf16[1024,1024]{1,0:T(8,128)(2,1)} %get-tuple-element.191), channel_id=1, source_target_pairs={{0,1},{1,0},{2,3},{3,2},{4,5},{5,4},{6,7},{7,6},{8,9},{9,8},{10,11... | collective-permute-start | bytes 6291464 | tf_op jit(solution)/shard_map/ppermute | solution.py:1185
  223.8 14.7 %collective-permute-start.15 = (bf16[1024,1024]{1,0:T(8,128)(2,1)}, bf16[1024,1024]{1,0:T(8,128)(2,1)S(1)}, u32[]{:S(2)}, u32[]{:S(2)}) collective-permute-start(bf16[1024,1024]{1,0:T(8,128)(2,1)} %get-tuple-element.190), channel_id=1, source_target_pairs={{0,1},{1,0},{2,3},{3,2},{4,5},{5,4},{6,7},{7,6},{8,9},{9,8},{10,11... | collective-permute-start | bytes 6291464 | tf_op jit(solution)/shard_map/ppermute | solution.py:1185
  238.1 48.0 %collective-permute-start.17 = (bf16[1024,1024]{1,0:T(8,128)(2,1)}, bf16[1024,1024]{1,0:T(8,128)(2,1)}, u32[]{:S(2)}, u32[]{:S(2)}) collective-permute-start(bf16[1024,1024]{1,0:T(8,128)(2,1)} %get-tuple-element.204), channel_id=1, source_target_pairs={{0,2},{1,3},{2,0},{3,1},{4,6},{5,7},{6,4},{7,5},{8,10},{9,11},{10,... | collective-permute-start | bytes 6291464 | tf_op jit(solution)/shard_map/ppermute | solution.py:1185
  266.0 53.1 %collective-permute-start.21 = (bf16[512,1024]{1,0:T(8,128)(2,1)}, bf16[512,1024]{1,0:T(8,128)(2,1)S(1)}, u32[]{:S(2)}, u32[]{:S(2)}) collective-permute-start(bf16[512,1024]{1,0:T(8,128)(2,1)} %get-tuple-element.215), channel_id=1, source_target_pairs={{0,4},{4,0},{8,12},{12,8},{16,20},{20,16},{24,28},{28,24},{1,5},{5... | collective-permute-start | bytes 3145736 | tf_op jit(solution)/shard_map/ppermute | solution.py:1197
  280.9 38.2 %collective-permute-start.22 = (bf16[512,1024]{1,0:T(8,128)(2,1)}, bf16[512,1024]{1,0:T(8,128)(2,1)S(1)}, u32[]{:S(2)}, u32[]{:S(2)}) collective-permute-start(bf16[512,1024]{1,0:T(8,128)(2,1)} %get-tuple-element.216), channel_id=1, source_target_pairs={{0,4},{4,0},{8,12},{12,8},{16,20},{20,16},{24,28},{28,24},{1,5},{5... | collective-permute-start | bytes 3145736 | tf_op jit(solution)/shard_map/ppermute | solution.py:1197
  296.2 28.4 %collective-permute-start.18 = (bf16[1024,256]{1,0:T(8,128)(2,1)}, bf16[1024,256]{1,0:T(8,128)(2,1)S(1)}, u32[]{:S(2)}, u32[]{:S(2)}) collective-permute-start(bf16[1024,256]{1,0:T(8,128)(2,1)} %get-tuple-element.207), channel_id=1, source_target_pairs={{0,1},{1,0},{2,3},{3,2},{4,5},{5,4},{6,7},{7,6},{8,9},{9,8},{10,11... | collective-permute-start | bytes 1572872 | tf_op jit(solution)/shard_map/ppermute | solution.py:1185
  296.3 28.3 %collective-permute-start.19 = (bf16[1024,256]{1,0:T(8,128)(2,1)}, bf16[1024,256]{1,0:T(8,128)(2,1)S(1)}, u32[]{:S(2)}, u32[]{:S(2)}) collective-permute-start(bf16[1024,256]{1,0:T(8,128)(2,1)} %get-tuple-element.208), channel_id=1, source_target_pairs={{0,2},{1,3},{2,0},{3,1},{4,6},{5,7},{6,4},{7,5},{8,10},{9,11},{10,... | collective-permute-start | bytes 1572872 | tf_op jit(solution)/shard_map/ppermute | solution.py:1185
  296.8 27.8 %collective-permute-start.20 = (bf16[1024,256]{1,0:T(8,128)(2,1)}, bf16[1024,256]{1,0:T(8,128)(2,1)S(1)}, u32[]{:S(2)}, u32[]{:S(2)}) collective-permute-start(bf16[1024,256]{1,0:T(8,128)(2,1)} %get-tuple-element.209), channel_id=1, source_target_pairs={{0,3},{1,2},{2,1},{3,0},{4,7},{5,6},{6,5},{7,4},{8,11},{9,10},{10,... | collective-permute-start | bytes 1572872 | tf_op jit(solution)/shard_map/ppermute | solution.py:1185
  324.7 75.0 %collective-permute-start.23 = (bf16[2048,256]{1,0:T(8,128)(2,1)}, bf16[2048,256]{1,0:T(8,128)(2,1)S(1)}, u32[]{:S(2)}, u32[]{:S(2)}) collective-permute-start(bf16[2048,256]{1,0:T(8,128)(2,1)} %get-tuple-element.226), channel_id=1, source_target_pairs={{0,1},{1,0},{2,3},{3,2},{4,5},{5,4},{6,7},{7,6},{8,9},{9,8},{10,11... | collective-permute-start | bytes 3145736 | tf_op jit(solution)/shard_map/ppermute | solution.py:1185
  325.1 76.3 %collective-permute-start.27 = (bf16[256,1024]{1,0:T(8,128)(2,1)}, bf16[256,1024]{1,0:T(8,128)(2,1)S(1)}, u32[]{:S(2)}, u32[]{:S(2)}) collective-permute-start(bf16[256,1024]{1,0:T(8,128)(2,1)} %get-tuple-element.241), channel_id=1, source_target_pairs={{0,24},{4,28},{8,16},{12,20},{16,8},{20,12},{24,0},{28,4},{1,25},{... | collective-permute-start | bytes 1572872 | tf_op jit(solution)/shard_map/ppermute | solution.py:1197
  328.7 72.7 %collective-permute-start.26 = (bf16[256,1024]{1,0:T(8,128)(2,1)}, bf16[256,1024]{1,0:T(8,128)(2,1)S(1)}, u32[]{:S(2)}, u32[]{:S(2)}) collective-permute-start(bf16[256,1024]{1,0:T(8,128)(2,1)} %get-tuple-element.240), channel_id=1, source_target_pairs={{0,16},{4,20},{8,24},{12,28},{16,0},{20,4},{24,8},{28,12},{1,17},{... | collective-permute-start | bytes 1572872 | tf_op jit(solution)/shard_map/ppermute | solution.py:1197
  328.7 72.7 %collective-permute-start.25 = (bf16[256,1024]{1,0:T(8,128)(2,1)}, bf16[256,1024]{1,0:T(8,128)(2,1)}, u32[]{:S(2)}, u32[]{:S(2)}) collective-permute-start(bf16[256,1024]{1,0:T(8,128)(2,1)} %get-tuple-element.239), channel_id=1, source_target_pairs={{0,8},{4,12},{8,0},{12,4},{16,24},{20,28},{24,16},{28,20},{1,9},{5... | collective-permute-start | bytes 1572872 | tf_op jit(solution)/shard_map/ppermute | solution.py:1197
  329.5 89.4 %collective-permute-start.28 = (bf16[2048,1024]{1,0:T(8,128)(2,1)}, bf16[2048,1024]{1,0:T(8,128)(2,1)}, u32[]{:S(2)}, u32[]{:S(2)}) collective-permute-start(bf16[2048,1024]{1,0:T(8,128)(2,1)} %get-tuple-element.243), channel_id=1, source_target_pairs={{0,1},{1,0},{2,3},{3,2},{4,5},{5,4},{6,7},{7,6},{8,9},{9,8},{10,11... | collective-permute-start | bytes 12582920 | tf_op jit(solution)/shard_map/ppermute | solution.py:1185
  329.5 70.2 %copy-start.19 = (bf16[2048,256]{1,0:T(8,128)(2,1)S(1)}, bf16[2048,256]{1,0:T(8,128)(2,1)}, u32[]{:S(2)}) copy-start(bf16[2048,256]{1,0:T(8,128)(2,1)} %get-tuple-element.225) | copy-start | bytes 3145732
  400.9 14.5 %collective-permute-start.24 = (bf16[1024,256]{1,0:T(8,128)(2,1)}, bf16[1024,256]{1,0:T(8,128)(2,1)S(1)}, u32[]{:S(2)}, u32[]{:S(2)}) collective-permute-start(bf16[1024,256]{1,0:T(8,128)(2,1)} %get-tuple-element.230), channel_id=1, source_target_pairs={{0,2},{1,3},{2,0},{3,1},{4,6},{5,7},{6,4},{7,5},{8,10},{9,11},{10,... | collective-permute-start | bytes 1572872 | tf_op jit(solution)/shard_map/ppermute | solution.py:1185
  402.8 24.9 %copy-start.15 = (bf16[256,1024]{1,0:T(8,128)(2,1)}, bf16[256,1024]{1,0:T(8,128)(2,1)S(1)}, u32[]{:S(2)}) copy-start(bf16[256,1024]{1,0:T(8,128)(2,1)S(1)} %add_convert_fusion.3.refs_0_) | copy-start | bytes 1572868
  402.8 16.1 %copy-start.4 = (bf16[2048,1024]{1,0:T(8,128)(2,1)S(1)}, bf16[2048,1024]{1,0:T(8,128)(2,1)}, u32[]{:S(2)}) copy-start(bf16[2048,1024]{1,0:T(8,128)(2,1)} %get-tuple-element.242) | copy-start | bytes 12582916
  423.5 76.4 %collective-permute-start.30 = (bf16[256,1024]{1,0:T(8,128)(2,1)S(1)}, bf16[256,1024]{1,0:T(8,128)(2,1)S(1)}, u32[]{:S(2)}, u32[]{:S(2)}) collective-permute-start(bf16[256,1024]{1,0:T(8,128)(2,1)S(1)} %add_convert_fusion.3.refs_0_), channel_id=1, source_target_pairs={{0,8},{4,12},{8,0},{12,4},{16,24},{20,28},{24,16},{28,20},{1,9},{5... | collective-permute-start | bytes 1572872 | tf_op jit(solution)/shard_map/ppermute | solution.py:1197
  424.7 75.2 %collective-permute-start.31 = (bf16[256,1024]{1,0:T(8,128)(2,1)S(1)}, bf16[256,1024]{1,0:T(8,128)(2,1)}, u32[]{:S(2)}, u32[]{:S(2)}) collective-permute-start(bf16[256,1024]{1,0:T(8,128)(2,1)S(1)} %add_convert_fusion.3.refs_0_), channel_id=1, source_target_pairs={{0,16},{4,20},{8,24},{12,28},{16,0},{20,4},{24,8},{28,12},{1,17},{... | collective-permute-start | bytes 1572872 | tf_op jit(solution)/shard_map/ppermute | solution.py:1197
  427.7 72.3 %collective-permute-start.32 = (bf16[256,1024]{1,0:T(8,128)(2,1)S(1)}, bf16[256,1024]{1,0:T(8,128)(2,1)}, u32[]{:S(2)}, u32[]{:S(2)}) collective-permute-start(bf16[256,1024]{1,0:T(8,128)(2,1)S(1)} %add_convert_fusion.3.refs_0_), channel_id=1, source_target_pairs={{0,24},{4,28},{8,16},{12,20},{16,8},{20,12},{24,0},{28,4},{1,25},{... | collective-permute-start | bytes 1572872 | tf_op jit(solution)/shard_map/ppermute | solution.py:1197
  427.9 72.1 %collective-permute-start.29 = (bf16[512,640]{1,0:T(8,128)(2,1)}, bf16[512,640]{1,0:T(8,128)(2,1)S(1)}, u32[]{:S(2)}, u32[]{:S(2)}) collective-permute-start(bf16[512,640]{1,0:T(8,128)(2,1)} %get-tuple-element.248), channel_id=1, source_target_pairs={{0,4},{4,0},{8,12},{12,8},{16,20},{20,16},{24,28},{28,24},{1,5},{5... | collective-permute-start | bytes 1966088 | tf_op jit(solution)/shard_map/ppermute | solution.py:1197
  429.4 70.6 %collective-permute-start.33 = (bf16[1024,1024]{1,0:T(8,128)(2,1)}, bf16[1024,1024]{1,0:T(8,128)(2,1)}, u32[]{:S(2)}, u32[]{:S(2)}) collective-permute-start(bf16[1024,1024]{1,0:T(8,128)(2,1)} %get-tuple-element.251), channel_id=1, source_target_pairs={{0,2},{1,3},{2,0},{3,1},{4,6},{5,7},{6,4},{7,5},{8,10},{9,11},{10,... | collective-permute-start | bytes 6291464 | tf_op jit(solution)/shard_map/ppermute | solution.py:1185
  499.9 10.0 %copy-start.27 = (bf16[256,1024]{1,0:T(8,128)(2,1)}, bf16[256,1024]{1,0:T(8,128)(2,1)S(1)}, u32[]{:S(2)}) copy-start(bf16[256,1024]{1,0:T(8,128)(2,1)S(1)} %collective-permute-done.30.refs_1_) | copy-start | bytes 1572868
  500.0 10.0 %copy-start.24 = (bf16[512,640]{1,0:T(8,128)(2,1)}, bf16[512,640]{1,0:T(8,128)(2,1)S(1)}, u32[]{:S(2)}) copy-start(bf16[512,640]{1,0:T(8,128)(2,1)S(1)} %collective-permute-done.29.refs_1_) | copy-start | bytes 1966084
  510.0 11.1 %collective-permute-start.34 = (bf16[512,384]{1,0:T(8,128)(2,1)}, bf16[512,384]{1,0:T(8,128)(2,1)S(1)}, u32[]{:S(2)}, u32[]{:S(2)}) collective-permute-start(bf16[512,384]{1,0:T(8,128)(2,1)} %get-tuple-element.269), channel_id=1, source_target_pairs={{0,4},{4,0},{8,12},{12,8},{16,20},{20,16},{24,28},{28,24},{1,5},{5... | collective-permute-start | bytes 1179656 | tf_op jit(solution)/shard_map/ppermute | solution.py:1197
  512.0 9.0 %copy-start.29 = (f32[16,1024]{1,0:T(8,128)S(1)}, f32[16,1024]{1,0:T(8,128)}, u32[]{:S(2)}) copy-start(f32[16,1024]{1,0:T(8,128)} %pack.1) | copy-start | bytes 196612
  512.1 9.0 %collective-permute-start.35 = (f32[16,1024]{1,0:T(8,128)}, f32[16,1024]{1,0:T(8,128)S(1)}, u32[]{:S(2)}, u32[]{:S(2)}) collective-permute-start(f32[16,1024]{1,0:T(8,128)} %pack.1), channel_id=1, source_target_pairs={{0,4},{4,0},{8,12},{12,8},{16,20},{20,16},{24,28},{28,24},{1,5},{5... | collective-permute-start | bytes 196616 | tf_op jit(solution)/shard_map/ppermute | solution.py:1197
  526.3 6.1 collective-permute-start.36
  531.4 9.3 %collective-permute-start.37 = (bf16[1024,1024]{1,0:T(8,128)(2,1)}, bf16[1024,1024]{1,0:T(8,128)(2,1)}, u32[]{:S(2)}, u32[]{:S(2)}) collective-permute-start(bf16[1024,1024]{1,0:T(8,128)(2,1)} %unproject.5), channel_id=1, source_target_pairs={{0,1},{1,0},{2,3},{3,2},{4,5},{5,4},{6,7},{7,6},{8,9},{9,8},{10,11... | collective-permute-start | bytes 6291464 | tf_op jit(solution)/shard_map/ppermute | solution.py:1185
  531.8 51.5 %collective-permute-start.45 = (bf16[1024,1024]{1,0:T(8,128)(2,1)}, bf16[1024,1024]{1,0:T(8,128)(2,1)}, u32[]{:S(2)}, u32[]{:S(2)}) collective-permute-start(bf16[1024,1024]{1,0:T(8,128)(2,1)} %stack_step.2.even_ref), channel_id=1, source_target_pairs={{0,4},{4,0},{8,12},{12,8},{16,20},{20,16},{24,28},{28,24},{1,5},{5... | collective-permute-start | bytes 6291464 | tf_op jit(solution)/shard_map/ppermute | solution.py:1197
  539.1 51.3 %collective-permute-start.44 = (bf16[1024,1024]{1,0:T(8,128)(2,1)}, bf16[1024,1024]{1,0:T(8,128)(2,1)}, u32[]{:S(2)}, u32[]{:S(2)}) collective-permute-start(bf16[1024,1024]{1,0:T(8,128)(2,1)} %unproject.6), channel_id=1, source_target_pairs={{0,2},{1,3},{2,0},{3,1},{4,6},{5,7},{6,4},{7,5},{8,10},{9,11},{10,... | collective-permute-start | bytes 6291464 | tf_op jit(solution)/shard_map/ppermute | solution.py:1185
  540.7 38.6 %copy-start = (f32[1024,1024]{1,0:T(8,128)S(1)}, f32[1024,1024]{1,0:T(8,128)}, u32[]{:S(2)}) copy-start(f32[1024,1024]{1,0:T(8,128)} %get-tuple-element.205.refs_2_) | copy-start | bytes 12582916
  546.4 6.9 %copy-start.33 = (bf16[1024]{0:T(1024)(128)(2,1)S(1)}, bf16[1024]{0:T(1024)(128)(2,1)}, u32[]{:S(2)}) copy-start(bf16[1024]{0:T(1024)(128)(2,1)} %param.34) | copy-start | bytes 6148
  548.9 11.3 %collective-permute-start.40 = (bf16[128,1024]{1,0:T(8,128)(2,1)}, bf16[128,1024]{1,0:T(8,128)(2,1)S(1)}, u32[]{:S(2)}, u32[]{:S(2)}) collective-permute-start(bf16[128,1024]{1,0:T(8,128)(2,1)} %get-tuple-element.278), channel_id=1, source_target_pairs={{0,24},{4,28},{8,16},{12,20},{16,8},{20,12},{24,0},{28,4},{1,25},{... | collective-permute-start | bytes 786440 | tf_op jit(solution)/shard_map/ppermute | solution.py:1197
  552.4 21.2 %collective-permute-start.39 = (bf16[128,1024]{1,0:T(8,128)(2,1)}, bf16[128,1024]{1,0:T(8,128)(2,1)S(1)}, u32[]{:S(2)}, u32[]{:S(2)}) collective-permute-start(bf16[128,1024]{1,0:T(8,128)(2,1)} %get-tuple-element.277), channel_id=1, source_target_pairs={{0,16},{4,20},{8,24},{12,28},{16,0},{20,4},{24,8},{28,12},{1,17},{... | collective-permute-start | bytes 786440 | tf_op jit(solution)/shard_map/ppermute | solution.py:1197
  552.4 21.2 %collective-permute-start.38 = (bf16[128,1024]{1,0:T(8,128)(2,1)}, bf16[128,1024]{1,0:T(8,128)(2,1)S(1)}, u32[]{:S(2)}, u32[]{:S(2)}) collective-permute-start(bf16[128,1024]{1,0:T(8,128)(2,1)} %get-tuple-element.276), channel_id=1, source_target_pairs={{0,8},{4,12},{8,0},{12,4},{16,24},{20,28},{24,16},{28,20},{1,9},{5... | collective-permute-start | bytes 786440 | tf_op jit(solution)/shard_map/ppermute | solution.py:1197
  574.8 8.5 %copy-start.23 = (bf16[128,1024]{1,0:T(8,128)(2,1)}, bf16[128,1024]{1,0:T(8,128)(2,1)S(1)}, u32[]{:S(2)}) copy-start(bf16[128,1024]{1,0:T(8,128)(2,1)S(1)} %add_convert_fusion.6.refs_0_) | copy-start | bytes 786436
  574.8 23.3 %collective-permute-start.41 = (bf16[128,1024]{1,0:T(8,128)(2,1)S(1)}, bf16[128,1024]{1,0:T(8,128)(2,1)S(1)}, u32[]{:S(2)}, u32[]{:S(2)}) collective-permute-start(bf16[128,1024]{1,0:T(8,128)(2,1)S(1)} %add_convert_fusion.6.refs_0_), channel_id=1, source_target_pairs={{0,8},{4,12},{8,0},{12,4},{16,24},{20,28},{24,16},{28,20},{1,9},{5... | collective-permute-start | bytes 786440 | tf_op jit(solution)/shard_map/ppermute | solution.py:1197
  574.9 23.2 %collective-permute-start.42 = (bf16[128,1024]{1,0:T(8,128)(2,1)S(1)}, bf16[128,1024]{1,0:T(8,128)(2,1)S(1)}, u32[]{:S(2)}, u32[]{:S(2)}) collective-permute-start(bf16[128,1024]{1,0:T(8,128)(2,1)S(1)} %add_convert_fusion.6.refs_0_), channel_id=1, source_target_pairs={{0,16},{4,20},{8,24},{12,28},{16,0},{20,4},{24,8},{28,12},{1,17},{... | collective-permute-start | bytes 786440 | tf_op jit(solution)/shard_map/ppermute | solution.py:1197
  577.8 20.3 %collective-permute-start.43 = (bf16[128,1024]{1,0:T(8,128)(2,1)S(1)}, bf16[128,1024]{1,0:T(8,128)(2,1)S(1)}, u32[]{:S(2)}, u32[]{:S(2)}) collective-permute-start(bf16[128,1024]{1,0:T(8,128)(2,1)S(1)} %add_convert_fusion.6.refs_0_), channel_id=1, source_target_pairs={{0,24},{4,28},{8,16},{12,20},{16,8},{20,12},{24,0},{28,4},{1,25},{... | collective-permute-start | bytes 786440 | tf_op jit(solution)/shard_map/ppermute | solution.py:1197
  601.9 23.0 %collective-permute-start.50 = (bf16[512,1024]{1,0:T(8,128)(2,1)}, bf16[512,1024]{1,0:T(8,128)(2,1)S(1)}, u32[]{:S(2)}, u32[]{:S(2)}) collective-permute-start(bf16[512,1024]{1,0:T(8,128)(2,1)} %stack_step.3.even_ref), channel_id=1, source_target_pairs={{0,4},{4,0},{8,12},{12,8},{16,20},{20,16},{24,28},{28,24},{1,5},{5... | collective-permute-start | bytes 3145736 | tf_op jit(solution)/shard_map/ppermute | solution.py:1197
  603.3 5.0 collective-permute-start.46
  608.3 5.9 collective-permute-start.47
  614.3 4.0 collective-permute-start.48
  618.3 1.2 collective-permute-start.49
  (24 other events, 44.4 us)

commit v9 on v6

--- a/solution.py
+++ b/solution.py
@@ -75,13 +75,11 @@
     return low(jnp.where(lane < HD, widen(head), extra))
 
 
-def query_columns(head, first, slope, apart, log_total=None):
+def query_columns(head, first, slope, apart):
     count = head.shape[0]
     lane, place = lanes(count), places(count, first)
     extra = pick3(jnp.where(lane < 67, lane - 64, lane - 67), split3(slope))
     extra = jnp.where(lane < 70, extra, 0.0)
-    if log_total is not None:
-        extra = jnp.where((lane >= 70) & (lane < 73), pick3(lane - 70, split3(log_total)), extra)
     extra = jnp.where(lane == 73, jnp.where(place >= SHORT, apart, 0.0), extra)
     return low(jnp.where(lane < HD, widen(head), extra))
 
@@ -109,7 +107,7 @@
 
 
 def attend_kernel(
-    me_ref, apart_ref, slope_ref, q_ref, k_ref, v_ref, o_ref, lse_ref, qa, ka, va, *, slots, pair, tile
+    me_ref, apart_ref, slope_ref, q_ref, k_ref, v_ref, o_ref, qa, ka, va, *, slots, pair, tile
 ):
     me = me_ref[0]
     total = q_ref.shape[0]
@@ -131,6 +129,7 @@
         jnp.int32, (tile, tile), 0
     )
     piece = min(rows, tile)
+    lane = lanes(tile)
 
     def query_tile(index, _):
         first = pl.multiple_of(index * tile, tile)
@@ -161,7 +160,10 @@
             top, mix = carry[s]
             weight = mix[:, HD : HD + 1]
             outs.append(mix[:, :HD] * (1.0 / weight))
-            lse_ref[s, 0, pl.ds(first, tile)] = (top + jnp.log2(weight))[:, 0]
+            log_total = pick3(lane - 70, split3(top + jnp.log2(weight)))
+            qa[s, pl.ds(first, tile), :] = low(
+                jnp.where((lane >= 70) & (lane < 73), log_total, queries[s].astype(F32))
+            )
         out = low(jnp.concatenate(outs, axis=1))
         for part in range(tile // piece):
             block = (index * (tile // piece) + part) // (rows // piece)
@@ -185,13 +187,15 @@
         in_specs=[scalars] * 3 + [spec] * 3,
         out_specs=[
             pl.BlockSpec((total, cols), lambda g: (0, 0)),
-            pl.BlockSpec((pair, 1, total), lambda g: (0, 0, 0)),
+            pl.BlockSpec((pair, total, 128), lambda g: (0, 0, 0)),
+            pl.BlockSpec((pair, total, 128), lambda g: (0, 0, 0)),
         ],
         out_shape=[
             jax.ShapeDtypeStruct((total, cols), BF16),
-            jax.ShapeDtypeStruct((pair, 1, total), F32),
+            jax.ShapeDtypeStruct((pair, total, 128), BF16),
+            jax.ShapeDtypeStruct((pair, total, 128), BF16),
         ],
-        scratch_shapes=[pltpu.VMEM((pair, total, 128), BF16)] * 3,
+        scratch_shapes=[pltpu.VMEM((pair, total, 128), BF16)],
         compiler_params=pltpu.CompilerParams(vmem_limit_bytes=56 << 20),
         cost_estimate=pl.CostEstimate(
             flops=pair * 1200 * total * total, transcendentals=0, bytes_accessed=8 * total * cols
@@ -201,26 +205,21 @@
 
 
 def attend_back_kernel(*refs, slots, pair, tile, key_tile):
-    me_ref, apart_ref, slope_ref, q_ref, k_ref, v_ref, o_ref, lse_ref = refs[:8]
-    g_refs = refs[8 : 8 + slots]
-    out_ref, qa, ka, va, ga, kt, dq_sum = refs[8 + slots :]
+    me_ref, qa, ka, v_ref, o_ref = refs[:5]
+    g_refs = refs[5 : 5 + slots]
+    out_ref, va, ga, kt, dq_sum = refs[5 + slots :]
     cols = pair * HD
     me = me_ref[0]
-    total = q_ref.shape[0]
+    total = v_ref.shape[0]
     rows = total // slots
     chunk = min(rows, 512)
-    apart = apart_ref[0].astype(F32)
 
     def prepare(slot, inner, spot, place):
         place = pl.multiple_of(place, chunk)
         home = pl.ds(place, chunk)
         for s in range(pair):
             mine = slice(s * HD, (s + 1) * HD)
-            log_total = lse_ref[s, :, home].T
-            qa[s, home, :] = query_columns(q_ref[spot, mine], place, slope_ref[s], apart, log_total)
-            keys = key_columns(k_ref[spot, mine], place)
-            ka[s, home, :] = keys
-            kt[s, :, home] = low(keys.astype(F32).T)
+            kt[s, :, home] = low(ka[s, home, :].astype(F32).T)
             va[s, home, :] = ones_columns(v_ref[spot, mine], 3)
             grad = g_refs[slot][inner, mine]
             row_dot = jnp.sum(
@@ -299,45 +298,31 @@
     each_chunk(me, slots, rows, finish)
 
 
-def attend_back(
-    me, apart, slopes, queries, key_rows, values, mixed, log_total, grads, group, tile=1024, key_tile=512
-):
+def attend_back(me, columns, values, mixed, grads, group, tile=1024, key_tile=512):
     slots = len(grads)
-    total, width = queries.shape
-    pair = min(2, width // HD)
+    total, width = values.shape
+    pair = columns[0].shape[0]
     cols = pair * HD
-    spec = pl.BlockSpec((total, cols), lambda g: (0, group))
     out_spec = pl.BlockSpec((total, cols), lambda g: (0, 0))
-    scalars = pl.BlockSpec(memory_space=pltpu.SMEM)
+    column_spec = pl.BlockSpec((pair, total, 128), lambda g: (0, 0, 0))
     return pl.pallas_call(
         functools.partial(
             attend_back_kernel, slots=slots, pair=pair, tile=tile, key_tile=key_tile
         ),
         grid=(1,),
-        in_specs=[scalars] * 3
-        + [spec] * 3
-        + [out_spec, pl.BlockSpec((pair, 1, total), lambda g: (0, 0, 0))]
+        in_specs=[pl.BlockSpec(memory_space=pltpu.SMEM), column_spec, column_spec]
+        + [pl.BlockSpec((total, cols), lambda g: (0, group)), out_spec]
         + [pl.BlockSpec((total // slots, cols), lambda g: (0, group))] * slots,
         out_specs=pl.BlockSpec((total, 3 * cols), lambda g: (0, 0)),
         out_shape=jax.ShapeDtypeStruct((total, 3 * cols), BF16),
-        scratch_shapes=[pltpu.VMEM((pair, total, 128), BF16)] * 4
+        scratch_shapes=[pltpu.VMEM((pair, total, 128), BF16)] * 2
         + [pltpu.VMEM((pair, 128, total), BF16), pltpu.VMEM((pair, 128, total), F32)],
         compiler_params=pltpu.CompilerParams(vmem_limit_bytes=60 << 20),
         cost_estimate=pl.CostEstimate(
             flops=pair * 2400 * total * total, transcendentals=0, bytes_accessed=16 * total * cols
         ),
         name="attend_back",
-    )(
-        me,
-        apart,
-        slopes[group * pair : (group + 1) * pair],
-        queries,
-        key_rows,
-        values,
-        mixed,
-        log_total,
-        *grads,
-    )
+    )(me, *columns, values, mixed, *grads)
 
 
 def whole(shape):
@@ -1165,9 +1150,9 @@
     slopes = jnp.exp2(-8.0 * (heads + 1).astype(F32) / HEADS) * LOG2E
     apart = (row_ids[:1] != row_ids[SHORT : SHORT + 1]).astype(jnp.int32)
 
-    mixed_own, log_totals, mixed_parts = [], [], []
+    mixed_own, columns, mixed_parts = [], [], []
     for group in range(groups):
-        mixed, log_total = attend(
+        mixed, *held_columns = attend(
             me_word,
             apart,
             slopes,
@@ -1178,7 +1163,7 @@
             group,
         )
         mixed_own.append(mixed)
-        log_totals.append(log_total)
+        columns.append(held_columns)
         if not group:
             keys = sorted(cot_held)
             held = lax.optimization_barrier((*[cot_held[key] for key in keys], mixed))[:-1]
@@ -1249,16 +1234,7 @@
 
     def backward(group):
         return attend_back(
-            me_word,
-            apart,
-            slopes,
-            queries,
-            key_rows,
-            values,
-            mixed_own[group],
-            log_totals[group],
-            mixed_grads,
-            group,
+            me_word, columns[group], values, mixed_own[group], mixed_grads, group
         )
 
     dense_sums = partner_sums(dense_even, dense_come)

time: 633 us -> 627 us (level)
    pallas_call x2, Pallas kernels: 140 us -> 129 us  [attend_back(): pl.pallas_call(functools.partial(attend_back_kernel, slots=slots, pair=pa...]
where the time goes in v9:
time: 627 us; the launch traced here: 618 us
  Pallas kernels  445 us (71%)
  waiting for transfers between devices  96.3 us (15%)
  starting transfers between devices  43.5 us (7%)
  local copies, waits for them, and re-layouts  17.6 us (3%)
  other arithmetic  12.4 us (2%)
    pallas_call x28, Pallas kernels, kernel_call(): pl.pallas_call(kernel, grid=grid, in_specs=in_specs + [pl.BlockSpec(memor...  238 us
    pallas_call x2, Pallas kernels, attend_back(): pl.pallas_call(functools.partial(attend_back_kernel, slots=slots, pair=pa...  129 us
    pallas_call x2, Pallas kernels, attend(): pl.pallas_call(functools.partial(attend_kernel, slots=slots, pair=pair, t...  77.9 us
    ppermute x30, waiting for transfers between devices, swap(): return lax.ppermute(array, 'tensor', [(i, i ^ mask) for i in range(slots)])  58.7 us
    ppermute x21, waiting for transfers between devices, swap_data(): return lax.ppermute(array, 'dp', [(i, i ^ mask) for i in range(streams)])  37.5 us
    ppermute x21, starting transfers between devices, swap_data(): return lax.ppermute(array, 'dp', [(i, i ^ mask) for i in range(streams)])  28.2 us
    ppermute x30, starting transfers between devices, swap(): return lax.ppermute(array, 'tensor', [(i, i ^ mask) for i in range(slots)])  15.3 us
    unnamed x72, local copies, waits for them, and re-layouts  14 us
  transfers between devices with their start and end apart: 51, of which 15 were waited for; matrix products, arithmetic and copies ran while one was open for 2% of the time, Pallas kernels for 63%

profile of v9, /device:TPU:0, one launch (start us, length us, event | category | flops | bytes accessed | tf_op | source)
XLA Modules:
  0.0 617.7 jit_solution(7793981573178650081)
XLA Ops:
  1.2 2.6 collective-permute-start
  3.8 1.4 collective-permute-done.1.refs_1_.refs_9_
  6.5 9.2 %project.2 = (bf16[4096,1024]{1,0:T(8,128)(2,1)}, bf16[4096,256]{1,0:T(8,128)(2,1)}, bf16[4096,256]{1,0:T(8,128)(2,1)}, bf16[4096,256]{1,0:T(8,128)(2,1)}) custom-call(bf16[1024,1024]{1,0:T(8,128)(2,1)} %refs_2_.23, bf16[1024,1024]{1,0:T(8,128)(2,1)} %copy-done.2, bf16[1024]{0:T(1024)(128)(2,1)} %refs_4_.17, bf16[1024]{0:T(1024)(128)(2,1)} %refs_2_.18, ...), custom_call_target="tpu_custom_call" | custom-call | flops 1 | bytes 1 | tf_op jit(solution)/shard_map/project/pallas_call | solution.py:360
  15.8 34.6 %collective-permute-done.refs_0_.refs_10_ = bf16[1024,1024]{1,0:T(8,128)(2,1)} collective-permute-done((bf16[1024,1024]{1,0:T(8,128)(2,1)}, bf16[1024,1024]{1,0:T(8,128)(2,1)}, u32[]{:S(2)}, u32[]{:S(2)}) %collective-permute-start) | collective-permute-done | bytes 2097184 | tf_op jit(solution)/shard_map/ppermute | solution.py:1069
  53.5 1.8 collective-permute-start.3
  55.5 9.3 %project.3 = (bf16[4096,1024]{1,0:T(8,128)(2,1)}, bf16[4096,256]{1,0:T(8,128)(2,1)}, bf16[4096,256]{1,0:T(8,128)(2,1)}, bf16[4096,256]{1,0:T(8,128)(2,1)}) custom-call(bf16[1024,1024]{1,0:T(8,128)(2,1)} %collective-permute-done.refs_0_.refs_10_, ...), custom_call_target="tpu_custom_call", output_to_operand_aliasing={{0}: (9, {}), {1}: (10, {}), {2}: (11, {}), {3}: (12, {})} | custom-call | flops 1 | bytes 1 | tf_op jit(solution)/shard_map/project/pallas_call | solution.py:360
  64.8 38.7 %attend.2 = (bf16[4096,128]{1,0:T(8,128)(2,1)}, bf16[2,4096,128]{2,1,0:T(8,128)(2,1)}, bf16[2,4096,128]{2,1,0:T(8,128)(2,1)}) custom-call(s32[1]{0:T(128)} %bitcast.1.me_ref.refs_0_, s32[1]{0:T(128)S(6)} %convert_element_type.84.apart_ref, f32[2]{0:T(128)} %get-tuple-element.306.slope_ref, bf16[4096,256]{1,0:T(8,128)(2,1)} %get-tuple-element.169.q_ref, ...), custom_call_target="tpu_custom_call" | custom-call | flops 40265318400 | bytes 4194304 | tf_op jit(solution)/shard_map/attend/pallas_call | solution.py:184
  103.4 1.8 collective-permute-start.6
  105.7 39.2 %attend.3 = (bf16[4096,128]{1,0:T(8,128)(2,1)}, bf16[2,4096,128]{2,1,0:T(8,128)(2,1)}, bf16[2,4096,128]{2,1,0:T(8,128)(2,1)}) custom-call(s32[1]{0:T(128)} %bitcast.1.me_ref.refs_0_, s32[1]{0:T(128)S(6)} %convert_element_type.84.apart_ref, f32[2]{0:T(128)} %get-tuple-element.305.slope_ref, bf16[4096,256]{1,0:T(8,128)(2,1)} %get-tuple-element.169.q_ref, ...), custom_call_target="tpu_custom_call" | custom-call | flops 40265318400 | bytes 4194304 | tf_op jit(solution)/shard_map/attend/pallas_call | solution.py:184
  147.9 15.3 %act_grad.1 = (bf16[4096,1024]{1,0:T(8,128)(2,1)}, bf16[4096,1024]{1,0:T(8,128)(2,1)}) custom-call(bf16[1024,1024]{1,0:T(8,128)(2,1)} %refs_3_.17, bf16[1024,1024]{1,0:T(8,128)(2,1)} %collective-permute-done.8.refs_1_, bf16[1024,1024]{1,0:T(8,128)(2,1)} %collective-permute-done.3.refs_2_, bf16[1024,1024]{1,0:T(8,128)(2,1)} %collective-permute-done.9.refs_3_, ...), custom_call_target="tpu_custom_call" | custom-call | flops 1 | bytes 1 | tf_op jit(solution)/shard_map/act_grad/pallas_call | solution.py:360
  163.2 7.0 %collective-permute-done.7.refs_5_ = bf16[4096,128]{1,0:T(8,128)(2,1)S(1)} collective-permute-done((bf16[4096,128]{1,0:T(8,128)(2,1)}, bf16[4096,128]{1,0:T(8,128)(2,1)S(1)}, u32[]{:S(2)}, u32[]{:S(2)}) %collective-permute-start.7) | collective-permute-done | bytes 1048608 | tf_op jit(solution)/shard_map/ppermute | solution.py:1069
  170.7 2.7 collective-permute-done.14.refs_13_.refs_6_
  176.2 22.8 %post_norm.1 = (bf16[4096,1024]{1,0:T(8,128)(2,1)}, f32[1024,1024]{1,0:T(8,128)}) custom-call(bf16[4096,128]{1,0:T(8,128)(2,1)} %get-tuple-element.166.refs_0_.refs_4_, bf16[4096,128]{1,0:T(8,128)(2,1)} %get-tuple-element.170.refs_1_.refs_4_, bf16[4096,128]{1,0:T(8,128)(2,1)} %copy-done.7, bf16[4096,128]{1,0:T(8,128)(2,1)} %copy-done.8, ...), custom_call_target="tpu_custom_call" | custom-call | flops 1 | bytes 1 | tf_op jit(solution)/shard_map/post_norm/pallas_call | solution.py:360
  199.0 11.7 %feed.4 = (bf16[4096,1024]{1,0:T(8,128)(2,1)}, bf16[4096,1024]{1,0:T(8,128)(2,1)}, f32[1,1024]{1,0:T(1,128)}, bf16[1024,1024]{1,0:T(8,128)(2,1)}) custom-call(bf16[4096,1024]{1,0:T(8,128)(2,1)} %get-tuple-element.179.refs_0_.right_ref, bf16[4096,1024]{1,0:T(8,128)(2,1)} %get-tuple-element.180.refs_1_, bf16[1024,1024]{1,0:T(8,128)(2,1)} %refs_2_.17, ...), custom_call_target="tpu_custom_call" | custom-call | flops 1 | bytes 1 | tf_op jit(solution)/shard_map/feed/pallas_call | solution.py:360
  211.0 11.6 %feed.5 = (bf16[4096,1024]{1,0:T(8,128)(2,1)}, bf16[4096,1024]{1,0:T(8,128)(2,1)}, f32[1,1024]{1,0:T(1,128)}, bf16[1024,1024]{1,0:T(8,128)(2,1)}) custom-call(bf16[4096,1024]{1,0:T(8,128)(2,1)} %get-tuple-element.179.refs_0_.right_ref, bf16[4096,1024]{1,0:T(8,128)(2,1)} %get-tuple-element.180.refs_1_, ...), custom_call_target="tpu_custom_call", output_to_operand_aliasing={{0}: (4, {}), {1}: (5, {})} | custom-call | flops 1 | bytes 1 | tf_op jit(solution)/shard_map/feed/pallas_call | solution.py:360
  222.8 1.3 copy-done.12
  224.1 12.6 %feed.6 = (bf16[4096,1024]{1,0:T(8,128)(2,1)}, bf16[4096,1024]{1,0:T(8,128)(2,1)}, f32[1,1024]{1,0:T(1,128)}, bf16[1024,1024]{1,0:T(8,128)(2,1)}) custom-call(bf16[4096,1024]{1,0:T(8,128)(2,1)} %get-tuple-element.179.refs_0_.right_ref, bf16[4096,1024]{1,0:T(8,128)(2,1)} %get-tuple-element.180.refs_1_, ...), custom_call_target="tpu_custom_call", output_to_operand_aliasing={{0}: (5, {}), {1}: (6, {})} | custom-call | flops 1 | bytes 1 | tf_op jit(solution)/shard_map/feed/pallas_call | solution.py:360
  238.3 13.0 %feed.7 = (bf16[4096,1024]{1,0:T(8,128)(2,1)}, bf16[4096,1024]{1,0:T(8,128)(2,1)}, f32[1,1024]{1,0:T(1,128)}, bf16[1024,1024]{1,0:T(8,128)(2,1)}) custom-call(bf16[4096,1024]{1,0:T(8,128)(2,1)} %get-tuple-element.179.refs_0_.right_ref, bf16[4096,1024]{1,0:T(8,128)(2,1)} %get-tuple-element.180.refs_1_, ...), custom_call_target="tpu_custom_call", output_to_operand_aliasing={{0}: (5, {}), {1}: (6, {})} | custom-call | flops 1 | bytes 1 | tf_op jit(solution)/shard_map/feed/pallas_call | solution.py:360
  251.3 13.3 %outer_step.2 = (bf16[512,1024]{1,0:T(8,128)(2,1)}, bf16[512,1024]{1,0:T(8,128)(2,1)}) custom-call(s32[1]{0:T(128)} %bitcast.me_ref, bf16[4096,1024]{1,0:T(8,128)(2,1)} %get-tuple-element.192.left_ref, bf16[4096,1024]{1,0:T(8,128)(2,1)} %get-tuple-element.179.refs_0_.right_ref), custom_call_target="tpu_custom_call" | custom-call | flops 1 | bytes 1 | tf_op jit(solution)/shard_map/outer_step/pallas_call | solution.py:360
  264.6 1.7 collective-permute-start.21
  266.3 13.3 %outer_step.3 = (bf16[512,1024]{1,0:T(8,128)(2,1)}, bf16[512,1024]{1,0:T(8,128)(2,1)}) custom-call(s32[1]{0:T(128)} %bitcast.me_ref, bf16[4096,1024]{1,0:T(8,128)(2,1)} %get-tuple-element.205.left_ref.active_ref, bf16[4096,1024]{1,0:T(8,128)(2,1)} %get-tuple-element.194.right_ref), custom_call_target="tpu_custom_call" | custom-call | flops 1 | bytes 1 | tf_op jit(solution)/shard_map/outer_step/pallas_call | solution.py:360
  279.9 5.0 collective-permute-done.17.refs_1_
  284.9 10.2 %resid_step.1 = (f32[1024,1024]{1,0:T(8,128)}, bf16[1024,1024]{1,0:T(8,128)(2,1)}, f32[8,1024]{1,0:T(8,128)}, bf16[1024,256]{1,0:T(8,128)(2,1)}, bf16[1024,256]{...) custom-call(bf16[1024,1024]{1,0:T(8,128)(2,1)} %get-tuple-element.196.refs_0_, ...), custom_call_target="tpu_custom_call" | custom-call | flops 1 | bytes 1 | tf_op jit(solution)/shard_map/resid_step/pallas_call | solution.py:360
  295.5 1.5 collective-permute-start.20
  297.0 6.0 dense_grad.1
  303.1 14.5 %ffn_step.1 = (bf16[2048,1024]{1,0:T(8,128)(2,1)}, bf16[2048,1024]{1,0:T(8,128)(2,1)}) custom-call(bf16[4096,1024]{1,0:T(8,128)(2,1)} %get-tuple-element.205.left_ref.active_ref, bf16[1024,1024]{1,0:T(8,128)(2,1)} %weight_ref.1), custom_call_target="tpu_custom_call" | custom-call | flops 1 | bytes 1 | tf_op jit(solution)/shard_map/ffn_step/pallas_call | solution.py:360
  319.5 3.7 pair_step.1
  323.6 3.6 collective-permute-start.27
  328.1 64.6 %attend_back.2.grad_ref.refs_0_ = bf16[4096,384]{1,0:T(8,128)(2,1)} custom-call(s32[1]{0:T(128)} %bitcast.1.me_ref.refs_0_, bf16[2,4096,128]{2,1,0:T(8,128)(2,1)} %get-tuple-element.164.refs_1_, bf16[2,4096,128]{2,1,0:T(8,128)(2,1)} %get-tuple-element.165.refs_2_, bf16[4096,256]{1,0:T(8,128)(2,1)} %get-tuple-element.163.v_ref.refs_3_, ...), custom_call_target="tpu_custom_call" | custom-call | flops 80530636800 | bytes 8388608 | tf_op jit(solution)/shard_map/attend_back/pallas_call | solution.py:308
  394.2 1.4 add_convert_fusion.3.refs_0_
  395.7 9.6 %weight_step.2 = (bf16[1024,384]{1,0:T(8,128)(2,1)}, f32[8,1024]{1,0:T(8,128)}, f32[1,384]{1,0:T(1,128)}) custom-call(s32[1]{0:T(128)} %bitcast.me_ref, bf16[4096,1024]{1,0:T(8,128)(2,1)} %get-tuple-element.160.normed_ref, bf16[4096,384]{1,0:T(8,128)(2,1)} %attend_back.2.grad_ref.refs_0_, bf16[1024,256]{1,0:T(8,128)(2,1)} %refs_5_.12, ...), custom_call_target="tpu_custom_call" | custom-call | flops 1 | bytes 1 | tf_op jit(solution)/shard_map/weight_step/pallas_call | solution.py:360
  405.3 3.2 collective-permute-done.24.refs_2_
  409.3 2.6 join_step.1
  411.9 4.6 add_convert_fusion.1
  417.7 2.9 collective-permute-start.31
  420.8 1.5 collective-permute-start.29
  422.8 64.9 %attend_back.3.grad_ref.refs_1_ = bf16[4096,384]{1,0:T(8,128)(2,1)} custom-call(s32[1]{0:T(128)} %bitcast.1.me_ref.refs_0_, bf16[2,4096,128]{2,1,0:T(8,128)(2,1)} %get-tuple-element.225.refs_1_, bf16[2,4096,128]{2,1,0:T(8,128)(2,1)} %get-tuple-element.226.refs_2_, bf16[4096,256]{1,0:T(8,128)(2,1)} %get-tuple-element.163.v_ref.refs_3_, ...), custom_call_target="tpu_custom_call" | custom-call | flops 80530636800 | bytes 8388608 | tf_op jit(solution)/shard_map/attend_back/pallas_call | solution.py:308
  487.8 9.7 %weight_step.3 = (bf16[512,384]{1,0:T(8,128)(2,1)}, bf16[512,384]{1,0:T(8,128)(2,1)}, f32[8,1024]{1,0:T(8,128)}, f32[1,384]{1,0:T(1,128)}) custom-call(s32[1]{0:T(128)} %bitcast.me_ref, bf16[4096,1024]{1,0:T(8,128)(2,1)} %get-tuple-element.160.normed_ref, bf16[4096,384]{1,0:T(8,128)(2,1)} %attend_back.3.grad_ref.refs_1_, bf16[1024,256]{1,0:T(8,128)(2,1)} %refs_5_.12, ...), custom_call_target="tpu_custom_call" | custom-call | flops 1 | bytes 1 | tf_op jit(solution)/shard_map/weight_step/pallas_call | solution.py:360
  497.9 1.5 pack.1
  499.4 1.7 collective-permute-start.35
  501.1 3.1 stack_step.2.even_ref
  504.2 4.4 collective-permute-done.35
  508.6 5.2 unproject.4
  513.8 5.3 unproject.5
  521.4 5.5 unproject.6
  526.9 1.5 collective-permute-start.44
  528.5 5.7 unproject.7.refs_0_
  534.1 2.5 late_step.1
  536.7 3.5 collective-permute-start.40
  541.1 7.0 %collective-permute-done.40 = bf16[128,1024]{1,0:T(8,128)(2,1)S(1)} collective-permute-done((bf16[128,1024]{1,0:T(8,128)(2,1)}, bf16[128,1024]{1,0:T(8,128)(2,1)S(1)}, u32[]{:S(2)}, u32[]{:S(2)}) %collective-permute-start.40) | collective-permute-done | bytes 262176 | tf_op jit(solution)/shard_map/ppermute | solution.py:1081
  548.0 13.4 %collective-permute-done.39 = bf16[128,1024]{1,0:T(8,128)(2,1)S(1)} collective-permute-done((bf16[128,1024]{1,0:T(8,128)(2,1)}, bf16[128,1024]{1,0:T(8,128)(2,1)S(1)}, u32[]{:S(2)}, u32[]{:S(2)}) %collective-permute-start.39) | collective-permute-done | bytes 262176 | tf_op jit(solution)/shard_map/ppermute | solution.py:1081
  562.7 2.9 collective-permute-start.42
  565.6 1.5 collective-permute-start.43
  567.0 4.1 add_convert_fusion
  571.1 7.1 %feed_grads.1 = (f32[1024,1024]{1,0:T(8,128)}, f32[1024,1024]{1,0:T(8,128)}) custom-call(s32[1]{0:T(128)} %bitcast.me_ref, bf16[1024,1024]{1,0:T(8,128)(2,1)} %stack_step.2.even_ref, bf16[1024,1024]{1,0:T(8,128)(2,1)} %collective-permute-done.45.odd_ref), custom_call_target="tpu_custom_call" | custom-call | flops 1 | bytes 1 | tf_op jit(solution)/shard_map/feed_grads/pallas_call | solution.py:360
  578.2 7.7 %input_step.1 = f32[1024,1024]{1,0:T(8,128)} custom-call(bf16[1024,1024]{1,0:T(8,128)(2,1)} %unproject.7.refs_0_, bf16[1024,1024]{1,0:T(8,128)(2,1)} %collective-permute-done.44.refs_1_, bf16[1024,1024]{1,0:T(8,128)(2,1)} %refs_2_.23, f32[1024,1024]{1,0:T(8,128)} %get-tuple-element.278.refs_3_, bf16[1024]{0:T(1024)(128)(2,1)} %refs_4_.17), custom_call_target="tpu_custom_call" | custom-call | flops 1 | bytes 1 | tf_op jit(solution)/shard_map/input_step/pallas_call | solution.py:360
  587.4 2.2 stack_step.3.even_ref
  589.6 1.5 collective-permute-start.50
  592.3 3.8 collective-permute-done.46
  596.1 1.8 collective-permute-start.47
  597.8 4.1 collective-permute-done.47
  602.6 3.4 collective-permute-done.48
  607.8 4.8 collective-permute-done.50.odd_ref
  613.6 4.0 spread.1
  (160 shorter events, 31.9 us)
Async XLA Ops:
  0.7 52.8 %copy-start.1 = (bf16[1024,1024]{1,0:T(8,128)(2,1)S(1)}, bf16[1024,1024]{1,0:T(8,128)(2,1)}, u32[]{:S(2)}) copy-start(bf16[1024,1024]{1,0:T(8,128)(2,1)} %refs_3_.17) | copy-start | bytes 6291460
  0.7 54.6 %copy-start.15 = (bf16[256,1024]{1,0:T(8,128)(2,1)S(1)}, bf16[256,1024]{1,0:T(8,128)(2,1)}, u32[]{:S(2)}) copy-start(bf16[256,1024]{1,0:T(8,128)(2,1)} %refs_5_.8) | copy-start | bytes 1572868
  0.7 4.5 collective-permute-start.1
  1.2 49.1 %collective-permute-start = (bf16[1024,1024]{1,0:T(8,128)(2,1)}, bf16[1024,1024]{1,0:T(8,128)(2,1)}, u32[]{:S(2)}, u32[]{:S(2)}) collective-permute-start(bf16[1024,1024]{1,0:T(8,128)(2,1)} %refs_2_.23), channel_id=1, source_target_pairs={{0,2},{1,3},{2,0},{3,1},{4,6},{5,7},{6,4},{7,5},{8,10},{9,11},{10,... | collective-permute-start | bytes 6291464 | tf_op jit(solution)/shard_map/ppermute | solution.py:1069
  50.3 5.2 collective-permute-start.2
  53.5 51.7 %collective-permute-start.3 = (bf16[1024,1024]{1,0:T(8,128)(2,1)S(1)}, bf16[1024,1024]{1,0:T(8,128)(2,1)}, u32[]{:S(2)}, u32[]{:S(2)}) collective-permute-start(bf16[1024,1024]{1,0:T(8,128)(2,1)S(1)} %copy-done.1), channel_id=1, source_target_pairs={{0,2},{1,3},{2,0},{3,1},{4,6},{5,7},{6,4},{7,5},{8,10},{9,11},{10,... | collective-permute-start | bytes 6291464 | tf_op jit(solution)/shard_map/ppermute | solution.py:1069
  55.2 89.9 %collective-permute-start.10 = (bf16[256,1024]{1,0:T(8,128)(2,1)S(1)}, bf16[256,1024]{1,0:T(8,128)(2,1)S(1)}, u32[]{:S(2)}, u32[]{:S(2)}) collective-permute-start(bf16[256,1024]{1,0:T(8,128)(2,1)S(1)} %copy-done.15), channel_id=1, source_target_pairs={{0,2},{1,3},{2,0},{3,1},{4,6},{5,7},{6,4},{7,5},{8,10},{9,11},{10,... | collective-permute-start | bytes 1572872 | tf_op jit(solution)/shard_map/ppermute | solution.py:1069
  103.4 43.9 %collective-permute-start.6 = (bf16[4096,128]{1,0:T(8,128)(2,1)}, bf16[4096,128]{1,0:T(8,128)(2,1)S(1)}, u32[]{:S(2)}, u32[]{:S(2)}) collective-permute-start(bf16[4096,128]{1,0:T(8,128)(2,1)} %get-tuple-element.166.refs_0_.refs_4_), channel_id=1, source_target_pairs={{0,2},{1,3},{2,0},{3,1},{4,6},{5,7},{6,4},{7,5},{8,10},{9,11},{10,... | collective-permute-start | bytes 3145736 | tf_op jit(solution)/shard_map/ppermute | solution.py:1069
  105.2 42.7 %collective-permute-start.9 = (bf16[1024,1024]{1,0:T(8,128)(2,1)}, bf16[1024,1024]{1,0:T(8,128)(2,1)}, u32[]{:S(2)}, u32[]{:S(2)}) collective-permute-start(bf16[1024,1024]{1,0:T(8,128)(2,1)} %collective-permute-done.3.refs_2_), channel_id=1, source_target_pairs={{0,1},{1,0},{2,3},{3,2},{4,5},{5,4},{6,7},{7,6},{8,9},{9,8},{10,11... | collective-permute-start | bytes 6291464 | tf_op jit(solution)/shard_map/ppermute | solution.py:1069
  105.2 42.6 %collective-permute-start.8 = (bf16[1024,1024]{1,0:T(8,128)(2,1)S(1)}, bf16[1024,1024]{1,0:T(8,128)(2,1)}, u32[]{:S(2)}, u32[]{:S(2)}) collective-permute-start(bf16[1024,1024]{1,0:T(8,128)(2,1)S(1)} %copy-done.1), channel_id=1, source_target_pairs={{0,1},{1,0},{2,3},{3,2},{4,5},{5,4},{6,7},{7,6},{8,9},{9,8},{10,11... | collective-permute-start | bytes 6291464 | tf_op jit(solution)/shard_map/ppermute | solution.py:1069
  105.7 41.5 %copy-start.4 = (bf16[4096,128]{1,0:T(8,128)(2,1)S(1)}, bf16[4096,128]{1,0:T(8,128)(2,1)}, u32[]{:S(2)}) copy-start(bf16[4096,128]{1,0:T(8,128)(2,1)} %get-tuple-element.166.refs_0_.refs_4_) | copy-start | bytes 3145732
  144.9 25.3 %collective-permute-start.7 = (bf16[4096,128]{1,0:T(8,128)(2,1)}, bf16[4096,128]{1,0:T(8,128)(2,1)S(1)}, u32[]{:S(2)}, u32[]{:S(2)}) collective-permute-start(bf16[4096,128]{1,0:T(8,128)(2,1)} %get-tuple-element.170.refs_1_.refs_4_), channel_id=1, source_target_pairs={{0,2},{1,3},{2,0},{3,1},{4,6},{5,7},{6,4},{7,5},{8,10},{9,11},{10,... | collective-permute-start | bytes 3145736 | tf_op jit(solution)/shard_map/ppermute | solution.py:1069
  145.2 2.0 collective-permute-start.11
  147.2 26.2 %collective-permute-start.4 = (bf16[4096,128]{1,0:T(8,128)(2,1)S(1)}, bf16[4096,128]{1,0:T(8,128)(2,1)S(1)}, u32[]{:S(2)}, u32[]{:S(2)}) collective-permute-start(bf16[4096,128]{1,0:T(8,128)(2,1)S(1)} %copy-done.4), channel_id=1, source_target_pairs={{0,1},{1,0},{2,3},{3,2},{4,5},{5,4},{6,7},{7,6},{8,9},{9,8},{10,11... | collective-permute-start | bytes 3145736 | tf_op jit(solution)/shard_map/ppermute | solution.py:1069
  147.4 15.8 %copy-start.5 = (bf16[4096,128]{1,0:T(8,128)(2,1)}, bf16[4096,128]{1,0:T(8,128)(2,1)S(1)}, u32[]{:S(2)}) copy-start(bf16[4096,128]{1,0:T(8,128)(2,1)S(1)} %collective-permute-done.6.refs_4_) | copy-start | bytes 3145732
  147.4 26.1 %collective-permute-start.5 = (bf16[4096,128]{1,0:T(8,128)(2,1)}, bf16[4096,128]{1,0:T(8,128)(2,1)S(1)}, u32[]{:S(2)}, u32[]{:S(2)}) collective-permute-start(bf16[4096,128]{1,0:T(8,128)(2,1)} %get-tuple-element.170.refs_1_.refs_4_), channel_id=1, source_target_pairs={{0,1},{1,0},{2,3},{3,2},{4,5},{5,4},{6,7},{7,6},{8,9},{9,8},{10,11... | collective-permute-start | bytes 3145736 | tf_op jit(solution)/shard_map/ppermute | solution.py:1069
  147.7 25.7 %collective-permute-start.12 = (bf16[4096,128]{1,0:T(8,128)(2,1)S(1)}, bf16[4096,128]{1,0:T(8,128)(2,1)S(1)}, u32[]{:S(2)}, u32[]{:S(2)}) collective-permute-start(bf16[4096,128]{1,0:T(8,128)(2,1)S(1)} %collective-permute-done.6.refs_4_), channel_id=1, source_target_pairs={{0,1},{1,0},{2,3},{3,2},{4,5},{5,4},{6,7},{7,6},{8,9},{9,8},{10,11... | collective-permute-start | bytes 3145736 | tf_op jit(solution)/shard_map/ppermute | solution.py:1069
  170.2 3.4 collective-permute-start.13
  170.2 3.2 collective-permute-start.14
  210.7 12.1 %collective-permute-start.16 = (bf16[1024,1024]{1,0:T(8,128)(2,1)}, bf16[1024,1024]{1,0:T(8,128)(2,1)S(1)}, u32[]{:S(2)}, u32[]{:S(2)}) collective-permute-start(bf16[1024,1024]{1,0:T(8,128)(2,1)} %get-tuple-element.184), channel_id=1, source_target_pairs={{0,1},{1,0},{2,3},{3,2},{4,5},{5,4},{6,7},{7,6},{8,9},{9,8},{10,11... | collective-permute-start | bytes 6291464 | tf_op jit(solution)/shard_map/ppermute | solution.py:1069
  222.6 14.4 %collective-permute-start.15 = (bf16[1024,1024]{1,0:T(8,128)(2,1)}, bf16[1024,1024]{1,0:T(8,128)(2,1)S(1)}, u32[]{:S(2)}, u32[]{:S(2)}) collective-permute-start(bf16[1024,1024]{1,0:T(8,128)(2,1)} %get-tuple-element.183), channel_id=1, source_target_pairs={{0,1},{1,0},{2,3},{3,2},{4,5},{5,4},{6,7},{7,6},{8,9},{9,8},{10,11... | collective-permute-start | bytes 6291464 | tf_op jit(solution)/shard_map/ppermute | solution.py:1069
  236.7 48.2 %collective-permute-start.17 = (bf16[1024,1024]{1,0:T(8,128)(2,1)}, bf16[1024,1024]{1,0:T(8,128)(2,1)}, u32[]{:S(2)}, u32[]{:S(2)}) collective-permute-start(bf16[1024,1024]{1,0:T(8,128)(2,1)} %get-tuple-element.197), channel_id=1, source_target_pairs={{0,2},{1,3},{2,0},{3,1},{4,6},{5,7},{6,4},{7,5},{8,10},{9,11},{10,... | collective-permute-start | bytes 6291464 | tf_op jit(solution)/shard_map/ppermute | solution.py:1069
  264.6 53.0 %collective-permute-start.21 = (bf16[512,1024]{1,0:T(8,128)(2,1)}, bf16[512,1024]{1,0:T(8,128)(2,1)S(1)}, u32[]{:S(2)}, u32[]{:S(2)}) collective-permute-start(bf16[512,1024]{1,0:T(8,128)(2,1)} %get-tuple-element.208), channel_id=1, source_target_pairs={{0,4},{4,0},{8,12},{12,8},{16,20},{20,16},{24,28},{28,24},{1,5},{5... | collective-permute-start | bytes 3145736 | tf_op jit(solution)/shard_map/ppermute | solution.py:1081
  279.6 38.0 %collective-permute-start.22 = (bf16[512,1024]{1,0:T(8,128)(2,1)}, bf16[512,1024]{1,0:T(8,128)(2,1)S(1)}, u32[]{:S(2)}, u32[]{:S(2)}) collective-permute-start(bf16[512,1024]{1,0:T(8,128)(2,1)} %get-tuple-element.209), channel_id=1, source_target_pairs={{0,4},{4,0},{8,12},{12,8},{16,20},{20,16},{24,28},{28,24},{1,5},{5... | collective-permute-start | bytes 3145736 | tf_op jit(solution)/shard_map/ppermute | solution.py:1081
  295.1 28.1 %collective-permute-start.18 = (bf16[1024,256]{1,0:T(8,128)(2,1)}, bf16[1024,256]{1,0:T(8,128)(2,1)S(1)}, u32[]{:S(2)}, u32[]{:S(2)}) collective-permute-start(bf16[1024,256]{1,0:T(8,128)(2,1)} %get-tuple-element.200), channel_id=1, source_target_pairs={{0,1},{1,0},{2,3},{3,2},{4,5},{5,4},{6,7},{7,6},{8,9},{9,8},{10,11... | collective-permute-start | bytes 1572872 | tf_op jit(solution)/shard_map/ppermute | solution.py:1069
  295.1 28.0 %collective-permute-start.19 = (bf16[1024,256]{1,0:T(8,128)(2,1)}, bf16[1024,256]{1,0:T(8,128)(2,1)S(1)}, u32[]{:S(2)}, u32[]{:S(2)}) collective-permute-start(bf16[1024,256]{1,0:T(8,128)(2,1)} %get-tuple-element.201), channel_id=1, source_target_pairs={{0,2},{1,3},{2,0},{3,1},{4,6},{5,7},{6,4},{7,5},{8,10},{9,11},{10,... | collective-permute-start | bytes 1572872 | tf_op jit(solution)/shard_map/ppermute | solution.py:1069
  295.5 27.7 %collective-permute-start.20 = (bf16[1024,256]{1,0:T(8,128)(2,1)}, bf16[1024,256]{1,0:T(8,128)(2,1)S(1)}, u32[]{:S(2)}, u32[]{:S(2)}) collective-permute-start(bf16[1024,256]{1,0:T(8,128)(2,1)} %get-tuple-element.202), channel_id=1, source_target_pairs={{0,3},{1,2},{2,1},{3,0},{4,7},{5,6},{6,5},{7,4},{8,11},{9,10},{10,... | collective-permute-start | bytes 1572872 | tf_op jit(solution)/shard_map/ppermute | solution.py:1069
  323.2 69.5 %collective-permute-start.23 = (bf16[2048,256]{1,0:T(8,128)(2,1)}, bf16[2048,256]{1,0:T(8,128)(2,1)S(1)}, u32[]{:S(2)}, u32[]{:S(2)}) collective-permute-start(bf16[2048,256]{1,0:T(8,128)(2,1)} %get-tuple-element.219), channel_id=1, source_target_pairs={{0,1},{1,0},{2,3},{3,2},{4,5},{5,4},{6,7},{7,6},{8,9},{9,8},{10,11... | collective-permute-start | bytes 3145736 | tf_op jit(solution)/shard_map/ppermute | solution.py:1069
  323.6 70.6 %collective-permute-start.27 = (bf16[256,1024]{1,0:T(8,128)(2,1)}, bf16[256,1024]{1,0:T(8,128)(2,1)S(1)}, u32[]{:S(2)}, u32[]{:S(2)}) collective-permute-start(bf16[256,1024]{1,0:T(8,128)(2,1)} %get-tuple-element.235), channel_id=1, source_target_pairs={{0,24},{4,28},{8,16},{12,20},{16,8},{20,12},{24,0},{28,4},{1,25},{... | collective-permute-start | bytes 1572872 | tf_op jit(solution)/shard_map/ppermute | solution.py:1081
  327.2 67.0 %collective-permute-start.26 = (bf16[256,1024]{1,0:T(8,128)(2,1)}, bf16[256,1024]{1,0:T(8,128)(2,1)S(1)}, u32[]{:S(2)}, u32[]{:S(2)}) collective-permute-start(bf16[256,1024]{1,0:T(8,128)(2,1)} %get-tuple-element.234), channel_id=1, source_target_pairs={{0,16},{4,20},{8,24},{12,28},{16,0},{20,4},{24,8},{28,12},{1,17},{... | collective-permute-start | bytes 1572872 | tf_op jit(solution)/shard_map/ppermute | solution.py:1081
  327.2 67.0 %collective-permute-start.25 = (bf16[256,1024]{1,0:T(8,128)(2,1)}, bf16[256,1024]{1,0:T(8,128)(2,1)}, u32[]{:S(2)}, u32[]{:S(2)}) collective-permute-start(bf16[256,1024]{1,0:T(8,128)(2,1)} %get-tuple-element.233), channel_id=1, source_target_pairs={{0,8},{4,12},{8,0},{12,4},{16,24},{20,28},{24,16},{28,20},{1,9},{5... | collective-permute-start | bytes 1572872 | tf_op jit(solution)/shard_map/ppermute | solution.py:1081
  328.0 83.9 %collective-permute-start.28 = (bf16[2048,1024]{1,0:T(8,128)(2,1)}, bf16[2048,1024]{1,0:T(8,128)(2,1)}, u32[]{:S(2)}, u32[]{:S(2)}) collective-permute-start(bf16[2048,1024]{1,0:T(8,128)(2,1)} %get-tuple-element.237), channel_id=1, source_target_pairs={{0,1},{1,0},{2,3},{3,2},{4,5},{5,4},{6,7},{7,6},{8,9},{9,8},{10,11... | collective-permute-start | bytes 12582920 | tf_op jit(solution)/shard_map/ppermute | solution.py:1069
  328.0 64.7 %copy-start.18 = (bf16[2048,256]{1,0:T(8,128)(2,1)S(1)}, bf16[2048,256]{1,0:T(8,128)(2,1)}, u32[]{:S(2)}) copy-start(bf16[2048,256]{1,0:T(8,128)(2,1)} %get-tuple-element.218) | copy-start | bytes 3145732
  393.9 14.5 %collective-permute-start.24 = (bf16[1024,256]{1,0:T(8,128)(2,1)}, bf16[1024,256]{1,0:T(8,128)(2,1)S(1)}, u32[]{:S(2)}, u32[]{:S(2)}) collective-permute-start(bf16[1024,256]{1,0:T(8,128)(2,1)} %get-tuple-element.223), channel_id=1, source_target_pairs={{0,2},{1,3},{2,0},{3,1},{4,6},{5,7},{6,4},{7,5},{8,10},{9,11},{10,... | collective-permute-start | bytes 1572872 | tf_op jit(solution)/shard_map/ppermute | solution.py:1069
  395.7 25.0 %copy-start.14 = (bf16[256,1024]{1,0:T(8,128)(2,1)}, bf16[256,1024]{1,0:T(8,128)(2,1)S(1)}, u32[]{:S(2)}) copy-start(bf16[256,1024]{1,0:T(8,128)(2,1)S(1)} %add_convert_fusion.3.refs_0_) | copy-start | bytes 1572868
  395.7 16.2 %copy-start.3 = (bf16[2048,1024]{1,0:T(8,128)(2,1)S(1)}, bf16[2048,1024]{1,0:T(8,128)(2,1)}, u32[]{:S(2)}) copy-start(bf16[2048,1024]{1,0:T(8,128)(2,1)} %get-tuple-element.236) | copy-start | bytes 12582916
  416.4 71.3 %collective-permute-start.30 = (bf16[256,1024]{1,0:T(8,128)(2,1)S(1)}, bf16[256,1024]{1,0:T(8,128)(2,1)S(1)}, u32[]{:S(2)}, u32[]{:S(2)}) collective-permute-start(bf16[256,1024]{1,0:T(8,128)(2,1)S(1)} %add_convert_fusion.3.refs_0_), channel_id=1, source_target_pairs={{0,8},{4,12},{8,0},{12,4},{16,24},{20,28},{24,16},{28,20},{1,9},{5... | collective-permute-start | bytes 1572872 | tf_op jit(solution)/shard_map/ppermute | solution.py:1081
  417.7 70.0 %collective-permute-start.31 = (bf16[256,1024]{1,0:T(8,128)(2,1)S(1)}, bf16[256,1024]{1,0:T(8,128)(2,1)}, u32[]{:S(2)}, u32[]{:S(2)}) collective-permute-start(bf16[256,1024]{1,0:T(8,128)(2,1)S(1)} %add_convert_fusion.3.refs_0_), channel_id=1, source_target_pairs={{0,16},{4,20},{8,24},{12,28},{16,0},{20,4},{24,8},{28,12},{1,17},{... | collective-permute-start | bytes 1572872 | tf_op jit(solution)/shard_map/ppermute | solution.py:1081
  420.6 67.1 %collective-permute-start.32 = (bf16[256,1024]{1,0:T(8,128)(2,1)S(1)}, bf16[256,1024]{1,0:T(8,128)(2,1)}, u32[]{:S(2)}, u32[]{:S(2)}) collective-permute-start(bf16[256,1024]{1,0:T(8,128)(2,1)S(1)} %add_convert_fusion.3.refs_0_), channel_id=1, source_target_pairs={{0,24},{4,28},{8,16},{12,20},{16,8},{20,12},{24,0},{28,4},{1,25},{... | collective-permute-start | bytes 1572872 | tf_op jit(solution)/shard_map/ppermute | solution.py:1081
  420.8 66.9 %collective-permute-start.29 = (bf16[512,640]{1,0:T(8,128)(2,1)}, bf16[512,640]{1,0:T(8,128)(2,1)S(1)}, u32[]{:S(2)}, u32[]{:S(2)}) collective-permute-start(bf16[512,640]{1,0:T(8,128)(2,1)} %get-tuple-element.242), channel_id=1, source_target_pairs={{0,4},{4,0},{8,12},{12,8},{16,20},{20,16},{24,28},{28,24},{1,5},{5... | collective-permute-start | bytes 1966088 | tf_op jit(solution)/shard_map/ppermute | solution.py:1081
  422.3 65.4 %collective-permute-start.33 = (bf16[1024,1024]{1,0:T(8,128)(2,1)}, bf16[1024,1024]{1,0:T(8,128)(2,1)}, u32[]{:S(2)}, u32[]{:S(2)}) collective-permute-start(bf16[1024,1024]{1,0:T(8,128)(2,1)} %get-tuple-element.245), channel_id=1, source_target_pairs={{0,2},{1,3},{2,0},{3,1},{4,6},{5,7},{6,4},{7,5},{8,10},{9,11},{10,... | collective-permute-start | bytes 6291464 | tf_op jit(solution)/shard_map/ppermute | solution.py:1069
  487.7 9.8 %copy-start.26 = (bf16[256,1024]{1,0:T(8,128)(2,1)}, bf16[256,1024]{1,0:T(8,128)(2,1)S(1)}, u32[]{:S(2)}) copy-start(bf16[256,1024]{1,0:T(8,128)(2,1)S(1)} %collective-permute-done.30.refs_1_) | copy-start | bytes 1572868
  487.7 9.8 %copy-start.23 = (bf16[512,640]{1,0:T(8,128)(2,1)}, bf16[512,640]{1,0:T(8,128)(2,1)S(1)}, u32[]{:S(2)}) copy-start(bf16[512,640]{1,0:T(8,128)(2,1)S(1)} %collective-permute-done.29.refs_1_) | copy-start | bytes 1966084
  497.5 11.1 %collective-permute-start.34 = (bf16[512,384]{1,0:T(8,128)(2,1)}, bf16[512,384]{1,0:T(8,128)(2,1)S(1)}, u32[]{:S(2)}, u32[]{:S(2)}) collective-permute-start(bf16[512,384]{1,0:T(8,128)(2,1)} %get-tuple-element.263), channel_id=1, source_target_pairs={{0,4},{4,0},{8,12},{12,8},{16,20},{20,16},{24,28},{28,24},{1,5},{5... | collective-permute-start | bytes 1179656 | tf_op jit(solution)/shard_map/ppermute | solution.py:1081
  499.4 9.2 %copy-start.28 = (f32[16,1024]{1,0:T(8,128)S(1)}, f32[16,1024]{1,0:T(8,128)}, u32[]{:S(2)}) copy-start(f32[16,1024]{1,0:T(8,128)} %pack.1) | copy-start | bytes 196612
  499.4 9.2 %collective-permute-start.35 = (f32[16,1024]{1,0:T(8,128)}, f32[16,1024]{1,0:T(8,128)S(1)}, u32[]{:S(2)}, u32[]{:S(2)}) collective-permute-start(f32[16,1024]{1,0:T(8,128)} %pack.1), channel_id=1, source_target_pairs={{0,4},{4,0},{8,12},{12,8},{16,20},{20,16},{24,28},{28,24},{1,5},{5... | collective-permute-start | bytes 196616 | tf_op jit(solution)/shard_map/ppermute | solution.py:1081
  513.8 6.3 %collective-permute-start.36 = (bf16[1024,1024]{1,0:T(8,128)(2,1)}, bf16[1024,1024]{1,0:T(8,128)(2,1)S(1)}, u32[]{:S(2)}, u32[]{:S(2)}) collective-permute-start(bf16[1024,1024]{1,0:T(8,128)(2,1)} %unproject.4), channel_id=1, source_target_pairs={{0,1},{1,0},{2,3},{3,2},{4,5},{5,4},{6,7},{7,6},{8,9},{9,8},{10,11... | collective-permute-start | bytes 6291464 | tf_op jit(solution)/shard_map/ppermute | solution.py:1069
  519.1 9.4 %collective-permute-start.37 = (bf16[1024,1024]{1,0:T(8,128)(2,1)}, bf16[1024,1024]{1,0:T(8,128)(2,1)}, u32[]{:S(2)}, u32[]{:S(2)}) collective-permute-start(bf16[1024,1024]{1,0:T(8,128)(2,1)} %unproject.5), channel_id=1, source_target_pairs={{0,1},{1,0},{2,3},{3,2},{4,5},{5,4},{6,7},{7,6},{8,9},{9,8},{10,11... | collective-permute-start | bytes 6291464 | tf_op jit(solution)/shard_map/ppermute | solution.py:1069
  519.6 51.6 %collective-permute-start.45 = (bf16[1024,1024]{1,0:T(8,128)(2,1)}, bf16[1024,1024]{1,0:T(8,128)(2,1)}, u32[]{:S(2)}, u32[]{:S(2)}) collective-permute-start(bf16[1024,1024]{1,0:T(8,128)(2,1)} %stack_step.2.even_ref), channel_id=1, source_target_pairs={{0,4},{4,0},{8,12},{12,8},{16,20},{20,16},{24,28},{28,24},{1,5},{5... | collective-permute-start | bytes 6291464 | tf_op jit(solution)/shard_map/ppermute | solution.py:1081
  526.9 51.3 %collective-permute-start.44 = (bf16[1024,1024]{1,0:T(8,128)(2,1)}, bf16[1024,1024]{1,0:T(8,128)(2,1)}, u32[]{:S(2)}, u32[]{:S(2)}) collective-permute-start(bf16[1024,1024]{1,0:T(8,128)(2,1)} %unproject.6), channel_id=1, source_target_pairs={{0,2},{1,3},{2,0},{3,1},{4,6},{5,7},{6,4},{7,5},{8,10},{9,11},{10,... | collective-permute-start | bytes 6291464 | tf_op jit(solution)/shard_map/ppermute | solution.py:1069
  528.5 38.6 %copy-start = (f32[1024,1024]{1,0:T(8,128)S(1)}, f32[1024,1024]{1,0:T(8,128)}, u32[]{:S(2)}) copy-start(f32[1024,1024]{1,0:T(8,128)} %get-tuple-element.198.refs_2_) | copy-start | bytes 12582916
  534.1 6.9 %copy-start.32 = (bf16[1024]{0:T(1024)(128)(2,1)S(1)}, bf16[1024]{0:T(1024)(128)(2,1)}, u32[]{:S(2)}) copy-start(bf16[1024]{0:T(1024)(128)(2,1)} %param.34) | copy-start | bytes 6148
  536.7 11.3 %collective-permute-start.40 = (bf16[128,1024]{1,0:T(8,128)(2,1)}, bf16[128,1024]{1,0:T(8,128)(2,1)S(1)}, u32[]{:S(2)}, u32[]{:S(2)}) collective-permute-start(bf16[128,1024]{1,0:T(8,128)(2,1)} %get-tuple-element.272), channel_id=1, source_target_pairs={{0,24},{4,28},{8,16},{12,20},{16,8},{20,12},{24,0},{28,4},{1,25},{... | collective-permute-start | bytes 786440 | tf_op jit(solution)/shard_map/ppermute | solution.py:1081
  540.2 21.2 %collective-permute-start.39 = (bf16[128,1024]{1,0:T(8,128)(2,1)}, bf16[128,1024]{1,0:T(8,128)(2,1)S(1)}, u32[]{:S(2)}, u32[]{:S(2)}) collective-permute-start(bf16[128,1024]{1,0:T(8,128)(2,1)} %get-tuple-element.271), channel_id=1, source_target_pairs={{0,16},{4,20},{8,24},{12,28},{16,0},{20,4},{24,8},{28,12},{1,17},{... | collective-permute-start | bytes 786440 | tf_op jit(solution)/shard_map/ppermute | solution.py:1081
  540.2 21.2 %collective-permute-start.38 = (bf16[128,1024]{1,0:T(8,128)(2,1)}, bf16[128,1024]{1,0:T(8,128)(2,1)S(1)}, u32[]{:S(2)}, u32[]{:S(2)}) collective-permute-start(bf16[128,1024]{1,0:T(8,128)(2,1)} %get-tuple-element.270), channel_id=1, source_target_pairs={{0,8},{4,12},{8,0},{12,4},{16,24},{20,28},{24,16},{28,20},{1,9},{5... | collective-permute-start | bytes 786440 | tf_op jit(solution)/shard_map/ppermute | solution.py:1081
  562.6 8.5 %copy-start.22 = (bf16[128,1024]{1,0:T(8,128)(2,1)}, bf16[128,1024]{1,0:T(8,128)(2,1)S(1)}, u32[]{:S(2)}) copy-start(bf16[128,1024]{1,0:T(8,128)(2,1)S(1)} %add_convert_fusion.6.refs_0_) | copy-start | bytes 786436
  562.6 23.3 %collective-permute-start.41 = (bf16[128,1024]{1,0:T(8,128)(2,1)S(1)}, bf16[128,1024]{1,0:T(8,128)(2,1)S(1)}, u32[]{:S(2)}, u32[]{:S(2)}) collective-permute-start(bf16[128,1024]{1,0:T(8,128)(2,1)S(1)} %add_convert_fusion.6.refs_0_), channel_id=1, source_target_pairs={{0,8},{4,12},{8,0},{12,4},{16,24},{20,28},{24,16},{28,20},{1,9},{5... | collective-permute-start | bytes 786440 | tf_op jit(solution)/shard_map/ppermute | solution.py:1081
  562.7 23.2 %collective-permute-start.42 = (bf16[128,1024]{1,0:T(8,128)(2,1)S(1)}, bf16[128,1024]{1,0:T(8,128)(2,1)S(1)}, u32[]{:S(2)}, u32[]{:S(2)}) collective-permute-start(bf16[128,1024]{1,0:T(8,128)(2,1)S(1)} %add_convert_fusion.6.refs_0_), channel_id=1, source_target_pairs={{0,16},{4,20},{8,24},{12,28},{16,0},{20,4},{24,8},{28,12},{1,17},{... | collective-permute-start | bytes 786440 | tf_op jit(solution)/shard_map/ppermute | solution.py:1081
  565.6 20.4 %collective-permute-start.43 = (bf16[128,1024]{1,0:T(8,128)(2,1)S(1)}, bf16[128,1024]{1,0:T(8,128)(2,1)S(1)}, u32[]{:S(2)}, u32[]{:S(2)}) collective-permute-start(bf16[128,1024]{1,0:T(8,128)(2,1)S(1)} %add_convert_fusion.6.refs_0_), channel_id=1, source_target_pairs={{0,24},{4,28},{8,16},{12,20},{16,8},{20,12},{24,0},{28,4},{1,25},{... | collective-permute-start | bytes 786440 | tf_op jit(solution)/shard_map/ppermute | solution.py:1081
  589.6 23.0 %collective-permute-start.50 = (bf16[512,1024]{1,0:T(8,128)(2,1)}, bf16[512,1024]{1,0:T(8,128)(2,1)S(1)}, u32[]{:S(2)}, u32[]{:S(2)}) collective-permute-start(bf16[512,1024]{1,0:T(8,128)(2,1)} %stack_step.3.even_ref), channel_id=1, source_target_pairs={{0,4},{4,0},{8,12},{12,8},{16,20},{20,16},{24,28},{28,24},{1,5},{5... | collective-permute-start | bytes 3145736 | tf_op jit(solution)/shard_map/ppermute | solution.py:1081
  591.1 4.9 collective-permute-start.46
  596.1 5.9 collective-permute-start.47
  602.0 4.0 collective-permute-start.48
  606.0 1.2 collective-permute-start.49
  (23 other events, 42.8 us)

commit v10 on v9

--- a/solution.py
+++ b/solution.py
@@ -451,7 +451,7 @@
 def post_norm(mixed, x_parts, weights, bias, gain, shift):
     slots, groups = len(mixed), len(mixed[0])
     rows, width = x_parts[0].shape
-    block = min(rows, 512)
+    block = min(rows, 1024)
     per = rows // block
     blocks = slots * per
     order = lambda i: (i + blocks // 2) % blocks

time: 627 us -> 628 us (level)
  no operation moved by 1% of the time
where the time goes in v10:
time: 628 us; the launch traced here: 618 us
  Pallas kernels  446 us (71%)
  waiting for transfers between devices  96.2 us (15%)
  starting transfers between devices  43.6 us (7%)
  local copies, waits for them, and re-layouts  17.6 us (3%)
  other arithmetic  12.4 us (2%)
    pallas_call x28, Pallas kernels, kernel_call(): pl.pallas_call(kernel, grid=grid, in_specs=in_specs + [pl.BlockSpec(memor...  238 us
    pallas_call x2, Pallas kernels, attend_back(): pl.pallas_call(functools.partial(attend_back_kernel, slots=slots, pair=pa...  129 us
    pallas_call x2, Pallas kernels, attend(): pl.pallas_call(functools.partial(attend_kernel, slots=slots, pair=pair, t...  77.9 us
    ppermute x30, waiting for transfers between devices, swap(): return lax.ppermute(array, 'tensor', [(i, i ^ mask) for i in range(slots)])  58.8 us
    ppermute x21, waiting for transfers between devices, swap_data(): return lax.ppermute(array, 'dp', [(i, i ^ mask) for i in range(streams)])  37.4 us
    ppermute x21, starting transfers between devices, swap_data(): return lax.ppermute(array, 'dp', [(i, i ^ mask) for i in range(streams)])  28.3 us
    ppermute x30, starting transfers between devices, swap(): return lax.ppermute(array, 'tensor', [(i, i ^ mask) for i in range(slots)])  15.3 us
    unnamed x72, local copies, waits for them, and re-layouts  14 us
  transfers between devices with their start and end apart: 51, of which 15 were waited for; matrix products, arithmetic and copies ran while one was open for 2% of the time, Pallas kernels for 63%

profile of v10, /device:TPU:0, one launch (start us, length us, event | category | flops | bytes accessed | tf_op | source)
XLA Modules:
  0.0 618.5 jit_solution(4048375833416779020)
XLA Ops:
  1.2 2.6 collective-permute-start
  3.8 1.4 collective-permute-done.1.refs_1_.refs_9_
  6.5 9.2 %project.2 = (bf16[4096,1024]{1,0:T(8,128)(2,1)}, bf16[4096,256]{1,0:T(8,128)(2,1)}, bf16[4096,256]{1,0:T(8,128)(2,1)}, bf16[4096,256]{1,0:T(8,128)(2,1)}) custom-call(bf16[1024,1024]{1,0:T(8,128)(2,1)} %refs_2_.23, bf16[1024,1024]{1,0:T(8,128)(2,1)} %copy-done.2, bf16[1024]{0:T(1024)(128)(2,1)} %refs_4_.17, bf16[1024]{0:T(1024)(128)(2,1)} %refs_2_.18, ...), custom_call_target="tpu_custom_call" | custom-call | flops 1 | bytes 1 | tf_op jit(solution)/shard_map/project/pallas_call | solution.py:360
  15.8 34.6 %collective-permute-done.refs_0_.refs_10_ = bf16[1024,1024]{1,0:T(8,128)(2,1)} collective-permute-done((bf16[1024,1024]{1,0:T(8,128)(2,1)}, bf16[1024,1024]{1,0:T(8,128)(2,1)}, u32[]{:S(2)}, u32[]{:S(2)}) %collective-permute-start) | collective-permute-done | bytes 2097184 | tf_op jit(solution)/shard_map/ppermute | solution.py:1069
  53.5 1.8 collective-permute-start.3
  55.5 9.3 %project.3 = (bf16[4096,1024]{1,0:T(8,128)(2,1)}, bf16[4096,256]{1,0:T(8,128)(2,1)}, bf16[4096,256]{1,0:T(8,128)(2,1)}, bf16[4096,256]{1,0:T(8,128)(2,1)}) custom-call(bf16[1024,1024]{1,0:T(8,128)(2,1)} %collective-permute-done.refs_0_.refs_10_, ...), custom_call_target="tpu_custom_call", output_to_operand_aliasing={{0}: (9, {}), {1}: (10, {}), {2}: (11, {}), {3}: (12, {})} | custom-call | flops 1 | bytes 1 | tf_op jit(solution)/shard_map/project/pallas_call | solution.py:360
  64.8 38.7 %attend.2 = (bf16[4096,128]{1,0:T(8,128)(2,1)}, bf16[2,4096,128]{2,1,0:T(8,128)(2,1)}, bf16[2,4096,128]{2,1,0:T(8,128)(2,1)}) custom-call(s32[1]{0:T(128)} %bitcast.1.me_ref.refs_0_, s32[1]{0:T(128)S(6)} %convert_element_type.84.apart_ref, f32[2]{0:T(128)} %get-tuple-element.306.slope_ref, bf16[4096,256]{1,0:T(8,128)(2,1)} %get-tuple-element.169.q_ref, ...), custom_call_target="tpu_custom_call" | custom-call | flops 40265318400 | bytes 4194304 | tf_op jit(solution)/shard_map/attend/pallas_call | solution.py:184
  103.4 1.8 collective-permute-start.6
  105.7 39.2 %attend.3 = (bf16[4096,128]{1,0:T(8,128)(2,1)}, bf16[2,4096,128]{2,1,0:T(8,128)(2,1)}, bf16[2,4096,128]{2,1,0:T(8,128)(2,1)}) custom-call(s32[1]{0:T(128)} %bitcast.1.me_ref.refs_0_, s32[1]{0:T(128)S(6)} %convert_element_type.84.apart_ref, f32[2]{0:T(128)} %get-tuple-element.305.slope_ref, bf16[4096,256]{1,0:T(8,128)(2,1)} %get-tuple-element.169.q_ref, ...), custom_call_target="tpu_custom_call" | custom-call | flops 40265318400 | bytes 4194304 | tf_op jit(solution)/shard_map/attend/pallas_call | solution.py:184
  147.9 15.3 %act_grad.1 = (bf16[4096,1024]{1,0:T(8,128)(2,1)}, bf16[4096,1024]{1,0:T(8,128)(2,1)}) custom-call(bf16[1024,1024]{1,0:T(8,128)(2,1)} %refs_3_.17, bf16[1024,1024]{1,0:T(8,128)(2,1)} %collective-permute-done.8.refs_1_, bf16[1024,1024]{1,0:T(8,128)(2,1)} %collective-permute-done.3.refs_2_, bf16[1024,1024]{1,0:T(8,128)(2,1)} %collective-permute-done.9.refs_3_, ...), custom_call_target="tpu_custom_call" | custom-call | flops 1 | bytes 1 | tf_op jit(solution)/shard_map/act_grad/pallas_call | solution.py:360
  163.2 7.0 %collective-permute-done.7.refs_5_ = bf16[4096,128]{1,0:T(8,128)(2,1)S(1)} collective-permute-done((bf16[4096,128]{1,0:T(8,128)(2,1)}, bf16[4096,128]{1,0:T(8,128)(2,1)S(1)}, u32[]{:S(2)}, u32[]{:S(2)}) %collective-permute-start.7) | collective-permute-done | bytes 1048608 | tf_op jit(solution)/shard_map/ppermute | solution.py:1069
  170.7 2.7 collective-permute-done.14.refs_13_.refs_6_
  176.2 23.2 %post_norm.1 = (bf16[4096,1024]{1,0:T(8,128)(2,1)}, f32[1024,1024]{1,0:T(8,128)}) custom-call(bf16[4096,128]{1,0:T(8,128)(2,1)} %get-tuple-element.166.refs_0_.refs_4_, bf16[4096,128]{1,0:T(8,128)(2,1)} %get-tuple-element.170.refs_1_.refs_4_, bf16[4096,128]{1,0:T(8,128)(2,1)} %copy-done.7, bf16[4096,128]{1,0:T(8,128)(2,1)} %copy-done.8, ...), custom_call_target="tpu_custom_call" | custom-call | flops 1 | bytes 1 | tf_op jit(solution)/shard_map/post_norm/pallas_call | solution.py:360
  199.4 11.7 %feed.4 = (bf16[4096,1024]{1,0:T(8,128)(2,1)}, bf16[4096,1024]{1,0:T(8,128)(2,1)}, f32[1,1024]{1,0:T(1,128)}, bf16[1024,1024]{1,0:T(8,128)(2,1)}) custom-call(bf16[4096,1024]{1,0:T(8,128)(2,1)} %get-tuple-element.179.refs_0_.right_ref, bf16[4096,1024]{1,0:T(8,128)(2,1)} %get-tuple-element.180.refs_1_, bf16[1024,1024]{1,0:T(8,128)(2,1)} %refs_2_.17, ...), custom_call_target="tpu_custom_call" | custom-call | flops 1 | bytes 1 | tf_op jit(solution)/shard_map/feed/pallas_call | solution.py:360
  211.4 11.6 %feed.5 = (bf16[4096,1024]{1,0:T(8,128)(2,1)}, bf16[4096,1024]{1,0:T(8,128)(2,1)}, f32[1,1024]{1,0:T(1,128)}, bf16[1024,1024]{1,0:T(8,128)(2,1)}) custom-call(bf16[4096,1024]{1,0:T(8,128)(2,1)} %get-tuple-element.179.refs_0_.right_ref, bf16[4096,1024]{1,0:T(8,128)(2,1)} %get-tuple-element.180.refs_1_, ...), custom_call_target="tpu_custom_call", output_to_operand_aliasing={{0}: (4, {}), {1}: (5, {})} | custom-call | flops 1 | bytes 1 | tf_op jit(solution)/shard_map/feed/pallas_call | solution.py:360
  223.2 1.3 copy-done.12
  224.5 12.8 %feed.6 = (bf16[4096,1024]{1,0:T(8,128)(2,1)}, bf16[4096,1024]{1,0:T(8,128)(2,1)}, f32[1,1024]{1,0:T(1,128)}, bf16[1024,1024]{1,0:T(8,128)(2,1)}) custom-call(bf16[4096,1024]{1,0:T(8,128)(2,1)} %get-tuple-element.179.refs_0_.right_ref, bf16[4096,1024]{1,0:T(8,128)(2,1)} %get-tuple-element.180.refs_1_, ...), custom_call_target="tpu_custom_call", output_to_operand_aliasing={{0}: (5, {}), {1}: (6, {})} | custom-call | flops 1 | bytes 1 | tf_op jit(solution)/shard_map/feed/pallas_call | solution.py:360
  238.9 12.6 %feed.7 = (bf16[4096,1024]{1,0:T(8,128)(2,1)}, bf16[4096,1024]{1,0:T(8,128)(2,1)}, f32[1,1024]{1,0:T(1,128)}, bf16[1024,1024]{1,0:T(8,128)(2,1)}) custom-call(bf16[4096,1024]{1,0:T(8,128)(2,1)} %get-tuple-element.179.refs_0_.right_ref, bf16[4096,1024]{1,0:T(8,128)(2,1)} %get-tuple-element.180.refs_1_, ...), custom_call_target="tpu_custom_call", output_to_operand_aliasing={{0}: (5, {}), {1}: (6, {})} | custom-call | flops 1 | bytes 1 | tf_op jit(solution)/shard_map/feed/pallas_call | solution.py:360
  251.4 13.3 %outer_step.2 = (bf16[512,1024]{1,0:T(8,128)(2,1)}, bf16[512,1024]{1,0:T(8,128)(2,1)}) custom-call(s32[1]{0:T(128)} %bitcast.me_ref, bf16[4096,1024]{1,0:T(8,128)(2,1)} %get-tuple-element.192.left_ref, bf16[4096,1024]{1,0:T(8,128)(2,1)} %get-tuple-element.179.refs_0_.right_ref), custom_call_target="tpu_custom_call" | custom-call | flops 1 | bytes 1 | tf_op jit(solution)/shard_map/outer_step/pallas_call | solution.py:360
  264.7 1.7 collective-permute-start.21
  266.5 13.7 %outer_step.3 = (bf16[512,1024]{1,0:T(8,128)(2,1)}, bf16[512,1024]{1,0:T(8,128)(2,1)}) custom-call(s32[1]{0:T(128)} %bitcast.me_ref, bf16[4096,1024]{1,0:T(8,128)(2,1)} %get-tuple-element.205.left_ref.active_ref, bf16[4096,1024]{1,0:T(8,128)(2,1)} %get-tuple-element.194.right_ref), custom_call_target="tpu_custom_call" | custom-call | flops 1 | bytes 1 | tf_op jit(solution)/shard_map/outer_step/pallas_call | solution.py:360
  280.4 5.1 collective-permute-done.17.refs_1_
  285.5 10.2 %resid_step.1 = (f32[1024,1024]{1,0:T(8,128)}, bf16[1024,1024]{1,0:T(8,128)(2,1)}, f32[8,1024]{1,0:T(8,128)}, bf16[1024,256]{1,0:T(8,128)(2,1)}, bf16[1024,256]{...) custom-call(bf16[1024,1024]{1,0:T(8,128)(2,1)} %get-tuple-element.196.refs_0_, ...), custom_call_target="tpu_custom_call" | custom-call | flops 1 | bytes 1 | tf_op jit(solution)/shard_map/resid_step/pallas_call | solution.py:360
  296.1 1.5 collective-permute-start.20
  297.6 5.9 dense_grad.1
  303.5 14.5 %ffn_step.1 = (bf16[2048,1024]{1,0:T(8,128)(2,1)}, bf16[2048,1024]{1,0:T(8,128)(2,1)}) custom-call(bf16[4096,1024]{1,0:T(8,128)(2,1)} %get-tuple-element.205.left_ref.active_ref, bf16[1024,1024]{1,0:T(8,128)(2,1)} %weight_ref.1), custom_call_target="tpu_custom_call" | custom-call | flops 1 | bytes 1 | tf_op jit(solution)/shard_map/ffn_step/pallas_call | solution.py:360
  320.0 3.7 pair_step.1
  324.1 3.6 collective-permute-start.27
  328.5 64.8 %attend_back.2.grad_ref.refs_0_ = bf16[4096,384]{1,0:T(8,128)(2,1)} custom-call(s32[1]{0:T(128)} %bitcast.1.me_ref.refs_0_, bf16[2,4096,128]{2,1,0:T(8,128)(2,1)} %get-tuple-element.164.refs_1_, bf16[2,4096,128]{2,1,0:T(8,128)(2,1)} %get-tuple-element.165.refs_2_, bf16[4096,256]{1,0:T(8,128)(2,1)} %get-tuple-element.163.v_ref.refs_3_, ...), custom_call_target="tpu_custom_call" | custom-call | flops 80530636800 | bytes 8388608 | tf_op jit(solution)/shard_map/attend_back/pallas_call | solution.py:308
  394.9 1.4 add_convert_fusion.3.refs_0_
  396.3 9.6 %weight_step.2 = (bf16[1024,384]{1,0:T(8,128)(2,1)}, f32[8,1024]{1,0:T(8,128)}, f32[1,384]{1,0:T(1,128)}) custom-call(s32[1]{0:T(128)} %bitcast.me_ref, bf16[4096,1024]{1,0:T(8,128)(2,1)} %get-tuple-element.160.normed_ref, bf16[4096,384]{1,0:T(8,128)(2,1)} %attend_back.2.grad_ref.refs_0_, bf16[1024,256]{1,0:T(8,128)(2,1)} %refs_5_.12, ...), custom_call_target="tpu_custom_call" | custom-call | flops 1 | bytes 1 | tf_op jit(solution)/shard_map/weight_step/pallas_call | solution.py:360
  405.9 3.2 collective-permute-done.24.refs_2_
  409.9 2.6 join_step.1
  412.5 4.6 add_convert_fusion.1
  418.3 2.9 collective-permute-start.31
  421.4 1.5 collective-permute-start.29
  423.4 64.7 %attend_back.3.grad_ref.refs_1_ = bf16[4096,384]{1,0:T(8,128)(2,1)} custom-call(s32[1]{0:T(128)} %bitcast.1.me_ref.refs_0_, bf16[2,4096,128]{2,1,0:T(8,128)(2,1)} %get-tuple-element.225.refs_1_, bf16[2,4096,128]{2,1,0:T(8,128)(2,1)} %get-tuple-element.226.refs_2_, bf16[4096,256]{1,0:T(8,128)(2,1)} %get-tuple-element.163.v_ref.refs_3_, ...), custom_call_target="tpu_custom_call" | custom-call | flops 80530636800 | bytes 8388608 | tf_op jit(solution)/shard_map/attend_back/pallas_call | solution.py:308
  488.2 9.7 %weight_step.3 = (bf16[512,384]{1,0:T(8,128)(2,1)}, bf16[512,384]{1,0:T(8,128)(2,1)}, f32[8,1024]{1,0:T(8,128)}, f32[1,384]{1,0:T(1,128)}) custom-call(s32[1]{0:T(128)} %bitcast.me_ref, bf16[4096,1024]{1,0:T(8,128)(2,1)} %get-tuple-element.160.normed_ref, bf16[4096,384]{1,0:T(8,128)(2,1)} %attend_back.3.grad_ref.refs_1_, bf16[1024,256]{1,0:T(8,128)(2,1)} %refs_5_.12, ...), custom_call_target="tpu_custom_call" | custom-call | flops 1 | bytes 1 | tf_op jit(solution)/shard_map/weight_step/pallas_call | solution.py:360
  498.3 1.5 pack.1
  499.9 1.7 collective-permute-start.35
  501.5 3.1 stack_step.2.even_ref
  504.6 4.4 collective-permute-done.35
  509.0 5.2 unproject.4
  514.2 5.4 unproject.5
  521.9 5.5 unproject.6
  527.4 1.5 collective-permute-start.44
  528.9 5.7 unproject.7.refs_0_
  534.6 2.5 late_step.1
  537.1 3.5 collective-permute-start.40
  541.5 7.0 %collective-permute-done.40 = bf16[128,1024]{1,0:T(8,128)(2,1)S(1)} collective-permute-done((bf16[128,1024]{1,0:T(8,128)(2,1)}, bf16[128,1024]{1,0:T(8,128)(2,1)S(1)}, u32[]{:S(2)}, u32[]{:S(2)}) %collective-permute-start.40) | collective-permute-done | bytes 262176 | tf_op jit(solution)/shard_map/ppermute | solution.py:1081
  548.5 13.4 %collective-permute-done.39 = bf16[128,1024]{1,0:T(8,128)(2,1)S(1)} collective-permute-done((bf16[128,1024]{1,0:T(8,128)(2,1)}, bf16[128,1024]{1,0:T(8,128)(2,1)S(1)}, u32[]{:S(2)}, u32[]{:S(2)}) %collective-permute-start.39) | collective-permute-done | bytes 262176 | tf_op jit(solution)/shard_map/ppermute | solution.py:1081
  563.1 2.9 collective-permute-start.42
  566.0 1.5 collective-permute-start.43
  567.5 4.1 add_convert_fusion
  571.6 7.1 %feed_grads.1 = (f32[1024,1024]{1,0:T(8,128)}, f32[1024,1024]{1,0:T(8,128)}) custom-call(s32[1]{0:T(128)} %bitcast.me_ref, bf16[1024,1024]{1,0:T(8,128)(2,1)} %stack_step.2.even_ref, bf16[1024,1024]{1,0:T(8,128)(2,1)} %collective-permute-done.45.odd_ref), custom_call_target="tpu_custom_call" | custom-call | flops 1 | bytes 1 | tf_op jit(solution)/shard_map/feed_grads/pallas_call | solution.py:360
  578.7 7.7 %input_step.1 = f32[1024,1024]{1,0:T(8,128)} custom-call(bf16[1024,1024]{1,0:T(8,128)(2,1)} %unproject.7.refs_0_, bf16[1024,1024]{1,0:T(8,128)(2,1)} %collective-permute-done.44.refs_1_, bf16[1024,1024]{1,0:T(8,128)(2,1)} %refs_2_.23, f32[1024,1024]{1,0:T(8,128)} %get-tuple-element.278.refs_3_, bf16[1024]{0:T(1024)(128)(2,1)} %refs_4_.17), custom_call_target="tpu_custom_call" | custom-call | flops 1 | bytes 1 | tf_op jit(solution)/shard_map/input_step/pallas_call | solution.py:360
  587.8 2.2 stack_step.3.even_ref
  590.1 1.5 collective-permute-start.50
  592.8 3.7 collective-permute-done.46
  596.6 1.8 collective-permute-start.47
  598.4 4.1 collective-permute-done.47
  603.1 3.4 collective-permute-done.48
  608.3 4.8 collective-permute-done.50.odd_ref
  614.1 4.0 spread.1
  (160 shorter events, 32.0 us)
Async XLA Ops:
  0.7 52.8 %copy-start.1 = (bf16[1024,1024]{1,0:T(8,128)(2,1)S(1)}, bf16[1024,1024]{1,0:T(8,128)(2,1)}, u32[]{:S(2)}) copy-start(bf16[1024,1024]{1,0:T(8,128)(2,1)} %refs_3_.17) | copy-start | bytes 6291460
  0.7 54.6 %copy-start.15 = (bf16[256,1024]{1,0:T(8,128)(2,1)S(1)}, bf16[256,1024]{1,0:T(8,128)(2,1)}, u32[]{:S(2)}) copy-start(bf16[256,1024]{1,0:T(8,128)(2,1)} %refs_5_.8) | copy-start | bytes 1572868
  0.7 4.5 collective-permute-start.1
  1.2 49.1 %collective-permute-start = (bf16[1024,1024]{1,0:T(8,128)(2,1)}, bf16[1024,1024]{1,0:T(8,128)(2,1)}, u32[]{:S(2)}, u32[]{:S(2)}) collective-permute-start(bf16[1024,1024]{1,0:T(8,128)(2,1)} %refs_2_.23), channel_id=1, source_target_pairs={{0,2},{1,3},{2,0},{3,1},{4,6},{5,7},{6,4},{7,5},{8,10},{9,11},{10,... | collective-permute-start | bytes 6291464 | tf_op jit(solution)/shard_map/ppermute | solution.py:1069
  50.3 5.2 collective-permute-start.2
  53.5 51.7 %collective-permute-start.3 = (bf16[1024,1024]{1,0:T(8,128)(2,1)S(1)}, bf16[1024,1024]{1,0:T(8,128)(2,1)}, u32[]{:S(2)}, u32[]{:S(2)}) collective-permute-start(bf16[1024,1024]{1,0:T(8,128)(2,1)S(1)} %copy-done.1), channel_id=1, source_target_pairs={{0,2},{1,3},{2,0},{3,1},{4,6},{5,7},{6,4},{7,5},{8,10},{9,11},{10,... | collective-permute-start | bytes 6291464 | tf_op jit(solution)/shard_map/ppermute | solution.py:1069
  55.2 89.9 %collective-permute-start.10 = (bf16[256,1024]{1,0:T(8,128)(2,1)S(1)}, bf16[256,1024]{1,0:T(8,128)(2,1)S(1)}, u32[]{:S(2)}, u32[]{:S(2)}) collective-permute-start(bf16[256,1024]{1,0:T(8,128)(2,1)S(1)} %copy-done.15), channel_id=1, source_target_pairs={{0,2},{1,3},{2,0},{3,1},{4,6},{5,7},{6,4},{7,5},{8,10},{9,11},{10,... | collective-permute-start | bytes 1572872 | tf_op jit(solution)/shard_map/ppermute | solution.py:1069
  103.4 43.9 %collective-permute-start.6 = (bf16[4096,128]{1,0:T(8,128)(2,1)}, bf16[4096,128]{1,0:T(8,128)(2,1)S(1)}, u32[]{:S(2)}, u32[]{:S(2)}) collective-permute-start(bf16[4096,128]{1,0:T(8,128)(2,1)} %get-tuple-element.166.refs_0_.refs_4_), channel_id=1, source_target_pairs={{0,2},{1,3},{2,0},{3,1},{4,6},{5,7},{6,4},{7,5},{8,10},{9,11},{10,... | collective-permute-start | bytes 3145736 | tf_op jit(solution)/shard_map/ppermute | solution.py:1069
  105.2 42.7 %collective-permute-start.9 = (bf16[1024,1024]{1,0:T(8,128)(2,1)}, bf16[1024,1024]{1,0:T(8,128)(2,1)}, u32[]{:S(2)}, u32[]{:S(2)}) collective-permute-start(bf16[1024,1024]{1,0:T(8,128)(2,1)} %collective-permute-done.3.refs_2_), channel_id=1, source_target_pairs={{0,1},{1,0},{2,3},{3,2},{4,5},{5,4},{6,7},{7,6},{8,9},{9,8},{10,11... | collective-permute-start | bytes 6291464 | tf_op jit(solution)/shard_map/ppermute | solution.py:1069
  105.2 42.6 %collective-permute-start.8 = (bf16[1024,1024]{1,0:T(8,128)(2,1)S(1)}, bf16[1024,1024]{1,0:T(8,128)(2,1)}, u32[]{:S(2)}, u32[]{:S(2)}) collective-permute-start(bf16[1024,1024]{1,0:T(8,128)(2,1)S(1)} %copy-done.1), channel_id=1, source_target_pairs={{0,1},{1,0},{2,3},{3,2},{4,5},{5,4},{6,7},{7,6},{8,9},{9,8},{10,11... | collective-permute-start | bytes 6291464 | tf_op jit(solution)/shard_map/ppermute | solution.py:1069
  105.7 41.5 %copy-start.4 = (bf16[4096,128]{1,0:T(8,128)(2,1)S(1)}, bf16[4096,128]{1,0:T(8,128)(2,1)}, u32[]{:S(2)}) copy-start(bf16[4096,128]{1,0:T(8,128)(2,1)} %get-tuple-element.166.refs_0_.refs_4_) | copy-start | bytes 3145732
  144.9 25.3 %collective-permute-start.7 = (bf16[4096,128]{1,0:T(8,128)(2,1)}, bf16[4096,128]{1,0:T(8,128)(2,1)S(1)}, u32[]{:S(2)}, u32[]{:S(2)}) collective-permute-start(bf16[4096,128]{1,0:T(8,128)(2,1)} %get-tuple-element.170.refs_1_.refs_4_), channel_id=1, source_target_pairs={{0,2},{1,3},{2,0},{3,1},{4,6},{5,7},{6,4},{7,5},{8,10},{9,11},{10,... | collective-permute-start | bytes 3145736 | tf_op jit(solution)/shard_map/ppermute | solution.py:1069
  145.2 2.0 collective-permute-start.11
  147.2 26.2 %collective-permute-start.4 = (bf16[4096,128]{1,0:T(8,128)(2,1)S(1)}, bf16[4096,128]{1,0:T(8,128)(2,1)S(1)}, u32[]{:S(2)}, u32[]{:S(2)}) collective-permute-start(bf16[4096,128]{1,0:T(8,128)(2,1)S(1)} %copy-done.4), channel_id=1, source_target_pairs={{0,1},{1,0},{2,3},{3,2},{4,5},{5,4},{6,7},{7,6},{8,9},{9,8},{10,11... | collective-permute-start | bytes 3145736 | tf_op jit(solution)/shard_map/ppermute | solution.py:1069
  147.4 15.8 %copy-start.5 = (bf16[4096,128]{1,0:T(8,128)(2,1)}, bf16[4096,128]{1,0:T(8,128)(2,1)S(1)}, u32[]{:S(2)}) copy-start(bf16[4096,128]{1,0:T(8,128)(2,1)S(1)} %collective-permute-done.6.refs_4_) | copy-start | bytes 3145732
  147.4 26.1 %collective-permute-start.5 = (bf16[4096,128]{1,0:T(8,128)(2,1)}, bf16[4096,128]{1,0:T(8,128)(2,1)S(1)}, u32[]{:S(2)}, u32[]{:S(2)}) collective-permute-start(bf16[4096,128]{1,0:T(8,128)(2,1)} %get-tuple-element.170.refs_1_.refs_4_), channel_id=1, source_target_pairs={{0,1},{1,0},{2,3},{3,2},{4,5},{5,4},{6,7},{7,6},{8,9},{9,8},{10,11... | collective-permute-start | bytes 3145736 | tf_op jit(solution)/shard_map/ppermute | solution.py:1069
  147.7 25.7 %collective-permute-start.12 = (bf16[4096,128]{1,0:T(8,128)(2,1)S(1)}, bf16[4096,128]{1,0:T(8,128)(2,1)S(1)}, u32[]{:S(2)}, u32[]{:S(2)}) collective-permute-start(bf16[4096,128]{1,0:T(8,128)(2,1)S(1)} %collective-permute-done.6.refs_4_), channel_id=1, source_target_pairs={{0,1},{1,0},{2,3},{3,2},{4,5},{5,4},{6,7},{7,6},{8,9},{9,8},{10,11... | collective-permute-start | bytes 3145736 | tf_op jit(solution)/shard_map/ppermute | solution.py:1069
  170.2 3.4 collective-permute-start.13
  170.2 3.2 collective-permute-start.14
  211.1 12.1 %collective-permute-start.16 = (bf16[1024,1024]{1,0:T(8,128)(2,1)}, bf16[1024,1024]{1,0:T(8,128)(2,1)S(1)}, u32[]{:S(2)}, u32[]{:S(2)}) collective-permute-start(bf16[1024,1024]{1,0:T(8,128)(2,1)} %get-tuple-element.184), channel_id=1, source_target_pairs={{0,1},{1,0},{2,3},{3,2},{4,5},{5,4},{6,7},{7,6},{8,9},{9,8},{10,11... | collective-permute-start | bytes 6291464 | tf_op jit(solution)/shard_map/ppermute | solution.py:1069
  223.0 14.5 %collective-permute-start.15 = (bf16[1024,1024]{1,0:T(8,128)(2,1)}, bf16[1024,1024]{1,0:T(8,128)(2,1)S(1)}, u32[]{:S(2)}, u32[]{:S(2)}) collective-permute-start(bf16[1024,1024]{1,0:T(8,128)(2,1)} %get-tuple-element.183), channel_id=1, source_target_pairs={{0,1},{1,0},{2,3},{3,2},{4,5},{5,4},{6,7},{7,6},{8,9},{9,8},{10,11... | collective-permute-start | bytes 6291464 | tf_op jit(solution)/shard_map/ppermute | solution.py:1069
  237.3 48.2 %collective-permute-start.17 = (bf16[1024,1024]{1,0:T(8,128)(2,1)}, bf16[1024,1024]{1,0:T(8,128)(2,1)}, u32[]{:S(2)}, u32[]{:S(2)}) collective-permute-start(bf16[1024,1024]{1,0:T(8,128)(2,1)} %get-tuple-element.197), channel_id=1, source_target_pairs={{0,2},{1,3},{2,0},{3,1},{4,6},{5,7},{6,4},{7,5},{8,10},{9,11},{10,... | collective-permute-start | bytes 6291464 | tf_op jit(solution)/shard_map/ppermute | solution.py:1069
  264.7 53.3 %collective-permute-start.21 = (bf16[512,1024]{1,0:T(8,128)(2,1)}, bf16[512,1024]{1,0:T(8,128)(2,1)S(1)}, u32[]{:S(2)}, u32[]{:S(2)}) collective-permute-start(bf16[512,1024]{1,0:T(8,128)(2,1)} %get-tuple-element.208), channel_id=1, source_target_pairs={{0,4},{4,0},{8,12},{12,8},{16,20},{20,16},{24,28},{28,24},{1,5},{5... | collective-permute-start | bytes 3145736 | tf_op jit(solution)/shard_map/ppermute | solution.py:1081
  280.2 37.9 %collective-permute-start.22 = (bf16[512,1024]{1,0:T(8,128)(2,1)}, bf16[512,1024]{1,0:T(8,128)(2,1)S(1)}, u32[]{:S(2)}, u32[]{:S(2)}) collective-permute-start(bf16[512,1024]{1,0:T(8,128)(2,1)} %get-tuple-element.209), channel_id=1, source_target_pairs={{0,4},{4,0},{8,12},{12,8},{16,20},{20,16},{24,28},{28,24},{1,5},{5... | collective-permute-start | bytes 3145736 | tf_op jit(solution)/shard_map/ppermute | solution.py:1081
  295.7 28.0 %collective-permute-start.18 = (bf16[1024,256]{1,0:T(8,128)(2,1)}, bf16[1024,256]{1,0:T(8,128)(2,1)S(1)}, u32[]{:S(2)}, u32[]{:S(2)}) collective-permute-start(bf16[1024,256]{1,0:T(8,128)(2,1)} %get-tuple-element.200), channel_id=1, source_target_pairs={{0,1},{1,0},{2,3},{3,2},{4,5},{5,4},{6,7},{7,6},{8,9},{9,8},{10,11... | collective-permute-start | bytes 1572872 | tf_op jit(solution)/shard_map/ppermute | solution.py:1069
  295.7 27.9 %collective-permute-start.19 = (bf16[1024,256]{1,0:T(8,128)(2,1)}, bf16[1024,256]{1,0:T(8,128)(2,1)S(1)}, u32[]{:S(2)}, u32[]{:S(2)}) collective-permute-start(bf16[1024,256]{1,0:T(8,128)(2,1)} %get-tuple-element.201), channel_id=1, source_target_pairs={{0,2},{1,3},{2,0},{3,1},{4,6},{5,7},{6,4},{7,5},{8,10},{9,11},{10,... | collective-permute-start | bytes 1572872 | tf_op jit(solution)/shard_map/ppermute | solution.py:1069
  296.1 27.5 %collective-permute-start.20 = (bf16[1024,256]{1,0:T(8,128)(2,1)}, bf16[1024,256]{1,0:T(8,128)(2,1)S(1)}, u32[]{:S(2)}, u32[]{:S(2)}) collective-permute-start(bf16[1024,256]{1,0:T(8,128)(2,1)} %get-tuple-element.202), channel_id=1, source_target_pairs={{0,3},{1,2},{2,1},{3,0},{4,7},{5,6},{6,5},{7,4},{8,11},{9,10},{10,... | collective-permute-start | bytes 1572872 | tf_op jit(solution)/shard_map/ppermute | solution.py:1069
  323.7 69.6 %collective-permute-start.23 = (bf16[2048,256]{1,0:T(8,128)(2,1)}, bf16[2048,256]{1,0:T(8,128)(2,1)S(1)}, u32[]{:S(2)}, u32[]{:S(2)}) collective-permute-start(bf16[2048,256]{1,0:T(8,128)(2,1)} %get-tuple-element.219), channel_id=1, source_target_pairs={{0,1},{1,0},{2,3},{3,2},{4,5},{5,4},{6,7},{7,6},{8,9},{9,8},{10,11... | collective-permute-start | bytes 3145736 | tf_op jit(solution)/shard_map/ppermute | solution.py:1069
  324.1 70.8 %collective-permute-start.27 = (bf16[256,1024]{1,0:T(8,128)(2,1)}, bf16[256,1024]{1,0:T(8,128)(2,1)S(1)}, u32[]{:S(2)}, u32[]{:S(2)}) collective-permute-start(bf16[256,1024]{1,0:T(8,128)(2,1)} %get-tuple-element.235), channel_id=1, source_target_pairs={{0,24},{4,28},{8,16},{12,20},{16,8},{20,12},{24,0},{28,4},{1,25},{... | collective-permute-start | bytes 1572872 | tf_op jit(solution)/shard_map/ppermute | solution.py:1081
  327.7 67.2 %collective-permute-start.26 = (bf16[256,1024]{1,0:T(8,128)(2,1)}, bf16[256,1024]{1,0:T(8,128)(2,1)S(1)}, u32[]{:S(2)}, u32[]{:S(2)}) collective-permute-start(bf16[256,1024]{1,0:T(8,128)(2,1)} %get-tuple-element.234), channel_id=1, source_target_pairs={{0,16},{4,20},{8,24},{12,28},{16,0},{20,4},{24,8},{28,12},{1,17},{... | collective-permute-start | bytes 1572872 | tf_op jit(solution)/shard_map/ppermute | solution.py:1081
  327.7 67.2 %collective-permute-start.25 = (bf16[256,1024]{1,0:T(8,128)(2,1)}, bf16[256,1024]{1,0:T(8,128)(2,1)}, u32[]{:S(2)}, u32[]{:S(2)}) collective-permute-start(bf16[256,1024]{1,0:T(8,128)(2,1)} %get-tuple-element.233), channel_id=1, source_target_pairs={{0,8},{4,12},{8,0},{12,4},{16,24},{20,28},{24,16},{28,20},{1,9},{5... | collective-permute-start | bytes 1572872 | tf_op jit(solution)/shard_map/ppermute | solution.py:1081
  328.5 84.0 %collective-permute-start.28 = (bf16[2048,1024]{1,0:T(8,128)(2,1)}, bf16[2048,1024]{1,0:T(8,128)(2,1)}, u32[]{:S(2)}, u32[]{:S(2)}) collective-permute-start(bf16[2048,1024]{1,0:T(8,128)(2,1)} %get-tuple-element.237), channel_id=1, source_target_pairs={{0,1},{1,0},{2,3},{3,2},{4,5},{5,4},{6,7},{7,6},{8,9},{9,8},{10,11... | collective-permute-start | bytes 12582920 | tf_op jit(solution)/shard_map/ppermute | solution.py:1069
  328.5 64.8 %copy-start.18 = (bf16[2048,256]{1,0:T(8,128)(2,1)S(1)}, bf16[2048,256]{1,0:T(8,128)(2,1)}, u32[]{:S(2)}) copy-start(bf16[2048,256]{1,0:T(8,128)(2,1)} %get-tuple-element.218) | copy-start | bytes 3145732
  394.5 14.5 %collective-permute-start.24 = (bf16[1024,256]{1,0:T(8,128)(2,1)}, bf16[1024,256]{1,0:T(8,128)(2,1)S(1)}, u32[]{:S(2)}, u32[]{:S(2)}) collective-permute-start(bf16[1024,256]{1,0:T(8,128)(2,1)} %get-tuple-element.223), channel_id=1, source_target_pairs={{0,2},{1,3},{2,0},{3,1},{4,6},{5,7},{6,4},{7,5},{8,10},{9,11},{10,... | collective-permute-start | bytes 1572872 | tf_op jit(solution)/shard_map/ppermute | solution.py:1069
  396.3 24.9 %copy-start.14 = (bf16[256,1024]{1,0:T(8,128)(2,1)}, bf16[256,1024]{1,0:T(8,128)(2,1)S(1)}, u32[]{:S(2)}) copy-start(bf16[256,1024]{1,0:T(8,128)(2,1)S(1)} %add_convert_fusion.3.refs_0_) | copy-start | bytes 1572868
  396.3 16.2 %copy-start.3 = (bf16[2048,1024]{1,0:T(8,128)(2,1)S(1)}, bf16[2048,1024]{1,0:T(8,128)(2,1)}, u32[]{:S(2)}) copy-start(bf16[2048,1024]{1,0:T(8,128)(2,1)} %get-tuple-element.236) | copy-start | bytes 12582916
  417.0 71.1 %collective-permute-start.30 = (bf16[256,1024]{1,0:T(8,128)(2,1)S(1)}, bf16[256,1024]{1,0:T(8,128)(2,1)S(1)}, u32[]{:S(2)}, u32[]{:S(2)}) collective-permute-start(bf16[256,1024]{1,0:T(8,128)(2,1)S(1)} %add_convert_fusion.3.refs_0_), channel_id=1, source_target_pairs={{0,8},{4,12},{8,0},{12,4},{16,24},{20,28},{24,16},{28,20},{1,9},{5... | collective-permute-start | bytes 1572872 | tf_op jit(solution)/shard_map/ppermute | solution.py:1081
  418.3 69.8 %collective-permute-start.31 = (bf16[256,1024]{1,0:T(8,128)(2,1)S(1)}, bf16[256,1024]{1,0:T(8,128)(2,1)}, u32[]{:S(2)}, u32[]{:S(2)}) collective-permute-start(bf16[256,1024]{1,0:T(8,128)(2,1)S(1)} %add_convert_fusion.3.refs_0_), channel_id=1, source_target_pairs={{0,16},{4,20},{8,24},{12,28},{16,0},{20,4},{24,8},{28,12},{1,17},{... | collective-permute-start | bytes 1572872 | tf_op jit(solution)/shard_map/ppermute | solution.py:1081
  421.2 66.9 %collective-permute-start.32 = (bf16[256,1024]{1,0:T(8,128)(2,1)S(1)}, bf16[256,1024]{1,0:T(8,128)(2,1)}, u32[]{:S(2)}, u32[]{:S(2)}) collective-permute-start(bf16[256,1024]{1,0:T(8,128)(2,1)S(1)} %add_convert_fusion.3.refs_0_), channel_id=1, source_target_pairs={{0,24},{4,28},{8,16},{12,20},{16,8},{20,12},{24,0},{28,4},{1,25},{... | collective-permute-start | bytes 1572872 | tf_op jit(solution)/shard_map/ppermute | solution.py:1081
  421.4 66.7 %collective-permute-start.29 = (bf16[512,640]{1,0:T(8,128)(2,1)}, bf16[512,640]{1,0:T(8,128)(2,1)S(1)}, u32[]{:S(2)}, u32[]{:S(2)}) collective-permute-start(bf16[512,640]{1,0:T(8,128)(2,1)} %get-tuple-element.242), channel_id=1, source_target_pairs={{0,4},{4,0},{8,12},{12,8},{16,20},{20,16},{24,28},{28,24},{1,5},{5... | collective-permute-start | bytes 1966088 | tf_op jit(solution)/shard_map/ppermute | solution.py:1081
  422.9 65.2 %collective-permute-start.33 = (bf16[1024,1024]{1,0:T(8,128)(2,1)}, bf16[1024,1024]{1,0:T(8,128)(2,1)}, u32[]{:S(2)}, u32[]{:S(2)}) collective-permute-start(bf16[1024,1024]{1,0:T(8,128)(2,1)} %get-tuple-element.245), channel_id=1, source_target_pairs={{0,2},{1,3},{2,0},{3,1},{4,6},{5,7},{6,4},{7,5},{8,10},{9,11},{10,... | collective-permute-start | bytes 6291464 | tf_op jit(solution)/shard_map/ppermute | solution.py:1069
  488.1 9.8 %copy-start.26 = (bf16[256,1024]{1,0:T(8,128)(2,1)}, bf16[256,1024]{1,0:T(8,128)(2,1)S(1)}, u32[]{:S(2)}) copy-start(bf16[256,1024]{1,0:T(8,128)(2,1)S(1)} %collective-permute-done.30.refs_1_) | copy-start | bytes 1572868
  488.1 9.8 %copy-start.23 = (bf16[512,640]{1,0:T(8,128)(2,1)}, bf16[512,640]{1,0:T(8,128)(2,1)S(1)}, u32[]{:S(2)}) copy-start(bf16[512,640]{1,0:T(8,128)(2,1)S(1)} %collective-permute-done.29.refs_1_) | copy-start | bytes 1966084
  497.9 11.1 %collective-permute-start.34 = (bf16[512,384]{1,0:T(8,128)(2,1)}, bf16[512,384]{1,0:T(8,128)(2,1)S(1)}, u32[]{:S(2)}, u32[]{:S(2)}) collective-permute-start(bf16[512,384]{1,0:T(8,128)(2,1)} %get-tuple-element.263), channel_id=1, source_target_pairs={{0,4},{4,0},{8,12},{12,8},{16,20},{20,16},{24,28},{28,24},{1,5},{5... | collective-permute-start | bytes 1179656 | tf_op jit(solution)/shard_map/ppermute | solution.py:1081
  499.9 9.1 %copy-start.28 = (f32[16,1024]{1,0:T(8,128)S(1)}, f32[16,1024]{1,0:T(8,128)}, u32[]{:S(2)}) copy-start(f32[16,1024]{1,0:T(8,128)} %pack.1) | copy-start | bytes 196612
  499.9 9.1 %collective-permute-start.35 = (f32[16,1024]{1,0:T(8,128)}, f32[16,1024]{1,0:T(8,128)S(1)}, u32[]{:S(2)}, u32[]{:S(2)}) collective-permute-start(f32[16,1024]{1,0:T(8,128)} %pack.1), channel_id=1, source_target_pairs={{0,4},{4,0},{8,12},{12,8},{16,20},{20,16},{24,28},{28,24},{1,5},{5... | collective-permute-start | bytes 196616 | tf_op jit(solution)/shard_map/ppermute | solution.py:1081
  514.2 6.4 %collective-permute-start.36 = (bf16[1024,1024]{1,0:T(8,128)(2,1)}, bf16[1024,1024]{1,0:T(8,128)(2,1)S(1)}, u32[]{:S(2)}, u32[]{:S(2)}) collective-permute-start(bf16[1024,1024]{1,0:T(8,128)(2,1)} %unproject.4), channel_id=1, source_target_pairs={{0,1},{1,0},{2,3},{3,2},{4,5},{5,4},{6,7},{7,6},{8,9},{9,8},{10,11... | collective-permute-start | bytes 6291464 | tf_op jit(solution)/shard_map/ppermute | solution.py:1069
  519.6 9.3 %collective-permute-start.37 = (bf16[1024,1024]{1,0:T(8,128)(2,1)}, bf16[1024,1024]{1,0:T(8,128)(2,1)}, u32[]{:S(2)}, u32[]{:S(2)}) collective-permute-start(bf16[1024,1024]{1,0:T(8,128)(2,1)} %unproject.5), channel_id=1, source_target_pairs={{0,1},{1,0},{2,3},{3,2},{4,5},{5,4},{6,7},{7,6},{8,9},{9,8},{10,11... | collective-permute-start | bytes 6291464 | tf_op jit(solution)/shard_map/ppermute | solution.py:1069
  520.0 51.5 %collective-permute-start.45 = (bf16[1024,1024]{1,0:T(8,128)(2,1)}, bf16[1024,1024]{1,0:T(8,128)(2,1)}, u32[]{:S(2)}, u32[]{:S(2)}) collective-permute-start(bf16[1024,1024]{1,0:T(8,128)(2,1)} %stack_step.2.even_ref), channel_id=1, source_target_pairs={{0,4},{4,0},{8,12},{12,8},{16,20},{20,16},{24,28},{28,24},{1,5},{5... | collective-permute-start | bytes 6291464 | tf_op jit(solution)/shard_map/ppermute | solution.py:1081
  527.4 51.3 %collective-permute-start.44 = (bf16[1024,1024]{1,0:T(8,128)(2,1)}, bf16[1024,1024]{1,0:T(8,128)(2,1)}, u32[]{:S(2)}, u32[]{:S(2)}) collective-permute-start(bf16[1024,1024]{1,0:T(8,128)(2,1)} %unproject.6), channel_id=1, source_target_pairs={{0,2},{1,3},{2,0},{3,1},{4,6},{5,7},{6,4},{7,5},{8,10},{9,11},{10,... | collective-permute-start | bytes 6291464 | tf_op jit(solution)/shard_map/ppermute | solution.py:1069
  528.9 38.6 %copy-start = (f32[1024,1024]{1,0:T(8,128)S(1)}, f32[1024,1024]{1,0:T(8,128)}, u32[]{:S(2)}) copy-start(f32[1024,1024]{1,0:T(8,128)} %get-tuple-element.198.refs_2_) | copy-start | bytes 12582916
  534.6 6.9 %copy-start.32 = (bf16[1024]{0:T(1024)(128)(2,1)S(1)}, bf16[1024]{0:T(1024)(128)(2,1)}, u32[]{:S(2)}) copy-start(bf16[1024]{0:T(1024)(128)(2,1)} %param.34) | copy-start | bytes 6148
  537.1 11.3 %collective-permute-start.40 = (bf16[128,1024]{1,0:T(8,128)(2,1)}, bf16[128,1024]{1,0:T(8,128)(2,1)S(1)}, u32[]{:S(2)}, u32[]{:S(2)}) collective-permute-start(bf16[128,1024]{1,0:T(8,128)(2,1)} %get-tuple-element.272), channel_id=1, source_target_pairs={{0,24},{4,28},{8,16},{12,20},{16,8},{20,12},{24,0},{28,4},{1,25},{... | collective-permute-start | bytes 786440 | tf_op jit(solution)/shard_map/ppermute | solution.py:1081
  540.7 21.2 %collective-permute-start.39 = (bf16[128,1024]{1,0:T(8,128)(2,1)}, bf16[128,1024]{1,0:T(8,128)(2,1)S(1)}, u32[]{:S(2)}, u32[]{:S(2)}) collective-permute-start(bf16[128,1024]{1,0:T(8,128)(2,1)} %get-tuple-element.271), channel_id=1, source_target_pairs={{0,16},{4,20},{8,24},{12,28},{16,0},{20,4},{24,8},{28,12},{1,17},{... | collective-permute-start | bytes 786440 | tf_op jit(solution)/shard_map/ppermute | solution.py:1081
  540.7 21.2 %collective-permute-start.38 = (bf16[128,1024]{1,0:T(8,128)(2,1)}, bf16[128,1024]{1,0:T(8,128)(2,1)S(1)}, u32[]{:S(2)}, u32[]{:S(2)}) collective-permute-start(bf16[128,1024]{1,0:T(8,128)(2,1)} %get-tuple-element.270), channel_id=1, source_target_pairs={{0,8},{4,12},{8,0},{12,4},{16,24},{20,28},{24,16},{28,20},{1,9},{5... | collective-permute-start | bytes 786440 | tf_op jit(solution)/shard_map/ppermute | solution.py:1081
  563.0 8.5 %copy-start.22 = (bf16[128,1024]{1,0:T(8,128)(2,1)}, bf16[128,1024]{1,0:T(8,128)(2,1)S(1)}, u32[]{:S(2)}) copy-start(bf16[128,1024]{1,0:T(8,128)(2,1)S(1)} %add_convert_fusion.6.refs_0_) | copy-start | bytes 786436
  563.0 23.3 %collective-permute-start.41 = (bf16[128,1024]{1,0:T(8,128)(2,1)S(1)}, bf16[128,1024]{1,0:T(8,128)(2,1)S(1)}, u32[]{:S(2)}, u32[]{:S(2)}) collective-permute-start(bf16[128,1024]{1,0:T(8,128)(2,1)S(1)} %add_convert_fusion.6.refs_0_), channel_id=1, source_target_pairs={{0,8},{4,12},{8,0},{12,4},{16,24},{20,28},{24,16},{28,20},{1,9},{5... | collective-permute-start | bytes 786440 | tf_op jit(solution)/shard_map/ppermute | solution.py:1081
  563.1 23.2 %collective-permute-start.42 = (bf16[128,1024]{1,0:T(8,128)(2,1)S(1)}, bf16[128,1024]{1,0:T(8,128)(2,1)S(1)}, u32[]{:S(2)}, u32[]{:S(2)}) collective-permute-start(bf16[128,1024]{1,0:T(8,128)(2,1)S(1)} %add_convert_fusion.6.refs_0_), channel_id=1, source_target_pairs={{0,16},{4,20},{8,24},{12,28},{16,0},{20,4},{24,8},{28,12},{1,17},{... | collective-permute-start | bytes 786440 | tf_op jit(solution)/shard_map/ppermute | solution.py:1081
  566.0 20.4 %collective-permute-start.43 = (bf16[128,1024]{1,0:T(8,128)(2,1)S(1)}, bf16[128,1024]{1,0:T(8,128)(2,1)S(1)}, u32[]{:S(2)}, u32[]{:S(2)}) collective-permute-start(bf16[128,1024]{1,0:T(8,128)(2,1)S(1)} %add_convert_fusion.6.refs_0_), channel_id=1, source_target_pairs={{0,24},{4,28},{8,16},{12,20},{16,8},{20,12},{24,0},{28,4},{1,25},{... | collective-permute-start | bytes 786440 | tf_op jit(solution)/shard_map/ppermute | solution.py:1081
  590.1 23.0 %collective-permute-start.50 = (bf16[512,1024]{1,0:T(8,128)(2,1)}, bf16[512,1024]{1,0:T(8,128)(2,1)S(1)}, u32[]{:S(2)}, u32[]{:S(2)}) collective-permute-start(bf16[512,1024]{1,0:T(8,128)(2,1)} %stack_step.3.even_ref), channel_id=1, source_target_pairs={{0,4},{4,0},{8,12},{12,8},{16,20},{20,16},{24,28},{28,24},{1,5},{5... | collective-permute-start | bytes 3145736 | tf_op jit(solution)/shard_map/ppermute | solution.py:1081
  591.6 5.0 collective-permute-start.46
  596.6 5.9 collective-permute-start.47
  602.5 4.0 collective-permute-start.48
  606.5 1.2 collective-permute-start.49
  (23 other events, 42.8 us)
